TPU v7x, 32 devices: a whole 2x2x4 slice. The times are simulated.
32 devices in a mesh: batch: 8 (over z, x), tok: 4 (over y, core).
Axes of the slice: x: 2, y: 2, z: 4, core: 2. Of those that a mesh axis runs over, the one named last changes fastest.
Arguments:
- patches: bfloat16 [24, 1024, 768], P('batch', 'tok'), may hold values from -6 to 6
- image_ids: int32 [24, 1024], P('batch', 'tok'), may hold values from -1 to 3, as said below
- cotangent: bfloat16 [24, 1024, 768], P('batch', 'tok'), may hold values from -6 to 6
- norm_gain: float32 [768], replicated, may hold values from 0.25 to 1.75
- query_gain: float32 [64], replicated, may hold values from 0.25 to 1.75
- key_gain: float32 [64], replicated, may hold values from 0.25 to 1.75
- in_weight: bfloat16 [768, 5376], P(('batch', 'tok')), may hold values from -0.21875 to 0.21875
- out_weight: bfloat16 [3840, 768], P(('batch', 'tok')), may hold values from -0.6538492 to 0.6538492
Outputs:
- block_out: bfloat16 [24, 1024, 768], P('batch', 'tok')
- patch_grad: bfloat16 [24, 1024, 768], P('batch', 'tok')
- norm_grad: float32 [768], replicated
- query_grad: float32 [64], replicated
- key_grad: float32 [64], replicated
- in_grad: float32 [768, 5376], P(('batch', 'tok'))
- out_grad: float32 [3840, 768], P(('batch', 'tok'))
Inputs may be any that keep to these rules, and one draw needn't show every extreme that they name: `image_ids`: in each sequence the ids of the live tokens run 0, 1, 2, 3 in contiguous non-decreasing runs (a run may be empty; the last image is never empty), followed by at least one padding slot of -1 at the end of the sequence.
All inputs are finite; a program needn't handle non-finite values.
Results may differ from a plain program's by a relative error of at most 0.0097.
Values may be sent and summed in bfloat16 or wider, within the bound.
No kernel may reach another device: no remote copies, remote signals or barrier semaphores. Data moves between devices by JAX's collectives and lax.ppermute only.
A program may use at most 192 MiB of HBM per device.

v0:
```python
import functools
import math

import jax
import jax.numpy as jnp
import numpy as np
from jax import lax
from jax.experimental import pallas as pl
from jax.experimental.pallas import tpu as pltpu
from jax.sharding import PartitionSpec as P

H = 12
HD = 64
SLOTS = 4
EPS = 1e-06
BIG = 2048.0
LOG2E = 1.4426950408889634
BF = jnp.bfloat16
F32 = jnp.float32
NN = (((1,), (0,)), ((), ()))
NT = (((1,), (1,)), ((), ()))
TN = (((0,), (0,)), ((), ()))
MIB = 1 << 20

VMEM = pl.BlockSpec(memory_space=pltpu.VMEM)
SMEM = pl.BlockSpec(memory_space=pltpu.SMEM)
ANY = pl.BlockSpec(memory_space=pl.ANY)


def mm(a, b, dims=NN):
    return lax.dot_general(a, b, dims, preferred_element_type=F32)


def normalize(values):
    center = values - jnp.mean(values, axis=-1, keepdims=True)
    inverse = lax.rsqrt(jnp.mean(center * center, axis=-1, keepdims=True) + EPS)
    return center * inverse, inverse


def norm_back(grad_unit, unit_rows, inverse):
    return inverse * (
        grad_unit
        - jnp.mean(grad_unit, axis=-1, keepdims=True)
        - unit_rows * jnp.mean(grad_unit * unit_rows, axis=-1, keepdims=True)
    )


def column(row):
    return jnp.broadcast_to(row, (8, row.shape[1])).T[:, 0:1]


def before_kernel(at_ref, table_ref, ids_ref, x_ref, cot_ref, gain_ref, win_ref, wout_ref, *outs):
    seqs, part, _ = x_ref.shape
    pays, (src_ref, *unit_refs) = outs[:seqs], outs[seqs:]
    nt, rows = src_ref.shape[0], win_ref.shape[0]
    local = H * HD // nt
    units = (win_ref.shape[1] - 3 * H * HD) // nt
    for k, ref in enumerate(unit_refs):
        ref[...] = wout_ref[table_ref[at_ref[0], k]]
    for t in range(nt):
        for k in range(3):
            src_ref[t, :rows, k * local : (k + 1) * local] = win_ref[:, k * H * HD + t * local : k * H * HD + (t + 1) * local]
        src_ref[t, :rows, 3 * local :] = win_ref[:, 3 * H * HD + t * units : 3 * H * HD + (t + 1) * units]
        for s in range(seqs):
            src_ref[t, rows:, s * part : (s + 1) * part] = ids_ref[s : s + 1, :].astype(F32).astype(BF)
        src_ref[t, rows:, seqs * part :] = jnp.zeros((1, 3 * local + units - seqs * part), BF)
    for s, pay in enumerate(pays):
        unit, _ = normalize(x_ref[s].astype(F32))
        live = column(jnp.where(ids_ref[s : s + 1, :] >= 0, 1.0, 0.0))
        pay[0] = (unit * gain_ref[...]).astype(BF)
        pay[1] = (live * cot_ref[s].astype(F32)).astype(BF)


def before(at, table, ids, x, cot, gain, w_in, w_out):
    seqs, part, dim = x.shape
    per, unit, _ = w_out.shape
    rows, wide = w_in.shape
    outs = [jax.ShapeDtypeStruct((2, part, dim), BF)] * seqs
    outs += [jax.ShapeDtypeStruct((SLOTS, rows + 1, wide // SLOTS), BF)]
    outs += [jax.ShapeDtypeStruct((unit, dim), BF)] * per
    return pl.pallas_call(
        before_kernel,
        out_shape=outs,
        in_specs=[SMEM] * 2 + [VMEM] * 6,
        out_specs=[VMEM] * len(outs),
        cost_estimate=pl.CostEstimate(flops=x.size * 8, transcendentals=0, bytes_accessed=x.size * 8),
        compiler_params=pltpu.CompilerParams(vmem_limit_bytes=32 * MIB),
        name="before",
    )(at, table, ids, x, cot, gain, w_in, w_out)


def pack_kernel(at_ref, table_ref, win_ref, *refs):
    got, (a_ref, b_ref, ids_ref) = refs[:-3], refs[-3:]
    nt, rows = a_ref.shape[:2]
    per = len(got)
    local = a_ref.shape[2] // 4
    seqs, _, length = ids_ref.shape
    part = length // nt
    for t in range(nt):
        a_ref[t, :, : 3 * local] = win_ref[t, :rows, : 3 * local]
        b_ref[0, t] = win_ref[t, :rows, 3 * local :]
        row = win_ref[at_ref[1] ^ t, rows:, : seqs * part].astype(F32).astype(jnp.int32)
        for s in range(seqs):
            ids_ref[s, :, t * part : (t + 1) * part] = row[:, s * part : (s + 1) * part]
    for k, ref in enumerate(got):
        slot = table_ref[at_ref[0], per + k]

        @pl.when(slot == 0)
        def _():
            for c in range(nt):
                a_ref[c, :, 3 * local :] = ref[:, c * local : (c + 1) * local]

        @pl.when(slot > 0)
        def _():
            b_ref[1, jnp.maximum(slot, 1) - 1] = ref[...]


def pack(at, table, w_in, got, seqs, part):
    unit, dim = got[0].shape
    return pl.pallas_call(
        pack_kernel,
        out_shape=[
            jax.ShapeDtypeStruct((SLOTS, unit, dim), BF),
            jax.ShapeDtypeStruct((2, SLOTS, unit, dim), BF),
            jax.ShapeDtypeStruct((seqs, 1, SLOTS * part), jnp.int32),
        ],
        in_specs=[SMEM] * 2 + [VMEM] * (1 + len(got)),
        out_specs=[VMEM] * 3,
        cost_estimate=pl.CostEstimate(flops=1000, transcendentals=0, bytes_accessed=unit * dim * 60),
        name="pack",
    )(at, table, w_in, *got)


def join_kernel(at_ref, here_ref, there_ref, wqkv_ref, wo_ref, all_ref):
    halves, nt, unit, dim = here_ref.shape
    local = dim // nt
    high, low = at_ref[2] >> 1, at_ref[2] & 1
    for i in range(halves):
        all_ref[((high ^ i) << 1) | low] = here_ref[i]
        all_ref[((high ^ i) << 1) | (1 - low)] = there_ref[i]
    whole = all_ref[...]
    wqkv_ref[...] = whole.reshape(dim, dim)[:, : 3 * local].T
    for c in range(nt):
        wo_ref[:, c * local : (c + 1) * local] = whole[:, c, :, 3 * local :].reshape(2 * halves * unit, local)


def join(at, here, there):
    halves, nt, unit, dim = here.shape
    local = dim // nt
    return pl.pallas_call(
        join_kernel,
        out_shape=[jax.ShapeDtypeStruct((3 * local, dim), BF), jax.ShapeDtypeStruct((local, dim), BF)],
        in_specs=[SMEM, VMEM, VMEM],
        out_specs=[VMEM] * 2,
        scratch_shapes=[pltpu.VMEM((2 * halves, nt, unit, dim), BF)],
        cost_estimate=pl.CostEstimate(flops=1000, transcendentals=0, bytes_accessed=dim * dim * 8),
        compiler_params=pltpu.CompilerParams(vmem_limit_bytes=32 * MIB),
        name="join",
    )(at, here, there)


def resplit(total, rows):
    first = total[rows : rows + 1] + total[rows + 1 : rows + 2]
    second = total[rows + 2 : rows + 3] + total[rows + 3 : rows + 4]
    return term_rows(first, second)


def term_rows(first, second):
    def terms(v):
        hi = v.astype(BF).astype(F32)
        return [hi, (v - hi).astype(BF).astype(F32)]

    return jnp.concatenate(terms(first) + terms(second) + [jnp.zeros((4, first.shape[1]), F32)], axis=0)


def fold(rows, low, at, keep, got):
    n, high, dim = keep.shape

    def kernel(at_ref, keep_ref, *refs):
        got_refs, (own_ref, *send_refs) = refs[: len(got)], refs[len(got) :]
        mine = (at_ref[2] >> low) & 3
        for i in range(n // 4):
            for s, to in enumerate([own_ref] + send_refs):
                at_block = i * 4 + (mine ^ s)
                total = keep_ref[at_block]
                for ref in got_refs:
                    total = total + ref[at_block].astype(F32)
                if rows:
                    to[i, :rows] = total[:rows].astype(to.dtype)
                    to[i, rows:] = resplit(total, rows).astype(to.dtype)
                else:
                    to[i] = total.astype(to.dtype)

    out = lambda t: jax.ShapeDtypeStruct((n // 4, high, dim), t)
    return pl.pallas_call(
        kernel,
        out_shape=[out(F32)] + [out(BF)] * 3,
        in_specs=[SMEM] + [VMEM] * (1 + len(got)),
        out_specs=[VMEM] * 4,
        cost_estimate=pl.CostEstimate(flops=keep.size, transcendentals=0, bytes_accessed=keep.size * 8),
        compiler_params=pltpu.CompilerParams(vmem_limit_bytes=48 * MIB),
        name="fold",
    )(at, keep, *got)


def leave(at, table, a_parts, f_units, local):
    own = a_parts[0]
    per = f_units.shape[0] + 1
    _, unit, dim = f_units.shape
    rows = SLOTS * unit
    width = 3 * local

    def kernel(at_ref, table_ref, p0, p1, p2, p3, f_ref, src_ref, *outs):
        out_refs, (all_ref,) = outs[:-1], outs[-1:]
        total = (p0[0] + p1[0].astype(F32)) + (p2[0].astype(F32) + p3[0].astype(F32))
        first = total[rows : rows + 1] + total[rows + 1 : rows + 2]
        second = total[rows + 2 : rows + 3] + total[rows + 3 : rows + 4]
        for t in range(SLOTS):
            src_ref[t, :unit] = total[t * unit : (t + 1) * unit, :width]
            src_ref[t, unit : unit + 1] = first[:, :width]
            src_ref[t, unit + 1 : unit + 2] = jnp.concatenate(
                [first[:, width:], second[:, :128], jnp.zeros((1, 2 * width - dim - 128), F32)], axis=1
            )
        for c in range(SLOTS):
            all_ref[0, :, c * local : (c + 1) * local] = total[c * unit : (c + 1) * unit, width:]
        for k in range(per - 1):
            all_ref[k + 1] = f_ref[k]
        for k, ref in enumerate(out_refs):
            ref[...] = all_ref[table_ref[at_ref[0], per + k]]

    return pl.pallas_call(
        kernel,
        out_shape=[jax.ShapeDtypeStruct((SLOTS, unit + 2, width), F32)] + [jax.ShapeDtypeStruct((unit, dim), F32)] * per,
        in_specs=[SMEM] * 2 + [VMEM] * 5,
        out_specs=[VMEM] * (1 + per),
        scratch_shapes=[pltpu.VMEM((per, unit, dim), F32)],
        cost_estimate=pl.CostEstimate(flops=own.size, transcendentals=0, bytes_accessed=own.size * 20),
        name="leave",
    )(at, table, *a_parts, f_units)


def place(at, table, qkv, up, got):
    nt, high, width = qkv.shape
    unit, dim = got[0].shape
    per = len(got)
    local = width // 3
    wide = nt * (width + up.shape[2])

    def kernel(at_ref, table_ref, qkv_ref, up_ref, *refs):
        got_refs, (in_ref, out_ref, small_ref) = refs[:per], refs[per:]
        for t in range(nt):
            for k in range(3):
                in_ref[:, k * nt * local + t * local : k * nt * local + (t + 1) * local] = qkv_ref[t, :unit, k * local : (k + 1) * local]
            in_ref[:, nt * width + t * dim : nt * width + (t + 1) * dim] = up_ref[t]
        for k, ref in enumerate(got_refs):
            out_ref[table_ref[at_ref[0], k]] = ref[...]
        total = qkv_ref[0, unit:]
        for t in range(1, nt):
            total = total + qkv_ref[t, unit:]
        small_ref[:, :width] = total[0:1]
        small_ref[:, width:] = total[1:2, : dim + 128 - width]

    return pl.pallas_call(
        kernel,
        out_shape=[
            jax.ShapeDtypeStruct((unit, wide), F32),
            jax.ShapeDtypeStruct((per, unit, dim), F32),
            jax.ShapeDtypeStruct((1, dim + 128), F32),
        ],
        in_specs=[SMEM] * 2 + [VMEM] * (2 + per),
        out_specs=[VMEM] * 3,
        cost_estimate=pl.CostEstimate(flops=1000, transcendentals=0, bytes_accessed=unit * wide * 16),
        name="place",
    )(at, table, qkv, up, *got)


def after_kernel(s, ids_ref, x_ref, cot_ref, gain_ref, keep_ref, near_ref, far_ref, *rest):
    out_ref, grad_ref = rest[-2:]
    unit, inverse = normalize(x_ref[0].astype(F32))
    live = column(jnp.where(ids_ref[s : s + 1, :] >= 0, 1.0, 0.0))
    both = keep_ref[0].astype(F32) + near_ref[0].astype(F32) + far_ref[...].astype(F32)
    out_ref[0] = (live * (x_ref[0].astype(F32) + both[0])).astype(BF)
    grad_ref[0] = (
        live * cot_ref[0].astype(F32) + norm_back(both[1] * gain_ref[...], unit, inverse)
    ).astype(BF)


def after(s, ids, x, cot, gain, keep, near, far, earlier):
    seqs, part, dim = x.shape
    one = pl.BlockSpec((1, part, dim), lambda i: (s, 0, 0))
    pair = pl.BlockSpec((1, 2, part, dim), lambda i: (0, 0, 0, 0))
    fixed = lambda a: pl.BlockSpec(a.shape, lambda i: (0,) * a.ndim)
    return pl.pallas_call(
        functools.partial(after_kernel, s),
        grid=(1,),
        out_shape=[jax.ShapeDtypeStruct(x.shape, BF)] * 2,
        in_specs=[fixed(ids), one, one, fixed(gain), pair, pair, fixed(far)] + [ANY] * len(earlier),
        out_specs=[one, one],
        input_output_aliases={7 + i: i for i in range(len(earlier))},
        cost_estimate=pl.CostEstimate(flops=part * dim * 20, transcendentals=0, bytes_accessed=part * dim * 20),
        compiler_params=pltpu.CompilerParams(vmem_limit_bytes=32 * MIB),
        name="after",
    )(ids, x, cot, gain, keep, near, far, *earlier)


def split_rows(odd, grad, send_ref, keep_ref, parts, rows, store):
    for z in range(parts):
        low = grad[2 * z * rows : (2 * z + 1) * rows]
        high = grad[(2 * z + 1) * rows : (2 * z + 2) * rows]
        store(send_ref, z, jnp.where(odd, low, high).astype(BF))
        store(keep_ref, z, jnp.where(odd, high, low))


def attention_kernel(
    heads, block, first, last,
    odd_ref, ids_ref, wqkv_ref, wo_ref, qg_ref, kg_ref, *refs,
):
    pays, refs = refs[:SLOTS], refs[SLOTS:]
    if not first:
        (accq_ref, acco_ref, acc_sums_ref), refs = refs[:3], refs[3:]
    if last:
        (fnp_ref, gain_ref, o_ref, grad_ref, send_ref, keep_ref, sums_ref), refs = refs[:7], refs[7:]
    else:
        (o_ref, grad_ref, sums_ref, newq_ref, newo_ref), refs = refs[:5], refs[5:]
    norm_ref, gb_ref, raw_ref, qt_ref, qn_ref, kt_ref, ka_ref, vt_ref, va_ref, do_ref, dq_ref, dk_ref, dv_ref, pad_ref, vm_ref, sem = refs
    length, dim = norm_ref.shape
    part = length // SLOTS
    width = heads * HD
    blocks = length // block
    copies = []
    for j in range(2):
        for i, pay in enumerate(pays):
            to = (norm_ref, gb_ref)[j].at[pl.ds(i * part, part), :]
            copies.append(pltpu.make_async_copy(pay.at[j], to, sem.at[j * SLOTS + i]))
            copies[-1].start()
    ids = ids_ref[...]
    marks = lax.broadcasted_iota(jnp.int32, (HD, length), 0)
    same = marks == ids + 1
    k_tail = jnp.where(same, 1.0, 0.0).T.astype(BF)
    q_tail = jnp.where((same & (ids >= 0)) | (marks > 4), 0.0, -BIG).astype(BF)
    v_tail = jnp.where(lax.broadcasted_iota(jnp.int32, (length, HD), 1) < 2, 1.0, 0.0).astype(BF)
    ones = jnp.where(lax.broadcasted_iota(jnp.int32, (16, length), 0) == 0, 1.0, 0.0).astype(BF)
    pad = jnp.where(ids < 0, 1.0, 0.0)
    cut = lambda a, i: a[:, i * block : (i + 1) * block]
    for i in range(blocks):
        pad_ref[i] = cut(pad, i)
    for i in range(SLOTS):
        copies[i].wait()
    raw_ref[...] = mm(wqkv_ref[...], norm_ref[...], NT)
    for i in range(SLOTS):
        copies[SLOTS + i].wait()
    do_all = mm(wo_ref[...], gb_ref[...], NT).astype(BF)
    for h in range(heads):
        for i in range(blocks):
            do_ref[h * blocks + i] = cut(do_all[h * HD : (h + 1) * HD], i)
    gain_q = qg_ref[...]
    gain_k = kg_ref[...]

    def unit_of(row):
        raw = raw_ref[pl.ds(pl.multiple_of(row, HD), HD), :]
        center = raw - jnp.mean(raw, axis=0, keepdims=True)
        inverse = lax.rsqrt(jnp.mean(center * center, axis=0, keepdims=True) + EPS)
        return center * inverse, inverse

    def prepare(h, carry):
        q_unit, _ = unit_of(h * HD)
        q = q_unit * gain_q
        qn = q.T.astype(BF)
        for i in range(blocks):
            qt_ref[h * blocks + i, :HD] = cut(q, i).astype(BF)
            qt_ref[h * blocks + i, HD:] = cut(q_tail, i)
            qn_ref[h * blocks + i] = qn[i * block : (i + 1) * block]
        k_unit, _ = unit_of(width + h * HD)
        k = k_unit * gain_k
        kt_ref[h] = k.astype(BF)
        ka_ref[h, :, :HD] = k.T.astype(BF)
        ka_ref[h, :, HD:] = k_tail
        v = raw_ref[pl.ds(pl.multiple_of(2 * width + h * HD, HD), HD), :]
        vb = v.astype(BF)
        vt_ref[h, :HD] = vb
        vt_ref[h, HD:] = ones
        va_ref[h, :, :HD] = v.T.astype(BF)
        va_ref[h, :, HD:] = v_tail
        vm_ref[h] = jnp.mean(vb.astype(F32), axis=1, keepdims=True)
        dk_ref[h] = jnp.zeros(dk_ref.shape[1:], F32)
        dv_ref[h] = jnp.zeros(dv_ref.shape[1:], F32)
        return carry

    lax.fori_loop(0, heads, prepare, 0)
    spot = lax.broadcasted_iota(jnp.int32, (HD, block), 0)

    def step(n, carry):
        h = n // blocks
        padb = pad_ref[n % blocks]
        e = jnp.exp2(mm(ka_ref[h], qt_ref[n]) * (LOG2E / math.sqrt(HD)))
        eb = e.astype(BF)
        oa = mm(vt_ref[h], eb)
        inv = 1.0 / (oa[HD : HD + 1] + padb)
        o = oa[:HD] * inv
        dos = (do_ref[n].astype(F32) * inv).astype(BF)
        delta = jnp.sum(dos.astype(F32) * o, axis=0, keepdims=True)
        d0 = delta.astype(BF).astype(F32)
        tail = jnp.where(spot == 0, -d0, jnp.where(spot == 1, d0 - delta, 0.0))
        doa = jnp.concatenate([dos.astype(F32), tail], axis=0)
        ds = (e * mm(va_ref[h], doa.astype(BF))).astype(BF)
        dq_ref[n] = mm(kt_ref[h], ds)
        dk_ref[h] += mm(ds, qn_ref[n])
        dv_ref[h] += mm(eb, doa.T.astype(BF))
        do_ref[n] = jnp.where(padb > 0, vm_ref[h], o).astype(BF)
        return carry

    lax.fori_loop(0, heads * blocks, step, 0)
    scale = 1.0 / math.sqrt(HD)

    def lanes(a):
        total = a[:, :128]
        for i in range(1, length // 128):
            total = total + a[:, i * 128 : (i + 1) * 128]
        return total

    def finish(h, carry):
        rows = lambda at: pl.ds(pl.multiple_of(at + h * HD, HD), HD)
        gq = jnp.concatenate([dq_ref[h * blocks + i] for i in range(blocks)], axis=1)
        gk = dk_ref[h].T
        for k, (g, gain_col) in enumerate(((gq, gain_q), (gk, gain_k))):
            unit, inverse = unit_of(k * width + h * HD)
            g = (g * scale).astype(BF).astype(F32)
            sums_ref[k] += lanes(g * unit)
            g = g * gain_col
            back = inverse * (
                g - jnp.mean(g, axis=0, keepdims=True) - unit * jnp.mean(g * unit, axis=0, keepdims=True)
            )
            grad_ref[rows(k * width), :] = back.astype(BF)
        grad_ref[rows(2 * width), :] = dv_ref[h].T[:HD].astype(BF)
        for i in range(blocks):
            o_ref[rows(0), pl.ds(i * block, block)] = do_ref[h * blocks + i]
        return carry

    sums_ref[...] = jnp.zeros_like(sums_ref) if first else acc_sums_ref[...]
    lax.fori_loop(0, heads, finish, 0)
    g_q = mm(grad_ref[...], norm_ref[...])
    g_o = mm(o_ref[...], gb_ref[...])
    if not first:
        g_q = g_q + accq_ref[...]
        g_o = g_o + acco_ref[...]
    if not last:
        newq_ref[...] = g_q
        newo_ref[...] = g_o
        return
    first_row = (jnp.sum(wqkv_ref[...].astype(F32) * g_q, axis=0, keepdims=True) + fnp_ref[...]) / gain_ref[...]
    second_row = jnp.concatenate(
        [jnp.sum(sums_ref[k].T, axis=0, keepdims=True) for k in range(2)] + [jnp.zeros((1, dim - 2 * HD), F32)], axis=1
    )
    g_q = g_q.T
    odd = odd_ref[0] > 0
    parts, rows, _ = send_ref.shape
    rows = rows - 8
    extra = term_rows(first_row, second_row)
    for z in range(parts):
        send_ref[z, rows:] = extra.astype(BF)
        keep_ref[z, rows:] = extra
    unit = width // (2 * parts)

    def put_q(ref, z, value):
        ref[z, :rows, : 3 * width] = value

    def put_o(ref, z, value):
        for c in range(dim // width):
            ref[z, c * unit : (c + 1) * unit, 3 * width :] = value[:, c * width : (c + 1) * width]

    split_rows(odd, g_q, send_ref, keep_ref, parts, rows, put_q)
    split_rows(odd, g_o, send_ref, keep_ref, parts, unit, put_o)


def attention(odd, ids, wqkv, wo, qg, kg, pays, acc, last, halves, more=()):
    wide, dim = wqkv.shape
    width = wo.shape[0]
    heads = width // HD
    length = pays[0].shape[1] * SLOTS
    block = 512
    blocks = length // block
    first = acc is None
    ins = [odd, ids, wqkv, wo, qg, kg, *pays] + ([] if first else list(acc)) + list(more)
    specs = [SMEM] + [VMEM] * 5 + [ANY] * SLOTS + ([] if first else [VMEM] * 3) + [VMEM] * len(more)
    outs = [jax.ShapeDtypeStruct((width, length), BF), jax.ShapeDtypeStruct((wide, length), BF)]
    scratch = []
    if last:
        rows = dim // (2 * halves)
        outs += [
            jax.ShapeDtypeStruct((halves, rows + 8, wide + width), BF),
            jax.ShapeDtypeStruct((halves, rows + 8, wide + width), F32),
        ]
        scratch = [pltpu.VMEM((2, HD, 128), F32)]
    else:
        outs += [
            jax.ShapeDtypeStruct((2, HD, 128), F32),
            jax.ShapeDtypeStruct((wide, dim), F32),
            jax.ShapeDtypeStruct((width, dim), F32),
        ]
    flops = 2 * length * dim * width * 8 + heads * 6 * 2 * length * length * HD
    return pl.pallas_call(
        functools.partial(attention_kernel, heads, block, first, last),
        out_shape=outs,
        in_specs=specs,
        out_specs=[VMEM] * len(outs),
        scratch_shapes=scratch
        + [
            pltpu.VMEM((length, dim), BF),
            pltpu.VMEM((length, dim), BF),
            pltpu.VMEM((wide, length), F32),
            pltpu.VMEM((heads * blocks, 2 * HD, block), BF),
            pltpu.VMEM((heads * blocks, block, HD), BF),
            pltpu.VMEM((heads, HD, length), BF),
            pltpu.VMEM((heads, length, 2 * HD), BF),
            pltpu.VMEM((heads, HD + 16, length), BF),
            pltpu.VMEM((heads, length, 2 * HD), BF),
            pltpu.VMEM((heads * blocks, HD, block), BF),
            pltpu.VMEM((heads * blocks, HD, block), F32),
            pltpu.VMEM((heads, length, HD), F32),
            pltpu.VMEM((heads, length, 2 * HD), F32),
            pltpu.VMEM((blocks, 1, block), F32),
            pltpu.VMEM((heads, HD, 1), F32),
            pltpu.SemaphoreType.DMA((2 * SLOTS,)),
        ],
        cost_estimate=pl.CostEstimate(flops=flops * 3, transcendentals=heads * length * length, bytes_accessed=8 * length * dim),
        compiler_params=pltpu.CompilerParams(vmem_limit_bytes=56 * MIB),
        name="attention",
    )(*ins)


def ffn_kernel(count, at_ref, here_ref, there_ref, *refs):
    pays, refs = refs[:count], refs[count:]
    (hid_ref, gup_ref, send_ref, keep_ref, np_ref, wup_ref, wff_ref), refs = refs[:7], refs[7:]
    pay_ref, hidv_ref, gupv_ref, gin_ref, gff_ref, sem, out_sem, w_sem = refs
    dim = wup_ref.shape[0]
    halves = here_ref.shape[0]
    unit = dim // (2 * halves * SLOTS)
    copies = []
    for i in range(halves):
        for j, ref in enumerate((here_ref, there_ref)):
            b = (((at_ref[2] >> 1) ^ i) << 1) | ((at_ref[2] & 1) ^ j)
            for k, to in enumerate((wup_ref, wff_ref)):
                start = pl.multiple_of(b * SLOTS * unit, SLOTS * unit)
                copies.append(pltpu.make_async_copy(ref.at[i, k], to.at[pl.ds(start, SLOTS * unit), :], w_sem.at[(i * 2 + j) * 2 + k]))
                copies[-1].start()
    for i, pay in enumerate(pays):
        pltpu.make_async_copy(pay, pay_ref.at[i], sem.at[i]).start()
    for copy in copies:
        copy.wait()
    gin_ref[...] = jnp.zeros_like(gin_ref)
    gff_ref[...] = jnp.zeros_like(gff_ref)
    c0 = math.sqrt(2.0 / math.pi)
    c1 = 0.044715

    def outs(i):
        return (
            pltpu.make_async_copy(hidv_ref.at[i], hid_ref.at[i], out_sem.at[0, i]),
            pltpu.make_async_copy(gupv_ref.at[i], gup_ref.at[i], out_sem.at[1, i]),
        )

    def step(i, carry):
        pltpu.make_async_copy(pays[0], pay_ref.at[i], sem.at[i]).wait()
        normed = pay_ref[i, 0]
        gb = pay_ref[i, 1]
        up = mm(normed, wup_ref[...])
        gh = mm(gb, wff_ref[...], NT)
        sq = up * up
        t = jnp.tanh(up * (c0 + (c0 * c1) * sq))
        half = 0.5 + 0.5 * t
        hid = (up * half).astype(BF)
        gup = (gh * (half + (0.5 * up) * (1.0 - t * t) * (c0 + (3.0 * c0 * c1) * sq))).astype(BF)
        hidv_ref[i] = hid
        gupv_ref[i] = gup
        for copy in outs(i):
            copy.start()
        gin_ref[...] += mm(normed, gup, TN)
        gff_ref[...] += mm(hid, gb, TN)
        return carry

    lax.fori_loop(0, count, step, 0)
    odd = (at_ref[2] & 1) > 0
    parts, _, rows, _ = send_ref.shape
    line = jnp.sum(wup_ref[...].astype(F32) * gin_ref[...], axis=1, keepdims=True)
    np_ref[...] = jnp.broadcast_to(line, (dim, 128)).T[0:1]
    for k, g in enumerate((gin_ref, gff_ref)):

        def put(ref, z, value, k=k):
            ref[z, k] = value

        split_rows(odd, g[...], send_ref, keep_ref, parts, rows, put)

    def drain(i, carry):
        for copy in outs(i):
            copy.wait()
        return carry

    lax.fori_loop(0, count, drain, 0)


def ffn(at, here, there, pays):
    _, part, dim = pays[0].shape
    units = dim
    halves = here.shape[0]
    count = len(pays)
    rows = dim // (2 * halves)
    act = jax.ShapeDtypeStruct((count, part, units), BF)
    return pl.pallas_call(
        functools.partial(ffn_kernel, count),
        out_shape=[
            act,
            act,
            jax.ShapeDtypeStruct((halves, 2, rows, dim), BF),
            jax.ShapeDtypeStruct((halves, 2, rows, dim), F32),
            jax.ShapeDtypeStruct((1, dim), F32),
            jax.ShapeDtypeStruct((dim, units), BF),
            jax.ShapeDtypeStruct((units, dim), BF),
        ],
        in_specs=[SMEM] + [ANY] * (2 + count),
        out_specs=[ANY, ANY] + [VMEM] * 5,
        scratch_shapes=[
            pltpu.VMEM((count, 2, part, dim), BF),
            pltpu.VMEM((count, part, units), BF),
            pltpu.VMEM((count, part, units), BF),
            pltpu.VMEM((dim, units), F32),
            pltpu.VMEM((units, dim), F32),
            pltpu.SemaphoreType.DMA((count,)),
            pltpu.SemaphoreType.DMA((2, count)),
            pltpu.SemaphoreType.DMA((4 * halves,)),
        ],
        cost_estimate=pl.CostEstimate(
            flops=8 * count * part * dim * units, transcendentals=count * part * units, bytes_accessed=count * part * dim * 8
        ),
        compiler_params=pltpu.CompilerParams(vmem_limit_bytes=58 * MIB),
        name="ffn",
    )(at, here, there, *pays)


def out_kernel(o_ref, hid_ref, gq_ref, gu_ref, wo_ref, wff_ref, wqkv_ref, wup_ref, keep_ref, send_ref):
    branch = (mm(o_ref[...], wo_ref[...], TN) + mm(hid_ref[0], wff_ref[...])).astype(BF)
    gn = (mm(gq_ref[...], wqkv_ref[...], TN) + mm(gu_ref[0], wup_ref[...], NT)).astype(BF)
    away = pl.program_id(0) % 2

    @pl.when(away == 0)
    def _():
        keep_ref[0, 0] = branch
        keep_ref[0, 1] = gn

    @pl.when(away == 1)
    def _():
        send_ref[0, 0] = branch
        send_ref[0, 1] = gn


def outputs(s, o, hid, gq, gu, wo, wff, wqkv, wup):
    part, dim = hid.shape[1], wo.shape[1]
    row = lambda a: pl.BlockSpec((a.shape[0], part), lambda i: (0, i))
    act = pl.BlockSpec((1, part, hid.shape[2]), lambda i: (s * SLOTS + i, 0, 0))
    whole = lambda a: pl.BlockSpec(a.shape, lambda i: (0, 0), pipeline_mode=pl.Buffered(1))
    out = pl.BlockSpec((1, 2, part, dim), lambda i: (i // 2, 0, 0, 0))
    return pl.pallas_call(
        out_kernel,
        grid=(SLOTS,),
        out_shape=[jax.ShapeDtypeStruct((SLOTS // 2, 2, part, dim), BF)] * 2,
        in_specs=[row(o), act, row(gq), act, whole(wo), whole(wff), whole(wqkv), whole(wup)],
        out_specs=[out, out],
        cost_estimate=pl.CostEstimate(
            flops=2 * SLOTS * part * dim * (o.shape[0] + 2 * hid.shape[2] + gq.shape[0]),
            transcendentals=0, bytes_accessed=SLOTS * part * dim * 10),
        compiler_params=pltpu.CompilerParams(vmem_limit_bytes=40 * MIB),
        name="outputs",
    )(o, hid, gq, gu, wo, wff, wqkv, wup)


def swap(value, axis, count, mask):
    return lax.ppermute(value, axis, [(i, i ^ mask) for i in range(count)])


def bit_groups(count):
    bits = list(range(count.bit_length() - 1))[::-1]
    groups = []
    while bits:
        take = 2 if len(bits) > 1 else 1
        groups.append(bits[:take])
        bits = bits[take:]
    assert len(groups[-1]) == 1
    return groups


def tie(value, *after):
    return lax.optimization_barrier((value,) + after)[0]


def gather_high(block, count, bits):
    low = bits[-1]
    return [block] + [swap(block, "batch", count, s << low) for s in range(1, 1 << len(bits))]


def matchings(edges, devices, per_device):
    left = [[] for _ in range(devices)]
    for e, (source, _, _) in enumerate(edges):
        left[source].append(e)
    rounds = []
    for _ in range(per_device):
        owner = [-1] * devices

        def place(source, seen):
            for e in left[source]:
                target = edges[e][1]
                if target in seen:
                    continue
                seen.add(target)
                if owner[target] < 0 or place(edges[owner[target]][0], seen):
                    owner[target] = e
                    return True
            return False

        for source in range(devices):
            place(source, set())
        rounds.append(list(owner))
        for e in owner:
            left[edges[e][0]].remove(e)
    return rounds


def unit_plan(nb, nt, rows, width, hidden):
    unit = math.gcd(math.gcd(rows, width // nt), hidden // nt)
    per = rows // unit
    head_units, hid_units = width // nt // unit, hidden // nt // unit
    assert head_units == nb and hid_units % nb == 0
    c = hid_units // nb
    edges = []
    for t in range(nt):
        for b in range(nb):
            want = [t * head_units + b]
            want += [nt * head_units + t * hid_units + b * c + i for i in range(c)]
            for slot, u in enumerate(want):
                edges.append((u // per, b * nt + t, (u % per, slot)))
    table = np.zeros((nb * nt, 2 * per), np.int32)
    perms = []
    for k, owner in enumerate(matchings(edges, nb * nt, per)):
        perms.append([(edges[e][0], edges[e][1]) for e in owner])
        for e in owner:
            table[edges[e][0], k] = edges[e][2][0]
            table[edges[e][1], per + k] = edges[e][2][1]
    return unit, per, perms, table


def per_device(
    nb, nt, patches, image_ids, cotangent, norm_gain, query_gain, key_gain, in_weight, out_weight
):
    seqs, part, dim = patches.shape
    width = H * HD
    local = width // nt
    units = (in_weight.shape[1] - 3 * width) // nt
    halves = nb // 2
    rows_in = in_weight.shape[0]
    unit, per, perms, table = unit_plan(nb, nt, out_weight.shape[0], width, units * nt)
    assert nt == SLOTS and units == dim and unit == rows_in and dim == nt * local and per == nt + 1
    both = ("batch", "tok")
    me_b = lax.axis_index("batch")
    me_t = lax.axis_index("tok")
    at = jnp.stack([me_b * nt + me_t, me_t, me_b])
    odd = (me_b & 1).reshape(1)
    table = jnp.asarray(table)
    gain = norm_gain.reshape(1, dim)
    groups = bit_groups(nb)

    outs = before(at, table, image_ids, patches, cotangent, gain, in_weight, out_weight.reshape(per, unit, dim))
    pays, a2a_src, unit_sends = outs[:seqs], outs[seqs], outs[seqs + 1 :]
    far = [swap(pays[0], "tok", nt, 2)]
    w_in = lax.all_to_all(a2a_src, "tok", split_axis=0, concat_axis=0, tiled=True)
    got = [lax.ppermute(value, both, perm) for value, perm in zip(unit_sends, perms)]
    chunk_a, chunk_b, ids = pack(at, table, w_in, got, seqs, part)

    chunk_b = chunk_b.reshape(2, nt * unit, dim)
    held_a, held_b = chunk_a[None], chunk_b[None]
    for bits in groups[:-1]:
        parts = gather_high(held_a, nb, bits)
        held_a = jnp.stack(parts, axis=1).reshape((-1,) + chunk_a.shape)
        held_b = tie(held_b, parts[-1])
        parts = gather_high(held_b, nb, bits)
        held_b = jnp.stack(parts, axis=1).reshape((-1,) + chunk_b.shape)
    there_a = swap(held_a, "batch", nb, 1)
    there_b = swap(tie(held_b, there_a), "batch", nb, 1)
    wqkv, wo = join(at, held_a, there_a)

    pay_s = []
    for s in range(seqs):
        if s:
            far.append(swap(tie(pays[s], far[s - 1]), "tok", nt, 2))
        pay_s.append([pays[s], swap(pays[s], "tok", nt, 1), far[s], swap(far[s], "tok", nt, 1)])

    qg = query_gain.reshape(HD, 1)
    kg = key_gain.reshape(HD, 1)
    acc = None
    earlier = []
    behind = None
    for s in range(seqs):
        last = s == seqs - 1
        own = pay_s[s] if behind is None else [tie(pay_s[s][0], behind)] + pay_s[s][1:]
        att = attention(odd, ids[s], wqkv, wo, qg, kg, own, acc, last, halves, (f_np, gain) if last else ())
        if not last:
            acc = (att[3], att[4], att[2])
        if s == 0:
            pieces = [p for q in pay_s for p in q]
            pieces[0] = tie(pieces[0], att[0])
            hid, gup, f_send, f_keep, f_np, wup, wff = ffn(at, held_b, there_b, pieces)
        keep, send = outputs(s, att[0], hid, att[1], gup, wo, wff, wqkv, wup)
        behind = keep
        near = swap(send, "tok", nt, 1)
        away = swap((keep[1].astype(F32) + near[1].astype(F32)).astype(BF), "tok", nt, 2)
        earlier = after(s, image_ids, patches, cotangent, gain, keep, near, away, earlier)
    block_out, patch_grad = earlier
    _, _, a_send, a_keep = att

    def reduce_batch(send, keep, rows):
        flat = lambda a: a.reshape((a.shape[0], -1, dim))
        parts = [flat(keep), flat(swap(send, "batch", nb, 1))]
        for bits in groups[:-1][::-1]:
            own, *sends = fold(rows, bits[-1], at, parts[0], parts[1:])
            parts = [own] + [swap(value, "batch", nb, (s + 1) << bits[-1]) for s, value in enumerate(sends)]
        return parts

    f_parts = reduce_batch(f_send, f_keep, 0)
    f_mine = f_parts[0] + sum(p.astype(F32) for p in f_parts[1:])
    f_mine = f_mine.reshape(2, nt, unit, dim)
    up = lax.all_to_all(f_mine[0], "tok", split_axis=0, concat_axis=0, tiled=True)
    a_parts = reduce_batch(a_send, a_keep, nt * unit)
    src, *sends = leave(at, table, a_parts, f_mine[1], local)
    qkv = lax.all_to_all(src, "tok", split_axis=0, concat_axis=0, tiled=True)
    got = [lax.ppermute(v, both, [(b, a) for a, b in perm]) for v, perm in zip(sends, perms)]
    in_grad, out_grad, small = place(at, table, qkv, up, got)
    small = small[0]
    return (
        block_out,
        patch_grad,
        small[:dim],
        small[dim : dim + HD],
        small[dim + HD :],
        in_grad,
        out_grad.reshape(per * unit, dim),
    )


def solution(mesh):
    rows = P("batch", "tok", None)
    weights = P(("batch", "tok"), None)
    return jax.shard_map(
        functools.partial(per_device, mesh.shape["batch"], mesh.shape["tok"]),
        mesh=mesh,
        in_specs=(rows, P("batch", "tok"), rows, P(), P(), P(), weights, weights),
        out_specs=(rows, rows, P(), P(), P(), weights, weights),
        check_vma=False,
    )
```

profile of v0, /device:TPU:2, one launch (start us, length us, event | category | flops | bytes accessed | tf_op | source)
XLA Modules:
  0.0 399.4 jit_solution(4443164257937599240)
XLA Ops:
  11.7 17.8 %collective-permute-done.10.refs_2_ = bf16[2,256,768]{2,1,0:T(8,128)(2,1)S(1)} collective-permute-done((bf16[2,256,768]{2,1,0:T(8,128)(2,1)S(1)}, bf16[2,256,768]{2,1,0:T(8,128)(2,1)S(1)}, u32[]{:S(2)}, u32[]{:S(2)}) %collective-permute-start.10) | collective-permute-done | bytes 786464 | tf_op jit(solution)/shard_map/ppermute | solution.py:675
  35.3 5.9 %collective-permute-start = (bf16[24,768]{1,0:T(8,128)(2,1)S(1)}, bf16[24,768]{1,0:T(8,128)(2,1)S(1)}, u32[]{:S(2)}, u32[]{:S(2)}) collective-permute-start(bf16[24,768]{1,0:T(8,128)(2,1)S(1)} %get-tuple-element.79), channel_id=1, source_target_pairs={{7,0},{13,1},{3,2},{26,3},{0,4},{14,5},{20,6},{27,7},{8,8},{15,9},... | collective-permute-start | bytes 110600 | tf_op jit(solution)/shard_map/ppermute | solution.py:772
  50.3 9.3 %collective-permute-start.4 = (bf16[24,768]{1,0:T(8,128)(2,1)S(1)}, bf16[24,768]{1,0:T(8,128)(2,1)S(1)}, u32[]{:S(2)}, u32[]{:S(2)}) collective-permute-start(bf16[24,768]{1,0:T(8,128)(2,1)S(1)} %get-tuple-element.83), channel_id=1, source_target_pairs={{6,0},{12,1},{19,2},{25,3},{7,4},{13,5},{3,6},{26,7},{0,8},{14,9},... | collective-permute-start | bytes 110600 | tf_op jit(solution)/shard_map/ppermute | solution.py:772
  64.8 8.8 %collective-permute-done.7 = bf16[1,4,24,768]{3,2,1,0:T(8,128)(2,1)S(1)} collective-permute-done((bf16[1,4,24,768]{3,2,1,0:T(8,128)(2,1)}, bf16[1,4,24,768]{3,2,1,0:T(8,128)(2,1)S(1)}, u32[]{:S(2)}, u32[]{:S(2)}) %collective-permute-start.7) | collective-permute-done | bytes 147488 | tf_op jit(solution)/shard_map/ppermute | solution.py:675
  73.5 4.7 %collective-permute-start.5 = (bf16[1,4,24,768]{3,2,1,0:T(8,128)(2,1)}, bf16[1,4,24,768]{3,2,1,0:T(8,128)(2,1)S(1)}, u32[]{:S(2)}, u32[]{:S(2)}) collective-permute-start(bf16[1,4,24,768]{3,2,1,0:T(8,128)(2,1)} %bitcast.56), channel_id=1, source_target_pairs={{0,8},{4,12},{8,0},{12,4},{16,24},{20,28},{24,16},{28,20},{1,9},{5... | collective-permute-start | bytes 442376 | tf_op jit(solution)/shard_map/ppermute | solution.py:675
  78.8 4.0 collective-permute-start.20
  85.5 4.9 %collective-permute-start.8 = (bf16[4,4,24,768]{3,2,1,0:T(8,128)(2,1)S(1)}, bf16[4,4,24,768]{3,2,1,0:T(8,128)(2,1)S(1)}, u32[]{:S(2)}, u32[]{:S(2)}) collective-permute-start(bf16[4,4,24,768]{3,2,1,0:T(8,128)(2,1)S(1)} %maximum_bitcast_fusion.1.here_ref), channel_id=1, source_target_pairs={{0,4},{4,0},{8,12},{12,8},{16,20},{20,16},{24,28},{28,24},{1,5},{5... | collective-permute-start | bytes 1769480 | tf_op jit(solution)/shard_map/ppermute | solution.py:675
  90.4 9.2 %collective-permute-done.13 = bf16[1,2,96,768]{3,2,1,0:T(8,128)(2,1)S(1)} collective-permute-done((bf16[1,2,96,768]{3,2,1,0:T(8,128)(2,1)}, bf16[1,2,96,768]{3,2,1,0:T(8,128)(2,1)S(1)}, u32[]{:S(2)}, u32[]{:S(2)}) %collective-permute-start.13) | collective-permute-done | bytes 294944 | tf_op jit(solution)/shard_map/ppermute | solution.py:675
  102.4 5.8 %collective-permute-done.12 = bf16[1,2,96,768]{3,2,1,0:T(8,128)(2,1)} collective-permute-done((bf16[1,2,96,768]{3,2,1,0:T(8,128)(2,1)}, bf16[1,2,96,768]{3,2,1,0:T(8,128)(2,1)}, u32[]{:S(2)}, u32[]{:S(2)}) %collective-permute-start.12) | collective-permute-done | bytes 294944 | tf_op jit(solution)/shard_map/ppermute | solution.py:675
  115.1 21.4 %attention.3 = (bf16[192,1024]{1,0:T(8,128)(2,1)}, bf16[576,1024]{1,0:T(8,128)(2,1)}, f32[2,64,128]{2,1,0:T(8,128)}, f32[576,768]{1,0:T(8,128)}, f32[192,768]{1,0:T(8,128)}) custom-call(s32[1]{0:T(128)} %bitcast.odd_ref, s32[1,1024]{1,0:T(1,128)} %get-tuple-element.151.ids_ref, bf16[576,768]{1,0:T(8,128)(2,1)} %copy-done.9, bf16[192,768]{1,0:T(8,128)(2,1)} %copy-done.27, ...), custom_call_target="tpu_custom_call" | custom-call | flops 14495514624 | bytes 6291456 | tf_op jit(solution)/shard_map/attention/pallas_call | solution.py:501
  136.6 4.1 %collective-permute-done.15.there_ref = bf16[4,2,96,768]{3,2,1,0:T(8,128)(2,1)S(1)} collective-permute-done((bf16[4,2,96,768]{3,2,1,0:T(8,128)(2,1)S(1)}, bf16[4,2,96,768]{3,2,1,0:T(8,128)(2,1)S(1)}, u32[]{:S(2)}, u32[]{:S(2)}) %collective-permute-start.15) | collective-permute-done | bytes 1179680 | tf_op jit(solution)/shard_map/ppermute | solution.py:675
  141.8 28.6 %ffn.1 = (bf16[12,256,768]{2,1,0:T(8,128)(2,1)}, bf16[12,256,768]{2,1,0:T(8,128)(2,1)}, bf16[4,2,96,768]{3,2,1,0:T(8,128)(2,1)}, f32[4,2,96,768]{3,2,1,0:T(8,128...) custom-call(s32[3]{0:T(128)} %copy-done.47, bf16[4,2,96,768]{3,2,1,0:T(8,128)(2,1)} %copy-done.54, ...), custom_call_target="tpu_custom_call" | custom-call | flops 14495514624 | bytes 18874368 | tf_op jit(solution)/shard_map/ffn/pallas_call | solution.py:607
  177.1 7.4 %outputs.3 = (bf16[2,2,256,768]{3,2,1,0:T(8,128)(2,1)S(1)}, bf16[2,2,256,768]{3,2,1,0:T(8,128)(2,1)}) custom-call(bf16[192,1024]{1,0:T(8,128)(2,1)S(1)} %copy-done.36, bf16[12,256,768]{2,1,0:T(8,128)(2,1)S(1)} %copy-done, bf16[576,1024]{1,0:T(8,128)(2,1)S(1)} %copy-done.33, bf16[12,256,768]{2,1,0:T(8,128)(2,1)} %get-tuple-element.100.gu_ref, ...), custom_call_target="tpu_custom_call" | custom-call | flops 3623878656 | bytes 7864320 | tf_op jit(solution)/shard_map/outputs/pallas_call | solution.py:660
  185.7 22.5 %attention.4 = (bf16[192,1024]{1,0:T(8,128)(2,1)}, bf16[576,1024]{1,0:T(8,128)(2,1)}, f32[2,64,128]{2,1,0:T(8,128)}, f32[576,768]{1,0:T(8,128)}, f32[192,768]{1,0:T(8,128)}) custom-call(s32[1]{0:T(128)} %bitcast.odd_ref, s32[1,1024]{1,0:T(1,128)} %get-tuple-element.152.ids_ref, bf16[576,768]{1,0:T(8,128)(2,1)} %copy-done.9, bf16[192,768]{1,0:T(8,128)(2,1)} %copy-done.27, ...), custom_call_target="tpu_custom_call" | custom-call | flops 14495514624 | bytes 6291456 | tf_op jit(solution)/shard_map/attention/pallas_call | solution.py:501
  210.5 7.3 %outputs.4 = (bf16[2,2,256,768]{3,2,1,0:T(8,128)(2,1)S(1)}, bf16[2,2,256,768]{3,2,1,0:T(8,128)(2,1)}) custom-call(bf16[192,1024]{1,0:T(8,128)(2,1)S(1)} %copy-done.38, bf16[12,256,768]{2,1,0:T(8,128)(2,1)S(1)} %bitcast.43, bf16[576,1024]{1,0:T(8,128)(2,1)S(1)} %copy-done.35, bf16[12,256,768]{2,1,0:T(8,128)(2,1)} %get-tuple-element.100.gu_ref, ...), custom_call_target="tpu_custom_call" | custom-call | flops 3623878656 | bytes 7864320 | tf_op jit(solution)/shard_map/outputs/pallas_call | solution.py:660
  218.9 22.2 %attention.5 = (bf16[192,1024]{1,0:T(8,128)(2,1)}, bf16[576,1024]{1,0:T(8,128)(2,1)}, bf16[4,104,768]{2,1,0:T(8,128)(2,1)}, f32[4,104,768]{2,1,0:T(8,128)}) custom-call(s32[1]{0:T(128)} %bitcast.odd_ref, s32[1,1024]{1,0:T(1,128)} %get-tuple-element.153.ids_ref, bf16[576,768]{1,0:T(8,128)(2,1)} %copy-done.9, bf16[192,768]{1,0:T(8,128)(2,1)} %copy-done.27, ...), custom_call_target="tpu_custom_call" | custom-call | flops 14495514624 | bytes 6291456 | tf_op jit(solution)/shard_map/attention/pallas_call | solution.py:501
  243.4 7.2 %outputs.5 = (bf16[2,2,256,768]{3,2,1,0:T(8,128)(2,1)S(1)}, bf16[2,2,256,768]{3,2,1,0:T(8,128)(2,1)}) custom-call(bf16[192,1024]{1,0:T(8,128)(2,1)S(1)} %copy-done.37, bf16[12,256,768]{2,1,0:T(8,128)(2,1)S(1)} %bitcast.43, bf16[576,1024]{1,0:T(8,128)(2,1)S(1)} %copy-done.34, bf16[12,256,768]{2,1,0:T(8,128)(2,1)} %get-tuple-element.100.gu_ref, ...), custom_call_target="tpu_custom_call" | custom-call | flops 3623878656 | bytes 7864320 | tf_op jit(solution)/shard_map/outputs/pallas_call | solution.py:660
  255.2 12.5 %collective-permute-done.28.refs_0_ = bf16[4,104,768]{2,1,0:T(8,128)(2,1)S(1)} collective-permute-done((bf16[4,104,768]{2,1,0:T(8,128)(2,1)}, bf16[4,104,768]{2,1,0:T(8,128)(2,1)S(1)}, u32[]{:S(2)}, u32[]{:S(2)}) %collective-permute-start.28) | collective-permute-done | bytes 639008 | tf_op jit(solution)/shard_map/ppermute | solution.py:675
  271.0 18.0 %collective-permute-done.34 = bf16[1,192,768]{2,1,0:T(8,128)(2,1)S(1)} collective-permute-done((bf16[1,192,768]{2,1,0:T(8,128)(2,1)S(1)}, bf16[1,192,768]{2,1,0:T(8,128)(2,1)S(1)}, u32[]{:S(2)}, u32[]{:S(2)}) %collective-permute-start.34) | collective-permute-done | bytes 294944 | tf_op jit(solution)/shard_map/ppermute | solution.py:675
  289.1 7.2 %collective-permute-start.30 = (bf16[1,104,768]{2,1,0:T(8,128)(2,1)S(1)}, bf16[1,104,768]{2,1,0:T(8,128)(2,1)S(1)}, u32[]{:S(2)}, u32[]{:S(2)}) collective-permute-start(bf16[1,104,768]{2,1,0:T(8,128)(2,1)S(1)} %get-tuple-element.132), channel_id=1, source_target_pairs={{0,16},{4,20},{8,24},{12,28},{16,0},{20,4},{24,8},{28,12},{1,17},{... | collective-permute-start | bytes 479240 | tf_op jit(solution)/shard_map/ppermute | solution.py:675
  318.2 40.3 %all-to-all-done.1.qkv_ref = f32[4,26,576]{2,1,0:T(8,128)S(1)} async-done(((f32[4,26,576]{2,1,0:T(8,128)}), f32[4,26,576]{2,1,0:T(8,128)S(1)}, u32[]{:S(2)}, u32[]{:S(2)}) %all-to-all-start.1) | async-done | bytes 239648 | tf_op jit(solution)/shard_map/all_to_all | solution.py:830
  358.5 4.1 %all-to-all-start.2 = ((f32[4,24,768]{2,1,0:T(8,128)}), f32[4,24,768]{2,1,0:T(8,128)}, u32[]{:S(2)}, u32[]{:S(2)}) async-start(f32[4,24,768]{2,1,0:T(8,128)} %bitcast.46), calls=%async_computation.2 | async-start | bytes 589824 | tf_op jit(solution)/shard_map/all_to_all | solution.py:827
  368.3 3.9 collective-permute-done.37.refs_1_
  374.1 4.1 %collective-permute-start.40 = (f32[24,768]{1,0:T(8,128)}, f32[24,768]{1,0:T(8,128)}, u32[]{:S(2)}, u32[]{:S(2)}) collective-permute-start(f32[24,768]{1,0:T(8,128)} %get-tuple-element.145), channel_id=1, source_target_pairs={{0,6},{1,12},{2,19},{3,25},{4,7},{5,13},{6,3},{7,26},{8,0},{9,14},... | collective-permute-start | bytes 221192 | tf_op jit(solution)/shard_map/ppermute | solution.py:831
  (240 shorter events, 116.8 us)
Async XLA Ops:
  10.1 19.3 %collective-permute-start.10 = (bf16[2,256,768]{2,1,0:T(8,128)(2,1)S(1)}, bf16[2,256,768]{2,1,0:T(8,128)(2,1)S(1)}, u32[]{:S(2)}, u32[]{:S(2)}) collective-permute-start(bf16[2,256,768]{2,1,0:T(8,128)(2,1)S(1)} %get-tuple-element.95.refs_0_), channel_id=1, source_target_pairs={{0,2},{1,3},{2,0},{3,1},{4,6},{5,7},{6,4},{7,5},{8,10},{9,11},{10,... | collective-permute-start | bytes 2359304 | tf_op jit(solution)/shard_map/ppermute | solution.py:675
  30.3 48.0 %collective-permute-start.17 = (bf16[2,256,768]{2,1,0:T(8,128)(2,1)}, bf16[2,256,768]{2,1,0:T(8,128)(2,1)}, u32[]{:S(2)}, u32[]{:S(2)}) collective-permute-start(bf16[2,256,768]{2,1,0:T(8,128)(2,1)} %get-tuple-element.104.refs_4_.refs_0_), channel_id=1, source_target_pairs={{0,2},{1,3},{2,0},{3,1},{4,6},{5,7},{6,4},{7,5},{8,10},{9,11},{10,... | collective-permute-start | bytes 2359304 | tf_op jit(solution)/shard_map/ppermute | solution.py:675
  31.9 29.4 %all-to-all-start = ((bf16[4,25,1344]{2,1,0:T(8,128)(2,1)}), bf16[4,25,1344]{2,1,0:T(8,128)(2,1)S(1)}, u32[]{:S(2)}, u32[]{:S(2)}) async-start(bf16[4,25,1344]{2,1,0:T(8,128)(2,1)} %get-tuple-element.78), calls=%async_computation | async-start | bytes 720896 | tf_op jit(solution)/shard_map/all_to_all | solution.py:771
  78.3 34.5 %collective-permute-start.9 = (bf16[2,256,768]{2,1,0:T(8,128)(2,1)S(1)}, bf16[2,256,768]{2,1,0:T(8,128)(2,1)}, u32[]{:S(2)}, u32[]{:S(2)}) collective-permute-start(bf16[2,256,768]{2,1,0:T(8,128)(2,1)S(1)} %get-tuple-element.95.refs_0_), channel_id=1, source_target_pairs={{0,1},{1,0},{2,3},{3,2},{4,5},{5,4},{6,7},{7,6},{8,9},{9,8},{10,11... | collective-permute-start | bytes 2359304 | tf_op jit(solution)/shard_map/ppermute | solution.py:675
  78.3 36.2 %collective-permute-start.11 = (bf16[2,256,768]{2,1,0:T(8,128)(2,1)}, bf16[2,256,768]{2,1,0:T(8,128)(2,1)}, u32[]{:S(2)}, u32[]{:S(2)}) collective-permute-start(bf16[2,256,768]{2,1,0:T(8,128)(2,1)} %copy-done.67), channel_id=1, source_target_pairs={{0,1},{1,0},{2,3},{3,2},{4,5},{5,4},{6,7},{7,6},{8,9},{9,8},{10,11... | collective-permute-start | bytes 2359304 | tf_op jit(solution)/shard_map/ppermute | solution.py:675
  78.8 35.7 %collective-permute-start.20 = (bf16[2,256,768]{2,1,0:T(8,128)(2,1)S(1)}, bf16[2,256,768]{2,1,0:T(8,128)(2,1)}, u32[]{:S(2)}, u32[]{:S(2)}) collective-permute-start(bf16[2,256,768]{2,1,0:T(8,128)(2,1)S(1)} %get-tuple-element.111.refs_8_.refs_0_), channel_id=1, source_target_pairs={{0,2},{1,3},{2,0},{3,1},{4,6},{5,7},{6,4},{7,5},{8,10},{9,11},{10,... | collective-permute-start | bytes 2359304 | tf_op jit(solution)/shard_map/ppermute | solution.py:675
  85.5 24.0 %collective-permute-start.8 = (bf16[4,4,24,768]{3,2,1,0:T(8,128)(2,1)S(1)}, bf16[4,4,24,768]{3,2,1,0:T(8,128)(2,1)S(1)}, u32[]{:S(2)}, u32[]{:S(2)}) collective-permute-start(bf16[4,4,24,768]{3,2,1,0:T(8,128)(2,1)S(1)} %maximum_bitcast_fusion.1.here_ref), channel_id=1, source_target_pairs={{0,4},{4,0},{8,12},{12,8},{16,20},{20,16},{24,28},{28,24},{1,5},{5... | collective-permute-start | bytes 1769480 | tf_op jit(solution)/shard_map/ppermute | solution.py:675
  108.2 28.3 %collective-permute-start.19 = (bf16[2,256,768]{2,1,0:T(8,128)(2,1)S(1)}, bf16[2,256,768]{2,1,0:T(8,128)(2,1)S(1)}, u32[]{:S(2)}, u32[]{:S(2)}) collective-permute-start(bf16[2,256,768]{2,1,0:T(8,128)(2,1)S(1)} %get-tuple-element.111.refs_8_.refs_0_), channel_id=1, source_target_pairs={{0,1},{1,0},{2,3},{3,2},{4,5},{5,4},{6,7},{7,6},{8,9},{9,8},{10,11... | collective-permute-start | bytes 2359304 | tf_op jit(solution)/shard_map/ppermute | solution.py:675
  109.5 27.1 %collective-permute-start.16 = (bf16[2,256,768]{2,1,0:T(8,128)(2,1)}, bf16[2,256,768]{2,1,0:T(8,128)(2,1)S(1)}, u32[]{:S(2)}, u32[]{:S(2)}) collective-permute-start(bf16[2,256,768]{2,1,0:T(8,128)(2,1)} %get-tuple-element.104.refs_4_.refs_0_), channel_id=1, source_target_pairs={{0,1},{1,0},{2,3},{3,2},{4,5},{5,4},{6,7},{7,6},{8,9},{9,8},{10,11... | collective-permute-start | bytes 2359304 | tf_op jit(solution)/shard_map/ppermute | solution.py:675
  112.8 27.9 %collective-permute-start.15 = (bf16[4,2,96,768]{3,2,1,0:T(8,128)(2,1)S(1)}, bf16[4,2,96,768]{3,2,1,0:T(8,128)(2,1)S(1)}, u32[]{:S(2)}, u32[]{:S(2)}) collective-permute-start(bf16[4,2,96,768]{3,2,1,0:T(8,128)(2,1)S(1)} %maximum_bitcast_fusion.here_ref), channel_id=1, source_target_pairs={{0,4},{4,0},{8,12},{12,8},{16,20},{20,16},{24,28},{28,24},{1,5},{5... | collective-permute-start | bytes 3538952 | tf_op jit(solution)/shard_map/ppermute | solution.py:675
  114.6 27.2 %collective-permute-start.18 = (bf16[2,256,768]{2,1,0:T(8,128)(2,1)}, bf16[2,256,768]{2,1,0:T(8,128)(2,1)}, u32[]{:S(2)}, u32[]{:S(2)}) collective-permute-start(bf16[2,256,768]{2,1,0:T(8,128)(2,1)} %collective-permute-done.17.refs_6_.refs_2_), channel_id=1, source_target_pairs={{0,1},{1,0},{2,3},{3,2},{4,5},{5,4},{6,7},{7,6},{8,9},{9,8},{10,11... | collective-permute-start | bytes 2359304 | tf_op jit(solution)/shard_map/ppermute | solution.py:675
  114.6 27.2 %collective-permute-start.21 = (bf16[2,256,768]{2,1,0:T(8,128)(2,1)}, bf16[2,256,768]{2,1,0:T(8,128)(2,1)}, u32[]{:S(2)}, u32[]{:S(2)}) collective-permute-start(bf16[2,256,768]{2,1,0:T(8,128)(2,1)} %collective-permute-done.20.refs_10_.refs_2_), channel_id=1, source_target_pairs={{0,1},{1,0},{2,3},{3,2},{4,5},{5,4},{6,7},{7,6},{8,9},{9,8},{10,11... | collective-permute-start | bytes 2359304 | tf_op jit(solution)/shard_map/ppermute | solution.py:675
  170.4 81.0 %collective-permute-start.32 = (bf16[4,2,96,768]{3,2,1,0:T(8,128)(2,1)}, bf16[4,2,96,768]{3,2,1,0:T(8,128)(2,1)}, u32[]{:S(2)}, u32[]{:S(2)}) collective-permute-start(bf16[4,2,96,768]{3,2,1,0:T(8,128)(2,1)} %get-tuple-element.135), channel_id=1, source_target_pairs={{0,4},{4,0},{8,12},{12,8},{16,20},{20,16},{24,28},{28,24},{1,5},{5... | collective-permute-start | bytes 3538952 | tf_op jit(solution)/shard_map/ppermute | solution.py:675
  250.7 45.8 %collective-permute-start.22 = (bf16[2,2,256,768]{3,2,1,0:T(8,128)(2,1)}, bf16[2,2,256,768]{3,2,1,0:T(8,128)(2,1)S(1)}, u32[]{:S(2)}, u32[]{:S(2)}) collective-permute-start(bf16[2,2,256,768]{3,2,1,0:T(8,128)(2,1)} %get-tuple-element.119), channel_id=1, source_target_pairs={{0,1},{1,0},{2,3},{3,2},{4,5},{5,4},{6,7},{7,6},{8,9},{9,8},{10,11... | collective-permute-start | bytes 4718600 | tf_op jit(solution)/shard_map/ppermute | solution.py:675
  250.7 49.0 %collective-permute-start.24 = (bf16[2,2,256,768]{3,2,1,0:T(8,128)(2,1)}, bf16[2,2,256,768]{3,2,1,0:T(8,128)(2,1)S(1)}, u32[]{:S(2)}, u32[]{:S(2)}) collective-permute-start(bf16[2,2,256,768]{3,2,1,0:T(8,128)(2,1)} %get-tuple-element.120), channel_id=1, source_target_pairs={{0,1},{1,0},{2,3},{3,2},{4,5},{5,4},{6,7},{7,6},{8,9},{9,8},{10,11... | collective-permute-start | bytes 4718600 | tf_op jit(solution)/shard_map/ppermute | solution.py:675
  251.5 52.0 %collective-permute-start.26 = (bf16[2,2,256,768]{3,2,1,0:T(8,128)(2,1)}, bf16[2,2,256,768]{3,2,1,0:T(8,128)(2,1)S(1)}, u32[]{:S(2)}, u32[]{:S(2)}) collective-permute-start(bf16[2,2,256,768]{3,2,1,0:T(8,128)(2,1)} %get-tuple-element.121), channel_id=1, source_target_pairs={{0,1},{1,0},{2,3},{3,2},{4,5},{5,4},{6,7},{7,6},{8,9},{9,8},{10,11... | collective-permute-start | bytes 4718600 | tf_op jit(solution)/shard_map/ppermute | solution.py:675
  267.7 21.4 %collective-permute-start.34 = (bf16[1,192,768]{2,1,0:T(8,128)(2,1)S(1)}, bf16[1,192,768]{2,1,0:T(8,128)(2,1)S(1)}, u32[]{:S(2)}, u32[]{:S(2)}) collective-permute-start(bf16[1,192,768]{2,1,0:T(8,128)(2,1)S(1)} %get-tuple-element.138), channel_id=1, source_target_pairs={{0,16},{4,20},{8,24},{12,28},{16,0},{20,4},{24,8},{28,12},{1,17},{... | collective-permute-start | bytes 884744 | tf_op jit(solution)/shard_map/ppermute | solution.py:675
  268.4 20.7 %collective-permute-start.35 = (bf16[1,192,768]{2,1,0:T(8,128)(2,1)S(1)}, bf16[1,192,768]{2,1,0:T(8,128)(2,1)S(1)}, u32[]{:S(2)}, u32[]{:S(2)}) collective-permute-start(bf16[1,192,768]{2,1,0:T(8,128)(2,1)S(1)} %get-tuple-element.139), channel_id=1, source_target_pairs={{0,24},{4,28},{8,16},{12,20},{16,8},{20,12},{24,0},{28,4},{1,25},{... | collective-permute-start | bytes 884744 | tf_op jit(solution)/shard_map/ppermute | solution.py:675
  299.6 98.1 %collective-permute-start.23 = (bf16[2,256,768]{2,1,0:T(8,128)(2,1)}, bf16[2,256,768]{2,1,0:T(8,128)(2,1)S(1)}, u32[]{:S(2)}, u32[]{:S(2)}) collective-permute-start(bf16[2,256,768]{2,1,0:T(8,128)(2,1)} %fusion), channel_id=1, source_target_pairs={{0,2},{1,3},{2,0},{3,1},{4,6},{5,7},{6,4},{7,5},{8,10},{9,11},{10,... | collective-permute-start | bytes 2359304 | tf_op jit(solution)/shard_map/ppermute | solution.py:675
  303.4 91.4 %collective-permute-start.25 = (bf16[2,256,768]{2,1,0:T(8,128)(2,1)}, bf16[2,256,768]{2,1,0:T(8,128)(2,1)}, u32[]{:S(2)}, u32[]{:S(2)}) collective-permute-start(bf16[2,256,768]{2,1,0:T(8,128)(2,1)} %fusion.1), channel_id=1, source_target_pairs={{0,2},{1,3},{2,0},{3,1},{4,6},{5,7},{6,4},{7,5},{8,10},{9,11},{10,... | collective-permute-start | bytes 2359304 | tf_op jit(solution)/shard_map/ppermute | solution.py:675
  304.8 84.2 %collective-permute-start.27 = (bf16[2,256,768]{2,1,0:T(8,128)(2,1)}, bf16[2,256,768]{2,1,0:T(8,128)(2,1)}, u32[]{:S(2)}, u32[]{:S(2)}) collective-permute-start(bf16[2,256,768]{2,1,0:T(8,128)(2,1)} %fusion.2), channel_id=1, source_target_pairs={{0,2},{1,3},{2,0},{3,1},{4,6},{5,7},{6,4},{7,5},{8,10},{9,11},{10,... | collective-permute-start | bytes 2359304 | tf_op jit(solution)/shard_map/ppermute | solution.py:675
  311.2 47.3 %all-to-all-start.1 = ((f32[4,26,576]{2,1,0:T(8,128)}), f32[4,26,576]{2,1,0:T(8,128)S(1)}, u32[]{:S(2)}, u32[]{:S(2)}) async-start(f32[4,26,576]{2,1,0:T(8,128)} %get-tuple-element.140), calls=%async_computation.1 | async-start | bytes 655360 | tf_op jit(solution)/shard_map/all_to_all | solution.py:830
  314.7 51.5 %collective-permute-start.36 = (f32[24,768]{1,0:T(8,128)}, f32[24,768]{1,0:T(8,128)S(1)}, u32[]{:S(2)}, u32[]{:S(2)}) collective-permute-start(f32[24,768]{1,0:T(8,128)} %get-tuple-element.141), channel_id=1, source_target_pairs={{0,7},{1,13},{2,3},{3,26},{4,0},{5,14},{6,20},{7,27},{8,8},{9,15},... | collective-permute-start | bytes 221192 | tf_op jit(solution)/shard_map/ppermute | solution.py:831
  358.5 25.7 %all-to-all-start.2 = ((f32[4,24,768]{2,1,0:T(8,128)}), f32[4,24,768]{2,1,0:T(8,128)}, u32[]{:S(2)}, u32[]{:S(2)}) async-start(f32[4,24,768]{2,1,0:T(8,128)} %bitcast.46), calls=%async_computation.2 | async-start | bytes 589824 | tf_op jit(solution)/shard_map/all_to_all | solution.py:827
  (92 other events, 1645.8 us)
where the time goes:
time: 401 us; the launch traced here: 399 us
  Pallas kernels  137 us (34%)
  waiting for transfers between devices  130 us (32%)
  starting transfers between devices  90.7 us (23%)
  local copies, waits for them, and re-layouts  34.9 us (9%)
  other arithmetic  5.94 us (1%)
    ppermute x31, waiting for transfers between devices, swap(): return lax.ppermute(value, axis, [(i, i ^ mask) for i in range(count)])  78.1 us
    pallas_call x3, Pallas kernels, attention(): pl.pallas_call(functools.partial(attention_kernel, heads, block, first, l...  66 us
    all_to_all x1, waiting for transfers between devices, per_device(): qkv = lax.all_to_all(src, 'tok', split_axis=0, concat_axis=0, tiled=True)  40.3 us
    ppermute x31, starting transfers between devices, swap(): return lax.ppermute(value, axis, [(i, i ^ mask) for i in range(count)])  40.2 us
    pallas_call x1, Pallas kernels, ffn(): pl.pallas_call(functools.partial(ffn_kernel, count), out_shape=[act, act,...  28.6 us
    unnamed x144, local copies, waits for them, and re-layouts  28 us
    ppermute x5, starting transfers between devices, per_device(): lax.ppermute(value, both, perm)  24.3 us
    pallas_call x3, Pallas kernels, outputs(): pl.pallas_call(out_kernel, grid=(SLOTS,), out_shape=[jax.ShapeDtypeStruct...  21.9 us
  transfers between devices with their start and end apart: 44, of which 14 were waited for; matrix products, arithmetic and copies ran while one was open for 3% of the time, Pallas kernels for 26%

commit v1 on v0

--- a/solution.py
+++ b/solution.py
@@ -49,12 +49,21 @@
     return jnp.broadcast_to(row, (8, row.shape[1])).T[:, 0:1]
 
 
-def before_kernel(at_ref, table_ref, ids_ref, x_ref, cot_ref, gain_ref, win_ref, wout_ref, *outs):
+def before_kernel(at_ref, table_ref, ids_ref, gain_ref, x_hbm, cot_hbm, win_hbm, wout_hbm, *refs):
+    outs, (x_ref, cot_ref, win_ref, wout_ref, pay_ref, in_sem, out_sem) = refs[:-7], refs[-7:]
     seqs, part, _ = x_ref.shape
-    pays, (src_ref, *unit_refs) = outs[:seqs], outs[seqs:]
+    pays, (src_ref, *unit_refs) = outs[:2], outs[2:]
+    ins = [
+        pltpu.make_async_copy(a, b, in_sem.at[i])
+        for i, (a, b) in enumerate(((win_hbm, win_ref), (wout_hbm, wout_ref), (x_hbm, x_ref), (cot_hbm, cot_ref)))
+    ]
+    for copy in ins:
+        copy.start()
     nt, rows = src_ref.shape[0], win_ref.shape[0]
     local = H * HD // nt
     units = (win_ref.shape[1] - 3 * H * HD) // nt
+    ins[0].wait()
+    ins[1].wait()
     for k, ref in enumerate(unit_refs):
         ref[...] = wout_ref[table_ref[at_ref[0], k]]
     for t in range(nt):
@@ -64,29 +73,45 @@
         for s in range(seqs):
             src_ref[t, rows:, s * part : (s + 1) * part] = ids_ref[s : s + 1, :].astype(F32).astype(BF)
         src_ref[t, rows:, seqs * part :] = jnp.zeros((1, 3 * local + units - seqs * part), BF)
-    for s, pay in enumerate(pays):
+    ins[2].wait()
+    ins[3].wait()
+    copies = []
+    for s in range(seqs):
         unit, _ = normalize(x_ref[s].astype(F32))
         live = column(jnp.where(ids_ref[s : s + 1, :] >= 0, 1.0, 0.0))
-        pay[0] = (unit * gain_ref[...]).astype(BF)
-        pay[1] = (live * cot_ref[s].astype(F32)).astype(BF)
-
-
-def before(at, table, ids, x, cot, gain, w_in, w_out):
+        pay_ref[s, 0] = (unit * gain_ref[...]).astype(BF)
+        pay_ref[s, 1] = (live * cot_ref[s].astype(F32)).astype(BF)
+        copies.append(pltpu.make_async_copy(pay_ref.at[s], pays[0] if s == 0 else pays[1].at[s - 1], out_sem.at[s]))
+        copies[-1].start()
+    for copy in copies:
+        copy.wait()
+
+
+def before(at, table, ids, gain, x, cot, w_in, w_out):
     seqs, part, dim = x.shape
     per, unit, _ = w_out.shape
     rows, wide = w_in.shape
-    outs = [jax.ShapeDtypeStruct((2, part, dim), BF)] * seqs
+    outs = [jax.ShapeDtypeStruct((2, part, dim), BF), jax.ShapeDtypeStruct((seqs - 1, 2, part, dim), BF)]
     outs += [jax.ShapeDtypeStruct((SLOTS, rows + 1, wide // SLOTS), BF)]
     outs += [jax.ShapeDtypeStruct((unit, dim), BF)] * per
     return pl.pallas_call(
         before_kernel,
         out_shape=outs,
-        in_specs=[SMEM] * 2 + [VMEM] * 6,
-        out_specs=[VMEM] * len(outs),
+        in_specs=[SMEM] * 2 + [VMEM] * 2 + [ANY] * 4,
+        out_specs=[ANY] * 2 + [VMEM] * (1 + per),
+        scratch_shapes=[
+            pltpu.VMEM(x.shape, BF),
+            pltpu.VMEM(x.shape, BF),
+            pltpu.VMEM(w_in.shape, BF),
+            pltpu.VMEM(w_out.shape, BF),
+            pltpu.VMEM((seqs, 2, part, dim), BF),
+            pltpu.SemaphoreType.DMA((4,)),
+            pltpu.SemaphoreType.DMA((seqs,)),
+        ],
         cost_estimate=pl.CostEstimate(flops=x.size * 8, transcendentals=0, bytes_accessed=x.size * 8),
         compiler_params=pltpu.CompilerParams(vmem_limit_bytes=32 * MIB),
         name="before",
-    )(at, table, ids, x, cot, gain, w_in, w_out)
+    )(at, table, ids, gain, x, cot, w_in, w_out)
 
 
 def pack_kernel(at_ref, table_ref, win_ref, *refs):
@@ -99,7 +124,7 @@
     for t in range(nt):
         a_ref[t, :, : 3 * local] = win_ref[t, :rows, : 3 * local]
         b_ref[0, t] = win_ref[t, :rows, 3 * local :]
-        row = win_ref[at_ref[1] ^ t, rows:, : seqs * part].astype(F32).astype(jnp.int32)
+        row = win_ref[t, rows:, : seqs * part].astype(F32).astype(jnp.int32)
         for s in range(seqs):
             ids_ref[s, :, t * part : (t + 1) * part] = row[:, s * part : (s + 1) * part]
     for k, ref in enumerate(got):
@@ -224,7 +249,7 @@
         for c in range(SLOTS):
             all_ref[0, :, c * local : (c + 1) * local] = total[c * unit : (c + 1) * unit, width:]
         for k in range(per - 1):
-            all_ref[k + 1] = f_ref[k]
+            all_ref[k + 1] = f_ref[k].astype(F32)
         for k, ref in enumerate(out_refs):
             ref[...] = all_ref[table_ref[at_ref[0], per + k]]
 
@@ -251,7 +276,7 @@
         for t in range(nt):
             for k in range(3):
                 in_ref[:, k * nt * local + t * local : k * nt * local + (t + 1) * local] = qkv_ref[t, :unit, k * local : (k + 1) * local]
-            in_ref[:, nt * width + t * dim : nt * width + (t + 1) * dim] = up_ref[t]
+            in_ref[:, nt * width + t * dim : nt * width + (t + 1) * dim] = up_ref[t].astype(F32)
         for k, ref in enumerate(got_refs):
             out_ref[table_ref[at_ref[0], k]] = ref[...]
         total = qkv_ref[0, unit:]
@@ -313,26 +338,34 @@
 
 def attention_kernel(
     heads, block, first, last,
-    odd_ref, ids_ref, wqkv_ref, wo_ref, qg_ref, kg_ref, *refs,
+    lead, odd_ref, ids_ref, qg_ref, kg_ref, wqkv_hbm, wo_hbm, pay_hbm, *refs,
 ):
-    pays, refs = refs[:SLOTS], refs[SLOTS:]
     if not first:
-        (accq_ref, acco_ref, acc_sums_ref), refs = refs[:3], refs[3:]
+        (acc_sums_ref, accq_hbm, acco_hbm), refs = refs[:3], refs[3:]
     if last:
-        (fnp_ref, gain_ref, o_ref, grad_ref, send_ref, keep_ref, sums_ref), refs = refs[:7], refs[7:]
+        (fnp_ref, gain_ref, o_hbm, grad_hbm, send_ref, keep_ref, sums_ref), refs = refs[:7], refs[7:]
     else:
-        (o_ref, grad_ref, sums_ref, newq_ref, newo_ref), refs = refs[:5], refs[5:]
-    norm_ref, gb_ref, raw_ref, qt_ref, qn_ref, kt_ref, ka_ref, vt_ref, va_ref, do_ref, dq_ref, dk_ref, dv_ref, pad_ref, vm_ref, sem = refs
+        (o_hbm, grad_hbm, sums_ref, newq_hbm, newo_hbm), refs = refs[:5], refs[5:]
+    wqkv_ref, wo_ref, o_ref, grad_ref, accq_ref, acco_ref, w_sem, norm_ref, gb_ref, raw_ref, qt_ref, qn_ref, kt_ref, ka_ref, vt_ref, va_ref, do_ref, dq_ref, dk_ref, dv_ref, pad_ref, vm_ref, sem = refs
     length, dim = norm_ref.shape
     part = length // SLOTS
     width = heads * HD
     blocks = length // block
+    loads = [pltpu.make_async_copy(wqkv_hbm, wqkv_ref, w_sem.at[0])]
+    loads[0].start()
     copies = []
     for j in range(2):
-        for i, pay in enumerate(pays):
+        for i in range(SLOTS):
             to = (norm_ref, gb_ref)[j].at[pl.ds(i * part, part), :]
-            copies.append(pltpu.make_async_copy(pay.at[j], to, sem.at[j * SLOTS + i]))
+            copies.append(pltpu.make_async_copy(pay_hbm.at[(i,) + lead + (j,)], to, sem.at[j * SLOTS + i]))
             copies[-1].start()
+    loads.append(pltpu.make_async_copy(wo_hbm, wo_ref, w_sem.at[1]))
+    loads[1].start()
+    if not first:
+        loads.append(pltpu.make_async_copy(accq_hbm, accq_ref, w_sem.at[2]))
+        loads.append(pltpu.make_async_copy(acco_hbm, acco_ref, w_sem.at[3]))
+        loads[2].start()
+        loads[3].start()
     ids = ids_ref[...]
     marks = lax.broadcasted_iota(jnp.int32, (HD, length), 0)
     same = marks == ids + 1
@@ -344,9 +377,11 @@
     cut = lambda a, i: a[:, i * block : (i + 1) * block]
     for i in range(blocks):
         pad_ref[i] = cut(pad, i)
+    loads[0].wait()
     for i in range(SLOTS):
         copies[i].wait()
     raw_ref[...] = mm(wqkv_ref[...], norm_ref[...], NT)
+    loads[1].wait()
     for i in range(SLOTS):
         copies[SLOTS + i].wait()
     do_all = mm(wo_ref[...], gb_ref[...], NT).astype(BF)
@@ -438,15 +473,27 @@
 
     sums_ref[...] = jnp.zeros_like(sums_ref) if first else acc_sums_ref[...]
     lax.fori_loop(0, heads, finish, 0)
+    stores = [pltpu.make_async_copy(o_ref, o_hbm, w_sem.at[4]), pltpu.make_async_copy(grad_ref, grad_hbm, w_sem.at[5])]
+    stores[0].start()
+    stores[1].start()
     g_q = mm(grad_ref[...], norm_ref[...])
     g_o = mm(o_ref[...], gb_ref[...])
     if not first:
+        loads[2].wait()
+        loads[3].wait()
         g_q = g_q + accq_ref[...]
         g_o = g_o + acco_ref[...]
     if not last:
-        newq_ref[...] = g_q
-        newo_ref[...] = g_o
+        accq_ref[...] = g_q
+        acco_ref[...] = g_o
+        stores += [pltpu.make_async_copy(accq_ref, newq_hbm, w_sem.at[6]), pltpu.make_async_copy(acco_ref, newo_hbm, w_sem.at[7])]
+        stores[2].start()
+        stores[3].start()
+        for copy in stores:
+            copy.wait()
         return
+    for copy in stores:
+        copy.wait()
     first_row = (jnp.sum(wqkv_ref[...].astype(F32) * g_q, axis=0, keepdims=True) + fnp_ref[...]) / gain_ref[...]
     second_row = jnp.concatenate(
         [jnp.sum(sums_ref[k].T, axis=0, keepdims=True) for k in range(2)] + [jnp.zeros((1, dim - 2 * HD), F32)], axis=1
@@ -472,16 +519,16 @@
     split_rows(odd, g_o, send_ref, keep_ref, parts, unit, put_o)
 
 
-def attention(odd, ids, wqkv, wo, qg, kg, pays, acc, last, halves, more=()):
+def attention(odd, ids, wqkv, wo, qg, kg, pay, lead, acc, last, halves, more=()):
     wide, dim = wqkv.shape
     width = wo.shape[0]
     heads = width // HD
-    length = pays[0].shape[1] * SLOTS
+    length = pay.shape[-2] * SLOTS
     block = 512
     blocks = length // block
     first = acc is None
-    ins = [odd, ids, wqkv, wo, qg, kg, *pays] + ([] if first else list(acc)) + list(more)
-    specs = [SMEM] + [VMEM] * 5 + [ANY] * SLOTS + ([] if first else [VMEM] * 3) + [VMEM] * len(more)
+    ins = [odd, ids, qg, kg, wqkv, wo, pay] + ([] if first else list(acc)) + list(more)
+    specs = [SMEM] + [VMEM] * 3 + [ANY] * 3 + ([] if first else [VMEM, ANY, ANY]) + [VMEM] * len(more)
     outs = [jax.ShapeDtypeStruct((width, length), BF), jax.ShapeDtypeStruct((wide, length), BF)]
     scratch = []
     if last:
@@ -499,12 +546,19 @@
         ]
     flops = 2 * length * dim * width * 8 + heads * 6 * 2 * length * length * HD
     return pl.pallas_call(
-        functools.partial(attention_kernel, heads, block, first, last),
+        functools.partial(attention_kernel, heads, block, first, last, lead),
         out_shape=outs,
         in_specs=specs,
-        out_specs=[VMEM] * len(outs),
+        out_specs=[ANY] * 2 + ([VMEM] * 2 if last else [VMEM, ANY, ANY]),
         scratch_shapes=scratch
         + [
+            pltpu.VMEM((wide, dim), BF),
+            pltpu.VMEM((width, dim), BF),
+            pltpu.VMEM((width, length), BF),
+            pltpu.VMEM((wide, length), BF),
+            pltpu.VMEM((wide, dim), F32),
+            pltpu.VMEM((width, dim), F32),
+            pltpu.SemaphoreType.DMA((8,)),
             pltpu.VMEM((length, dim), BF),
             pltpu.VMEM((length, dim), BF),
             pltpu.VMEM((wide, length), F32),
@@ -528,116 +582,123 @@
     )(*ins)
 
 
-def ffn_kernel(count, at_ref, here_ref, there_ref, *refs):
-    pays, refs = refs[:count], refs[count:]
-    (hid_ref, gup_ref, send_ref, keep_ref, np_ref, wup_ref, wff_ref), refs = refs[:7], refs[7:]
-    pay_ref, hidv_ref, gupv_ref, gin_ref, gff_ref, sem, out_sem, w_sem = refs
+def ffn_kernel(block, at_ref, here_ref, there_ref, pay0_hbm, pay1_hbm, *refs):
+    (hid_hbm, gup_hbm, wup_hbm, wff_hbm, send_ref, np_ref), refs = refs[:6], refs[6:]
+    norm_ref, gb_ref, hid_ref, gup_ref, wup_ref, wff_ref, gin_ref, gff_ref, sem, out_sem, w_sem = refs
     dim = wup_ref.shape[0]
     halves = here_ref.shape[0]
-    unit = dim // (2 * halves * SLOTS)
+    rows = dim // (2 * halves)
+    part = pay0_hbm.shape[2]
+    seqs = 1 + pay1_hbm.shape[1]
+    length = SLOTS * part
+    total = norm_ref.shape[0]
     copies = []
     for i in range(halves):
         for j, ref in enumerate((here_ref, there_ref)):
             b = (((at_ref[2] >> 1) ^ i) << 1) | ((at_ref[2] & 1) ^ j)
             for k, to in enumerate((wup_ref, wff_ref)):
-                start = pl.multiple_of(b * SLOTS * unit, SLOTS * unit)
-                copies.append(pltpu.make_async_copy(ref.at[i, k], to.at[pl.ds(start, SLOTS * unit), :], w_sem.at[(i * 2 + j) * 2 + k]))
+                start = pl.multiple_of(b * rows, rows)
+                copies.append(pltpu.make_async_copy(ref.at[i, k], to.at[pl.ds(start, rows), :], w_sem.at[(i * 2 + j) * 2 + k]))
                 copies[-1].start()
-    for i, pay in enumerate(pays):
-        pltpu.make_async_copy(pay, pay_ref.at[i], sem.at[i]).start()
+    for s in range(seqs):
+        for t in range(SLOTS):
+            at_rows = pl.ds((s * SLOTS + t) * part, part)
+            for k, to in enumerate((norm_ref, gb_ref)):
+                source = pay0_hbm.at[t, k] if s == 0 else pay1_hbm.at[t, s - 1, k]
+                pltpu.make_async_copy(source, to.at[at_rows, :], sem.at[s * SLOTS + t]).start()
+    gin_ref[...] = jnp.zeros_like(gin_ref)
+    gff_ref[...] = jnp.zeros_like(gff_ref)
     for copy in copies:
         copy.wait()
-    gin_ref[...] = jnp.zeros_like(gin_ref)
-    gff_ref[...] = jnp.zeros_like(gff_ref)
+    weights = [pltpu.make_async_copy(wup_ref, wup_hbm, w_sem.at[0]), pltpu.make_async_copy(wff_ref, wff_hbm, w_sem.at[1])]
+    for copy in weights:
+        copy.start()
     c0 = math.sqrt(2.0 / math.pi)
     c1 = 0.044715
 
     def outs(i):
+        at_rows = pl.ds(pl.multiple_of(i * block, block), block)
         return (
-            pltpu.make_async_copy(hidv_ref.at[i], hid_ref.at[i], out_sem.at[0, i]),
-            pltpu.make_async_copy(gupv_ref.at[i], gup_ref.at[i], out_sem.at[1, i]),
+            pltpu.make_async_copy(hid_ref.at[at_rows, :], hid_hbm.at[at_rows, :], out_sem.at[0, i]),
+            pltpu.make_async_copy(gup_ref.at[at_rows, :], gup_hbm.at[at_rows, :], out_sem.at[1, i]),
         )
 
     def step(i, carry):
-        pltpu.make_async_copy(pays[0], pay_ref.at[i], sem.at[i]).wait()
-        normed = pay_ref[i, 0]
-        gb = pay_ref[i, 1]
-        up = mm(normed, wup_ref[...])
-        gh = mm(gb, wff_ref[...], NT)
+        for k in range(block // part):
+            for to in (norm_ref, gb_ref):
+                pltpu.make_async_copy(pay0_hbm.at[0, 0], to.at[pl.ds(0, part), :], sem.at[i * (block // part) + k]).wait()
+        at_rows = pl.ds(pl.multiple_of(i * block, block), block)
+        up = mm(norm_ref[at_rows, :], wup_ref[...])
+        gh = mm(gb_ref[at_rows, :], wff_ref[...], NT)
         sq = up * up
         t = jnp.tanh(up * (c0 + (c0 * c1) * sq))
         half = 0.5 + 0.5 * t
-        hid = (up * half).astype(BF)
-        gup = (gh * (half + (0.5 * up) * (1.0 - t * t) * (c0 + (3.0 * c0 * c1) * sq))).astype(BF)
-        hidv_ref[i] = hid
-        gupv_ref[i] = gup
+        hid_ref[at_rows, :] = (up * half).astype(BF)
+        gup_ref[at_rows, :] = (gh * (half + (0.5 * up) * (1.0 - t * t) * (c0 + (3.0 * c0 * c1) * sq))).astype(BF)
         for copy in outs(i):
             copy.start()
-        gin_ref[...] += mm(normed, gup, TN)
-        gff_ref[...] += mm(hid, gb, TN)
+        gin_ref[...] += mm(norm_ref[at_rows, :], gup_ref[at_rows, :], TN)
+        gff_ref[...] += mm(hid_ref[at_rows, :], gb_ref[at_rows, :], TN)
         return carry
 
-    lax.fori_loop(0, count, step, 0)
-    odd = (at_ref[2] & 1) > 0
-    parts, _, rows, _ = send_ref.shape
+    lax.fori_loop(0, total // block, step, 0)
     line = jnp.sum(wup_ref[...].astype(F32) * gin_ref[...], axis=1, keepdims=True)
     np_ref[...] = jnp.broadcast_to(line, (dim, 128)).T[0:1]
-    for k, g in enumerate((gin_ref, gff_ref)):
-
-        def put(ref, z, value, k=k):
-            ref[z, k] = value
-
-        split_rows(odd, g[...], send_ref, keep_ref, parts, rows, put)
+    for b in range(2 * halves):
+        for k, g in enumerate((gin_ref, gff_ref)):
+            send_ref[b, k] = g[b * rows : (b + 1) * rows, :].astype(BF)
+    for copy in weights:
+        copy.wait()
 
     def drain(i, carry):
         for copy in outs(i):
             copy.wait()
         return carry
 
-    lax.fori_loop(0, count, drain, 0)
-
-
-def ffn(at, here, there, pays):
-    _, part, dim = pays[0].shape
+    lax.fori_loop(0, total // block, drain, 0)
+
+
+def ffn(at, here, there, pay0, pay1, block=512):
+    _, _, part, dim = pay0.shape
     units = dim
     halves = here.shape[0]
-    count = len(pays)
+    total = SLOTS * part * (1 + pay1.shape[1])
     rows = dim // (2 * halves)
-    act = jax.ShapeDtypeStruct((count, part, units), BF)
+    act = jax.ShapeDtypeStruct((total, units), BF)
     return pl.pallas_call(
-        functools.partial(ffn_kernel, count),
+        functools.partial(ffn_kernel, block),
         out_shape=[
             act,
             act,
-            jax.ShapeDtypeStruct((halves, 2, rows, dim), BF),
-            jax.ShapeDtypeStruct((halves, 2, rows, dim), F32),
-            jax.ShapeDtypeStruct((1, dim), F32),
             jax.ShapeDtypeStruct((dim, units), BF),
             jax.ShapeDtypeStruct((units, dim), BF),
+            jax.ShapeDtypeStruct((2 * halves, 2, rows, dim), BF),
+            jax.ShapeDtypeStruct((1, dim), F32),
         ],
-        in_specs=[SMEM] + [ANY] * (2 + count),
-        out_specs=[ANY, ANY] + [VMEM] * 5,
+        in_specs=[SMEM] + [ANY] * 4,
+        out_specs=[ANY] * 4 + [VMEM] * 2,
         scratch_shapes=[
-            pltpu.VMEM((count, 2, part, dim), BF),
-            pltpu.VMEM((count, part, units), BF),
-            pltpu.VMEM((count, part, units), BF),
+            pltpu.VMEM((total, dim), BF),
+            pltpu.VMEM((total, dim), BF),
+            pltpu.VMEM((total, units), BF),
+            pltpu.VMEM((total, units), BF),
+            pltpu.VMEM((dim, units), BF),
+            pltpu.VMEM((units, dim), BF),
             pltpu.VMEM((dim, units), F32),
             pltpu.VMEM((units, dim), F32),
-            pltpu.SemaphoreType.DMA((count,)),
-            pltpu.SemaphoreType.DMA((2, count)),
+            pltpu.SemaphoreType.DMA((total // part,)),
+            pltpu.SemaphoreType.DMA((2, total // block)),
             pltpu.SemaphoreType.DMA((4 * halves,)),
         ],
-        cost_estimate=pl.CostEstimate(
-            flops=8 * count * part * dim * units, transcendentals=count * part * units, bytes_accessed=count * part * dim * 8
-        ),
+        cost_estimate=pl.CostEstimate(flops=8 * total * dim * units, transcendentals=total * units, bytes_accessed=total * dim * 8),
         compiler_params=pltpu.CompilerParams(vmem_limit_bytes=58 * MIB),
         name="ffn",
-    )(at, here, there, *pays)
-
-
-def out_kernel(o_ref, hid_ref, gq_ref, gu_ref, wo_ref, wff_ref, wqkv_ref, wup_ref, keep_ref, send_ref):
-    branch = (mm(o_ref[...], wo_ref[...], TN) + mm(hid_ref[0], wff_ref[...])).astype(BF)
-    gn = (mm(gq_ref[...], wqkv_ref[...], TN) + mm(gu_ref[0], wup_ref[...], NT)).astype(BF)
+    )(at, here, there, pay0, pay1)
+
+
+def out_kernel(at_ref, o_ref, hid_ref, gq_ref, gu_ref, wo_ref, wff_ref, wqkv_ref, wup_ref, keep_ref, send_ref):
+    branch = (mm(o_ref[...], wo_ref[...], TN) + mm(hid_ref[...], wff_ref[...])).astype(BF)
+    gn = (mm(gq_ref[...], wqkv_ref[...], TN) + mm(gu_ref[...], wup_ref[...], NT)).astype(BF)
     away = pl.program_id(0) % 2
 
     @pl.when(away == 0)
@@ -651,24 +712,28 @@
         send_ref[0, 1] = gn
 
 
-def outputs(s, o, hid, gq, gu, wo, wff, wqkv, wup):
-    part, dim = hid.shape[1], wo.shape[1]
-    row = lambda a: pl.BlockSpec((a.shape[0], part), lambda i: (0, i))
-    act = pl.BlockSpec((1, part, hid.shape[2]), lambda i: (s * SLOTS + i, 0, 0))
-    whole = lambda a: pl.BlockSpec(a.shape, lambda i: (0, 0), pipeline_mode=pl.Buffered(1))
-    out = pl.BlockSpec((1, 2, part, dim), lambda i: (i // 2, 0, 0, 0))
+def outputs(s, at, o, hid, gq, gu, wo, wff, wqkv, wup):
+    dim = wo.shape[1]
+    part = o.shape[1] // SLOTS
+    row = lambda a: pl.BlockSpec((a.shape[0], part), lambda i, at: (0, at[1] ^ i))
+    act = pl.BlockSpec((part, hid.shape[1]), lambda i, at: (s * SLOTS + (at[1] ^ i), 0))
+    whole = lambda a: pl.BlockSpec(a.shape, lambda i, at: (0, 0), pipeline_mode=pl.Buffered(1))
+    out = pl.BlockSpec((1, 2, part, dim), lambda i, at: (i // 2, 0, 0, 0))
     return pl.pallas_call(
         out_kernel,
-        grid=(SLOTS,),
+        grid_spec=pltpu.PrefetchScalarGridSpec(
+            num_scalar_prefetch=1,
+            grid=(SLOTS,),
+            in_specs=[row(o), act, row(gq), act, whole(wo), whole(wff), whole(wqkv), whole(wup)],
+            out_specs=[out, out],
+        ),
         out_shape=[jax.ShapeDtypeStruct((SLOTS // 2, 2, part, dim), BF)] * 2,
-        in_specs=[row(o), act, row(gq), act, whole(wo), whole(wff), whole(wqkv), whole(wup)],
-        out_specs=[out, out],
         cost_estimate=pl.CostEstimate(
-            flops=2 * SLOTS * part * dim * (o.shape[0] + 2 * hid.shape[2] + gq.shape[0]),
+            flops=2 * SLOTS * part * dim * (o.shape[0] + 2 * hid.shape[1] + gq.shape[0]),
             transcendentals=0, bytes_accessed=SLOTS * part * dim * 10),
         compiler_params=pltpu.CompilerParams(vmem_limit_bytes=40 * MIB),
         name="outputs",
-    )(o, hid, gq, gu, wo, wff, wqkv, wup)
+    )(at, o, hid, gq, gu, wo, wff, wqkv, wup)
 
 
 def swap(value, axis, count, mask):
@@ -765,9 +830,11 @@
     gain = norm_gain.reshape(1, dim)
     groups = bit_groups(nb)
 
-    outs = before(at, table, image_ids, patches, cotangent, gain, in_weight, out_weight.reshape(per, unit, dim))
-    pays, a2a_src, unit_sends = outs[:seqs], outs[seqs], outs[seqs + 1 :]
-    far = [swap(pays[0], "tok", nt, 2)]
+    pay0, pay1, a2a_src, *unit_sends = before(
+        at, table, image_ids, gain, patches, cotangent, in_weight, out_weight.reshape(per, unit, dim)
+    )
+    full0 = lax.all_gather(pay0, "tok", axis=0)
+    full1 = lax.all_gather(pay1, "tok", axis=0)
     w_in = lax.all_to_all(a2a_src, "tok", split_axis=0, concat_axis=0, tiled=True)
     got = [lax.ppermute(value, both, perm) for value, perm in zip(unit_sends, perms)]
     chunk_a, chunk_b, ids = pack(at, table, w_in, got, seqs, part)
@@ -784,45 +851,57 @@
     there_b = swap(tie(held_b, there_a), "batch", nb, 1)
     wqkv, wo = join(at, held_a, there_a)
 
-    pay_s = []
-    for s in range(seqs):
-        if s:
-            far.append(swap(tie(pays[s], far[s - 1]), "tok", nt, 2))
-        pay_s.append([pays[s], swap(pays[s], "tok", nt, 1), far[s], swap(far[s], "tok", nt, 1)])
-
     qg = query_gain.reshape(HD, 1)
     kg = key_gain.reshape(HD, 1)
+    wo_s = wo
+
+    def attend(s, acc, wo_now, more=()):
+        last = s == seqs - 1
+        return attention(
+            odd, ids[s], wqkv, wo_now, qg, kg, full1 if s else full0, (s - 1,) if s else (), acc, last, halves, more
+        )
+
+    def leave_core(s, att):
+        keep, send = outputs(s, at, att[0], hid, att[1], gup, wo, wff, wqkv, wup)
+        return keep, swap(send, "tok", nt, 1)
+
+    def leave_chip(keep, near):
+        value = (keep[1].astype(F32) + near[1].astype(F32)).astype(BF)
+        return value, swap(value, "tok", nt, 2)
+
+    pending = []
     acc = None
     earlier = []
-    behind = None
     for s in range(seqs):
         last = s == seqs - 1
-        own = pay_s[s] if behind is None else [tie(pay_s[s][0], behind)] + pay_s[s][1:]
-        att = attention(odd, ids[s], wqkv, wo, qg, kg, own, acc, last, halves, (f_np, gain) if last else ())
+        att = attend(s, acc, wo_s, (f_np, gain) if last else ())
         if not last:
-            acc = (att[3], att[4], att[2])
+            acc = (att[2], att[3], att[4])
         if s == 0:
-            pieces = [p for q in pay_s for p in q]
-            pieces[0] = tie(pieces[0], att[0])
-            hid, gup, f_send, f_keep, f_np, wup, wff = ffn(at, held_b, there_b, pieces)
-        keep, send = outputs(s, att[0], hid, att[1], gup, wo, wff, wqkv, wup)
-        behind = keep
-        near = swap(send, "tok", nt, 1)
-        away = swap((keep[1].astype(F32) + near[1].astype(F32)).astype(BF), "tok", nt, 2)
+            hid, gup, wup, wff, f_grad, f_np = ffn(at, held_b, there_b, tie(full0, att[0]), full1)
+            f_mine = lax.psum_scatter(f_grad, "batch", scatter_dimension=0, tiled=True)
+        if s:
+            value, away = leave_chip(*pending[-1])
+            pending[-1] = pending[-1] + (away,)
+            att = [tie(att[0], value)] + list(att[1:])
+            if s > 1:
+                att = [tie(att[0], pending[0][2])] + list(att[1:])
+        keep, near = leave_core(s, att)
+        pending.append((keep, near))
+        wo_s = tie(wo, keep)
+    pending[-1] = pending[-1] + (leave_chip(*pending[-1])[1],)
+    for s, (keep, near, away) in enumerate(pending):
         earlier = after(s, image_ids, patches, cotangent, gain, keep, near, away, earlier)
     block_out, patch_grad = earlier
     _, _, a_send, a_keep = att
 
     def reduce_batch(send, keep, rows):
-        flat = lambda a: a.reshape((a.shape[0], -1, dim))
-        parts = [flat(keep), flat(swap(send, "batch", nb, 1))]
+        parts = [keep, swap(send, "batch", nb, 1)]
         for bits in groups[:-1][::-1]:
             own, *sends = fold(rows, bits[-1], at, parts[0], parts[1:])
             parts = [own] + [swap(value, "batch", nb, (s + 1) << bits[-1]) for s, value in enumerate(sends)]
         return parts
 
-    f_parts = reduce_batch(f_send, f_keep, 0)
-    f_mine = f_parts[0] + sum(p.astype(F32) for p in f_parts[1:])
     f_mine = f_mine.reshape(2, nt, unit, dim)
     up = lax.all_to_all(f_mine[0], "tok", split_axis=0, concat_axis=0, tiled=True)
     a_parts = reduce_batch(a_send, a_keep, nt * unit)

time: 401 us -> 331 us (0.83)
  waiting for transfers between devices: 130 us -> 58.2 us
  starting transfers between devices: 90.7 us -> 70.7 us
  between operations: 1.35 us -> 14.5 us
    all_to_all x1, waiting for transfers between devices: 40.3 us -> 0.01 us  [per_device(): qkv = lax.all_to_all(src, 'tok', split_axis=0, concat_axis=0, tiled=True)]
    ppermute x31 -> x18, waiting for transfers between devices: 78.1 us -> 46.5 us  [swap(): return lax.ppermute(value, axis, [(i, i ^ mask) for i in range(count)])]
    ppermute x31 -> x18, starting transfers between devices: 40.2 us -> 21.5 us  [swap(): return lax.ppermute(value, axis, [(i, i ^ mask) for i in range(count)])]
    ppermute x5, waiting for transfers between devices: 9.9 us -> 0.01 us  [per_device(): lax.ppermute(v, both, [(b, a) for a, b in perm])]
    all_to_all x1, waiting for transfers between devices: 0.01 us -> 9.36 us  [per_device(): lax.all_to_all(f_mine[0], 'tok', split_axis=0, concat_axis=0, tiled=True)]
    unnamed x144 -> x122, local copies, waits for them, and re-layouts: 28 us -> 28.9 us
  transfers between devices with their start and end apart: 44 -> 34, of which waited for: 14 -> 8; matrix products, arithmetic and copies ran while one was open for 3% -> 5% of each run, Pallas kernels for 26% -> 30%
where the time goes in v1:
time: 331 us; the launch traced here: 327 us
  Pallas kernels  138 us (42%)
  starting transfers between devices  70.7 us (21%)
  waiting for transfers between devices  58.2 us (18%)
  local copies, waits for them, and re-layouts  36.8 us (11%)
  between operations  14.5 us (4%)
  other arithmetic  8.6 us (3%)
    pallas_call x3, Pallas kernels, attention(): pl.pallas_call(functools.partial(attention_kernel, heads, block, first, l...  68.3 us
    ppermute x18, waiting for transfers between devices, swap(): return lax.ppermute(value, axis, [(i, i ^ mask) for i in range(count)])  46.5 us
    unnamed x122, local copies, waits for them, and re-layouts  28.9 us
    pallas_call x1, Pallas kernels, ffn(): pl.pallas_call(functools.partial(ffn_kernel, block), out_shape=[act, act,...  25.5 us
    pallas_call x3, Pallas kernels, outputs(): pl.pallas_call(out_kernel, grid_spec=pltpu.PrefetchScalarGridSpec(num_sca...  22.8 us
    ppermute x18, starting transfers between devices, swap(): return lax.ppermute(value, axis, [(i, i ^ mask) for i in range(count)])  21.5 us
    ppermute x5, starting transfers between devices, per_device(): lax.ppermute(value, both, perm)  20.5 us
    ppermute x5, starting transfers between devices, per_device(): lax.ppermute(v, both, [(b, a) for a, b in perm])  17.4 us
  transfers between devices with their start and end apart: 34, of which 8 were waited for; matrix products, arithmetic and copies ran while one was open for 5% of the time, Pallas kernels for 30%

profile of v1, /device:TPU:2, one launch (start us, length us, event | category | flops | bytes accessed | tf_op | source)
XLA Modules:
  0.0 326.8 jit_solution(16729468262137046161)
XLA Ops:
  13.8 5.1 %before.1 = (bf16[2,256,768]{2,1,0:T(8,128)(2,1)}, bf16[2,2,256,768]{3,2,1,0:T(8,128)(2,1)}, bf16[4,25,1344]{2,1,0:T(8,128)(2,1)}, bf16[24,768]{1,0:T(8,128)(2,1...) custom-call(s32[3]{0:T(128)S(1)} %pad_add_fusion.at_ref, ...), custom_call_target="tpu_custom_call" | custom-call | flops 4718592 | bytes 4718592 | tf_op jit(solution)/shard_map/before/pallas_call | solution.py:97
  19.8 3.5 %all-to-all-start = ((bf16[4,25,1344]{2,1,0:T(8,128)(2,1)}), bf16[4,25,1344]{2,1,0:T(8,128)(2,1)S(1)}, u32[]{:S(2)}, u32[]{:S(2)}) async-start(bf16[4,25,1344]{2,1,0:T(8,128)(2,1)} %get-tuple-element.73), calls=%async_computation | async-start | bytes 720896 | tf_op jit(solution)/shard_map/all_to_all | solution.py:838
  23.3 5.9 %collective-permute-start = (bf16[24,768]{1,0:T(8,128)(2,1)S(1)}, bf16[24,768]{1,0:T(8,128)(2,1)S(1)}, u32[]{:S(2)}, u32[]{:S(2)}) collective-permute-start(bf16[24,768]{1,0:T(8,128)(2,1)S(1)} %get-tuple-element.74), channel_id=1, source_target_pairs={{7,0},{13,1},{3,2},{26,3},{0,4},{14,5},{20,6},{27,7},{8,8},{15,9},... | collective-permute-start | bytes 110600 | tf_op jit(solution)/shard_map/ppermute | solution.py:839
  32.2 3.8 %collective-permute-start.2 = (bf16[24,768]{1,0:T(8,128)(2,1)S(1)}, bf16[24,768]{1,0:T(8,128)(2,1)S(1)}, u32[]{:S(2)}, u32[]{:S(2)}) collective-permute-start(bf16[24,768]{1,0:T(8,128)(2,1)S(1)} %get-tuple-element.76), channel_id=1, source_target_pairs={{6,0},{13,1},{19,2},{4,3},{7,4},{1,5},{20,6},{26,7},{8,8},{14,9},{... | collective-permute-start | bytes 110600 | tf_op jit(solution)/shard_map/ppermute | solution.py:839
  38.3 5.5 %collective-permute-start.4 = (bf16[24,768]{1,0:T(8,128)(2,1)S(1)}, bf16[24,768]{1,0:T(8,128)(2,1)S(1)}, u32[]{:S(2)}, u32[]{:S(2)}) collective-permute-start(bf16[24,768]{1,0:T(8,128)(2,1)S(1)} %get-tuple-element.78), channel_id=1, source_target_pairs={{6,0},{12,1},{19,2},{25,3},{7,4},{13,5},{3,6},{26,7},{0,8},{14,9},... | collective-permute-start | bytes 110600 | tf_op jit(solution)/shard_map/ppermute | solution.py:839
  53.3 3.8 %collective-permute-done.7 = bf16[1,4,24,768]{3,2,1,0:T(8,128)(2,1)S(1)} collective-permute-done((bf16[1,4,24,768]{3,2,1,0:T(8,128)(2,1)}, bf16[1,4,24,768]{3,2,1,0:T(8,128)(2,1)S(1)}, u32[]{:S(2)}, u32[]{:S(2)}) %collective-permute-start.7) | collective-permute-done | bytes 147488 | tf_op jit(solution)/shard_map/ppermute | solution.py:740
  57.0 5.2 %collective-permute-done.6 = bf16[1,4,24,768]{3,2,1,0:T(8,128)(2,1)S(1)} collective-permute-done((bf16[1,4,24,768]{3,2,1,0:T(8,128)(2,1)}, bf16[1,4,24,768]{3,2,1,0:T(8,128)(2,1)S(1)}, u32[]{:S(2)}, u32[]{:S(2)}) %collective-permute-start.6) | collective-permute-done | bytes 147488 | tf_op jit(solution)/shard_map/ppermute | solution.py:740
  71.3 4.9 %collective-permute-done.11 = bf16[1,2,96,768]{3,2,1,0:T(8,128)(2,1)S(1)} collective-permute-done((bf16[1,2,96,768]{3,2,1,0:T(8,128)(2,1)}, bf16[1,2,96,768]{3,2,1,0:T(8,128)(2,1)S(1)}, u32[]{:S(2)}, u32[]{:S(2)}) %collective-permute-start.11) | collective-permute-done | bytes 294944 | tf_op jit(solution)/shard_map/ppermute | solution.py:740
  76.2 14.1 %collective-permute-done.10 = bf16[1,2,96,768]{3,2,1,0:T(8,128)(2,1)S(1)} collective-permute-done((bf16[1,2,96,768]{3,2,1,0:T(8,128)(2,1)}, bf16[1,2,96,768]{3,2,1,0:T(8,128)(2,1)S(1)}, u32[]{:S(2)}, u32[]{:S(2)}) %collective-permute-start.10) | collective-permute-done | bytes 294944 | tf_op jit(solution)/shard_map/ppermute | solution.py:740
  94.7 22.5 %attention.3 = (bf16[192,1024]{1,0:T(8,128)(2,1)}, bf16[576,1024]{1,0:T(8,128)(2,1)}, f32[2,64,128]{2,1,0:T(8,128)}, f32[576,768]{1,0:T(8,128)}, f32[192,768]{1,0:T(8,128)}) custom-call(s32[1]{0:T(128)} %bitcast.3.odd_ref, s32[1,1024]{1,0:T(1,128)} %get-tuple-element.141.ids_ref, f32[64,1]{1,0:T(8,128)} %copy.30.qg_ref, f32[64,1]{1,0:T(8,128)} %copy.31.kg_ref, ...), custom_call_target="tpu_custom_call" | custom-call | flops 14495514624 | bytes 6291456 | tf_op jit(solution)/shard_map/attention/pallas_call | solution.py:548
  118.2 25.5 %ffn.1 = (bf16[3072,768]{1,0:T(8,128)(2,1)}, bf16[3072,768]{1,0:T(8,128)(2,1)}, bf16[768,768]{1,0:T(8,128)(2,1)}, bf16[768,768]{1,0:T(8,128)(2,1)}, bf16[8,2,96,768]{3,2,1,0:T(8,128)(2,1)}, /*index=5*/f32[1,768]{1,0:T(1,128)}) custom-call(s32[3]{0:T(128)} %copy-done.40, bf16[4,2,96,768]{3,2,1,0:T(8,128)(2,1)} %copy-done.45, ...), custom_call_target="tpu_custom_call" | custom-call | flops 14495514624 | bytes 18874368 | tf_op jit(solution)/shard_map/ffn/pallas_call | solution.py:668
  148.7 7.9 %outputs.3 = (bf16[2,2,256,768]{3,2,1,0:T(8,128)(2,1)S(1)}, bf16[2,2,256,768]{3,2,1,0:T(8,128)(2,1)}) custom-call(s32[3]{0:T(128)S(1)} %copy-done.42, bf16[192,1024]{1,0:T(8,128)(2,1)S(1)} %copy-done.30, bf16[3072,768]{1,0:T(8,128)(2,1)S(1)} %copy-done, bf16[576,1024]{1,0:T(8,128)(2,1)S(1)} %copy-done.27, bf16[3072,768]{1,0:T(8,128)(2,1)} %get-tuple-element.92.gu_ref, ...), custom_call_target="tpu_custom_call" | custom-call | flops 3623878656 | bytes 7864320 | tf_op jit(solution)/shard_map/outputs/pallas_call | solution.py:722
  157.8 23.1 %attention.4 = (bf16[192,1024]{1,0:T(8,128)(2,1)}, bf16[576,1024]{1,0:T(8,128)(2,1)}, f32[2,64,128]{2,1,0:T(8,128)}, f32[576,768]{1,0:T(8,128)}, f32[192,768]{1,0:T(8,128)}) custom-call(s32[1]{0:T(128)} %bitcast.3.odd_ref, s32[1,1024]{1,0:T(1,128)} %get-tuple-element.142.ids_ref, f32[64,1]{1,0:T(8,128)} %copy.30.qg_ref, f32[64,1]{1,0:T(8,128)} %copy.31.kg_ref, ...), custom_call_target="tpu_custom_call" | custom-call | flops 14495514624 | bytes 6291456 | tf_op jit(solution)/shard_map/attention/pallas_call | solution.py:548
  187.0 7.9 %outputs.4 = (bf16[2,2,256,768]{3,2,1,0:T(8,128)(2,1)S(1)}, bf16[2,2,256,768]{3,2,1,0:T(8,128)(2,1)}) custom-call(s32[3]{0:T(128)S(1)} %copy-done.42, bf16[192,1024]{1,0:T(8,128)(2,1)S(1)} %copy-done.31, bf16[3072,768]{1,0:T(8,128)(2,1)S(1)} %bitcast.43, bf16[576,1024]{1,0:T(8,128)(2,1)S(1)} %copy-done.28, bf16[3072,768]{1,0:T(8,128)(2,1)} %get-tuple-element.92.gu_ref, ...), custom_call_target="tpu_custom_call" | custom-call | flops 3623878656 | bytes 7864320 | tf_op jit(solution)/shard_map/outputs/pallas_call | solution.py:722
  196.7 5.4 %collective-permute-start.15 = (bf16[2,256,768]{2,1,0:T(8,128)(2,1)}, bf16[2,256,768]{2,1,0:T(8,128)(2,1)}, u32[]{:S(2)}, u32[]{:S(2)}) collective-permute-start(bf16[2,256,768]{2,1,0:T(8,128)(2,1)} %fusion), channel_id=1, source_target_pairs={{0,2},{1,3},{2,0},{3,1},{4,6},{5,7},{6,4},{7,5},{8,10},{9,11},{10,... | collective-permute-start | bytes 2359304 | tf_op jit(solution)/shard_map/ppermute | solution.py:740
  202.0 22.7 %attention.5 = (bf16[192,1024]{1,0:T(8,128)(2,1)}, bf16[576,1024]{1,0:T(8,128)(2,1)}, bf16[4,104,768]{2,1,0:T(8,128)(2,1)}, f32[4,104,768]{2,1,0:T(8,128)}) custom-call(s32[1]{0:T(128)} %bitcast.3.odd_ref, s32[1,1024]{1,0:T(1,128)} %get-tuple-element.143.ids_ref, f32[64,1]{1,0:T(8,128)} %copy.30.qg_ref, f32[64,1]{1,0:T(8,128)} %copy.31.kg_ref, ...), custom_call_target="tpu_custom_call" | custom-call | flops 14495514624 | bytes 6291456 | tf_op jit(solution)/shard_map/attention/pallas_call | solution.py:548
  228.4 6.9 %outputs.5 = (bf16[2,2,256,768]{3,2,1,0:T(8,128)(2,1)S(1)}, bf16[2,2,256,768]{3,2,1,0:T(8,128)(2,1)S(1)}) custom-call(s32[3]{0:T(128)S(1)} %copy-done.42, bf16[192,1024]{1,0:T(8,128)(2,1)S(1)} %copy-done.29, bf16[3072,768]{1,0:T(8,128)(2,1)S(1)} %bitcast.43, bf16[576,1024]{1,0:T(8,128)(2,1)S(1)} %copy-done.26, bf16[3072,768]{1,0:T(8,128)(2,1)} %get-tuple-element.92.gu_ref, ...), custom_call_target="tpu_custom_call" | custom-call | flops 3623878656 | bytes 7864320 | tf_op jit(solution)/shard_map/outputs/pallas_call | solution.py:722
  236.3 16.0 %collective-permute-done.19.refs_0_ = bf16[4,104,768]{2,1,0:T(8,128)(2,1)S(1)} collective-permute-done((bf16[4,104,768]{2,1,0:T(8,128)(2,1)S(1)}, bf16[4,104,768]{2,1,0:T(8,128)(2,1)S(1)}, u32[]{:S(2)}, u32[]{:S(2)}) %collective-permute-start.19) | collective-permute-done | bytes 639008 | tf_op jit(solution)/shard_map/ppermute | solution.py:740
  253.8 3.3 collective-permute-start.21
  262.2 4.2 %all-to-all-start.2 = ((bf16[4,24,768]{2,1,0:T(8,128)(2,1)}), bf16[4,24,768]{2,1,0:T(8,128)(2,1)}, u32[]{:S(2)}, u32[]{:S(2)}) async-start(bf16[4,24,768]{2,1,0:T(8,128)(2,1)} %bitcast.46), calls=%async_computation.3 | async-start | bytes 294912 | tf_op jit(solution)/shard_map/all_to_all | solution.py:906
  271.2 9.4 %all-to-all-done.2.up_ref = bf16[4,24,768]{2,1,0:T(8,128)(2,1)} async-done(((bf16[4,24,768]{2,1,0:T(8,128)(2,1)}), bf16[4,24,768]{2,1,0:T(8,128)(2,1)}, u32[]{:S(2)}, u32[]{:S(2)}) %all-to-all-start.2) | async-done | bytes 147488 | tf_op jit(solution)/shard_map/all_to_all | solution.py:906
  280.6 3.5 %all-to-all-start.1 = ((f32[4,26,576]{2,1,0:T(8,128)}), f32[4,26,576]{2,1,0:T(8,128)S(1)}, u32[]{:S(2)}, u32[]{:S(2)}) async-start(f32[4,26,576]{2,1,0:T(8,128)} %get-tuple-element.130), calls=%async_computation.2 | async-start | bytes 655360 | tf_op jit(solution)/shard_map/all_to_all | solution.py:909
  286.7 5.7 %collective-permute-start.24 = (f32[24,768]{1,0:T(8,128)}, f32[24,768]{1,0:T(8,128)S(1)}, u32[]{:S(2)}, u32[]{:S(2)}) collective-permute-start(f32[24,768]{1,0:T(8,128)} %get-tuple-element.132), channel_id=1, source_target_pairs={{0,0},{1,13},{2,19},{3,26},{4,7},{5,14},{6,20},{7,5},{8,8},{9,2},{... | collective-permute-start | bytes 221192 | tf_op jit(solution)/shard_map/ppermute | solution.py:910
  297.6 3.9 %collective-permute-start.27 = (f32[24,768]{1,0:T(8,128)}, f32[24,768]{1,0:T(8,128)}, u32[]{:S(2)}, u32[]{:S(2)}) collective-permute-start(f32[24,768]{1,0:T(8,128)} %get-tuple-element.135), channel_id=1, source_target_pairs={{0,6},{1,12},{2,19},{3,25},{4,7},{5,13},{6,3},{7,26},{8,0},{9,14},... | collective-permute-start | bytes 221192 | tf_op jit(solution)/shard_map/ppermute | solution.py:910
  (199 shorter events, 92.6 us)
Async XLA Ops:
  7.2 87.5 %all-gather.5.cloned.1.call-start = ((), (), s32[]{:S(2)}) async-start(), calls=%async_computation.5 | async-start | bytes 3932160 | tf_op jit(solution)/shard_map/all_gather | solution.py:836
  19.0 98.2 %all-gather.7.cloned.1.call-start = ((), (), s32[]{:S(2)}) async-start(), calls=%async_computation.6 | async-start | bytes 7864320 | tf_op jit(solution)/shard_map/all_gather | solution.py:837
  19.8 25.7 %all-to-all-start = ((bf16[4,25,1344]{2,1,0:T(8,128)(2,1)}), bf16[4,25,1344]{2,1,0:T(8,128)(2,1)S(1)}, u32[]{:S(2)}, u32[]{:S(2)}) async-start(bf16[4,25,1344]{2,1,0:T(8,128)(2,1)} %get-tuple-element.73), calls=%async_computation | async-start | bytes 720896 | tf_op jit(solution)/shard_map/all_to_all | solution.py:838
  23.2 237.1 %reduce-scatter.2.cloned.1.call-start = ((), (), s32[]{:S(2)}) async-start(), calls=%async_computation.4 | async-start | bytes 2654208 | tf_op jit(solution)/shard_map/reduce_scatter | solution.py:882
  23.3 20.5 %collective-permute-start = (bf16[24,768]{1,0:T(8,128)(2,1)S(1)}, bf16[24,768]{1,0:T(8,128)(2,1)S(1)}, u32[]{:S(2)}, u32[]{:S(2)}) collective-permute-start(bf16[24,768]{1,0:T(8,128)(2,1)S(1)} %get-tuple-element.74), channel_id=1, source_target_pairs={{7,0},{13,1},{3,2},{26,3},{0,4},{14,5},{20,6},{27,7},{8,8},{15,9},... | collective-permute-start | bytes 110600 | tf_op jit(solution)/shard_map/ppermute | solution.py:839
  29.2 14.7 %collective-permute-start.1 = (bf16[24,768]{1,0:T(8,128)(2,1)S(1)}, bf16[24,768]{1,0:T(8,128)(2,1)S(1)}, u32[]{:S(2)}, u32[]{:S(2)}) collective-permute-start(bf16[24,768]{1,0:T(8,128)(2,1)S(1)} %get-tuple-element.75), channel_id=1, source_target_pairs={{0,0},{13,1},{19,2},{26,3},{7,4},{14,5},{20,6},{5,7},{8,8},{2,9},{... | collective-permute-start | bytes 110600 | tf_op jit(solution)/shard_map/ppermute | solution.py:839
  63.3 28.2 %collective-permute-start.8 = (bf16[4,4,24,768]{3,2,1,0:T(8,128)(2,1)S(1)}, bf16[4,4,24,768]{3,2,1,0:T(8,128)(2,1)S(1)}, u32[]{:S(2)}, u32[]{:S(2)}) collective-permute-start(bf16[4,4,24,768]{3,2,1,0:T(8,128)(2,1)S(1)} %maximum_bitcast_fusion.1.here_ref), channel_id=1, source_target_pairs={{0,4},{4,0},{8,12},{12,8},{16,20},{20,16},{24,28},{28,24},{1,5},{5... | collective-permute-start | bytes 1769480 | tf_op jit(solution)/shard_map/ppermute | solution.py:740
  66.4 24.0 %collective-permute-start.10 = (bf16[1,2,96,768]{3,2,1,0:T(8,128)(2,1)}, bf16[1,2,96,768]{3,2,1,0:T(8,128)(2,1)S(1)}, u32[]{:S(2)}, u32[]{:S(2)}) collective-permute-start(bf16[1,2,96,768]{3,2,1,0:T(8,128)(2,1)} %bitcast.48), channel_id=1, source_target_pairs={{0,16},{4,20},{8,24},{12,28},{16,0},{20,4},{24,8},{28,12},{1,17},{... | collective-permute-start | bytes 884744 | tf_op jit(solution)/shard_map/ppermute | solution.py:740
  66.4 23.9 %collective-permute-start.9 = (bf16[1,2,96,768]{3,2,1,0:T(8,128)(2,1)}, bf16[1,2,96,768]{3,2,1,0:T(8,128)(2,1)S(1)}, u32[]{:S(2)}, u32[]{:S(2)}) collective-permute-start(bf16[1,2,96,768]{3,2,1,0:T(8,128)(2,1)} %bitcast.49), channel_id=1, source_target_pairs={{0,8},{4,12},{8,0},{12,4},{16,24},{20,28},{24,16},{28,20},{1,9},{5... | collective-permute-start | bytes 884744 | tf_op jit(solution)/shard_map/ppermute | solution.py:740
  91.5 25.7 %collective-permute-start.12 = (bf16[4,2,96,768]{3,2,1,0:T(8,128)(2,1)S(1)}, bf16[4,2,96,768]{3,2,1,0:T(8,128)(2,1)S(1)}, u32[]{:S(2)}, u32[]{:S(2)}) collective-permute-start(bf16[4,2,96,768]{3,2,1,0:T(8,128)(2,1)S(1)} %maximum_bitcast_fusion.here_ref), channel_id=1, source_target_pairs={{0,4},{4,0},{8,12},{12,8},{16,20},{20,16},{24,28},{28,24},{1,5},{5... | collective-permute-start | bytes 3538952 | tf_op jit(solution)/shard_map/ppermute | solution.py:740
  157.7 23.2 %collective-permute-start.13 = (bf16[2,2,256,768]{3,2,1,0:T(8,128)(2,1)}, bf16[2,2,256,768]{3,2,1,0:T(8,128)(2,1)}, u32[]{:S(2)}, u32[]{:S(2)}) collective-permute-start(bf16[2,2,256,768]{3,2,1,0:T(8,128)(2,1)} %get-tuple-element.101), channel_id=1, source_target_pairs={{0,1},{1,0},{2,3},{3,2},{4,5},{5,4},{6,7},{7,6},{8,9},{9,8},{10,11... | collective-permute-start | bytes 4718600 | tf_op jit(solution)/shard_map/ppermute | solution.py:740
  196.1 28.7 %collective-permute-start.14 = (bf16[2,2,256,768]{3,2,1,0:T(8,128)(2,1)}, bf16[2,2,256,768]{3,2,1,0:T(8,128)(2,1)}, u32[]{:S(2)}, u32[]{:S(2)}) collective-permute-start(bf16[2,2,256,768]{3,2,1,0:T(8,128)(2,1)} %get-tuple-element.111), channel_id=1, source_target_pairs={{0,1},{1,0},{2,3},{3,2},{4,5},{5,4},{6,7},{7,6},{8,9},{9,8},{10,11... | collective-permute-start | bytes 4718600 | tf_op jit(solution)/shard_map/ppermute | solution.py:740
  196.7 30.8 %collective-permute-start.15 = (bf16[2,256,768]{2,1,0:T(8,128)(2,1)}, bf16[2,256,768]{2,1,0:T(8,128)(2,1)}, u32[]{:S(2)}, u32[]{:S(2)}) collective-permute-start(bf16[2,256,768]{2,1,0:T(8,128)(2,1)} %fusion), channel_id=1, source_target_pairs={{0,2},{1,3},{2,0},{3,1},{4,6},{5,7},{6,4},{7,5},{8,10},{9,11},{10,... | collective-permute-start | bytes 2359304 | tf_op jit(solution)/shard_map/ppermute | solution.py:740
  235.4 22.6 %collective-permute-start.16 = (bf16[2,2,256,768]{3,2,1,0:T(8,128)(2,1)S(1)}, bf16[2,2,256,768]{3,2,1,0:T(8,128)(2,1)S(1)}, u32[]{:S(2)}, u32[]{:S(2)}) collective-permute-start(bf16[2,2,256,768]{3,2,1,0:T(8,128)(2,1)S(1)} %get-tuple-element.116), channel_id=1, source_target_pairs={{0,1},{1,0},{2,3},{3,2},{4,5},{5,4},{6,7},{7,6},{8,9},{9,8},{10,11... | collective-permute-start | bytes 4718600 | tf_op jit(solution)/shard_map/ppermute | solution.py:740
  235.5 16.8 %collective-permute-start.19 = (bf16[4,104,768]{2,1,0:T(8,128)(2,1)S(1)}, bf16[4,104,768]{2,1,0:T(8,128)(2,1)S(1)}, u32[]{:S(2)}, u32[]{:S(2)}) collective-permute-start(bf16[4,104,768]{2,1,0:T(8,128)(2,1)S(1)} %copy-done.58), channel_id=1, source_target_pairs={{0,4},{4,0},{8,12},{12,8},{16,20},{20,16},{24,28},{28,24},{1,5},{5... | collective-permute-start | bytes 1916936 | tf_op jit(solution)/shard_map/ppermute | solution.py:740
  236.3 58.1 %collective-permute-start.18 = (bf16[2,256,768]{2,1,0:T(8,128)(2,1)}, bf16[2,256,768]{2,1,0:T(8,128)(2,1)}, u32[]{:S(2)}, u32[]{:S(2)}) collective-permute-start(bf16[2,256,768]{2,1,0:T(8,128)(2,1)} %fusion.1), channel_id=1, source_target_pairs={{0,2},{1,3},{2,0},{3,1},{4,6},{5,7},{6,4},{7,5},{8,10},{9,11},{10,... | collective-permute-start | bytes 2359304 | tf_op jit(solution)/shard_map/ppermute | solution.py:740
  253.8 15.2 %collective-permute-start.21 = (bf16[1,104,768]{2,1,0:T(8,128)(2,1)S(1)}, bf16[1,104,768]{2,1,0:T(8,128)(2,1)}, u32[]{:S(2)}, u32[]{:S(2)}) collective-permute-start(bf16[1,104,768]{2,1,0:T(8,128)(2,1)S(1)} %get-tuple-element.127), channel_id=1, source_target_pairs={{0,16},{4,20},{8,24},{12,28},{16,0},{20,4},{24,8},{28,12},{1,17},{... | collective-permute-start | bytes 479240 | tf_op jit(solution)/shard_map/ppermute | solution.py:740
  260.3 55.5 %collective-permute-start.17 = (bf16[2,256,768]{2,1,0:T(8,128)(2,1)}, bf16[2,256,768]{2,1,0:T(8,128)(2,1)S(1)}, u32[]{:S(2)}, u32[]{:S(2)}) collective-permute-start(bf16[2,256,768]{2,1,0:T(8,128)(2,1)} %fusion.2), channel_id=1, source_target_pairs={{0,2},{1,3},{2,0},{3,1},{4,6},{5,7},{6,4},{7,5},{8,10},{9,11},{10,... | collective-permute-start | bytes 2359304 | tf_op jit(solution)/shard_map/ppermute | solution.py:740
  262.2 18.4 %all-to-all-start.2 = ((bf16[4,24,768]{2,1,0:T(8,128)(2,1)}), bf16[4,24,768]{2,1,0:T(8,128)(2,1)}, u32[]{:S(2)}, u32[]{:S(2)}) async-start(bf16[4,24,768]{2,1,0:T(8,128)(2,1)} %bitcast.46), calls=%async_computation.3 | async-start | bytes 294912 | tf_op jit(solution)/shard_map/all_to_all | solution.py:906
  280.6 29.7 %all-to-all-start.1 = ((f32[4,26,576]{2,1,0:T(8,128)}), f32[4,26,576]{2,1,0:T(8,128)S(1)}, u32[]{:S(2)}, u32[]{:S(2)}) async-start(f32[4,26,576]{2,1,0:T(8,128)} %get-tuple-element.130), calls=%async_computation.2 | async-start | bytes 655360 | tf_op jit(solution)/shard_map/all_to_all | solution.py:909
  284.0 13.5 %collective-permute-start.23 = (f32[24,768]{1,0:T(8,128)}, f32[24,768]{1,0:T(8,128)S(1)}, u32[]{:S(2)}, u32[]{:S(2)}) collective-permute-start(f32[24,768]{1,0:T(8,128)} %get-tuple-element.131), channel_id=1, source_target_pairs={{0,7},{1,13},{2,3},{3,26},{4,0},{5,14},{6,20},{7,27},{8,8},{9,15},... | collective-permute-start | bytes 221192 | tf_op jit(solution)/shard_map/ppermute | solution.py:910
  286.7 22.3 %collective-permute-start.24 = (f32[24,768]{1,0:T(8,128)}, f32[24,768]{1,0:T(8,128)S(1)}, u32[]{:S(2)}, u32[]{:S(2)}) collective-permute-start(f32[24,768]{1,0:T(8,128)} %get-tuple-element.132), channel_id=1, source_target_pairs={{0,0},{1,13},{2,19},{3,26},{4,7},{5,14},{6,20},{7,5},{8,8},{9,2},{... | collective-permute-start | bytes 221192 | tf_op jit(solution)/shard_map/ppermute | solution.py:910
  292.4 16.5 %collective-permute-start.25 = (f32[24,768]{1,0:T(8,128)}, f32[24,768]{1,0:T(8,128)S(1)}, u32[]{:S(2)}, u32[]{:S(2)}) collective-permute-start(f32[24,768]{1,0:T(8,128)} %get-tuple-element.133), channel_id=1, source_target_pairs={{0,6},{1,13},{2,19},{3,4},{4,7},{5,1},{6,20},{7,26},{8,8},{9,14},{... | collective-permute-start | bytes 221192 | tf_op jit(solution)/shard_map/ppermute | solution.py:910
  294.4 14.6 %collective-permute-start.26 = (f32[24,768]{1,0:T(8,128)}, f32[24,768]{1,0:T(8,128)S(1)}, u32[]{:S(2)}, u32[]{:S(2)}) collective-permute-start(f32[24,768]{1,0:T(8,128)} %get-tuple-element.134), channel_id=1, source_target_pairs={{0,6},{1,1},{2,19},{3,25},{4,7},{5,13},{6,20},{7,26},{8,8},{9,14},... | collective-permute-start | bytes 221192 | tf_op jit(solution)/shard_map/ppermute | solution.py:910
  (71 other events, 779.3 us)
Sparse Core Ops, SparseCore 0:
  19.1 31.9 all-gather.4
  52.6 46.2 all-gather.6
  157.9 72.6 reduce-scatter.1

commit v2 on v1

v2 whole, which is shorter than its diff:
```python
import functools
import math

import jax
import jax.numpy as jnp
import numpy as np
from jax import lax
from jax.experimental import pallas as pl
from jax.experimental.pallas import tpu as pltpu
from jax.sharding import PartitionSpec as P

H = 12
HD = 64
SLOTS = 4
EPS = 1e-06
BIG = 2048.0
LOG2E = 1.4426950408889634
BF = jnp.bfloat16
F32 = jnp.float32
NN = (((1,), (0,)), ((), ()))
NT = (((1,), (1,)), ((), ()))
TN = (((0,), (0,)), ((), ()))
MIB = 1 << 20

VMEM = pl.BlockSpec(memory_space=pltpu.VMEM)
SMEM = pl.BlockSpec(memory_space=pltpu.SMEM)
ANY = pl.BlockSpec(memory_space=pl.ANY)
HBM = pl.BlockSpec(memory_space=pltpu.HBM)


def mm(a, b, dims=NN):
    return lax.dot_general(a, b, dims, preferred_element_type=F32)


def normalize(values):
    center = values - jnp.mean(values, axis=-1, keepdims=True)
    inverse = lax.rsqrt(jnp.mean(center * center, axis=-1, keepdims=True) + EPS)
    return center * inverse, inverse


def norm_back(grad_unit, unit_rows, inverse):
    return inverse * (
        grad_unit
        - jnp.mean(grad_unit, axis=-1, keepdims=True)
        - unit_rows * jnp.mean(grad_unit * unit_rows, axis=-1, keepdims=True)
    )


def column(row):
    return jnp.broadcast_to(row, (8, row.shape[1])).T[:, 0:1]


def before_kernel(at_ref, table_ref, ids_ref, gain_ref, x_hbm, cot_hbm, win_hbm, wout_hbm, *refs):
    outs, (x_ref, cot_ref, win_ref, wout_ref, pay_ref, in_sem, out_sem) = refs[:-7], refs[-7:]
    seqs, part, _ = x_ref.shape
    pays, (src_ref, *unit_refs) = outs[:2], outs[2:]
    ins = [
        pltpu.make_async_copy(a, b, in_sem.at[i])
        for i, (a, b) in enumerate(((win_hbm, win_ref), (wout_hbm, wout_ref), (x_hbm, x_ref), (cot_hbm, cot_ref)))
    ]
    for copy in ins:
        copy.start()
    nt, rows = src_ref.shape[0], win_ref.shape[0]
    local = H * HD // nt
    units = (win_ref.shape[1] - 3 * H * HD) // nt
    ins[0].wait()
    ins[1].wait()
    for k, ref in enumerate(unit_refs):
        ref[...] = wout_ref[table_ref[at_ref[0], k]]
    for t in range(nt):
        for k in range(3):
            src_ref[t, :rows, k * local : (k + 1) * local] = win_ref[:, k * H * HD + t * local : k * H * HD + (t + 1) * local]
        src_ref[t, :rows, 3 * local :] = win_ref[:, 3 * H * HD + t * units : 3 * H * HD + (t + 1) * units]
        for s in range(seqs):
            src_ref[t, rows:, s * part : (s + 1) * part] = ids_ref[s : s + 1, :].astype(F32).astype(BF)
        src_ref[t, rows:, seqs * part :] = jnp.zeros((1, 3 * local + units - seqs * part), BF)
    ins[2].wait()
    ins[3].wait()
    copies = []
    for s in range(seqs):
        unit, _ = normalize(x_ref[s].astype(F32))
        live = column(jnp.where(ids_ref[s : s + 1, :] >= 0, 1.0, 0.0))
        pay_ref[s, 0] = (unit * gain_ref[...]).astype(BF)
        pay_ref[s, 1] = (live * cot_ref[s].astype(F32)).astype(BF)
        copies.append(pltpu.make_async_copy(pay_ref.at[s], pays[0].at[s] if s < seqs - 1 else pays[1], out_sem.at[s]))
        copies[-1].start()
    for copy in copies:
        copy.wait()


def before(at, table, ids, gain, x, cot, w_in, w_out):
    seqs, part, dim = x.shape
    per, unit, _ = w_out.shape
    rows, wide = w_in.shape
    outs = [jax.ShapeDtypeStruct((seqs - 1, 2, part, dim), BF), jax.ShapeDtypeStruct((2, part, dim), BF)]
    outs += [jax.ShapeDtypeStruct((SLOTS, rows + 1, wide // SLOTS), BF)]
    outs += [jax.ShapeDtypeStruct((unit, dim), BF)] * per
    return pl.pallas_call(
        before_kernel,
        out_shape=outs,
        in_specs=[SMEM] * 2 + [VMEM] * 2 + [HBM] * 4,
        out_specs=[HBM] * 2 + [VMEM] * (1 + per),
        scratch_shapes=[
            pltpu.VMEM(x.shape, BF),
            pltpu.VMEM(x.shape, BF),
            pltpu.VMEM(w_in.shape, BF),
            pltpu.VMEM(w_out.shape, BF),
            pltpu.VMEM((seqs, 2, part, dim), BF),
            pltpu.SemaphoreType.DMA((4,)),
            pltpu.SemaphoreType.DMA((seqs,)),
        ],
        cost_estimate=pl.CostEstimate(flops=x.size * 8, transcendentals=0, bytes_accessed=x.size * 8),
        compiler_params=pltpu.CompilerParams(vmem_limit_bytes=32 * MIB),
        name="before",
    )(at, table, ids, gain, x, cot, w_in, w_out)


def pack_in(w_in, seqs, part):
    nt, high, wide = w_in.shape
    unit = high - 1
    local = H * HD // nt
    length = nt * part

    def kernel(win_ref, a_ref, u_ref, ids_ref):
        for t in range(nt):
            a_ref[t] = win_ref[t, :unit, : 3 * local]
            u_ref[t] = win_ref[t, :unit, 3 * local :]
            row = win_ref[t, unit:, : seqs * part].astype(F32).astype(jnp.int32)
            for s in range(seqs):
                ids_ref[s, :, t * part : (t + 1) * part] = row[:, s * part : (s + 1) * part]

    return pl.pallas_call(
        kernel,
        out_shape=[
            jax.ShapeDtypeStruct((nt, unit, 3 * local), BF),
            jax.ShapeDtypeStruct((nt, unit, wide - 3 * local), BF),
            jax.ShapeDtypeStruct((seqs, 1, length), jnp.int32),
        ],
        in_specs=[VMEM],
        out_specs=[VMEM] * 3,
        cost_estimate=pl.CostEstimate(flops=1000, transcendentals=0, bytes_accessed=w_in.size * 4),
        name="pack_in",
    )(w_in)


def pack_out(at, table, got):
    unit, dim = got[0].shape
    per = len(got)

    def kernel(at_ref, table_ref, *refs):
        got_refs, (wo_ref, ff_ref, all_ref) = refs[:per], refs[per:]
        for k, ref in enumerate(got_refs):
            all_ref[table_ref[at_ref[0], per + k]] = ref[...]
        wo_ref[...] = all_ref[0]
        for k in range(per - 1):
            ff_ref[k] = all_ref[k + 1]

    return pl.pallas_call(
        kernel,
        out_shape=[jax.ShapeDtypeStruct((unit, dim), BF), jax.ShapeDtypeStruct((per - 1, unit, dim), BF)],
        in_specs=[SMEM] * 2 + [VMEM] * per,
        out_specs=[VMEM] * 2,
        scratch_shapes=[pltpu.VMEM((per, unit, dim), BF)],
        cost_estimate=pl.CostEstimate(flops=1000, transcendentals=0, bytes_accessed=unit * dim * 30),
        name="pack_out",
    )(at, table, *got)


def join(at, qkv_parts, wo_parts):
    nt, unit, wide = qkv_parts[0][0].shape[1:]
    dim = wo_parts[0][0].shape[2]
    count = sum(len(masks) for _, masks in qkv_parts)

    def kernel(at_ref, *refs):
        ins, (wqkv_ref, wo_ref, all_ref) = refs[:-3], refs[-3:]
        for k, (_, masks) in enumerate(qkv_parts + wo_parts):
            to = all_ref if k < len(qkv_parts) else wo_ref
            for i, mask in enumerate(masks):
                to[at_ref[2] ^ mask] = ins[k][i]
        wqkv_ref[...] = all_ref[...].reshape(dim, wide).T

    return pl.pallas_call(
        kernel,
        out_shape=[jax.ShapeDtypeStruct((wide, dim), BF), jax.ShapeDtypeStruct((count, unit, dim), BF)],
        in_specs=[SMEM] + [VMEM] * (len(qkv_parts) + len(wo_parts)),
        out_specs=[VMEM] * 2,
        scratch_shapes=[pltpu.VMEM((count, nt, unit, wide), BF)],
        cost_estimate=pl.CostEstimate(flops=1000, transcendentals=0, bytes_accessed=dim * dim * 8),
        compiler_params=pltpu.CompilerParams(vmem_limit_bytes=32 * MIB),
        name="join",
    )(at, *[a for a, _ in qkv_parts + wo_parts])


def resplit(total, rows):
    first = total[rows : rows + 1] + total[rows + 1 : rows + 2]
    second = total[rows + 2 : rows + 3] + total[rows + 3 : rows + 4]
    return term_rows(first, second)


def term_rows(first, second):
    def terms(v):
        hi = v.astype(BF).astype(F32)
        return [hi, (v - hi).astype(BF).astype(F32)]

    return jnp.concatenate(terms(first) + terms(second) + [jnp.zeros((4, first.shape[1]), F32)], axis=0)


def fold(rows, low, at, keep, got):
    n, high, dim = keep.shape

    def kernel(at_ref, keep_ref, *refs):
        got_refs, (own_ref, *send_refs) = refs[: len(got)], refs[len(got) :]
        mine = (at_ref[2] >> low) & 3
        for i in range(n // 4):
            for s, to in enumerate([own_ref] + send_refs):
                at_block = i * 4 + (mine ^ s)
                total = keep_ref[at_block]
                for ref in got_refs:
                    total = total + ref[at_block].astype(F32)
                if rows:
                    to[i, :rows] = total[:rows].astype(to.dtype)
                    to[i, rows:] = resplit(total, rows).astype(to.dtype)
                else:
                    to[i] = total.astype(to.dtype)

    out = lambda t: jax.ShapeDtypeStruct((n // 4, high, dim), t)
    return pl.pallas_call(
        kernel,
        out_shape=[out(F32)] + [out(BF)] * 3,
        in_specs=[SMEM] + [VMEM] * (1 + len(got)),
        out_specs=[VMEM] * 4,
        cost_estimate=pl.CostEstimate(flops=keep.size, transcendentals=0, bytes_accessed=keep.size * 8),
        compiler_params=pltpu.CompilerParams(vmem_limit_bytes=48 * MIB),
        name="fold",
    )(at, keep, *got)


def leave(at, table, a_parts, f_units, local):
    own = a_parts[0]
    per = f_units.shape[0] + 1
    _, unit, dim = f_units.shape
    rows = SLOTS * unit
    width = 3 * local

    def kernel(at_ref, table_ref, p0, p1, p2, p3, f_ref, src_ref, *outs):
        out_refs, (all_ref,) = outs[:-1], outs[-1:]
        total = (p0[0] + p1[0].astype(F32)) + (p2[0].astype(F32) + p3[0].astype(F32))
        first = total[rows : rows + 1] + total[rows + 1 : rows + 2]
        second = total[rows + 2 : rows + 3] + total[rows + 3 : rows + 4]
        for t in range(SLOTS):
            src_ref[t, :unit] = total[t * unit : (t + 1) * unit, :width]
            src_ref[t, unit : unit + 1] = first[:, :width]
            src_ref[t, unit + 1 : unit + 2] = jnp.concatenate(
                [first[:, width:], second[:, :128], jnp.zeros((1, 2 * width - dim - 128), F32)], axis=1
            )
        for c in range(SLOTS):
            all_ref[0, :, c * local : (c + 1) * local] = total[c * unit : (c + 1) * unit, width:]
        for k in range(per - 1):
            all_ref[k + 1] = f_ref[k].astype(F32)
        for k, ref in enumerate(out_refs):
            ref[...] = all_ref[table_ref[at_ref[0], per + k]]

    return pl.pallas_call(
        kernel,
        out_shape=[jax.ShapeDtypeStruct((SLOTS, unit + 2, width), F32)] + [jax.ShapeDtypeStruct((unit, dim), F32)] * per,
        in_specs=[SMEM] * 2 + [VMEM] * 5,
        out_specs=[VMEM] * (1 + per),
        scratch_shapes=[pltpu.VMEM((per, unit, dim), F32)],
        cost_estimate=pl.CostEstimate(flops=own.size, transcendentals=0, bytes_accessed=own.size * 20),
        name="leave",
    )(at, table, *a_parts, f_units)


def place(at, table, qkv, up, got):
    nt, high, width = qkv.shape
    unit, dim = got[0].shape
    per = len(got)
    local = width // 3
    wide = nt * (width + up.shape[2])

    def kernel(at_ref, table_ref, qkv_ref, up_ref, *refs):
        got_refs, (in_ref, out_ref, norm_ref, q_ref, k_ref) = refs[:per], refs[per:]
        for t in range(nt):
            for k in range(3):
                in_ref[:, k * nt * local + t * local : k * nt * local + (t + 1) * local] = qkv_ref[t, :unit, k * local : (k + 1) * local]
            in_ref[:, nt * width + t * dim : nt * width + (t + 1) * dim] = up_ref[t].astype(F32)
        for k, ref in enumerate(got_refs):
            out_ref[table_ref[at_ref[0], k]] = ref[...]
        total = qkv_ref[0, unit:]
        for t in range(1, nt):
            total = total + qkv_ref[t, unit:]
        norm_ref[:, :width] = total[0:1]
        norm_ref[:, width:] = total[1:2, : dim - width]
        q_ref[...] = total[1:2, dim - width : dim - width + HD]
        k_ref[...] = total[1:2, dim - width + HD : dim - width + 2 * HD]

    return pl.pallas_call(
        kernel,
        out_shape=[
            jax.ShapeDtypeStruct((unit, wide), F32),
            jax.ShapeDtypeStruct((per, unit, dim), F32),
            jax.ShapeDtypeStruct((1, dim), F32),
            jax.ShapeDtypeStruct((1, HD), F32),
            jax.ShapeDtypeStruct((1, HD), F32),
        ],
        in_specs=[SMEM] * 2 + [VMEM] * (2 + per),
        out_specs=[VMEM] * 5,
        cost_estimate=pl.CostEstimate(flops=1000, transcendentals=0, bytes_accessed=unit * wide * 16),
        name="place",
    )(at, table, qkv, up, *got)


def after_kernel(s, ids_ref, x_ref, cot_ref, gain_ref, keep_ref, near_ref, far_ref, *rest):
    out_ref, grad_ref = rest[-2:]
    unit, inverse = normalize(x_ref[0].astype(F32))
    live = column(jnp.where(ids_ref[s : s + 1, :] >= 0, 1.0, 0.0))
    both = keep_ref[0, 0].astype(F32) + near_ref[0, 0].astype(F32) + far_ref[0].astype(F32)
    out_ref[0] = (live * (x_ref[0].astype(F32) + both[0])).astype(BF)
    grad_ref[0] = (
        live * cot_ref[0].astype(F32) + norm_back(both[1] * gain_ref[...], unit, inverse)
    ).astype(BF)


def after(s, i, ids, x, cot, gain, keep, near, far, earlier):
    x, cot, keep, near, far = (pltpu.with_memory_space_constraint(a, pltpu.HBM) for a in (x, cot, keep, near, far))
    seqs, part, dim = x.shape
    one = pl.BlockSpec((1, part, dim), lambda g: (s, 0, 0))
    pair = pl.BlockSpec((1, 1, 2, part, dim), lambda g: (0, i, 0, 0, 0))
    lone = pl.BlockSpec((1, 2, part, dim), lambda g: (i, 0, 0, 0))
    fixed = lambda a: pl.BlockSpec(a.shape, lambda g: (0,) * a.ndim)
    return pl.pallas_call(
        functools.partial(after_kernel, s),
        grid=(1,),
        out_shape=[jax.ShapeDtypeStruct(x.shape, BF)] * 2,
        in_specs=[fixed(ids), one, one, fixed(gain), pair, pair, lone] + [ANY] * len(earlier),
        out_specs=[one, one],
        input_output_aliases={7 + i: i for i in range(len(earlier))},
        cost_estimate=pl.CostEstimate(flops=part * dim * 20, transcendentals=0, bytes_accessed=part * dim * 20),
        compiler_params=pltpu.CompilerParams(vmem_limit_bytes=32 * MIB),
        name="after",
    )(ids, x, cot, gain, keep, near, far, *earlier)


def split_rows(odd, grad, send_ref, keep_ref, parts, rows, store):
    for z in range(parts):
        low = grad[2 * z * rows : (2 * z + 1) * rows]
        high = grad[(2 * z + 1) * rows : (2 * z + 2) * rows]
        store(send_ref, z, jnp.where(odd, low, high).astype(BF))
        store(keep_ref, z, jnp.where(odd, high, low))


def attention_kernel(
    heads, block, last,
    odd_ref, ids_ref, qg_ref, kg_ref, wqkv_hbm, wo_hbm, pay_hbm, *refs,
):
    if last:
        (acc_sums_ref, fnp_ref, gain_ref, accq_hbm, acco_hbm), refs = refs[:5], refs[5:]
        (o_hbm, grad_hbm, send_ref, keep_ref, sums_ref), refs = refs[:5], refs[5:]
    else:
        (o_hbm, grad_hbm, sums_ref, newq_hbm, newo_hbm), refs = refs[:5], refs[5:]
    (
        wqkv_ref, wo_ref, norm_ref, gb_ref, o_ref, grad_ref, gq_ref, go_ref, raw_ref,
        qt_ref, qn_ref, kt_ref, ka_ref, vt_ref, va_ref, do_ref, dq_ref, dk_ref, dv_ref, pad_ref, vm_ref,
        w_sem, sem, out_sem,
    ) = refs
    seqs, length, dim = norm_ref.shape
    part = length // SLOTS
    width = heads * HD
    blocks = length // block
    loads = [pltpu.make_async_copy(wqkv_hbm, wqkv_ref, w_sem.at[0]), pltpu.make_async_copy(wo_hbm, wo_ref, w_sem.at[1])]
    loads[0].start()

    def pay_copy(s, j, t):
        to = (norm_ref, gb_ref)[j].at[s, pl.ds(t * part, part), :]
        return pltpu.make_async_copy(pay_hbm.at[t, s, j], to, sem.at[s, j * SLOTS + t])

    for s in range(seqs):
        for j in range(2):
            for t in range(SLOTS):
                pay_copy(s, j, t).start()
            if s + j == 0:
                loads[1].start()
    if last:
        loads.append(pltpu.make_async_copy(accq_hbm, gq_ref, w_sem.at[2]))
        loads.append(pltpu.make_async_copy(acco_hbm, go_ref, w_sem.at[3]))
        loads[2].start()
        loads[3].start()
        sums_ref[...] = acc_sums_ref[...]
    else:
        gq_ref[...] = jnp.zeros_like(gq_ref)
        go_ref[...] = jnp.zeros_like(go_ref)
        sums_ref[...] = jnp.zeros_like(sums_ref)
    gain_q = qg_ref[...]
    gain_k = kg_ref[...]
    marks = lax.broadcasted_iota(jnp.int32, (HD, length), 0)
    v_tail = jnp.where(lax.broadcasted_iota(jnp.int32, (length, HD), 1) < 2, 1.0, 0.0).astype(BF)
    ones = jnp.where(lax.broadcasted_iota(jnp.int32, (16, length), 0) == 0, 1.0, 0.0).astype(BF)
    spot = lax.broadcasted_iota(jnp.int32, (HD, block), 0)
    scale = 1.0 / math.sqrt(HD)
    cut = lambda a, i: a[:, i * block : (i + 1) * block]

    def unit_of(row):
        raw = raw_ref[pl.ds(pl.multiple_of(row, HD), HD), :]
        center = raw - jnp.mean(raw, axis=0, keepdims=True)
        inverse = lax.rsqrt(jnp.mean(center * center, axis=0, keepdims=True) + EPS)
        return center * inverse, inverse

    def lanes(a):
        total = a[:, :128]
        for i in range(1, length // 128):
            total = total + a[:, i * 128 : (i + 1) * 128]
        return total

    def stores(s):
        return [
            pltpu.make_async_copy(o_ref.at[s], o_hbm.at[s], out_sem.at[s, 0]),
            pltpu.make_async_copy(grad_ref.at[s], grad_hbm.at[s], out_sem.at[s, 1]),
        ]

    loads[0].wait()
    loads[1].wait()

    def sequence(s, carry):
        ids = ids_ref[s]
        same = marks == ids + 1
        k_tail = jnp.where(same, 1.0, 0.0).T.astype(BF)
        q_tail = jnp.where((same & (ids >= 0)) | (marks > 4), 0.0, -BIG).astype(BF)
        pad = jnp.where(ids < 0, 1.0, 0.0)
        for i in range(blocks):
            pad_ref[i] = cut(pad, i)
        for t in range(SLOTS):
            pay_copy(s, 0, t).wait()
        raw_ref[...] = mm(wqkv_ref[...], norm_ref[s], NT)
        for t in range(SLOTS):
            pay_copy(s, 1, t).wait()
        do_all = mm(wo_ref[...], gb_ref[s], NT).astype(BF)
        for h in range(heads):
            for i in range(blocks):
                do_ref[h * blocks + i] = cut(do_all[h * HD : (h + 1) * HD], i)

        def prepare(h, carry):
            q_unit, _ = unit_of(h * HD)
            q = q_unit * gain_q
            qn = q.T.astype(BF)
            for i in range(blocks):
                qt_ref[h * blocks + i, :HD] = cut(q, i).astype(BF)
                qt_ref[h * blocks + i, HD:] = cut(q_tail, i)
                qn_ref[h * blocks + i] = qn[i * block : (i + 1) * block]
            k_unit, _ = unit_of(width + h * HD)
            k = k_unit * gain_k
            kt_ref[h] = k.astype(BF)
            ka_ref[h, :, :HD] = k.T.astype(BF)
            ka_ref[h, :, HD:] = k_tail
            v = raw_ref[pl.ds(pl.multiple_of(2 * width + h * HD, HD), HD), :]
            vb = v.astype(BF)
            vt_ref[h, :HD] = vb
            vt_ref[h, HD:] = ones
            va_ref[h, :, :HD] = v.T.astype(BF)
            va_ref[h, :, HD:] = v_tail
            vm_ref[h] = jnp.mean(vb.astype(F32), axis=1, keepdims=True)
            dk_ref[h] = jnp.zeros(dk_ref.shape[1:], F32)
            dv_ref[h] = jnp.zeros(dv_ref.shape[1:], F32)
            return carry

        lax.fori_loop(0, heads, prepare, 0)

        def step(n, carry):
            h = n // blocks
            padb = pad_ref[n % blocks]
            e = jnp.exp2(mm(ka_ref[h], qt_ref[n]) * (LOG2E * scale))
            eb = e.astype(BF)
            oa = mm(vt_ref[h], eb)
            inv = 1.0 / (oa[HD : HD + 1] + padb)
            o = oa[:HD] * inv
            dos = (do_ref[n].astype(F32) * inv).astype(BF)
            delta = jnp.sum(dos.astype(F32) * o, axis=0, keepdims=True)
            d0 = delta.astype(BF).astype(F32)
            tail = jnp.where(spot == 0, -d0, jnp.where(spot == 1, d0 - delta, 0.0))
            doa = jnp.concatenate([dos.astype(F32), tail], axis=0)
            ds = (e * mm(va_ref[h], doa.astype(BF))).astype(BF)
            dq_ref[n] = mm(kt_ref[h], ds)
            dk_ref[h] += mm(ds, qn_ref[n])
            dv_ref[h] += mm(eb, doa.T.astype(BF))
            do_ref[n] = jnp.where(padb > 0, vm_ref[h], o).astype(BF)
            return carry

        lax.fori_loop(0, heads * blocks, step, 0)

        def finish(h, carry):
            rows = lambda at: pl.ds(pl.multiple_of(at + h * HD, HD), HD)
            gq = jnp.concatenate([dq_ref[h * blocks + i] for i in range(blocks)], axis=1)
            gk = dk_ref[h].T
            for k, (g, gain_col) in enumerate(((gq, gain_q), (gk, gain_k))):
                unit, inverse = unit_of(k * width + h * HD)
                g = (g * scale).astype(BF).astype(F32)
                sums_ref[k] += lanes(g * unit)
                g = g * gain_col
                back = inverse * (
                    g - jnp.mean(g, axis=0, keepdims=True) - unit * jnp.mean(g * unit, axis=0, keepdims=True)
                )
                grad_ref[s, rows(k * width), :] = back.astype(BF)
            grad_ref[s, rows(2 * width), :] = dv_ref[h].T[:HD].astype(BF)
            for i in range(blocks):
                o_ref[s, rows(0), pl.ds(i * block, block)] = do_ref[h * blocks + i]
            return carry

        lax.fori_loop(0, heads, finish, 0)
        for copy in stores(s):
            copy.start()
        if last:
            loads[2].wait()
            loads[3].wait()
        gq_ref[...] += mm(grad_ref[s], norm_ref[s])
        go_ref[...] += mm(o_ref[s], gb_ref[s])
        return carry

    if last:
        assert seqs == 1
        sequence(0, 0)
    else:
        lax.fori_loop(0, seqs, sequence, 0)
        ends = [pltpu.make_async_copy(gq_ref, newq_hbm, w_sem.at[2]), pltpu.make_async_copy(go_ref, newo_hbm, w_sem.at[3])]
        for copy in ends:
            copy.start()
        for copy in ends:
            copy.wait()
    for s in range(seqs):
        for copy in stores(s):
            copy.wait()
    if not last:
        return
    g_q = gq_ref[...]
    first_row = (jnp.sum(wqkv_ref[...].astype(F32) * g_q, axis=0, keepdims=True) + fnp_ref[...]) / gain_ref[...]
    second_row = jnp.concatenate(
        [jnp.sum(sums_ref[k].T, axis=0, keepdims=True) for k in range(2)] + [jnp.zeros((1, dim - 2 * HD), F32)], axis=1
    )
    g_q = g_q.T
    odd = odd_ref[0] > 0
    parts, rows, _ = send_ref.shape
    rows = rows - 8
    extra = term_rows(first_row, second_row)
    for z in range(parts):
        send_ref[z, rows:] = extra.astype(BF)
        keep_ref[z, rows:] = extra
    unit = width // (2 * parts)

    def put_q(ref, z, value):
        ref[z, :rows, : 3 * width] = value

    def put_o(ref, z, value):
        for c in range(dim // width):
            ref[z, c * unit : (c + 1) * unit, 3 * width :] = value[:, c * width : (c + 1) * width]

    split_rows(odd, g_q, send_ref, keep_ref, parts, rows, put_q)
    split_rows(odd, go_ref[...], send_ref, keep_ref, parts, unit, put_o)


def attention(odd, ids, wqkv, wo, qg, kg, pay, halves, more=()):
    wide, dim = wqkv.shape
    width = wo.shape[0]
    heads = width // HD
    seqs, part = pay.shape[1], pay.shape[3]
    length = part * SLOTS
    block = 512
    blocks = length // block
    last = bool(more)
    ins = [odd, ids, qg, kg, wqkv, wo, pay, *more]
    specs = [SMEM] + [VMEM] * 3 + [HBM] * 3 + ([VMEM] * 3 + [HBM] * 2 if last else [])
    outs = [jax.ShapeDtypeStruct((seqs, width, length), BF), jax.ShapeDtypeStruct((seqs, wide, length), BF)]
    scratch = []
    if last:
        rows = dim // (2 * halves)
        outs += [
            jax.ShapeDtypeStruct((halves, rows + 8, wide + width), BF),
            jax.ShapeDtypeStruct((halves, rows + 8, wide + width), F32),
        ]
        scratch = [pltpu.VMEM((2, HD, 128), F32)]
    else:
        outs += [
            jax.ShapeDtypeStruct((2, HD, 128), F32),
            jax.ShapeDtypeStruct((wide, dim), F32),
            jax.ShapeDtypeStruct((width, dim), F32),
        ]
    flops = seqs * (2 * length * dim * width * 8 + heads * 6 * 2 * length * length * HD)
    return pl.pallas_call(
        functools.partial(attention_kernel, heads, block, last),
        out_shape=outs,
        in_specs=specs,
        out_specs=[HBM] * 2 + ([VMEM] * 2 if last else [VMEM, HBM, HBM]),
        scratch_shapes=scratch
        + [
            pltpu.VMEM((wide, dim), BF),
            pltpu.VMEM((width, dim), BF),
            pltpu.VMEM((seqs, length, dim), BF),
            pltpu.VMEM((seqs, length, dim), BF),
            pltpu.VMEM((seqs, width, length), BF),
            pltpu.VMEM((seqs, wide, length), BF),
            pltpu.VMEM((wide, dim), F32),
            pltpu.VMEM((width, dim), F32),
            pltpu.VMEM((wide, length), F32),
            pltpu.VMEM((heads * blocks, 2 * HD, block), BF),
            pltpu.VMEM((heads * blocks, block, HD), BF),
            pltpu.VMEM((heads, HD, length), BF),
            pltpu.VMEM((heads, length, 2 * HD), BF),
            pltpu.VMEM((heads, HD + 16, length), BF),
            pltpu.VMEM((heads, length, 2 * HD), BF),
            pltpu.VMEM((heads * blocks, HD, block), BF),
            pltpu.VMEM((heads * blocks, HD, block), F32),
            pltpu.VMEM((heads, length, HD), F32),
            pltpu.VMEM((heads, length, 2 * HD), F32),
            pltpu.VMEM((blocks, 1, block), F32),
            pltpu.VMEM((heads, HD, 1), F32),
            pltpu.SemaphoreType.DMA((4,)),
            pltpu.SemaphoreType.DMA((seqs, 2 * SLOTS)),
            pltpu.SemaphoreType.DMA((seqs, 2)),
        ],
        cost_estimate=pl.CostEstimate(flops=flops * 3, transcendentals=seqs * heads * length * length, bytes_accessed=8 * seqs * length * dim),
        compiler_params=pltpu.CompilerParams(vmem_limit_bytes=56 * MIB),
        name="attention",
    )(*ins)


def ffn_kernel(block, plan, at_ref, pay0_hbm, pay1_hbm, *refs):
    pieces, refs = refs[: len(plan)], refs[len(plan) :]
    (hid_hbm, gup_hbm, wup_hbm, wff_hbm, send_ref, np_ref), refs = refs[:6], refs[6:]
    norm_ref, gb_ref, hid_ref, gup_ref, wup_ref, wff_ref, gin_ref, gff_ref, sem, out_sem, w_sem = refs
    dim = wup_ref.shape[0]
    rows = send_ref.shape[2]
    part, seqs = pay0_hbm.shape[3], pay0_hbm.shape[1] + 1
    length = SLOTS * part
    total = norm_ref.shape[0]
    copies = []
    for ref, (which, masks) in zip(pieces, plan):
        for i, mask in enumerate(masks):
            start = pl.multiple_of((at_ref[2] ^ mask) * rows, rows)
            to = (wup_ref, wff_ref)[which].at[pl.ds(start, rows), :]
            copies.append(pltpu.make_async_copy(ref.at[i], to, w_sem.at[len(copies)]))
            copies[-1].start()
    for s in range(seqs):
        for t in range(SLOTS):
            at_rows = pl.ds((s * SLOTS + t) * part, part)
            for k, to in enumerate((norm_ref, gb_ref)):
                source = pay0_hbm.at[t, s, k] if s < seqs - 1 else pay1_hbm.at[t, k]
                pltpu.make_async_copy(source, to.at[at_rows, :], sem.at[s * SLOTS + t]).start()
    gin_ref[...] = jnp.zeros_like(gin_ref)
    gff_ref[...] = jnp.zeros_like(gff_ref)
    for copy in copies:
        copy.wait()
    weights = [pltpu.make_async_copy(wup_ref, wup_hbm, w_sem.at[0]), pltpu.make_async_copy(wff_ref, wff_hbm, w_sem.at[1])]
    for copy in weights:
        copy.start()
    c0 = math.sqrt(2.0 / math.pi)
    c1 = 0.044715

    def outs(i):
        at_rows = pl.ds(pl.multiple_of(i * block, block), block)
        return (
            pltpu.make_async_copy(hid_ref.at[at_rows, :], hid_hbm.at[at_rows, :], out_sem.at[0, i]),
            pltpu.make_async_copy(gup_ref.at[at_rows, :], gup_hbm.at[at_rows, :], out_sem.at[1, i]),
        )

    def step(i, carry):
        for k in range(block // part):
            for to in (norm_ref, gb_ref):
                pltpu.make_async_copy(pay1_hbm.at[0, 0], to.at[pl.ds(0, part), :], sem.at[i * (block // part) + k]).wait()
        at_rows = pl.ds(pl.multiple_of(i * block, block), block)
        up = mm(norm_ref[at_rows, :], wup_ref[...])
        gh = mm(gb_ref[at_rows, :], wff_ref[...], NT)
        sq = up * up
        t = jnp.tanh(up * (c0 + (c0 * c1) * sq))
        half = 0.5 + 0.5 * t
        hid_ref[at_rows, :] = (up * half).astype(BF)
        gup_ref[at_rows, :] = (gh * (half + (0.5 * up) * (1.0 - t * t) * (c0 + (3.0 * c0 * c1) * sq))).astype(BF)
        for copy in outs(i):
            copy.start()
        gin_ref[...] += mm(norm_ref[at_rows, :], gup_ref[at_rows, :], TN)
        gff_ref[...] += mm(hid_ref[at_rows, :], gb_ref[at_rows, :], TN)
        return carry

    lax.fori_loop(0, total // block, step, 0)
    line = jnp.sum(wup_ref[...].astype(F32) * gin_ref[...], axis=1, keepdims=True)
    np_ref[...] = jnp.broadcast_to(line, (dim, 128)).T[0:1]
    for b in range(dim // rows):
        for k, g in enumerate((gin_ref, gff_ref)):
            send_ref[b, k] = g[b * rows : (b + 1) * rows, :].astype(BF)
    for copy in weights:
        copy.wait()

    def drain(i, carry):
        for copy in outs(i):
            copy.wait()
        return carry

    lax.fori_loop(0, total // block, drain, 0)


def ffn(at, up_parts, ff_parts, pay0, pay1, count, block=512):
    _, _, part, dim = pay1.shape
    units = dim
    total = SLOTS * part * (1 + pay0.shape[1])
    rows = dim // count
    plan = [(0, masks) for _, masks in up_parts] + [(1, masks) for _, masks in ff_parts]
    pieces = [a for a, _ in up_parts + ff_parts]
    act = jax.ShapeDtypeStruct((total, units), BF)
    return pl.pallas_call(
        functools.partial(ffn_kernel, block, plan),
        out_shape=[
            act,
            act,
            jax.ShapeDtypeStruct((dim, units), BF),
            jax.ShapeDtypeStruct((units, dim), BF),
            jax.ShapeDtypeStruct((count, 2, rows, dim), BF),
            jax.ShapeDtypeStruct((1, dim), F32),
        ],
        in_specs=[SMEM] + [HBM] * (2 + len(pieces)),
        out_specs=[HBM] * 4 + [VMEM] * 2,
        scratch_shapes=[
            pltpu.VMEM((total, dim), BF),
            pltpu.VMEM((total, dim), BF),
            pltpu.VMEM((total, units), BF),
            pltpu.VMEM((total, units), BF),
            pltpu.VMEM((dim, units), BF),
            pltpu.VMEM((units, dim), BF),
            pltpu.VMEM((dim, units), F32),
            pltpu.VMEM((units, dim), F32),
            pltpu.SemaphoreType.DMA((total // part,)),
            pltpu.SemaphoreType.DMA((2, total // block)),
            pltpu.SemaphoreType.DMA((2 * count,)),
        ],
        cost_estimate=pl.CostEstimate(flops=8 * total * dim * units, transcendentals=total * units, bytes_accessed=total * dim * 8),
        compiler_params=pltpu.CompilerParams(vmem_limit_bytes=58 * MIB),
        name="ffn",
    )(at, pay0, pay1, *pieces)


def outputs(start, at, o, hid, gq, gu, wo, wff, wqkv, wup):
    seqs, _, length = o.shape
    dim = wo.shape[1]
    part = length // SLOTS

    def kernel(at_ref, o_hbm, hid_hbm, gq_hbm, gu_hbm, wo_hbm, wff_hbm, wqkv_hbm, wup_hbm, keep_hbm, send_hbm, *scratch):
        o_ref, hid_ref, gq_ref, gu_ref, wo_ref, wff_ref, wqkv_ref, wup_ref, res_ref, w_sem, sem, out_sem = scratch

        def load(k, s):
            rows = pl.ds(pl.multiple_of((start + s) * length, length), length)
            source, to = (
                (hid_hbm.at[rows, :], hid_ref), (o_hbm.at[s], o_ref), (gu_hbm.at[rows, :], gu_ref), (gq_hbm.at[s], gq_ref)
            )[k]
            return pltpu.make_async_copy(source, to.at[s], sem.at[s, k])

        weights = [
            pltpu.make_async_copy(a, b, w_sem.at[k])
            for k, (a, b) in enumerate(((wff_hbm, wff_ref), (wo_hbm, wo_ref), (wup_hbm, wup_ref), (wqkv_hbm, wqkv_ref)))
        ]
        for k in range(4):
            weights[k].start()
            load(k, 0).start()
        for s in range(1, seqs):
            for k in range(4):
                load(k, s).start()

        def leave(s, j, t, act):
            slot = at_ref[1] ^ t
            for to, odd in ((keep_hbm, 0), (send_hbm, 1)):

                @pl.when((slot & 1) == odd)
                def _(to=to):
                    act(pltpu.make_async_copy(res_ref.at[s, j, pl.ds(t * part, part), :], to.at[slot >> 1, s, j], out_sem.at[s, j, t]))

        for copy in weights:
            copy.wait()

        def sequence(s, carry):
            for k in range(2):
                load(k, s).wait()
            res_ref[s, 0] = (mm(o_ref[s], wo_ref[...], TN) + mm(hid_ref[s], wff_ref[...])).astype(BF)
            for t in range(SLOTS):
                leave(s, 0, t, lambda copy: copy.start())
            for k in range(2, 4):
                load(k, s).wait()
            res_ref[s, 1] = (mm(gq_ref[s], wqkv_ref[...], TN) + mm(gu_ref[s], wup_ref[...], NT)).astype(BF)
            for t in range(SLOTS):
                leave(s, 1, t, lambda copy: copy.start())
            return carry

        lax.fori_loop(0, seqs, sequence, 0)
        for s in range(seqs):
            for j in range(2):
                for t in range(SLOTS):
                    leave(s, j, t, lambda copy: copy.wait())

    return pl.pallas_call(
        kernel,
        out_shape=[jax.ShapeDtypeStruct((SLOTS // 2, seqs, 2, part, dim), BF)] * 2,
        in_specs=[SMEM] + [HBM] * 8,
        out_specs=[HBM] * 2,
        scratch_shapes=[
            pltpu.VMEM(o.shape, BF),
            pltpu.VMEM((seqs, length, hid.shape[1]), BF),
            pltpu.VMEM(gq.shape, BF),
            pltpu.VMEM((seqs, length, gu.shape[1]), BF),
            pltpu.VMEM(wo.shape, BF),
            pltpu.VMEM(wff.shape, BF),
            pltpu.VMEM(wqkv.shape, BF),
            pltpu.VMEM(wup.shape, BF),
            pltpu.VMEM((seqs, 2, length, dim), BF),
            pltpu.SemaphoreType.DMA((4,)),
            pltpu.SemaphoreType.DMA((seqs, 4)),
            pltpu.SemaphoreType.DMA((seqs, 2, SLOTS)),
        ],
        cost_estimate=pl.CostEstimate(
            flops=2 * seqs * length * dim * (o.shape[1] + 2 * hid.shape[1] + gq.shape[1]),
            transcendentals=0, bytes_accessed=seqs * length * dim * 10),
        compiler_params=pltpu.CompilerParams(vmem_limit_bytes=48 * MIB),
        name="outputs",
    )(at, o, hid, gq, gu, wo, wff, wqkv, wup)


def swap(value, axis, count, mask):
    return lax.ppermute(value, axis, [(i, i ^ mask) for i in range(count)])


def bit_groups(count):
    bits = list(range(count.bit_length() - 1))[::-1]
    groups = []
    while bits:
        take = 2 if len(bits) > 1 else 1
        groups.append(bits[:take])
        bits = bits[take:]
    assert len(groups[-1]) == 1
    return groups


def tie(value, *after):
    return lax.optimization_barrier((value,) + after)[0]


def gather_batch(block, count, groups, after=None):
    held, masks = block[None], [0]
    for stage, bits in enumerate(groups):
        low = bits[-1]
        if after and after[stage] is not None:
            held = tie(held, after[stage])
        parts = [(held, masks)]
        for s in range(1, 1 << len(bits)):
            parts.append((swap(held, "batch", count, s << low), [m ^ (s << low) for m in masks]))
        yield parts
        held = jnp.concatenate([a for a, _ in parts], axis=0)
        masks = sum((m for _, m in parts), [])


def matchings(edges, devices, per_device):
    left = [[] for _ in range(devices)]
    for e, (source, _, _) in enumerate(edges):
        left[source].append(e)
    rounds = []
    for _ in range(per_device):
        owner = [-1] * devices

        def place(source, seen):
            for e in left[source]:
                target = edges[e][1]
                if target in seen:
                    continue
                seen.add(target)
                if owner[target] < 0 or place(edges[owner[target]][0], seen):
                    owner[target] = e
                    return True
            return False

        for source in range(devices):
            place(source, set())
        rounds.append(list(owner))
        for e in owner:
            left[edges[e][0]].remove(e)
    return rounds


def unit_plan(nb, nt, rows, width, hidden):
    unit = math.gcd(math.gcd(rows, width // nt), hidden // nt)
    per = rows // unit
    head_units, hid_units = width // nt // unit, hidden // nt // unit
    assert head_units == nb and hid_units % nb == 0
    c = hid_units // nb
    edges = []
    for t in range(nt):
        for b in range(nb):
            want = [t * head_units + b]
            want += [nt * head_units + t * hid_units + b * c + i for i in range(c)]
            for slot, u in enumerate(want):
                edges.append((u // per, b * nt + t, (u % per, slot)))
    table = np.zeros((nb * nt, 2 * per), np.int32)
    perms = []
    for k, owner in enumerate(matchings(edges, nb * nt, per)):
        perms.append([(edges[e][0], edges[e][1]) for e in owner])
        for e in owner:
            table[edges[e][0], k] = edges[e][2][0]
            table[edges[e][1], per + k] = edges[e][2][1]
    return unit, per, perms, table


def per_device(
    nb, nt, patches, image_ids, cotangent, norm_gain, query_gain, key_gain, in_weight, out_weight
):
    seqs, part, dim = patches.shape
    width = H * HD
    local = width // nt
    units = (in_weight.shape[1] - 3 * width) // nt
    halves = nb // 2
    rows_in = in_weight.shape[0]
    unit, per, perms, table = unit_plan(nb, nt, out_weight.shape[0], width, units * nt)
    assert nt == SLOTS and units == dim and unit == rows_in and dim == nt * local and per == nt + 1
    both = ("batch", "tok")
    me_b = lax.axis_index("batch")
    me_t = lax.axis_index("tok")
    at = jnp.stack([me_b * nt + me_t, me_t, me_b])
    odd = (me_b & 1).reshape(1)
    table = jnp.asarray(table)
    gain = norm_gain.reshape(1, dim)
    groups = bit_groups(nb)

    pay0, pay1, a2a_src, *unit_sends = before(
        at, table, image_ids, gain, patches, cotangent, in_weight, out_weight.reshape(per, unit, dim)
    )
    full0 = lax.all_gather(pay0, "tok", axis=0)
    full1 = lax.all_gather(pay1, "tok", axis=0)
    w_in = lax.all_to_all(a2a_src, "tok", split_axis=0, concat_axis=0, tiled=True)
    early = 2
    got = [lax.ppermute(v, both, perm) for v, perm in zip(unit_sends[:early], perms)]
    chunk_a, chunk_u, ids = pack_in(tie(w_in, *got), seqs, part)
    got += [lax.ppermute(tie(v, chunk_a), both, perm) for v, perm in zip(unit_sends[early:], perms[early:])]
    chunk_w, chunk_f = pack_out(at, table, got)
    chunk_u = chunk_u.reshape(nt * unit, dim)
    chunk_f = chunk_f.reshape(nt * unit, dim)

    *_, a_parts = gather_batch(chunk_a, nb, groups, [None] * (len(groups) - 1) + [got[-1]])
    *_, w_parts = gather_batch(chunk_w, nb, groups)
    a_there, w_there = a_parts[-1][0], w_parts[-1][0]
    w_high = w_parts[0][0]
    stages = len(groups)
    wqkv, wo = join(at, a_parts, w_parts)
    *_, u_parts = gather_batch(chunk_u, nb, groups, [w_high] + [None] * (stages - 2) + [wqkv])
    *_, f_parts = gather_batch(chunk_f, nb, groups[::-1], [a_there, wqkv] + [None] * (stages - 2))
    wo = wo.reshape(local, dim)

    qg = query_gain.reshape(HD, 1)
    kg = key_gain.reshape(HD, 1)

    def leave_core(start, o, gq):
        keep, send = outputs(start, at, o, hid, gq, gup, wo, wff, wqkv, wup)
        return keep, swap(send, "tok", nt, 1)

    def leave_chip(keep, near):
        value = (keep[1].astype(F32) + near[1].astype(F32)).astype(BF)
        return value, swap(value, "tok", nt, 2)

    o0, gq0, sums, acc_q, acc_o = attention(odd, ids[: seqs - 1], wqkv, wo, qg, kg, full0, halves)
    hid, gup, wup, wff, f_grad, f_np = ffn(at, u_parts, f_parts, full0, tie(full1, o0), nb)
    f_mine = lax.psum_scatter(f_grad, "batch", scatter_dimension=0, tiled=True)
    keep0, near0 = leave_core(0, o0, gq0)
    o1, gq1, a_send, a_keep = attention(
        odd, ids[seqs - 1 :], wqkv, tie(wo, keep0), qg, kg, full1[:, None], halves, (sums, f_np, gain, acc_q, acc_o)
    )

    a_send = swap(a_send, "batch", nb, 1)
    value0, away0 = leave_chip(keep0, near0)
    a_parts = [a_keep, a_send]
    for bits in groups[:-1][::-1]:
        own, *sends = fold(nt * unit, bits[-1], at, a_parts[0], a_parts[1:])
        a_parts = [own] + [swap(value, "batch", nb, (s + 1) << bits[-1]) for s, value in enumerate(sends)]
    keep1, near1 = leave_core(seqs - 1, tie(o1, own), gq1)
    value1, away1 = leave_chip(keep1, near1)

    f_mine = f_mine.reshape(2, nt, unit, dim)
    up = lax.all_to_all(f_mine[0], "tok", split_axis=0, concat_axis=0, tiled=True)
    src, *sends = leave(at, table, a_parts, f_mine[1], local)
    qkv = lax.all_to_all(src, "tok", split_axis=0, concat_axis=0, tiled=True)
    got = [lax.ppermute(v, both, [(b, a) for a, b in perm]) for v, perm in zip(sends, perms)]
    in_grad, out_grad, norm_grad, query_grad, key_grad = place(at, table, qkv, up, got)

    earlier = []
    for s in range(seqs):
        i, group = (s, (keep0, near0, away0)) if s < seqs - 1 else (0, (keep1, near1, away1))
        earlier = after(s, i, image_ids, patches, cotangent, gain, *group, earlier)
    block_out, patch_grad = earlier
    return (
        block_out,
        patch_grad,
        norm_grad.reshape(dim),
        query_grad.reshape(HD),
        key_grad.reshape(HD),
        in_grad,
        out_grad.reshape(per * unit, dim),
    )


def solution(mesh):
    rows = P("batch", "tok", None)
    weights = P(("batch", "tok"), None)
    return jax.shard_map(
        functools.partial(per_device, mesh.shape["batch"], mesh.shape["tok"]),
        mesh=mesh,
        in_specs=(rows, P("batch", "tok"), rows, P(), P(), P(), weights, weights),
        out_specs=(rows, rows, P(), P(), P(), weights, weights),
        check_vma=False,
    )
```

time: 331 us -> 343 us (1.036)
  waiting for transfers between devices: 58.2 us -> 78.5 us
  local copies, waits for them, and re-layouts: 36.8 us -> 23.5 us
  starting transfers between devices: 70.7 us -> 79.8 us
    all_to_all x1, waiting for transfers between devices: 9.36 us -> 33.3 us  [per_device(): lax.all_to_all(f_mine[0], 'tok', split_axis=0, concat_axis=0, tiled=True)]
    unnamed x122 -> x114, local copies, waits for them, and re-layouts: 28.9 us -> 18.5 us
    ppermute x18 -> x24, starting transfers between devices: 21.5 us -> 30.2 us  [swap(): return lax.ppermute(value, axis, [(i, i ^ mask) for i in range(count)])]
    ppermute x18 -> x24, waiting for transfers between devices: 46.5 us -> 38.2 us  [swap(): return lax.ppermute(value, axis, [(i, i ^ mask) for i in range(count)])]
    ppermute x5, waiting for transfers between devices: 1.54 us -> 6.19 us  [the longest x2 3.39 us: per_device(): lax.ppermute(v, both, perm)]
    convert_element_type x3 -> x2, other arithmetic: 6.32 us -> 2.87 us  [leave_chip(): value = (keep[1].astype(F32) + near[1].astype(F32)).astype(BF)]
    pallas_call x9 -> x8, Pallas kernels: 120 us -> 118 us  [the longest x2 63.7 us: attention(): pl.pallas_call(functools.partial(attention_kernel, heads, block, last), o...]
  transfers between devices with their start and end apart: 34 -> 40, of which waited for: 8 -> 13; matrix products, arithmetic and copies ran while one was open for 5% -> 3% of each run, Pallas kernels for 30% -> 31%
where the time goes in v2:
time: 343 us; the launch traced here: 341 us
  Pallas kernels  139 us (41%)
  starting transfers between devices  79.8 us (23%)
  waiting for transfers between devices  78.5 us (23%)
  local copies, waits for them, and re-layouts  23.5 us (7%)
  between operations  14.4 us (4%)
  other arithmetic  6.12 us (2%)
    pallas_call x2, Pallas kernels, attention(): pl.pallas_call(functools.partial(attention_kernel, heads, block, last), o...  63.7 us
    ppermute x24, waiting for transfers between devices, swap(): return lax.ppermute(value, axis, [(i, i ^ mask) for i in range(count)])  38.2 us
    all_to_all x1, waiting for transfers between devices, per_device(): lax.all_to_all(f_mine[0], 'tok', split_axis=0, concat_axis=0, tiled=True)  33.3 us
    ppermute x24, starting transfers between devices, swap(): return lax.ppermute(value, axis, [(i, i ^ mask) for i in range(count)])  30.2 us
    pallas_call x2, Pallas kernels, outputs(): pl.pallas_call(kernel, out_shape=[jax.ShapeDtypeStruct((SLOTS // 2, seqs,...  25.5 us
    pallas_call x1, Pallas kernels, ffn(): pl.pallas_call(functools.partial(ffn_kernel, block, plan), out_shape=[act...  24.8 us
    unnamed x114, local copies, waits for them, and re-layouts  18.5 us
    ppermute x5, starting transfers between devices, per_device(): lax.ppermute(v, both, [(b, a) for a, b in perm])  17.3 us
  transfers between devices with their start and end apart: 40, of which 13 were waited for; matrix products, arithmetic and copies ran while one was open for 3% of the time, Pallas kernels for 31%

profile of v2, /device:TPU:2, one launch (start us, length us, event | category | flops | bytes accessed | tf_op | source)
XLA Modules:
  0.0 341.3 jit_solution(16520392728423648408)
XLA Ops:
  13.8 5.1 %before.1 = (bf16[2,2,256,768]{3,2,1,0:T(8,128)(2,1)}, bf16[2,256,768]{2,1,0:T(8,128)(2,1)}, bf16[4,25,1344]{2,1,0:T(8,128)(2,1)}, bf16[24,768]{1,0:T(8,128)(2,1...) custom-call(s32[3]{0:T(128)S(1)} %pad_add_fusion.at_ref, ...), custom_call_target="tpu_custom_call" | custom-call | flops 4718592 | bytes 4718592 | tf_op jit(solution)/shard_map/before/pallas_call | solution.py:98
  19.7 3.5 %all-to-all-start = ((bf16[4,25,1344]{2,1,0:T(8,128)(2,1)}), bf16[4,25,1344]{2,1,0:T(8,128)(2,1)S(1)}, u32[]{:S(2)}, u32[]{:S(2)}) async-start(bf16[4,25,1344]{2,1,0:T(8,128)(2,1)} %get-tuple-element.74), calls=%async_computation | async-start | bytes 720896 | tf_op jit(solution)/shard_map/all_to_all | solution.py:927
  23.3 5.9 %collective-permute-start = (bf16[24,768]{1,0:T(8,128)(2,1)S(1)}, bf16[24,768]{1,0:T(8,128)(2,1)S(1)}, u32[]{:S(2)}, u32[]{:S(2)}) collective-permute-start(bf16[24,768]{1,0:T(8,128)(2,1)S(1)} %get-tuple-element.75), channel_id=1, source_target_pairs={{7,0},{13,1},{3,2},{26,3},{0,4},{14,5},{20,6},{27,7},{8,8},{15,9},... | collective-permute-start | bytes 110600 | tf_op jit(solution)/shard_map/ppermute | solution.py:929
  32.2 3.4 collective-permute-done.1.refs_1_
  42.4 3.7 %collective-permute-start.5 = (bf16[24,768]{1,0:T(8,128)(2,1)S(1)}, bf16[24,768]{1,0:T(8,128)(2,1)S(1)}, u32[]{:S(2)}, u32[]{:S(2)}) collective-permute-start(bf16[24,768]{1,0:T(8,128)(2,1)S(1)} %get-tuple-element.81), channel_id=1, source_target_pairs={{6,0},{12,1},{19,2},{25,3},{7,4},{13,5},{3,6},{26,7},{0,8},{14,9},... | collective-permute-start | bytes 110600 | tf_op jit(solution)/shard_map/ppermute | solution.py:931
  46.4 4.0 %collective-permute-done.3 = bf16[1,4,24,576]{3,2,1,0:T(8,128)(2,1)S(1)} collective-permute-done((bf16[1,4,24,576]{3,2,1,0:T(8,128)(2,1)}, bf16[1,4,24,576]{3,2,1,0:T(8,128)(2,1)S(1)}, u32[]{:S(2)}, u32[]{:S(2)}) %collective-permute-start.3) | collective-permute-done | bytes 110624 | tf_op jit(solution)/shard_map/ppermute | solution.py:820
  54.7 6.4 %collective-permute-start.8 = (bf16[24,768]{1,0:T(8,128)(2,1)S(1)}, bf16[24,768]{1,0:T(8,128)(2,1)S(1)}, u32[]{:S(2)}, u32[]{:S(2)}) collective-permute-start(bf16[24,768]{1,0:T(8,128)(2,1)S(1)} %get-tuple-element.86), channel_id=1, source_target_pairs={{6,0},{1,1},{19,2},{25,3},{7,4},{13,5},{20,6},{26,7},{8,8},{14,9},... | collective-permute-start | bytes 110600 | tf_op jit(solution)/shard_map/ppermute | solution.py:931
  66.9 4.3 %collective-permute-start.10 = (bf16[1,24,768]{2,1,0:T(8,128)(2,1)}, bf16[1,24,768]{2,1,0:T(8,128)(2,1)S(1)}, u32[]{:S(2)}, u32[]{:S(2)}) collective-permute-start(bf16[1,24,768]{2,1,0:T(8,128)(2,1)} %bitcast.41), channel_id=1, source_target_pairs={{0,16},{4,20},{8,24},{12,28},{16,0},{20,4},{24,8},{28,12},{1,17},{... | collective-permute-start | bytes 110600 | tf_op jit(solution)/shard_map/ppermute | solution.py:820
  85.0 5.2 %collective-permute-done.14 = bf16[1,96,768]{2,1,0:T(8,128)(2,1)S(1)} collective-permute-done((bf16[1,96,768]{2,1,0:T(8,128)(2,1)}, bf16[1,96,768]{2,1,0:T(8,128)(2,1)S(1)}, u32[]{:S(2)}, u32[]{:S(2)}) %collective-permute-start.14) | collective-permute-done | bytes 147488 | tf_op jit(solution)/shard_map/ppermute | solution.py:820
  98.2 40.8 %attention.2 = (bf16[2,192,1024]{2,1,0:T(8,128)(2,1)}, bf16[2,576,1024]{2,1,0:T(8,128)(2,1)}, f32[2,64,128]{2,1,0:T(8,128)}, f32[576,768]{1,0:T(8,128)}, f32[192,768]{1,0:T(8,128)}) custom-call(s32[1]{0:T(128)} %bitcast.3.odd_ref, s32[2,1,1024]{2,1,0:T(1,128)} %slice.27.ids_ref, f32[64,1]{1,0:T(8,128)} %copy.26.qg_ref, f32[64,1]{1,0:T(8,128)} %copy.27.kg_ref, ...), custom_call_target="tpu_custom_call" | custom-call | flops 28991029248 | bytes 12582912 | tf_op jit(solution)/shard_map/attention/pallas_call | solution.py:585
  140.9 24.8 %ffn.1 = (bf16[3072,768]{1,0:T(8,128)(2,1)}, bf16[3072,768]{1,0:T(8,128)(2,1)}, bf16[768,768]{1,0:T(8,128)(2,1)}, bf16[768,768]{1,0:T(8,128)(2,1)}, bf16[8,2,96,768]{3,2,1,0:T(8,128)(2,1)}, /*index=5*/f32[1,768]{1,0:T(1,128)}) custom-call(s32[3]{0:T(128)} %copy-done.21, bf16[4,2,2,256,768]{4,3,2,1,0:T(8,128)(2,1)} %bitcast.47, ...), custom_call_target="tpu_custom_call" | custom-call | flops 14495514624 | bytes 18874368 | tf_op jit(solution)/shard_map/ffn/pallas_call | solution.py:705
  168.5 15.7 %outputs.2 = (bf16[2,2,2,256,768]{4,3,2,1,0:T(8,128)(2,1)}, bf16[2,2,2,256,768]{4,3,2,1,0:T(8,128)(2,1)}) custom-call(s32[3]{0:T(128)S(1)} %copy-done.23, bf16[2,192,1024]{2,1,0:T(8,128)(2,1)S(1)} %copy-done.24, bf16[3072,768]{1,0:T(8,128)(2,1)} %get-tuple-element.100.hid_hbm, bf16[2,576,1024]{2,1,0:T(8,128)(2,1)} %get-tuple-element.101.gq_hbm, ...), custom_call_target="tpu_custom_call" | custom-call | flops 7247757312 | bytes 15728640 | tf_op jit(solution)/shard_map/outputs/pallas_call | solution.py:792
  184.9 22.9 %attention.3 = (bf16[1,192,1024]{2,1,0:T(8,128)(2,1)}, bf16[1,576,1024]{2,1,0:T(8,128)(2,1)}, bf16[4,104,768]{2,1,0:T(8,128)(2,1)}, f32[4,104,768]{2,1,0:T(8,128)}) custom-call(s32[1]{0:T(128)} %bitcast.3.odd_ref, s32[1,1,1024]{2,1,0:T(1,128)} %slice.26.ids_ref, f32[64,1]{1,0:T(8,128)} %copy.26.qg_ref, f32[64,1]{1,0:T(8,128)} %copy.27.kg_ref, ...), custom_call_target="tpu_custom_call" | custom-call | flops 14495514624 | bytes 6291456 | tf_op jit(solution)/shard_map/attention/pallas_call | solution.py:585
  208.9 19.1 %collective-permute-done.21.refs_0_ = bf16[4,104,768]{2,1,0:T(8,128)(2,1)S(1)} collective-permute-done((bf16[4,104,768]{2,1,0:T(8,128)(2,1)}, bf16[4,104,768]{2,1,0:T(8,128)(2,1)S(1)}, u32[]{:S(2)}, u32[]{:S(2)}) %collective-permute-start.21) | collective-permute-done | bytes 639008 | tf_op jit(solution)/shard_map/ppermute | solution.py:820
  230.6 9.7 %outputs.3 = (bf16[2,1,2,256,768]{4,3,2,1,0:T(8,128)(2,1)}, bf16[2,1,2,256,768]{4,3,2,1,0:T(8,128)(2,1)}) custom-call(s32[3]{0:T(128)S(1)} %copy-done.23, bf16[1,192,1024]{2,1,0:T(8,128)(2,1)S(1)} %copy-done.9, bf16[3072,768]{1,0:T(8,128)(2,1)} %get-tuple-element.100.hid_hbm, bf16[1,576,1024]{2,1,0:T(8,128)(2,1)S(1)} %copy-done.5, ...), custom_call_target="tpu_custom_call" | custom-call | flops 3623878656 | bytes 7864320 | tf_op jit(solution)/shard_map/outputs/pallas_call | solution.py:792
  257.1 5.3 %collective-permute-done.27.p2 = bf16[1,104,768]{2,1,0:T(8,128)(2,1)S(1)} collective-permute-done((bf16[1,104,768]{2,1,0:T(8,128)(2,1)S(1)}, bf16[1,104,768]{2,1,0:T(8,128)(2,1)S(1)}, u32[]{:S(2)}, u32[]{:S(2)}) %collective-permute-start.27) | collective-permute-done | bytes 159776 | tf_op jit(solution)/shard_map/ppermute | solution.py:820
  265.3 33.3 %all-to-all-done.2.up_ref = bf16[4,24,768]{2,1,0:T(8,128)(2,1)S(1)} async-done(((bf16[4,24,768]{2,1,0:T(8,128)(2,1)}), bf16[4,24,768]{2,1,0:T(8,128)(2,1)S(1)}, u32[]{:S(2)}, u32[]{:S(2)}) %all-to-all-start.2) | async-done | bytes 147488 | tf_op jit(solution)/shard_map/all_to_all | solution.py:975
  298.6 3.5 %all-to-all-start.1 = ((f32[4,26,576]{2,1,0:T(8,128)}), f32[4,26,576]{2,1,0:T(8,128)S(1)}, u32[]{:S(2)}, u32[]{:S(2)}) async-start(f32[4,26,576]{2,1,0:T(8,128)} %get-tuple-element.130), calls=%async_computation.2 | async-start | bytes 655360 | tf_op jit(solution)/shard_map/all_to_all | solution.py:977
  304.6 3.6 %collective-permute-start.30 = (f32[24,768]{1,0:T(8,128)}, f32[24,768]{1,0:T(8,128)S(1)}, u32[]{:S(2)}, u32[]{:S(2)}) collective-permute-start(f32[24,768]{1,0:T(8,128)} %get-tuple-element.132), channel_id=1, source_target_pairs={{0,0},{1,13},{2,19},{3,26},{4,7},{5,14},{6,20},{7,5},{8,8},{9,2},{... | collective-permute-start | bytes 221192 | tf_op jit(solution)/shard_map/ppermute | solution.py:978
  310.5 4.8 %collective-permute-start.32 = (f32[24,768]{1,0:T(8,128)}, f32[24,768]{1,0:T(8,128)S(1)}, u32[]{:S(2)}, u32[]{:S(2)}) collective-permute-start(f32[24,768]{1,0:T(8,128)} %get-tuple-element.134), channel_id=1, source_target_pairs={{0,6},{1,1},{2,19},{3,25},{4,7},{5,13},{6,20},{7,26},{8,8},{9,14},... | collective-permute-start | bytes 221192 | tf_op jit(solution)/shard_map/ppermute | solution.py:978
  315.4 4.0 %collective-permute-start.33 = (f32[24,768]{1,0:T(8,128)}, f32[24,768]{1,0:T(8,128)S(1)}, u32[]{:S(2)}, u32[]{:S(2)}) collective-permute-start(f32[24,768]{1,0:T(8,128)} %get-tuple-element.135), channel_id=1, source_target_pairs={{0,6},{1,12},{2,19},{3,25},{4,7},{5,13},{6,3},{7,26},{8,0},{9,14},... | collective-permute-start | bytes 221192 | tf_op jit(solution)/shard_map/ppermute | solution.py:978
  319.4 3.5 %after.3 = (bf16[3,256,768]{2,1,0:T(8,128)(2,1)}, bf16[3,256,768]{2,1,0:T(8,128)(2,1)}) custom-call(s32[3,256]{1,0:T(4,128)S(1)} %copy-done.20, bf16[3,256,768]{2,1,0:T(8,128)(2,1)} %x_ref.5, bf16[3,256,768]{2,1,0:T(8,128)(2,1)} %cot_ref.5, f32[1,768]{1,0:T(1,128)S(1)} %copy-done.18, bf16[2,2,2,256,768]{4,3,2,1,0:T(8,128)(2,1)} %get-tuple-element.105.keep_ref, ...), custom_call_target="tpu_custom_call" | custom-call | flops 3932160 | bytes 3932160 | tf_op jit(solution)/shard_map/after/pallas_call | solution.py:331
  322.9 3.5 %after.4 = (bf16[3,256,768]{2,1,0:T(8,128)(2,1)}, bf16[3,256,768]{2,1,0:T(8,128)(2,1)}) custom-call(s32[3,256]{1,0:T(4,128)S(1)} %copy-done.20, bf16[3,256,768]{2,1,0:T(8,128)(2,1)} %x_ref.5, bf16[3,256,768]{2,1,0:T(8,128)(2,1)} %cot_ref.5, f32[1,768]{1,0:T(1,128)S(1)} %copy-done.18, ...), custom_call_target="tpu_custom_call", output_to_operand_aliasing={{0}: (7, {}), {1}: (8, {})} | custom-call | flops 3932160 | bytes 3932160 | tf_op jit(solution)/shard_map/after/pallas_call | solution.py:331
  326.3 3.5 %after.5 = (bf16[3,256,768]{2,1,0:T(8,128)(2,1)}, bf16[3,256,768]{2,1,0:T(8,128)(2,1)}) custom-call(s32[3,256]{1,0:T(4,128)S(1)} %copy-done.20, bf16[3,256,768]{2,1,0:T(8,128)(2,1)} %x_ref.5, bf16[3,256,768]{2,1,0:T(8,128)(2,1)} %cot_ref.5, f32[1,768]{1,0:T(1,128)S(1)} %copy-done.18, ...), custom_call_target="tpu_custom_call", output_to_operand_aliasing={{0}: (7, {}), {1}: (8, {})} | custom-call | flops 3932160 | bytes 3932160 | tf_op jit(solution)/shard_map/after/pallas_call | solution.py:331
  (202 shorter events, 87.7 us)
Async XLA Ops:
  7.2 91.1 %all-gather.5.cloned.1.call-start = ((), (), s32[]{:S(2)}) async-start(), calls=%async_computation.5 | async-start | bytes 7864320 | tf_op jit(solution)/shard_map/all_gather | solution.py:925
  19.0 120.2 %all-gather.7.cloned.1.call-start = ((), (), s32[]{:S(2)}) async-start(), calls=%async_computation.6 | async-start | bytes 3932160 | tf_op jit(solution)/shard_map/all_gather | solution.py:926
  19.7 15.8 %all-to-all-start = ((bf16[4,25,1344]{2,1,0:T(8,128)(2,1)}), bf16[4,25,1344]{2,1,0:T(8,128)(2,1)S(1)}, u32[]{:S(2)}, u32[]{:S(2)}) async-start(bf16[4,25,1344]{2,1,0:T(8,128)(2,1)} %get-tuple-element.74), calls=%async_computation | async-start | bytes 720896 | tf_op jit(solution)/shard_map/all_to_all | solution.py:927
  23.2 228.8 %reduce-scatter.2.cloned.1.call-start = ((), (), s32[]{:S(2)}) async-start(), calls=%async_computation.4 | async-start | bytes 2654208 | tf_op jit(solution)/shard_map/reduce_scatter | solution.py:959
  51.5 29.7 %collective-permute-start.6 = (bf16[4,4,24,576]{3,2,1,0:T(8,128)(2,1)S(1)}, bf16[4,4,24,576]{3,2,1,0:T(8,128)(2,1)S(1)}, u32[]{:S(2)}, u32[]{:S(2)}) collective-permute-start(bf16[4,4,24,576]{3,2,1,0:T(8,128)(2,1)S(1)} %pad_maximum_fusion.1.refs_0_), channel_id=1, source_target_pairs={{0,4},{4,0},{8,12},{12,8},{16,20},{20,16},{24,28},{28,24},{1,5},{5... | collective-permute-start | bytes 1327112 | tf_op jit(solution)/shard_map/ppermute | solution.py:820
  77.8 12.3 %collective-permute-start.14 = (bf16[1,96,768]{2,1,0:T(8,128)(2,1)}, bf16[1,96,768]{2,1,0:T(8,128)(2,1)S(1)}, u32[]{:S(2)}, u32[]{:S(2)}) collective-permute-start(bf16[1,96,768]{2,1,0:T(8,128)(2,1)} %bitcast.31), channel_id=1, source_target_pairs={{0,16},{4,20},{8,24},{12,28},{16,0},{20,4},{24,8},{28,12},{1,17},{... | collective-permute-start | bytes 442376 | tf_op jit(solution)/shard_map/ppermute | solution.py:820
  81.2 12.5 %collective-permute-start.17 = (bf16[1,96,768]{2,1,0:T(8,128)(2,1)}, bf16[1,96,768]{2,1,0:T(8,128)(2,1)S(1)}, u32[]{:S(2)}, u32[]{:S(2)}) collective-permute-start(bf16[1,96,768]{2,1,0:T(8,128)(2,1)} %bitcast.34), channel_id=1, source_target_pairs={{0,4},{4,0},{8,12},{12,8},{16,20},{20,16},{24,28},{28,24},{1,5},{5... | collective-permute-start | bytes 442376 | tf_op jit(solution)/shard_map/ppermute | solution.py:820
  92.8 47.2 %collective-permute-start.16 = (bf16[4,96,768]{2,1,0:T(8,128)(2,1)S(1)}, bf16[4,96,768]{2,1,0:T(8,128)(2,1)S(1)}, u32[]{:S(2)}, u32[]{:S(2)}) collective-permute-start(bf16[4,96,768]{2,1,0:T(8,128)(2,1)S(1)} %pad_maximum_fusion.refs_0_), channel_id=1, source_target_pairs={{0,4},{4,0},{8,12},{12,8},{16,20},{20,16},{24,28},{28,24},{1,5},{5... | collective-permute-start | bytes 1769480 | tf_op jit(solution)/shard_map/ppermute | solution.py:820
  93.8 45.4 %collective-permute-start.20 = (bf16[2,96,768]{2,1,0:T(8,128)(2,1)S(1)}, bf16[2,96,768]{2,1,0:T(8,128)(2,1)S(1)}, u32[]{:S(2)}, u32[]{:S(2)}) collective-permute-start(bf16[2,96,768]{2,1,0:T(8,128)(2,1)S(1)} %pad_maximum_fusion.2.refs_2_), channel_id=1, source_target_pairs={{0,24},{4,28},{8,16},{12,20},{16,8},{20,12},{24,0},{28,4},{1,25},{... | collective-permute-start | bytes 884744 | tf_op jit(solution)/shard_map/ppermute | solution.py:820
  95.6 43.5 %collective-permute-start.19 = (bf16[2,96,768]{2,1,0:T(8,128)(2,1)S(1)}, bf16[2,96,768]{2,1,0:T(8,128)(2,1)S(1)}, u32[]{:S(2)}, u32[]{:S(2)}) collective-permute-start(bf16[2,96,768]{2,1,0:T(8,128)(2,1)S(1)} %pad_maximum_fusion.2.refs_2_), channel_id=1, source_target_pairs={{0,16},{4,20},{8,24},{12,28},{16,0},{20,4},{24,8},{28,12},{1,17},{... | collective-permute-start | bytes 884744 | tf_op jit(solution)/shard_map/ppermute | solution.py:820
  95.6 43.5 %collective-permute-start.18 = (bf16[2,96,768]{2,1,0:T(8,128)(2,1)S(1)}, bf16[2,96,768]{2,1,0:T(8,128)(2,1)S(1)}, u32[]{:S(2)}, u32[]{:S(2)}) collective-permute-start(bf16[2,96,768]{2,1,0:T(8,128)(2,1)S(1)} %pad_maximum_fusion.2.refs_2_), channel_id=1, source_target_pairs={{0,8},{4,12},{8,0},{12,4},{16,24},{20,28},{24,16},{28,20},{1,9},{5... | collective-permute-start | bytes 884744 | tf_op jit(solution)/shard_map/ppermute | solution.py:820
  184.2 56.3 %collective-permute-start.24 = (bf16[2,2,2,256,768]{4,3,2,1,0:T(8,128)(2,1)}, bf16[2,2,2,256,768]{4,3,2,1,0:T(8,128)(2,1)S(1)}, u32[]{:S(2)}, u32[]{:S(2)}) collective-permute-start(bf16[2,2,2,256,768]{4,3,2,1,0:T(8,128)(2,1)} %get-tuple-element.119), channel_id=1, source_target_pairs={{0,1},{1,0},{2,3},{3,2},{4,5},{5,4},{6,7},{7,6},{8,9},{9,8},{10,11... | collective-permute-start | bytes 9437192 | tf_op jit(solution)/shard_map/ppermute | solution.py:820
  207.7 20.2 %collective-permute-start.21 = (bf16[4,104,768]{2,1,0:T(8,128)(2,1)}, bf16[4,104,768]{2,1,0:T(8,128)(2,1)S(1)}, u32[]{:S(2)}, u32[]{:S(2)}) collective-permute-start(bf16[4,104,768]{2,1,0:T(8,128)(2,1)} %get-tuple-element.113), channel_id=1, source_target_pairs={{0,4},{4,0},{8,12},{12,8},{16,20},{20,16},{24,28},{28,24},{1,5},{5... | collective-permute-start | bytes 1916936 | tf_op jit(solution)/shard_map/ppermute | solution.py:820
  242.6 72.7 %collective-permute-start.25 = (bf16[2,2,256,768]{3,2,1,0:T(8,128)(2,1)}, bf16[2,2,256,768]{3,2,1,0:T(8,128)(2,1)S(1)}, u32[]{:S(2)}, u32[]{:S(2)}) collective-permute-start(bf16[2,2,256,768]{3,2,1,0:T(8,128)(2,1)} %fusion), channel_id=1, source_target_pairs={{0,2},{1,3},{2,0},{3,1},{4,6},{5,7},{6,4},{7,5},{8,10},{9,11},{10,... | collective-permute-start | bytes 4718600 | tf_op jit(solution)/shard_map/ppermute | solution.py:820
  246.2 64.4 %collective-permute-start.23 = (bf16[1,2,256,768]{3,2,1,0:T(8,128)(2,1)}, bf16[1,2,256,768]{3,2,1,0:T(8,128)(2,1)}, u32[]{:S(2)}, u32[]{:S(2)}) collective-permute-start(bf16[1,2,256,768]{3,2,1,0:T(8,128)(2,1)} %fusion.1), channel_id=1, source_target_pairs={{0,2},{1,3},{2,0},{3,1},{4,6},{5,7},{6,4},{7,5},{8,10},{9,11},{10,... | collective-permute-start | bytes 2359304 | tf_op jit(solution)/shard_map/ppermute | solution.py:820
  247.6 14.7 %collective-permute-start.27 = (bf16[1,104,768]{2,1,0:T(8,128)(2,1)S(1)}, bf16[1,104,768]{2,1,0:T(8,128)(2,1)S(1)}, u32[]{:S(2)}, u32[]{:S(2)}) collective-permute-start(bf16[1,104,768]{2,1,0:T(8,128)(2,1)S(1)} %get-tuple-element.127), channel_id=1, source_target_pairs={{0,16},{4,20},{8,24},{12,28},{16,0},{20,4},{24,8},{28,12},{1,17},{... | collective-permute-start | bytes 479240 | tf_op jit(solution)/shard_map/ppermute | solution.py:820
  249.9 12.4 %collective-permute-start.28 = (bf16[1,104,768]{2,1,0:T(8,128)(2,1)S(1)}, bf16[1,104,768]{2,1,0:T(8,128)(2,1)S(1)}, u32[]{:S(2)}, u32[]{:S(2)}) collective-permute-start(bf16[1,104,768]{2,1,0:T(8,128)(2,1)S(1)} %get-tuple-element.128), channel_id=1, source_target_pairs={{0,24},{4,28},{8,16},{12,20},{16,8},{20,12},{24,0},{28,4},{1,25},{... | collective-permute-start | bytes 479240 | tf_op jit(solution)/shard_map/ppermute | solution.py:820
  253.7 44.9 %all-to-all-start.2 = ((bf16[4,24,768]{2,1,0:T(8,128)(2,1)}), bf16[4,24,768]{2,1,0:T(8,128)(2,1)S(1)}, u32[]{:S(2)}, u32[]{:S(2)}) async-start(bf16[4,24,768]{2,1,0:T(8,128)(2,1)} %bitcast.18), calls=%async_computation.3 | async-start | bytes 294912 | tf_op jit(solution)/shard_map/all_to_all | solution.py:975
  298.6 31.3 %all-to-all-start.1 = ((f32[4,26,576]{2,1,0:T(8,128)}), f32[4,26,576]{2,1,0:T(8,128)S(1)}, u32[]{:S(2)}, u32[]{:S(2)}) async-start(f32[4,26,576]{2,1,0:T(8,128)} %get-tuple-element.130), calls=%async_computation.2 | async-start | bytes 655360 | tf_op jit(solution)/shard_map/all_to_all | solution.py:977
  302.1 27.7 %collective-permute-start.29 = (f32[24,768]{1,0:T(8,128)}, f32[24,768]{1,0:T(8,128)S(1)}, u32[]{:S(2)}, u32[]{:S(2)}) collective-permute-start(f32[24,768]{1,0:T(8,128)} %get-tuple-element.131), channel_id=1, source_target_pairs={{0,7},{1,13},{2,3},{3,26},{4,0},{5,14},{6,20},{7,27},{8,8},{9,15},... | collective-permute-start | bytes 221192 | tf_op jit(solution)/shard_map/ppermute | solution.py:978
  304.6 25.2 %collective-permute-start.30 = (f32[24,768]{1,0:T(8,128)}, f32[24,768]{1,0:T(8,128)S(1)}, u32[]{:S(2)}, u32[]{:S(2)}) collective-permute-start(f32[24,768]{1,0:T(8,128)} %get-tuple-element.132), channel_id=1, source_target_pairs={{0,0},{1,13},{2,19},{3,26},{4,7},{5,14},{6,20},{7,5},{8,8},{9,2},{... | collective-permute-start | bytes 221192 | tf_op jit(solution)/shard_map/ppermute | solution.py:978
  308.2 21.6 %collective-permute-start.31 = (f32[24,768]{1,0:T(8,128)}, f32[24,768]{1,0:T(8,128)S(1)}, u32[]{:S(2)}, u32[]{:S(2)}) collective-permute-start(f32[24,768]{1,0:T(8,128)} %get-tuple-element.133), channel_id=1, source_target_pairs={{0,6},{1,13},{2,19},{3,4},{4,7},{5,1},{6,20},{7,26},{8,8},{9,14},{... | collective-permute-start | bytes 221192 | tf_op jit(solution)/shard_map/ppermute | solution.py:978
  310.5 19.3 %collective-permute-start.32 = (f32[24,768]{1,0:T(8,128)}, f32[24,768]{1,0:T(8,128)S(1)}, u32[]{:S(2)}, u32[]{:S(2)}) collective-permute-start(f32[24,768]{1,0:T(8,128)} %get-tuple-element.134), channel_id=1, source_target_pairs={{0,6},{1,1},{2,19},{3,25},{4,7},{5,13},{6,20},{7,26},{8,8},{9,14},... | collective-permute-start | bytes 221192 | tf_op jit(solution)/shard_map/ppermute | solution.py:978
  315.4 14.4 %collective-permute-start.33 = (f32[24,768]{1,0:T(8,128)}, f32[24,768]{1,0:T(8,128)S(1)}, u32[]{:S(2)}, u32[]{:S(2)}) collective-permute-start(f32[24,768]{1,0:T(8,128)} %get-tuple-element.135), channel_id=1, source_target_pairs={{0,6},{1,12},{2,19},{3,25},{4,7},{5,13},{6,3},{7,26},{8,0},{9,14},... | collective-permute-start | bytes 221192 | tf_op jit(solution)/shard_map/ppermute | solution.py:978
  (73 other events, 1026.4 us)
Sparse Core Ops, SparseCore 0:
  19.1 49.5 all-gather.4
  70.8 28.1 all-gather.6
  165.9 70.1 reduce-scatter.1

commit v3 on v2

v3 whole, which is shorter than its diff:
```python
import functools
import math

import jax
import jax.numpy as jnp
import numpy as np
from jax import lax
from jax.experimental import pallas as pl
from jax.experimental.pallas import tpu as pltpu
from jax.sharding import PartitionSpec as P

H = 12
HD = 64
SLOTS = 4
EPS = 1e-06
BIG = 2048.0
LOG2E = 1.4426950408889634
BF = jnp.bfloat16
F32 = jnp.float32
NN = (((1,), (0,)), ((), ()))
NT = (((1,), (1,)), ((), ()))
TN = (((0,), (0,)), ((), ()))
MIB = 1 << 20
SMALL = pl.CostEstimate(flops=1, transcendentals=0, bytes_accessed=1)
LARGE = pl.CostEstimate(flops=60_000_000_000, transcendentals=0, bytes_accessed=1)

VMEM = pl.BlockSpec(memory_space=pltpu.VMEM)
SMEM = pl.BlockSpec(memory_space=pltpu.SMEM)
ANY = pl.BlockSpec(memory_space=pl.ANY)
HBM = pl.BlockSpec(memory_space=pltpu.HBM)


def hbm(*arrays):
    return [pltpu.with_memory_space_constraint(a, pltpu.HBM) for a in arrays]


def mm(a, b, dims=NN):
    return lax.dot_general(a, b, dims, preferred_element_type=F32)


def normalize(values):
    center = values - jnp.mean(values, axis=-1, keepdims=True)
    inverse = lax.rsqrt(jnp.mean(center * center, axis=-1, keepdims=True) + EPS)
    return center * inverse, inverse


def norm_back(grad_unit, unit_rows, inverse):
    return inverse * (
        grad_unit
        - jnp.mean(grad_unit, axis=-1, keepdims=True)
        - unit_rows * jnp.mean(grad_unit * unit_rows, axis=-1, keepdims=True)
    )


def column(row):
    return jnp.broadcast_to(row, (8, row.shape[1])).T[:, 0:1]


def prepare(ids, w_in, nb, nt):
    rows, wide = w_in.shape
    seqs, part = ids.shape
    width = H * HD
    local = width // nt
    units = (wide - 3 * width) // nt

    def kernel(ids_hbm, win_hbm, a_hbm, u_hbm, ids_ref, win_ref, a_ref, u_ref, in_sem, a_sem, u_sem):
        loads = [pltpu.make_async_copy(win_hbm, win_ref, in_sem.at[0]), pltpu.make_async_copy(ids_hbm, ids_ref, in_sem.at[1])]
        for copy in loads:
            copy.start()
        for copy in loads:
            copy.wait()
        row = jnp.concatenate([ids_ref[s : s + 1, :] for s in range(seqs)], axis=1).astype(F32).astype(BF)
        first = 3 * local
        second = jnp.concatenate([row[:, first:].astype(F32), jnp.zeros((1, 2 * first - seqs * part), F32)], axis=1).astype(BF)
        for t in range(nt):
            for k in range(3):
                a_ref[t, :rows, k * local : (k + 1) * local] = win_ref[:, k * width + t * local : k * width + (t + 1) * local]
            a_ref[t, rows : rows + 1] = row[:, :first]
            a_ref[t, rows + 1 :] = second
        for b in range(nb):
            pltpu.make_async_copy(a_ref, a_hbm.at[b], a_sem.at[b]).start()
        for t in range(nt):
            u_ref[t] = win_ref[:, 3 * width + t * units : 3 * width + (t + 1) * units]
        for b in range(nb):
            pltpu.make_async_copy(u_ref, u_hbm.at[b], u_sem.at[b]).start()
        for b in range(nb):
            pltpu.make_async_copy(a_ref, a_hbm.at[b], a_sem.at[b]).wait()
            pltpu.make_async_copy(u_ref, u_hbm.at[b], u_sem.at[b]).wait()

    return pl.pallas_call(
        kernel,
        out_shape=[
            jax.ShapeDtypeStruct((nb, nt, rows + 2, 3 * local), BF),
            jax.ShapeDtypeStruct((nb, nt, rows, units), BF),
        ],
        in_specs=[HBM] * 2,
        out_specs=[HBM] * 2,
        scratch_shapes=[
            pltpu.VMEM(ids.shape, jnp.int32),
            pltpu.VMEM(w_in.shape, BF),
            pltpu.VMEM((nt, rows + 2, 3 * local), BF),
            pltpu.VMEM((nt, rows, units), BF),
            pltpu.SemaphoreType.DMA((2,)),
            pltpu.SemaphoreType.DMA((nb,)),
            pltpu.SemaphoreType.DMA((nb,)),
        ],
        cost_estimate=SMALL,
        compiler_params=pltpu.CompilerParams(vmem_limit_bytes=16 * MIB),
        name="prepare",
    )(*hbm(ids, w_in))


def before_kernel(at_ref, table_hbm, ids_hbm, gain_hbm, x_hbm, cot_hbm, wout_hbm, *refs):
    outs, (table_ref, ids_ref, gain_ref, x_ref, cot_ref, wout_ref, pay_ref, in_sem, out_sem) = refs[:-9], refs[-9:]
    seqs = x_ref.shape[0]
    pays, unit_refs = outs[:2], outs[2:]
    ins = [
        pltpu.make_async_copy(a, b, in_sem.at[i])
        for i, (a, b) in enumerate(
            ((x_hbm, x_ref), (cot_hbm, cot_ref), (ids_hbm, ids_ref), (gain_hbm, gain_ref), (table_hbm, table_ref), (wout_hbm, wout_ref))
        )
    ]
    for copy in ins:
        copy.start()
    for copy in ins:
        copy.wait()
    for k, ref in enumerate(unit_refs):
        ref[...] = wout_ref[table_ref[at_ref[0], k]]
    copies = []
    for s in range(seqs):
        unit, _ = normalize(x_ref[s].astype(F32))
        live = column(jnp.where(ids_ref[s : s + 1, :] >= 0, 1.0, 0.0))
        pay_ref[s, 0] = (unit * gain_ref[...]).astype(BF)
        pay_ref[s, 1] = (live * cot_ref[s].astype(F32)).astype(BF)
        copies.append(pltpu.make_async_copy(pay_ref.at[s], pays[0].at[s] if s < seqs - 1 else pays[1].at[0], out_sem.at[s]))
        copies[-1].start()
    for copy in copies:
        copy.wait()


def before(at, table, ids, gain, x, cot, w_out):
    seqs, part, dim = x.shape
    per, unit, _ = w_out.shape
    outs = [jax.ShapeDtypeStruct((seqs - 1, 2, part, dim), BF), jax.ShapeDtypeStruct((1, 2, part, dim), BF)]
    outs += [jax.ShapeDtypeStruct((unit, dim), BF)] * per
    return pl.pallas_call(
        before_kernel,
        out_shape=outs,
        in_specs=[SMEM] + [HBM] * 6,
        out_specs=[HBM] * 2 + [VMEM] * per,
        scratch_shapes=[
            pltpu.SMEM(table.shape, jnp.int32),
            pltpu.VMEM(ids.shape, jnp.int32),
            pltpu.VMEM(gain.shape, F32),
            pltpu.VMEM(x.shape, BF),
            pltpu.VMEM(x.shape, BF),
            pltpu.VMEM(w_out.shape, BF),
            pltpu.VMEM((seqs, 2, part, dim), BF),
            pltpu.SemaphoreType.DMA((6,)),
            pltpu.SemaphoreType.DMA((seqs,)),
        ],
        cost_estimate=SMALL,
        compiler_params=pltpu.CompilerParams(vmem_limit_bytes=32 * MIB),
        name="before",
    )(at, *hbm(table, ids, gain, x, cot, w_out))


def join(at, got, seqs, part):
    count, high, wide = got.shape
    unit = high - 2
    dim = count * unit

    def kernel(at_ref, got_ref, w_ref, ids_ref, all_ref):
        def move(i, carry):
            all_ref[i] = got_ref[i, :unit]
            return carry

        lax.fori_loop(0, count, move, 0)
        w_ref[...] = all_ref[...].reshape(dim, wide).T
        for slot in range(SLOTS):
            i = at_ref[2] * SLOTS + (at_ref[1] ^ slot)
            row = jnp.concatenate([got_ref[i, unit : unit + 1], got_ref[i, unit + 1 :]], axis=1)
            row = row.astype(F32).astype(jnp.int32)
            for s in range(seqs):
                ids_ref[s, :, slot * part : (slot + 1) * part] = row[:, s * part : (s + 1) * part]

    return pl.pallas_call(
        kernel,
        out_shape=[jax.ShapeDtypeStruct((wide, dim), BF), jax.ShapeDtypeStruct((seqs, 1, SLOTS * part), jnp.int32)],
        in_specs=[SMEM, VMEM],
        out_specs=[VMEM] * 2,
        scratch_shapes=[pltpu.VMEM((count, unit, wide), BF)],
        cost_estimate=SMALL,
        compiler_params=pltpu.CompilerParams(vmem_limit_bytes=32 * MIB),
        name="join",
    )(at, got)


def pack_out(at, table, got, nb):
    unit, dim = got[0].shape
    per = len(got)

    def kernel(at_ref, table_ref, *refs):
        got_refs, (wo_hbm, ff_hbm, all_ref, wo_sem, ff_sem) = refs[:per], refs[per:]
        for k, ref in enumerate(got_refs):
            all_ref[table_ref[at_ref[0], per + k]] = ref[...]
        copies = [pltpu.make_async_copy(all_ref.at[0], wo_hbm.at[b], wo_sem.at[b]) for b in range(nb)]
        copies.append(pltpu.make_async_copy(all_ref.at[pl.ds(1, per - 1)], ff_hbm, ff_sem))
        for copy in copies:
            copy.start()
        for copy in copies:
            copy.wait()

    return pl.pallas_call(
        kernel,
        out_shape=[jax.ShapeDtypeStruct((nb, unit, dim), BF), jax.ShapeDtypeStruct((per - 1, unit, dim), BF)],
        in_specs=[SMEM] * 2 + [VMEM] * per,
        out_specs=[HBM] * 2,
        scratch_shapes=[
            pltpu.VMEM((per, unit, dim), BF),
            pltpu.SemaphoreType.DMA((nb,)),
            pltpu.SemaphoreType.DMA,
        ],
        cost_estimate=SMALL,
        name="pack_out",
    )(at, table, *got)


def add_blocks(ref, count, step, start, rows):
    total = ref[start, rows].astype(F32)
    for i in range(1, count):
        total = total + ref[start + i * step, rows].astype(F32)
    return total


def sum_qkv(up, nt):
    count, unit, dim = up.shape

    def kernel(up_ref, out_ref):
        for t in range(nt):
            out_ref[t] = add_blocks(up_ref, count // nt, nt, t, slice(None))

    return pl.pallas_call(
        kernel,
        out_shape=jax.ShapeDtypeStruct((nt, unit, dim), F32),
        in_specs=[VMEM],
        out_specs=VMEM,
        cost_estimate=SMALL,
        compiler_params=pltpu.CompilerParams(vmem_limit_bytes=32 * MIB),
        name="sum_qkv",
    )(up)


def fold(at, low, keep, got):
    n, high, dim = keep.shape

    def kernel(at_ref, keep_ref, *refs):
        got_refs, (own_ref, *send_refs) = refs[: len(got)], refs[len(got) :]
        mine = (at_ref[2] >> low) & 3
        for i in range(n // 4):
            for s, to in enumerate([own_ref] + send_refs):
                total = keep_ref[i * 4 + (mine ^ s)]
                for ref in got_refs:
                    total = total + ref[i * 4 + (mine ^ s)].astype(F32)
                to[i] = total.astype(to.dtype)

    out = lambda t: jax.ShapeDtypeStruct((n // 4, high, dim), t)
    return pl.pallas_call(
        kernel,
        out_shape=[out(F32)] + [out(BF)] * 3,
        in_specs=[SMEM] + [VMEM] * (1 + len(got)),
        out_specs=[VMEM] * 4,
        cost_estimate=SMALL,
        compiler_params=pltpu.CompilerParams(vmem_limit_bytes=32 * MIB),
        name="fold",
    )(at, keep, *got)


def split_rows(odd, grad, send_ref, keep_ref, start, rows):
    for z in range(send_ref.shape[0]):
        low = grad[2 * z * rows : (2 * z + 1) * rows]
        high = grad[(2 * z + 1) * rows : (2 * z + 2) * rows]
        send_ref[z, start : start + rows] = jnp.where(odd, low, high).astype(BF)
        keep_ref[z, start : start + rows] = jnp.where(odd, high, low)


def leave(at, table, terms):
    per = table.shape[1] // 2
    _, high, dim = terms[0].shape
    unit = high // per

    def kernel(at_ref, table_ref, *refs):
        term_refs, out_refs, all_ref = refs[: len(terms)], refs[len(terms) : -1], refs[-1]
        total = term_refs[0][0]
        for ref in term_refs[1:]:
            total = total + ref[0].astype(F32)
        for k in range(per):
            all_ref[k] = total[k * unit : (k + 1) * unit]
        for k, ref in enumerate(out_refs):
            ref[...] = all_ref[table_ref[at_ref[0], per + k]]

    return pl.pallas_call(
        kernel,
        out_shape=[jax.ShapeDtypeStruct((unit, dim), F32)] * per,
        in_specs=[SMEM] * 2 + [VMEM] * len(terms),
        out_specs=[VMEM] * per,
        scratch_shapes=[pltpu.VMEM((per, unit, dim), F32)],
        cost_estimate=SMALL,
        name="leave",
    )(at, table, *terms)


def place(at, table, qkv, up, got):
    nt, unit, width = qkv.shape
    count, high, dim = up.shape
    per = len(got)
    local = width // 3
    wide = nt * (width + dim)

    def kernel(at_ref, table_ref, qkv_ref, up_ref, *refs):
        got_refs, (in_ref, out_ref, norm_ref, q_ref, k_ref) = refs[:per], refs[per:]
        for t in range(nt):
            for k in range(3):
                to = k * nt * local + t * local
                in_ref[:, to : to + local] = qkv_ref[t, :, k * local : (k + 1) * local]
            to = nt * width + t * dim
            in_ref[:, to : to + dim] = add_blocks(up_ref, count // nt, nt, t, slice(0, unit))
        for k, ref in enumerate(got_refs):
            out_ref[table_ref[at_ref[0], k]] = ref[...]
        small = add_blocks(up_ref, count, 1, 0, slice(unit, high))
        small = small[0:2] + small[2:4]
        norm_ref[...] = small[0:1]
        q_ref[...] = small[1:2, :HD]
        k_ref[...] = small[1:2, HD : 2 * HD]

    return pl.pallas_call(
        kernel,
        out_shape=[
            jax.ShapeDtypeStruct((unit, wide), F32),
            jax.ShapeDtypeStruct((per, unit, dim), F32),
            jax.ShapeDtypeStruct((1, dim), F32),
            jax.ShapeDtypeStruct((1, HD), F32),
            jax.ShapeDtypeStruct((1, HD), F32),
        ],
        in_specs=[SMEM] * 2 + [VMEM] * (2 + per),
        out_specs=[VMEM] * 5,
        cost_estimate=SMALL,
        compiler_params=pltpu.CompilerParams(vmem_limit_bytes=32 * MIB),
        name="place",
    )(at, table, qkv, up, *got)


def after_kernel(s, ids_ref, x_ref, cot_ref, gain_ref, keep_ref, near_ref, far_ref, *rest):
    out_ref, grad_ref = rest[-2:]
    unit, inverse = normalize(x_ref[0].astype(F32))
    live = column(jnp.where(ids_ref[s : s + 1, :] >= 0, 1.0, 0.0))
    both = keep_ref[0, 0].astype(F32) + near_ref[0, 0].astype(F32) + far_ref[0].astype(F32)
    out_ref[0] = (live * (x_ref[0].astype(F32) + both[0])).astype(BF)
    grad_ref[0] = (
        live * cot_ref[0].astype(F32) + norm_back(both[1] * gain_ref[...], unit, inverse)
    ).astype(BF)


def after(s, i, ids, x, cot, gain, keep, near, far, earlier):
    x, cot, keep, near, far = (pltpu.with_memory_space_constraint(a, pltpu.HBM) for a in (x, cot, keep, near, far))
    seqs, part, dim = x.shape
    one = pl.BlockSpec((1, part, dim), lambda g: (s, 0, 0))
    pair = pl.BlockSpec((1, 1, 2, part, dim), lambda g: (0, i, 0, 0, 0))
    lone = pl.BlockSpec((1, 2, part, dim), lambda g: (i, 0, 0, 0))
    fixed = lambda a: pl.BlockSpec(a.shape, lambda g: (0,) * a.ndim)
    return pl.pallas_call(
        functools.partial(after_kernel, s),
        grid=(1,),
        out_shape=[jax.ShapeDtypeStruct(x.shape, BF)] * 2,
        in_specs=[fixed(ids), one, one, fixed(gain), pair, pair, lone] + [ANY] * len(earlier),
        out_specs=[one, one],
        input_output_aliases={7 + i: i for i in range(len(earlier))},
        cost_estimate=SMALL,
        compiler_params=pltpu.CompilerParams(vmem_limit_bytes=32 * MIB),
        name="after",
    )(ids, x, cot, gain, keep, near, far, *earlier)


def attention_kernel(
    heads, block, groups,
    ids_ref, qg_ref, kg_ref, wqkv_hbm, wo_hbm, *refs,
):
    pays, refs = refs[: SLOTS * len(groups)], refs[SLOTS * len(groups) :]
    (o_hbm, grad_hbm, sendq_ref, go_ref, np_ref, sums_ref), refs = refs[:6], refs[6:]
    (
        wqkv_ref, wo_ref, norm_ref, gb_ref, o_ref, grad_ref, gq_ref, acc_ref, raw_ref,
        qt_ref, qn_ref, kt_ref, ka_ref, vt_ref, va_ref, do_ref, dq_ref, dk_ref, dv_ref, pad_ref, vm_ref,
        w_sem, sem, out_sem,
    ) = refs
    seqs, length, dim = norm_ref.shape
    part = length // SLOTS
    width = heads * HD
    blocks = length // block
    loads = [pltpu.make_async_copy(wqkv_hbm, wqkv_ref, w_sem.at[0]), pltpu.make_async_copy(wo_hbm, wo_ref, w_sem.at[1])]
    loads[0].start()

    def pay_copy(s, j, t, source):
        to = (norm_ref, gb_ref)[j].at[s, pl.ds(t * part, part), :]
        return pltpu.make_async_copy(source, to, sem.at[s, j * SLOTS + t])

    s = 0
    for g, size in enumerate(groups):
        for i in range(size):
            for j in range(2):
                for t in range(SLOTS):
                    pay_copy(s, j, t, pays[g * SLOTS + t].at[i, j]).start()
                if s + j == 0:
                    loads[1].start()
            s += 1
    gq_ref[...] = jnp.zeros_like(gq_ref)
    go_ref[...] = jnp.zeros_like(go_ref)
    acc_ref[...] = jnp.zeros_like(acc_ref)
    gain_q = qg_ref[...]
    gain_k = kg_ref[...]
    marks = lax.broadcasted_iota(jnp.int32, (HD, length), 0)
    v_tail = jnp.where(lax.broadcasted_iota(jnp.int32, (length, HD), 1) < 2, 1.0, 0.0).astype(BF)
    ones = jnp.where(lax.broadcasted_iota(jnp.int32, (16, length), 0) == 0, 1.0, 0.0).astype(BF)
    spot = lax.broadcasted_iota(jnp.int32, (HD, block), 0)
    scale = 1.0 / math.sqrt(HD)
    cut = lambda a, i: a[:, i * block : (i + 1) * block]

    def unit_of(row):
        raw = raw_ref[pl.ds(pl.multiple_of(row, HD), HD), :]
        center = raw - jnp.mean(raw, axis=0, keepdims=True)
        inverse = lax.rsqrt(jnp.mean(center * center, axis=0, keepdims=True) + EPS)
        return center * inverse, inverse

    def lanes(a):
        total = a[:, :128]
        for i in range(1, length // 128):
            total = total + a[:, i * 128 : (i + 1) * 128]
        return total

    def stores(s):
        return [
            pltpu.make_async_copy(o_ref.at[s], o_hbm.at[s], out_sem.at[s, 0]),
            pltpu.make_async_copy(grad_ref.at[s], grad_hbm.at[s], out_sem.at[s, 1]),
        ]

    loads[0].wait()
    loads[1].wait()

    def sequence(s, carry):
        ids = ids_ref[s]
        same = marks == ids + 1
        k_tail = jnp.where(same, 1.0, 0.0).T.astype(BF)
        q_tail = jnp.where((same & (ids >= 0)) | (marks > 4), 0.0, -BIG).astype(BF)
        pad = jnp.where(ids < 0, 1.0, 0.0)
        for i in range(blocks):
            pad_ref[i] = cut(pad, i)
        for t in range(SLOTS):
            pay_copy(s, 0, t, pays[0].at[0, 0]).wait()
        raw_ref[...] = mm(wqkv_ref[...], norm_ref[s], NT)
        for t in range(SLOTS):
            pay_copy(s, 1, t, pays[0].at[0, 0]).wait()
        do_all = mm(wo_ref[...], gb_ref[s], NT).astype(BF)
        for h in range(heads):
            for i in range(blocks):
                do_ref[h * blocks + i] = cut(do_all[h * HD : (h + 1) * HD], i)

        def prepare(h, carry):
            q_unit, _ = unit_of(h * HD)
            q = q_unit * gain_q
            qn = q.T.astype(BF)
            for i in range(blocks):
                qt_ref[h * blocks + i, :HD] = cut(q, i).astype(BF)
                qt_ref[h * blocks + i, HD:] = cut(q_tail, i)
                qn_ref[h * blocks + i] = qn[i * block : (i + 1) * block]
            k_unit, _ = unit_of(width + h * HD)
            k = k_unit * gain_k
            kt_ref[h] = k.astype(BF)
            ka_ref[h, :, :HD] = k.T.astype(BF)
            ka_ref[h, :, HD:] = k_tail
            v = raw_ref[pl.ds(pl.multiple_of(2 * width + h * HD, HD), HD), :]
            vb = v.astype(BF)
            vt_ref[h, :HD] = vb
            vt_ref[h, HD:] = ones
            va_ref[h, :, :HD] = v.T.astype(BF)
            va_ref[h, :, HD:] = v_tail
            vm_ref[h] = jnp.mean(vb.astype(F32), axis=1, keepdims=True)
            dk_ref[h] = jnp.zeros(dk_ref.shape[1:], F32)
            dv_ref[h] = jnp.zeros(dv_ref.shape[1:], F32)
            return carry

        lax.fori_loop(0, heads, prepare, 0)

        def step(n, carry):
            h = n // blocks
            padb = pad_ref[n % blocks]
            e = jnp.exp2(mm(ka_ref[h], qt_ref[n]) * (LOG2E * scale))
            eb = e.astype(BF)
            oa = mm(vt_ref[h], eb)
            inv = 1.0 / (oa[HD : HD + 1] + padb)
            o = oa[:HD] * inv
            dos = (do_ref[n].astype(F32) * inv).astype(BF)
            delta = jnp.sum(dos.astype(F32) * o, axis=0, keepdims=True)
            d0 = delta.astype(BF).astype(F32)
            tail = jnp.where(spot == 0, -d0, jnp.where(spot == 1, d0 - delta, 0.0))
            doa = jnp.concatenate([dos.astype(F32), tail], axis=0)
            ds = (e * mm(va_ref[h], doa.astype(BF))).astype(BF)
            dq_ref[n] = mm(kt_ref[h], ds)
            dk_ref[h] += mm(ds, qn_ref[n])
            dv_ref[h] += mm(eb, doa.T.astype(BF))
            do_ref[n] = jnp.where(padb > 0, vm_ref[h], o).astype(BF)
            return carry

        lax.fori_loop(0, heads * blocks, step, 0)

        def finish(h, carry):
            rows = lambda at: pl.ds(pl.multiple_of(at + h * HD, HD), HD)
            gq = jnp.concatenate([dq_ref[h * blocks + i] for i in range(blocks)], axis=1)
            gk = dk_ref[h].T
            for k, (g, gain_col) in enumerate(((gq, gain_q), (gk, gain_k))):
                unit, inverse = unit_of(k * width + h * HD)
                g = (g * scale).astype(BF).astype(F32)
                acc_ref[k] += lanes(g * unit)
                g = g * gain_col
                back = inverse * (
                    g - jnp.mean(g, axis=0, keepdims=True) - unit * jnp.mean(g * unit, axis=0, keepdims=True)
                )
                grad_ref[s, rows(k * width), :] = back.astype(BF)
            grad_ref[s, rows(2 * width), :] = dv_ref[h].T[:HD].astype(BF)
            for i in range(blocks):
                o_ref[s, rows(0), pl.ds(i * block, block)] = do_ref[h * blocks + i]
            return carry

        lax.fori_loop(0, heads, finish, 0)
        for copy in stores(s):
            copy.start()
        gq_ref[...] += mm(grad_ref[s], norm_ref[s])
        go_ref[...] += mm(o_ref[s], gb_ref[s])
        return carry

    lax.fori_loop(0, seqs, sequence, 0)
    g_q = gq_ref[...]
    np_ref[...] = jnp.sum(wqkv_ref[...].astype(F32) * g_q, axis=0, keepdims=True)
    sums_ref[...] = jnp.concatenate([jnp.sum(acc_ref[k].T, axis=0, keepdims=True) for k in range(2)], axis=1)
    g_q = g_q.T.astype(BF)
    count, rows, _ = sendq_ref.shape
    for i in range(count):
        sendq_ref[i] = g_q[i * rows : (i + 1) * rows]
    for s in range(seqs):
        for copy in stores(s):
            copy.wait()


def attention(ids, wqkv, wo, qg, kg, groups, count):
    wide, dim = wqkv.shape
    width = wo.shape[0]
    heads = width // HD
    sizes = [g[0].shape[0] for g in groups]
    seqs, part = sum(sizes), groups[0][0].shape[2]
    length = part * SLOTS
    block = 512
    blocks = length // block
    ins = [ids, qg, kg, *hbm(wqkv, wo, *[p for g in groups for p in g])]
    outs = [
        jax.ShapeDtypeStruct((seqs, width, length), BF),
        jax.ShapeDtypeStruct((seqs, wide, length), BF),
        jax.ShapeDtypeStruct((count, dim // count, wide), BF),
        jax.ShapeDtypeStruct((width, dim), F32),
        jax.ShapeDtypeStruct((1, dim), F32),
        jax.ShapeDtypeStruct((1, 2 * HD), F32),
    ]
    flops = seqs * (2 * length * dim * width * 8 + heads * 6 * 2 * length * length * HD)
    return pl.pallas_call(
        functools.partial(attention_kernel, heads, block, sizes),
        out_shape=outs,
        in_specs=[VMEM] * 3 + [HBM] * (2 + SLOTS * len(groups)),
        out_specs=[HBM] * 2 + [VMEM] * 4,
        scratch_shapes=[
            pltpu.VMEM((wide, dim), BF),
            pltpu.VMEM((width, dim), BF),
            pltpu.VMEM((seqs, length, dim), BF),
            pltpu.VMEM((seqs, length, dim), BF),
            pltpu.VMEM((seqs, width, length), BF),
            pltpu.VMEM((seqs, wide, length), BF),
            pltpu.VMEM((wide, dim), F32),
            pltpu.VMEM((2, HD, 128), F32),
            pltpu.VMEM((wide, length), F32),
            pltpu.VMEM((heads * blocks, 2 * HD, block), BF),
            pltpu.VMEM((heads * blocks, block, HD), BF),
            pltpu.VMEM((heads, HD, length), BF),
            pltpu.VMEM((heads, length, 2 * HD), BF),
            pltpu.VMEM((heads, HD + 16, length), BF),
            pltpu.VMEM((heads, length, 2 * HD), BF),
            pltpu.VMEM((heads * blocks, HD, block), BF),
            pltpu.VMEM((heads * blocks, HD, block), F32),
            pltpu.VMEM((heads, length, HD), F32),
            pltpu.VMEM((heads, length, 2 * HD), F32),
            pltpu.VMEM((blocks, 1, block), F32),
            pltpu.VMEM((heads, HD, 1), F32),
            pltpu.SemaphoreType.DMA((4,)),
            pltpu.SemaphoreType.DMA((seqs, 2 * SLOTS)),
            pltpu.SemaphoreType.DMA((seqs, 2)),
        ],
        cost_estimate=LARGE,
        compiler_params=pltpu.CompilerParams(vmem_limit_bytes=56 * MIB),
        name="attention",
    )(*ins)


def ffn_kernel(block, groups, plan, at_ref, go_ref, anp_ref, sums_ref, gain_ref, wup_hbm, *refs):
    pieces, refs = refs[: len(plan)], refs[len(plan) :]
    pays, refs = refs[: len(groups) * SLOTS], refs[len(groups) * SLOTS :]
    (hid_hbm, gup_hbm, wff_hbm, sendu_ref, sendf_ref, keepf_ref), refs = refs[:6], refs[6:]
    norm_ref, gb_ref, hid_ref, gup_ref, wup_ref, wff_ref, gin_ref, gff_ref, sem, out_sem, w_sem = refs
    dim = wup_ref.shape[0]
    part = pays[0].shape[2]
    total = norm_ref.shape[0]
    weights = [pltpu.make_async_copy(wup_hbm, wup_ref, w_sem.at[0])]
    head_rows = go_ref.shape[0] // (2 * sendf_ref.shape[0])
    rows = sendf_ref.shape[1] - head_rows
    for ref, masks in zip(pieces, plan):
        for i, mask in enumerate(masks):
            to = wff_ref.at[pl.ds(pl.multiple_of((at_ref[2] ^ mask) * rows, rows), rows), :]
            weights.append(pltpu.make_async_copy(ref.at[i], to, w_sem.at[len(weights)]))
    for copy in weights:
        copy.start()
    n = 0
    for g, seqs in enumerate(groups):
        for s in range(seqs):
            for t in range(SLOTS):
                for k, to in enumerate((norm_ref, gb_ref)):
                    source = pays[g * SLOTS + t].at[s, k]
                    pltpu.make_async_copy(source, to.at[pl.ds(n * part, part), :], sem.at[k, n]).start()
                n += 1
    gin_ref[...] = jnp.zeros_like(gin_ref)
    gff_ref[...] = jnp.zeros_like(gff_ref)
    for copy in weights:
        copy.wait()
    joined = pltpu.make_async_copy(wff_ref, wff_hbm, w_sem.at[0])
    joined.start()
    c0 = math.sqrt(2.0 / math.pi)
    c1 = 0.044715

    def outs(i):
        at_rows = pl.ds(pl.multiple_of(i * block, block), block)
        return (
            pltpu.make_async_copy(hid_ref.at[at_rows, :], hid_hbm.at[at_rows, :], out_sem.at[0, i]),
            pltpu.make_async_copy(gup_ref.at[at_rows, :], gup_hbm.at[at_rows, :], out_sem.at[1, i]),
        )

    def step(i, carry):
        for j in range(block // part):
            for k, to in enumerate((norm_ref, gb_ref)):
                pltpu.make_async_copy(pays[0].at[0, 0], to.at[pl.ds(0, part), :], sem.at[k, i * (block // part) + j]).wait()
        at_rows = pl.ds(pl.multiple_of(i * block, block), block)
        up = mm(norm_ref[at_rows, :], wup_ref[...])
        gh = mm(gb_ref[at_rows, :], wff_ref[...], NT)
        sq = up * up
        t = jnp.tanh(up * (c0 + (c0 * c1) * sq))
        half = 0.5 + 0.5 * t
        hid_ref[at_rows, :] = (up * half).astype(BF)
        gup_ref[at_rows, :] = (gh * (half + (0.5 * up) * (1.0 - t * t) * (c0 + (3.0 * c0 * c1) * sq))).astype(BF)
        for copy in outs(i):
            copy.start()
        gin_ref[...] += mm(norm_ref[at_rows, :], gup_ref[at_rows, :], TN)
        gff_ref[...] += mm(hid_ref[at_rows, :], gb_ref[at_rows, :], TN)
        return carry

    lax.fori_loop(0, total // block, step, 0)
    line = jnp.sum(wup_ref[...].astype(F32) * gin_ref[...], axis=1, keepdims=True)
    first = (jnp.broadcast_to(line, (dim, 128)).T[0:1] + anp_ref[...]) / gain_ref[...]
    second = jnp.concatenate([sums_ref[...], jnp.zeros((1, dim - 2 * HD), F32)], axis=1)
    small = jnp.concatenate([first, second], axis=0)
    high = small.astype(BF).astype(F32)
    small = jnp.concatenate([high, small - high], axis=0).astype(BF)
    count, unit, _ = sendu_ref.shape
    unit = unit - 4
    for i in range(count):
        sendu_ref[i, :unit] = gin_ref[i * unit : (i + 1) * unit, :].astype(BF)
        sendu_ref[i, unit:] = small
    odd = (at_ref[2] & 1) > 0
    split_rows(odd, go_ref[...], sendf_ref, keepf_ref, 0, head_rows)
    split_rows(odd, gff_ref[...], sendf_ref, keepf_ref, head_rows, rows)
    joined.wait()

    def drain(i, carry):
        for copy in outs(i):
            copy.wait()
        return carry

    lax.fori_loop(0, total // block, drain, 0)


def ffn(at, go, anp, sums, gain, wup, ff_parts, groups, count, block=512):
    dim, units = wup.shape
    sizes = [g[0].shape[0] for g in groups]
    part = groups[0][0].shape[2]
    total = SLOTS * part * sum(sizes)
    pieces = [p for g in groups for p in g]
    act = jax.ShapeDtypeStruct((total, units), BF)
    return pl.pallas_call(
        functools.partial(ffn_kernel, block, sizes, [masks for _, masks in ff_parts]),
        out_shape=[
            act,
            act,
            jax.ShapeDtypeStruct((units, dim), BF),
            jax.ShapeDtypeStruct((count * SLOTS, dim // (count * SLOTS) + 4, units), BF),
            jax.ShapeDtypeStruct((count // 2, (units + go.shape[0]) // count, dim), BF),
            jax.ShapeDtypeStruct((count // 2, (units + go.shape[0]) // count, dim), F32),
        ],
        in_specs=[SMEM] + [VMEM] * 4 + [HBM] * (1 + len(ff_parts) + len(pieces)),
        out_specs=[HBM] * 3 + [VMEM] * 3,
        scratch_shapes=[
            pltpu.VMEM((total, dim), BF),
            pltpu.VMEM((total, dim), BF),
            pltpu.VMEM((total, units), BF),
            pltpu.VMEM((total, units), BF),
            pltpu.VMEM((dim, units), BF),
            pltpu.VMEM((units, dim), BF),
            pltpu.VMEM((dim, units), F32),
            pltpu.VMEM((units, dim), F32),
            pltpu.SemaphoreType.DMA((2, total // part)),
            pltpu.SemaphoreType.DMA((2, total // block)),
            pltpu.SemaphoreType.DMA((1 + count,)),
        ],
        cost_estimate=LARGE,
        compiler_params=pltpu.CompilerParams(vmem_limit_bytes=58 * MIB),
        name="ffn",
    )(at, go, anp, sums, gain, *hbm(wup, *[a for a, _ in ff_parts], *pieces))


def outputs(start, first, seqs, o, hid, gq, gu, wo, wff, wqkv, wup):
    length = o.shape[2]
    dim = wo.shape[1]
    part = length // SLOTS

    def kernel(o_hbm, hid_hbm, gq_hbm, gu_hbm, wo_hbm, wff_hbm, wqkv_hbm, wup_hbm, keep_hbm, send_hbm, *scratch):
        o_ref, hid_ref, gq_ref, gu_ref, wo_ref, wff_ref, wqkv_ref, wup_ref, res_ref, w_sem, sem, out_sem = scratch

        def load(k, s):
            rows = pl.ds((start + s) * length, length)
            source, to = (
                (hid_hbm.at[rows, :], hid_ref), (o_hbm.at[first + s], o_ref), (gu_hbm.at[rows, :], gu_ref), (gq_hbm.at[first + s], gq_ref)
            )[k]
            return pltpu.make_async_copy(source, to.at[s], sem.at[s, k])

        weights = [
            pltpu.make_async_copy(a, b, w_sem.at[k])
            for k, (a, b) in enumerate(((wff_hbm, wff_ref), (wo_hbm, wo_ref), (wup_hbm, wup_ref), (wqkv_hbm, wqkv_ref)))
        ]
        for k in range(4):
            weights[k].start()
            load(k, 0).start()
        for s in range(1, seqs):
            for k in range(4):
                load(k, s).start()

        weights[0].wait()
        weights[1].wait()
        half = length // 2

        def step(n, carry):
            s, i = n // 2, n % 2
            lanes = pl.ds(pl.multiple_of(i * half, half), half)

            @pl.when(i == 0)
            def _():
                load(0, s).wait()
                load(1, s).wait()

            res_ref[s, 0, lanes, :] = (mm(o_ref[s, :, lanes], wo_ref[...], TN) + mm(hid_ref[s, lanes, :], wff_ref[...])).astype(BF)

            @pl.when(n == 0)
            def _():
                weights[2].wait()
                weights[3].wait()

            @pl.when(i == 0)
            def _():
                load(2, s).wait()
                load(3, s).wait()

            res_ref[s, 1, lanes, :] = (
                mm(gq_ref[s, :, lanes], wqkv_ref[...], TN) + mm(gu_ref[s, lanes, :], wup_ref[...], NT)
            ).astype(BF)
            for copy in moves(s, i):
                copy.start()
            return carry

        def moves(s, i):
            out = []
            for j in range(2):
                for k, to in enumerate((keep_hbm, send_hbm)):
                    rows = pl.ds(pl.multiple_of(i * half + k * part, part), part)
                    out.append(pltpu.make_async_copy(res_ref.at[s, j, rows, :], to.at[i, s, j], out_sem.at[s, j, 2 * i + k]))
            return out

        lax.fori_loop(0, 2 * seqs, step, 0)
        for s in range(seqs):
            for i in range(2):
                for copy in moves(s, i):
                    copy.wait()

    return pl.pallas_call(
        kernel,
        out_shape=[jax.ShapeDtypeStruct((SLOTS // 2, seqs, 2, part, dim), BF)] * 2,
        in_specs=[HBM] * 8,
        out_specs=[HBM] * 2,
        scratch_shapes=[
            pltpu.VMEM((seqs,) + o.shape[1:], BF),
            pltpu.VMEM((seqs, length, hid.shape[1]), BF),
            pltpu.VMEM((seqs,) + gq.shape[1:], BF),
            pltpu.VMEM((seqs, length, gu.shape[1]), BF),
            pltpu.VMEM(wo.shape, BF),
            pltpu.VMEM(wff.shape, BF),
            pltpu.VMEM(wqkv.shape, BF),
            pltpu.VMEM(wup.shape, BF),
            pltpu.VMEM((seqs, 2, length, dim), BF),
            pltpu.SemaphoreType.DMA((4,)),
            pltpu.SemaphoreType.DMA((seqs, 4)),
            pltpu.SemaphoreType.DMA((seqs, 2, SLOTS)),
        ],
        cost_estimate=SMALL,
        compiler_params=pltpu.CompilerParams(vmem_limit_bytes=48 * MIB),
        name="outputs",
    )(*hbm(o, hid, gq, gu, wo, wff, wqkv, wup))


def swap(value, axis, count, mask):
    return lax.ppermute(value, axis, [(i, i ^ mask) for i in range(count)])


def tie(value, *after):
    return lax.optimization_barrier((value,) + after)[0]


def bit_groups(count):
    bits = list(range(count.bit_length() - 1))[::-1]
    groups = []
    while bits:
        take = 2 if len(bits) > 1 else 1
        groups.append(bits[:take])
        bits = bits[take:]
    assert len(groups[-1]) == 1
    return groups


def gather_batch(block, count, groups):
    held, masks = block[None], [0]
    for bits in groups:
        low = bits[-1]
        parts = [(held, masks)]
        for s in range(1, 1 << len(bits)):
            parts.append((swap(held, "batch", count, s << low), [m ^ (s << low) for m in masks]))
        held = jnp.concatenate([a for a, _ in parts], axis=0)
        masks = sum((m for _, m in parts), [])
    return parts


def matchings(edges, devices, per_device):
    left = [[] for _ in range(devices)]
    for e, (source, _, _) in enumerate(edges):
        left[source].append(e)
    rounds = []
    for _ in range(per_device):
        owner = [-1] * devices

        def place(source, seen):
            for e in left[source]:
                target = edges[e][1]
                if target in seen:
                    continue
                seen.add(target)
                if owner[target] < 0 or place(edges[owner[target]][0], seen):
                    owner[target] = e
                    return True
            return False

        for source in range(devices):
            place(source, set())
        rounds.append(list(owner))
        for e in owner:
            left[edges[e][0]].remove(e)
    return rounds


def unit_plan(nb, nt, rows, width, hidden):
    unit = math.gcd(math.gcd(rows, width // nt), hidden // nt)
    per = rows // unit
    head_units, hid_units = width // nt // unit, hidden // nt // unit
    assert head_units == nb and hid_units % nb == 0
    c = hid_units // nb
    edges = []
    for t in range(nt):
        for b in range(nb):
            want = [t * head_units + b]
            want += [nt * head_units + t * hid_units + b * c + i for i in range(c)]
            for slot, u in enumerate(want):
                edges.append((u // per, b * nt + t, (u % per, slot)))
    table = np.zeros((nb * nt, 2 * per), np.int32)
    perms = []
    for k, owner in enumerate(matchings(edges, nb * nt, per)):
        perms.append([(edges[e][0], edges[e][1]) for e in owner])
        for e in owner:
            table[edges[e][0], k] = edges[e][2][0]
            table[edges[e][1], per + k] = edges[e][2][1]
    return unit, per, perms, table


def per_device(
    nb, nt, patches, image_ids, cotangent, norm_gain, query_gain, key_gain, in_weight, out_weight
):
    seqs, part, dim = patches.shape
    width = H * HD
    local = width // nt
    units = (in_weight.shape[1] - 3 * width) // nt
    rows_in = in_weight.shape[0]
    unit, per, perms, table = unit_plan(nb, nt, out_weight.shape[0], width, units * nt)
    assert nt == SLOTS and units == dim and unit == rows_in and dim == nt * local and per == nt + 1
    both = ("batch", "tok")
    me_b = lax.axis_index("batch")
    me_t = lax.axis_index("tok")
    at = jnp.stack([me_b * nt + me_t, me_t, me_b])
    table = jnp.asarray(table)
    gain = norm_gain.reshape(1, dim)

    def exchange(value, axis):
        return lax.all_to_all(value, axis, split_axis=0, concat_axis=0, tiled=True)

    groups = bit_groups(nb)

    a_src, u_src = prepare(image_ids, in_weight, nb, nt)
    a_got = exchange(a_src.reshape(nb * nt, rows_in + 2, 3 * local), both)
    own0, own1, *unit_sends = before(
        at, table, image_ids, gain, tie(patches, a_src), cotangent, out_weight.reshape(per, unit, dim)
    )
    far0 = swap(own0, "tok", nt, 2)
    got = [lax.ppermute(v, both, perm) for v, perm in zip(unit_sends, perms)]
    wo_src, ff_src = pack_out(at, table, got, nb)
    ff_parts = gather_batch(ff_src.reshape((per - 1) * unit, dim), nb, groups[::-1])
    wo = exchange(tie(wo_src, a_got), "batch").reshape(local, dim)
    wqkv, ids = join(at, a_got, seqs, part)
    far1 = swap(tie(own1, far0, wo_src), "tok", nt, 2)
    slots0 = [own0, swap(own0, "tok", nt, 1), far0, swap(tie(far0, wo_src), "tok", nt, 1)]
    slots1 = [own1, swap(own1, "tok", nt, 1), far1, swap(far1, "tok", nt, 1)]
    wup = exchange(tie(u_src, wo).reshape(nb * nt, unit, dim), both).reshape(dim, units)

    qg = query_gain.reshape(HD, 1)
    kg = key_gain.reshape(HD, 1)

    def leave_core(s, i, o, gq):
        keep, send = outputs(s, i, 1, o, hid, gq, gup, wo, wff, wqkv, wup)
        return keep, swap(send, "tok", nt, 1)

    def leave_chip(keep, near):
        value = (keep[1].astype(F32) + near[1].astype(F32)).astype(BF)
        return value, swap(value, "tok", nt, 2)

    o, gq, a_q, go, a_np, sums = attention(ids, wqkv, tie(wo, ff_parts[0][0]), qg, kg, [slots0, slots1], nb * nt)
    a_q = sum_qkv(exchange(a_q, both), nt)
    hid, gup, wff, f_up, f_send, f_keep = ffn(at, go, a_np, sums, gain, wup, ff_parts, [slots0, slots1], nb)
    f_up = exchange(tie(f_up, a_q), both)
    terms = [f_keep, swap(f_send, "batch", nb, 1)]
    group = []
    o = tie(o, a_q)
    for s in range(seqs):
        if s == seqs - 1:
            value, away = leave_chip(*group[0])
            group[0].append(away)
            o = tie(o, value)
            for bits in groups[:-1][::-1]:
                own, *sends = fold(at, bits[-1], terms[0], terms[1:])
                terms = [own] + [swap(v, "batch", nb, (k + 1) << bits[-1]) for k, v in enumerate(sends)]
                o = tie(o, own)
        keep, near = leave_core(s, s, o, gq)
        group.append([keep, near])
        o = tie(o, keep)
    for s in range(1, seqs):
        group[s].append(leave_chip(*group[s])[1])

    sends = leave(at, table, terms)
    got = [lax.ppermute(v, both, [(b, a) for a, b in perm]) for v, perm in zip(sends, perms)]
    in_grad, out_grad, norm_grad, query_grad, key_grad = place(at, table, a_q, f_up, got)

    earlier = []
    for s in range(seqs):
        earlier = after(s, 0, image_ids, patches, cotangent, gain, *group[s], earlier)
    block_out, patch_grad = earlier
    return (
        block_out,
        patch_grad,
        norm_grad.reshape(dim),
        query_grad.reshape(HD),
        key_grad.reshape(HD),
        in_grad,
        out_grad.reshape(per * unit, dim),
    )


def solution(mesh):
    rows = P("batch", "tok", None)
    weights = P(("batch", "tok"), None)
    return jax.shard_map(
        functools.partial(per_device, mesh.shape["batch"], mesh.shape["tok"]),
        mesh=mesh,
        in_specs=(rows, P("batch", "tok"), rows, P(), P(), P(), weights, weights),
        out_specs=(rows, rows, P(), P(), P(), weights, weights),
        check_vma=False,
    )
```

time: 343 us -> 343 us (level)
  starting transfers between devices: 79.8 us -> 121 us
  local copies, waits for them, and re-layouts: 23.5 us -> 8.72 us
  waiting for transfers between devices: 78.5 us -> 64.6 us
  between operations: 14.4 us -> 1.24 us
    all_to_all x3 -> x5, waiting for transfers between devices: 33.3 us -> 0.01 us  [exchange(): return lax.all_to_all(value, axis, split_axis=0, concat_axis=0, tiled=True)]
    ppermute x5, starting transfers between devices: 17.3 us -> 37.4 us  [per_device(): lax.ppermute(v, both, [(b, a) for a, b in perm])]
    ppermute x5, starting transfers between devices: 21.9 us -> 42.1 us  [per_device(): got = [lax.ppermute(v, both, perm) for v, perm in zip(unit_sends, perms)]]
    unnamed x114 -> x66, local copies, waits for them, and re-layouts: 18.5 us -> 6.05 us
    ppermute x24 -> x20, waiting for transfers between devices: 38.2 us -> 49.8 us  [swap(): return lax.ppermute(value, axis, [(i, i ^ mask) for i in range(count)])]
    all_to_all x3 -> x5, starting transfers between devices: 10.3 us -> 21.7 us  [exchange(): return lax.all_to_all(value, axis, split_axis=0, concat_axis=0, tiled=True)]
    ppermute x24 -> x20, starting transfers between devices: 30.2 us -> 19.4 us  [swap(): return lax.ppermute(value, axis, [(i, i ^ mask) for i in range(count)])]
    ppermute x5, waiting for transfers between devices: 0.01 us -> 5.04 us  [per_device(): lax.ppermute(v, both, [(b, a) for a, b in perm])]
  transfers between devices with their start and end apart: 40 -> 35, of which waited for: 13 -> 9; matrix products, arithmetic and copies ran while one was open for 3% -> 2% of each run, Pallas kernels for 31% -> 35%
where the time goes in v3:
time: 343 us; the launch traced here: 342 us
  Pallas kernels  140 us (41%)
  starting transfers between devices  121 us (35%)
  waiting for transfers between devices  64.6 us (19%)
  local copies, waits for them, and re-layouts  8.72 us (3%)
  other arithmetic  6.56 us (2%)
    pallas_call x1, Pallas kernels, attention(): pl.pallas_call(functools.partial(attention_kernel, heads, block, sizes),...  58.9 us
    ppermute x20, waiting for transfers between devices, swap(): return lax.ppermute(value, axis, [(i, i ^ mask) for i in range(count)])  49.8 us
    ppermute x5, starting transfers between devices, per_device(): got = [lax.ppermute(v, both, perm) for v, perm in zip(unit_sends, perms)]  42.1 us
    ppermute x5, starting transfers between devices, per_device(): lax.ppermute(v, both, [(b, a) for a, b in perm])  37.4 us
    pallas_call x3, Pallas kernels, outputs(): pl.pallas_call(kernel, out_shape=[jax.ShapeDtypeStruct((SLOTS // 2, seqs,...  30.3 us
    pallas_call x1, Pallas kernels, ffn(): pl.pallas_call(functools.partial(ffn_kernel, block, sizes, [masks for _,...  25.8 us
    all_to_all x5, starting transfers between devices, exchange(): return lax.all_to_all(value, axis, split_axis=0, concat_axis=0, tiled=True)  21.7 us
    ppermute x20, starting transfers between devices, swap(): return lax.ppermute(value, axis, [(i, i ^ mask) for i in range(count)])  19.4 us
  transfers between devices with their start and end apart: 35, of which 9 were waited for; matrix products, arithmetic and copies ran while one was open for 2% of the time, Pallas kernels for 35%

profile of v3, /device:TPU:2, one launch (start us, length us, event | category | flops | bytes accessed | tf_op | source)
XLA Modules:
  0.0 341.6 jit_solution(12547097896723073915)
XLA Ops:
  4.6 3.7 %before.1 = (bf16[2,2,256,768]{3,2,1,0:T(8,128)(2,1)S(1)}, bf16[1,2,256,768]{3,2,1,0:T(8,128)(2,1)S(1)}, bf16[24,768]{1,0:T(8,128)(2,1)S(1)}, bf16[24,768]{1,0:T...) custom-call(s32[3]{0:T(128)S(1)} %pad_add_fusion.at_ref, ...), custom_call_target="tpu_custom_call" | custom-call | flops 1 | bytes 1 | tf_op jit(solution)/shard_map/before/pallas_call | solution.py:146
  10.7 5.2 %all-to-all-start = ((bf16[32,26,576]{2,1,0:T(8,128)(2,1)}), bf16[32,26,576]{2,1,0:T(8,128)(2,1)S(1)}, u32[]{:S(2)}, u32[]{:S(2)}) async-start(bf16[32,26,576]{2,1,0:T(8,128)(2,1)} %bitcast.3), calls=%async_computation | async-start | bytes 2621440 | tf_op jit(solution)/shard_map/all_to_all | solution.py:926
  15.9 5.2 %collective-permute-start = (bf16[24,768]{1,0:T(8,128)(2,1)S(1)}, bf16[24,768]{1,0:T(8,128)(2,1)S(1)}, u32[]{:S(2)}, u32[]{:S(2)}) collective-permute-start(bf16[24,768]{1,0:T(8,128)(2,1)S(1)} %get-tuple-element.74), channel_id=1, source_target_pairs={{7,0},{13,1},{3,2},{26,3},{0,4},{14,5},{20,6},{27,7},{8,8},{15,9},... | collective-permute-start | bytes 110600 | tf_op jit(solution)/shard_map/ppermute | solution.py:936
  24.2 3.7 %collective-permute-start.2 = (bf16[24,768]{1,0:T(8,128)(2,1)S(1)}, bf16[24,768]{1,0:T(8,128)(2,1)S(1)}, u32[]{:S(2)}, u32[]{:S(2)}) collective-permute-start(bf16[24,768]{1,0:T(8,128)(2,1)S(1)} %get-tuple-element.76), channel_id=1, source_target_pairs={{6,0},{13,1},{19,2},{4,3},{7,4},{1,5},{20,6},{26,7},{8,8},{14,9},{... | collective-permute-start | bytes 110600 | tf_op jit(solution)/shard_map/ppermute | solution.py:936
  30.6 8.2 %collective-permute-done.refs_0_ = bf16[24,768]{1,0:T(8,128)(2,1)S(1)} collective-permute-done((bf16[24,768]{1,0:T(8,128)(2,1)S(1)}, bf16[24,768]{1,0:T(8,128)(2,1)S(1)}, u32[]{:S(2)}, u32[]{:S(2)}) %collective-permute-start) | collective-permute-done | bytes 36896 | tf_op jit(solution)/shard_map/ppermute | solution.py:936
  38.9 27.3 %collective-permute-start.4 = (bf16[24,768]{1,0:T(8,128)(2,1)S(1)}, bf16[24,768]{1,0:T(8,128)(2,1)S(1)}, u32[]{:S(2)}, u32[]{:S(2)}) collective-permute-start(bf16[24,768]{1,0:T(8,128)(2,1)S(1)} %get-tuple-element.78), channel_id=1, source_target_pairs={{6,0},{12,1},{19,2},{25,3},{7,4},{13,5},{3,6},{26,7},{0,8},{14,9},... | collective-permute-start | bytes 110600 | tf_op jit(solution)/shard_map/ppermute | solution.py:936
  71.0 18.8 %collective-permute-done.10.refs_6_.refs_10_ = bf16[1,2,256,768]{3,2,1,0:T(8,128)(2,1)} collective-permute-done((bf16[1,2,256,768]{3,2,1,0:T(8,128)(2,1)}, bf16[1,2,256,768]{3,2,1,0:T(8,128)(2,1)}, u32[]{:S(2)}, u32[]{:S(2)}) %collective-permute-start.10) | collective-permute-done | bytes 786464 | tf_op jit(solution)/shard_map/ppermute | solution.py:828
  94.7 6.6 %collective-permute-done.5 = bf16[1,96,768]{2,1,0:T(8,128)(2,1)} collective-permute-done((bf16[1,96,768]{2,1,0:T(8,128)(2,1)}, bf16[1,96,768]{2,1,0:T(8,128)(2,1)}, u32[]{:S(2)}, u32[]{:S(2)}) %collective-permute-start.5) | collective-permute-done | bytes 147488 | tf_op jit(solution)/shard_map/ppermute | solution.py:828
  108.4 4.0 %all-to-all-start.3 = ((bf16[32,24,768]{2,1,0:T(8,128)(2,1)}), bf16[32,24,768]{2,1,0:T(8,128)(2,1)S(1)}, u32[]{:S(2)}, u32[]{:S(2)}) async-start(bf16[32,24,768]{2,1,0:T(8,128)(2,1)} %bitcast.9), calls=%async_computation.3 | async-start | bytes 2359296 | tf_op jit(solution)/shard_map/all_to_all | solution.py:926
  116.6 58.9 %attention.1 = (bf16[3,192,1024]{2,1,0:T(8,128)(2,1)}, bf16[3,576,1024]{2,1,0:T(8,128)(2,1)}, bf16[32,24,576]{2,1,0:T(8,128)(2,1)}, f32[192,768]{1,0:T(8,128)}, f32[1,768]{1,0:T(1,128)}, /*index=5*/f32[1,128]{1,0:T(1,128)}) custom-call(s32[3,1,1024]{2,1,0:T(1,128)} %copy-done.15, f32[64,1]{1,0:T(8,128)} %copy.20.qg_ref, f32[64,1]{1,0:T(8,128)} %copy.21.kg_ref, ...), custom_call_target="tpu_custom_call" | custom-call | flops 60000002048 | bytes 1 | tf_op jit(solution)/shard_map/attention/pallas_call | solution.py:571
  179.3 25.8 %ffn.1 = (bf16[3072,768]{1,0:T(8,128)(2,1)}, bf16[3072,768]{1,0:T(8,128)(2,1)}, bf16[768,768]{1,0:T(8,128)(2,1)}, bf16[32,28,768]{2,1,0:T(8,128)(2,1)}, bf16[4,1...) custom-call(s32[3]{0:T(128)} %copy-done.9, f32[192,768]{1,0:T(8,128)} %get-tuple-element.90.go_ref, ...), custom_call_target="tpu_custom_call" | custom-call | flops 60000002048 | bytes 1 | tf_op jit(solution)/shard_map/ffn/pallas_call | solution.py:699
  205.3 10.0 %outputs.3 = (bf16[2,1,2,256,768]{4,3,2,1,0:T(8,128)(2,1)S(1)}, bf16[2,1,2,256,768]{4,3,2,1,0:T(8,128)(2,1)}) custom-call(bf16[3,192,1024]{2,1,0:T(8,128)(2,1)} %get-tuple-element.108.o_hbm, bf16[3072,768]{1,0:T(8,128)(2,1)} %get-tuple-element.95.hid_hbm, bf16[3,576,1024]{2,1,0:T(8,128)(2,1)} %get-tuple-element.96.gq_hbm, ...), custom_call_target="tpu_custom_call" | custom-call | flops 1 | bytes 1 | tf_op jit(solution)/shard_map/outputs/pallas_call | solution.py:802
  215.9 6.1 %all-to-all-start.4 = ((bf16[32,28,768]{2,1,0:T(8,128)(2,1)}), bf16[32,28,768]{2,1,0:T(8,128)(2,1)S(1)}, u32[]{:S(2)}, u32[]{:S(2)}) async-start(bf16[32,28,768]{2,1,0:T(8,128)(2,1)} %get-tuple-element.119), calls=%async_computation.4 | async-start | bytes 3145728 | tf_op jit(solution)/shard_map/all_to_all | solution.py:926
  222.0 10.2 %outputs.4 = (bf16[2,1,2,256,768]{4,3,2,1,0:T(8,128)(2,1)S(1)}, bf16[2,1,2,256,768]{4,3,2,1,0:T(8,128)(2,1)S(1)}) custom-call(bf16[3,192,1024]{2,1,0:T(8,128)(2,1)} %get-tuple-element.108.o_hbm, bf16[3072,768]{1,0:T(8,128)(2,1)} %get-tuple-element.95.hid_hbm, bf16[3,576,1024]{2,1,0:T(8,128)(2,1)} %get-tuple-element.96.gq_hbm, ...), custom_call_target="tpu_custom_call" | custom-call | flops 1 | bytes 1 | tf_op jit(solution)/shard_map/outputs/pallas_call | solution.py:802
  232.4 11.8 %collective-permute-done.16.refs_0_ = bf16[4,120,768]{2,1,0:T(8,128)(2,1)} collective-permute-done((bf16[4,120,768]{2,1,0:T(8,128)(2,1)}, bf16[4,120,768]{2,1,0:T(8,128)(2,1)}, u32[]{:S(2)}, u32[]{:S(2)}) %collective-permute-start.16) | collective-permute-done | bytes 737312 | tf_op jit(solution)/shard_map/ppermute | solution.py:828
  247.9 10.1 %outputs.5 = (bf16[2,1,2,256,768]{4,3,2,1,0:T(8,128)(2,1)S(1)}, bf16[2,1,2,256,768]{4,3,2,1,0:T(8,128)(2,1)S(1)}) custom-call(bf16[3,192,1024]{2,1,0:T(8,128)(2,1)} %get-tuple-element.108.o_hbm, bf16[3072,768]{1,0:T(8,128)(2,1)} %get-tuple-element.95.hid_hbm, bf16[3,576,1024]{2,1,0:T(8,128)(2,1)} %get-tuple-element.96.gq_hbm, ...), custom_call_target="tpu_custom_call" | custom-call | flops 1 | bytes 1 | tf_op jit(solution)/shard_map/outputs/pallas_call | solution.py:802
  268.1 6.9 %collective-permute-done.22.refs_1_ = bf16[1,120,768]{2,1,0:T(8,128)(2,1)S(1)} collective-permute-done((bf16[1,120,768]{2,1,0:T(8,128)(2,1)S(1)}, bf16[1,120,768]{2,1,0:T(8,128)(2,1)S(1)}, u32[]{:S(2)}, u32[]{:S(2)}) %collective-permute-start.22) | collective-permute-done | bytes 184352 | tf_op jit(solution)/shard_map/ppermute | solution.py:828
  276.8 5.7 %collective-permute-done.24.refs_3_ = bf16[1,120,768]{2,1,0:T(8,128)(2,1)S(1)} collective-permute-done((bf16[1,120,768]{2,1,0:T(8,128)(2,1)S(1)}, bf16[1,120,768]{2,1,0:T(8,128)(2,1)S(1)}, u32[]{:S(2)}, u32[]{:S(2)}) %collective-permute-start.24) | collective-permute-done | bytes 184352 | tf_op jit(solution)/shard_map/ppermute | solution.py:828
  289.1 5.0 %collective-permute-done.25.refs_0_ = f32[24,768]{1,0:T(8,128)S(1)} collective-permute-done((f32[24,768]{1,0:T(8,128)}, f32[24,768]{1,0:T(8,128)S(1)}, u32[]{:S(2)}, u32[]{:S(2)}) %collective-permute-start.25) | collective-permute-done | bytes 73760 | tf_op jit(solution)/shard_map/ppermute | solution.py:980
  296.2 27.2 %collective-permute-start.28 = (f32[24,768]{1,0:T(8,128)}, f32[24,768]{1,0:T(8,128)S(1)}, u32[]{:S(2)}, u32[]{:S(2)}) collective-permute-start(f32[24,768]{1,0:T(8,128)} %get-tuple-element.126), channel_id=1, source_target_pairs={{0,6},{1,1},{2,19},{3,25},{4,7},{5,13},{6,20},{7,26},{8,8},{9,14},... | collective-permute-start | bytes 221192 | tf_op jit(solution)/shard_map/ppermute | solution.py:980
  323.5 4.3 %collective-permute-start.29 = (f32[24,768]{1,0:T(8,128)}, f32[24,768]{1,0:T(8,128)S(1)}, u32[]{:S(2)}, u32[]{:S(2)}) collective-permute-start(f32[24,768]{1,0:T(8,128)} %get-tuple-element.127), channel_id=1, source_target_pairs={{0,6},{1,12},{2,19},{3,25},{4,7},{5,13},{6,3},{7,26},{8,0},{9,14},... | collective-permute-start | bytes 221192 | tf_op jit(solution)/shard_map/ppermute | solution.py:980
  327.8 3.5 %after.3 = (bf16[3,256,768]{2,1,0:T(8,128)(2,1)}, bf16[3,256,768]{2,1,0:T(8,128)(2,1)}) custom-call(s32[3,256]{1,0:T(4,128)S(1)} %copy-done.7, bf16[3,256,768]{2,1,0:T(8,128)(2,1)} %x_ref.5, bf16[3,256,768]{2,1,0:T(8,128)(2,1)} %cot_ref.5, f32[1,768]{1,0:T(1,128)S(1)} %copy-done.8, bf16[2,1,2,256,768]{4,3,2,1,0:T(8,128)(2,1)} %copy-done.3, ...), custom_call_target="tpu_custom_call" | custom-call | flops 1 | bytes 1 | tf_op jit(solution)/shard_map/after/pallas_call | solution.py:371
  331.3 3.5 %after.4 = (bf16[3,256,768]{2,1,0:T(8,128)(2,1)}, bf16[3,256,768]{2,1,0:T(8,128)(2,1)}) custom-call(s32[3,256]{1,0:T(4,128)S(1)} %copy-done.7, bf16[3,256,768]{2,1,0:T(8,128)(2,1)} %x_ref.5, bf16[3,256,768]{2,1,0:T(8,128)(2,1)} %cot_ref.5, f32[1,768]{1,0:T(1,128)S(1)} %copy-done.8, ...), custom_call_target="tpu_custom_call", output_to_operand_aliasing={{0}: (7, {}), {1}: (8, {})} | custom-call | flops 1 | bytes 1 | tf_op jit(solution)/shard_map/after/pallas_call | solution.py:371
  338.1 3.5 %after.5 = (bf16[3,256,768]{2,1,0:T(8,128)(2,1)}, bf16[3,256,768]{2,1,0:T(8,128)(2,1)}) custom-call(s32[3,256]{1,0:T(4,128)S(1)} %copy-done.7, bf16[3,256,768]{2,1,0:T(8,128)(2,1)} %x_ref.5, bf16[3,256,768]{2,1,0:T(8,128)(2,1)} %cot_ref.5, f32[1,768]{1,0:T(1,128)S(1)} %copy-done.8, ...), custom_call_target="tpu_custom_call", output_to_operand_aliasing={{0}: (7, {}), {1}: (8, {})} | custom-call | flops 1 | bytes 1 | tf_op jit(solution)/shard_map/after/pallas_call | solution.py:371
  (137 shorter events, 65.3 us)
Async XLA Ops:
  9.2 61.2 %collective-permute-start.7 = (bf16[2,2,256,768]{3,2,1,0:T(8,128)(2,1)S(1)}, bf16[2,2,256,768]{3,2,1,0:T(8,128)(2,1)}, u32[]{:S(2)}, u32[]{:S(2)}) collective-permute-start(bf16[2,2,256,768]{3,2,1,0:T(8,128)(2,1)S(1)} %get-tuple-element.83.refs_0_.refs_4_), channel_id=1, source_target_pairs={{0,2},{1,3},{2,0},{3,1},{4,6},{5,7},{6,4},{7,5},{8,10},{9,11},{10,... | collective-permute-start | bytes 4718600 | tf_op jit(solution)/shard_map/ppermute | solution.py:828
  10.7 79.1 %all-to-all-start = ((bf16[32,26,576]{2,1,0:T(8,128)(2,1)}), bf16[32,26,576]{2,1,0:T(8,128)(2,1)S(1)}, u32[]{:S(2)}, u32[]{:S(2)}) async-start(bf16[32,26,576]{2,1,0:T(8,128)(2,1)} %bitcast.3), calls=%async_computation | async-start | bytes 2621440 | tf_op jit(solution)/shard_map/all_to_all | solution.py:926
  21.1 45.1 %collective-permute-start.1 = (bf16[24,768]{1,0:T(8,128)(2,1)S(1)}, bf16[24,768]{1,0:T(8,128)(2,1)S(1)}, u32[]{:S(2)}, u32[]{:S(2)}) collective-permute-start(bf16[24,768]{1,0:T(8,128)(2,1)S(1)} %get-tuple-element.75), channel_id=1, source_target_pairs={{0,0},{13,1},{19,2},{26,3},{7,4},{14,5},{20,6},{5,7},{8,8},{2,9},{... | collective-permute-start | bytes 110600 | tf_op jit(solution)/shard_map/ppermute | solution.py:936
  24.2 42.0 %collective-permute-start.2 = (bf16[24,768]{1,0:T(8,128)(2,1)S(1)}, bf16[24,768]{1,0:T(8,128)(2,1)S(1)}, u32[]{:S(2)}, u32[]{:S(2)}) collective-permute-start(bf16[24,768]{1,0:T(8,128)(2,1)S(1)} %get-tuple-element.76), channel_id=1, source_target_pairs={{6,0},{13,1},{19,2},{4,3},{7,4},{1,5},{20,6},{26,7},{8,8},{14,9},{... | collective-permute-start | bytes 110600 | tf_op jit(solution)/shard_map/ppermute | solution.py:936
  27.9 38.4 %collective-permute-start.3 = (bf16[24,768]{1,0:T(8,128)(2,1)S(1)}, bf16[24,768]{1,0:T(8,128)(2,1)S(1)}, u32[]{:S(2)}, u32[]{:S(2)}) collective-permute-start(bf16[24,768]{1,0:T(8,128)(2,1)S(1)} %get-tuple-element.77), channel_id=1, source_target_pairs={{6,0},{1,1},{19,2},{25,3},{7,4},{13,5},{20,6},{26,7},{8,8},{14,9},... | collective-permute-start | bytes 110600 | tf_op jit(solution)/shard_map/ppermute | solution.py:936
  38.9 29.0 %collective-permute-start.4 = (bf16[24,768]{1,0:T(8,128)(2,1)S(1)}, bf16[24,768]{1,0:T(8,128)(2,1)S(1)}, u32[]{:S(2)}, u32[]{:S(2)}) collective-permute-start(bf16[24,768]{1,0:T(8,128)(2,1)S(1)} %get-tuple-element.78), channel_id=1, source_target_pairs={{6,0},{12,1},{19,2},{25,3},{7,4},{13,5},{3,6},{26,7},{0,8},{14,9},... | collective-permute-start | bytes 110600 | tf_op jit(solution)/shard_map/ppermute | solution.py:936
  66.2 48.8 %collective-permute-start.6 = (bf16[2,2,256,768]{3,2,1,0:T(8,128)(2,1)S(1)}, bf16[2,2,256,768]{3,2,1,0:T(8,128)(2,1)}, u32[]{:S(2)}, u32[]{:S(2)}) collective-permute-start(bf16[2,2,256,768]{3,2,1,0:T(8,128)(2,1)S(1)} %get-tuple-element.83.refs_0_.refs_4_), channel_id=1, source_target_pairs={{0,1},{1,0},{2,3},{3,2},{4,5},{5,4},{6,7},{7,6},{8,9},{9,8},{10,11... | collective-permute-start | bytes 4718600 | tf_op jit(solution)/shard_map/ppermute | solution.py:828
  70.5 46.1 %collective-permute-start.8 = (bf16[2,2,256,768]{3,2,1,0:T(8,128)(2,1)}, bf16[2,2,256,768]{3,2,1,0:T(8,128)(2,1)}, u32[]{:S(2)}, u32[]{:S(2)}) collective-permute-start(bf16[2,2,256,768]{3,2,1,0:T(8,128)(2,1)} %collective-permute-done.7.refs_2_.refs_6_), channel_id=1, source_target_pairs={{0,1},{1,0},{2,3},{3,2},{4,5},{5,4},{6,7},{7,6},{8,9},{9,8},{10,11... | collective-permute-start | bytes 4718600 | tf_op jit(solution)/shard_map/ppermute | solution.py:828
  70.9 41.6 %collective-permute-start.9 = (bf16[1,2,256,768]{3,2,1,0:T(8,128)(2,1)}, bf16[1,2,256,768]{3,2,1,0:T(8,128)(2,1)}, u32[]{:S(2)}, u32[]{:S(2)}) collective-permute-start(bf16[1,2,256,768]{3,2,1,0:T(8,128)(2,1)} %copy-done.14), channel_id=1, source_target_pairs={{0,1},{1,0},{2,3},{3,2},{4,5},{5,4},{6,7},{7,6},{8,9},{9,8},{10,11... | collective-permute-start | bytes 2359304 | tf_op jit(solution)/shard_map/ppermute | solution.py:828
  102.3 76.2 %collective-permute-start.14 = (bf16[2,96,768]{2,1,0:T(8,128)(2,1)S(1)}, bf16[2,96,768]{2,1,0:T(8,128)(2,1)}, u32[]{:S(2)}, u32[]{:S(2)}) collective-permute-start(bf16[2,96,768]{2,1,0:T(8,128)(2,1)S(1)} %pad_maximum_fusion.refs_0_), channel_id=1, source_target_pairs={{0,24},{4,28},{8,16},{12,20},{16,8},{20,12},{24,0},{28,4},{1,25},{... | collective-permute-start | bytes 884744 | tf_op jit(solution)/shard_map/ppermute | solution.py:828
  108.4 67.0 %all-to-all-start.3 = ((bf16[32,24,768]{2,1,0:T(8,128)(2,1)}), bf16[32,24,768]{2,1,0:T(8,128)(2,1)S(1)}, u32[]{:S(2)}, u32[]{:S(2)}) async-start(bf16[32,24,768]{2,1,0:T(8,128)(2,1)} %bitcast.9), calls=%async_computation.3 | async-start | bytes 2359296 | tf_op jit(solution)/shard_map/all_to_all | solution.py:926
  112.5 66.1 %collective-permute-start.13 = (bf16[2,96,768]{2,1,0:T(8,128)(2,1)S(1)}, bf16[2,96,768]{2,1,0:T(8,128)(2,1)}, u32[]{:S(2)}, u32[]{:S(2)}) collective-permute-start(bf16[2,96,768]{2,1,0:T(8,128)(2,1)S(1)} %pad_maximum_fusion.refs_0_), channel_id=1, source_target_pairs={{0,16},{4,20},{8,24},{12,28},{16,0},{20,4},{24,8},{28,12},{1,17},{... | collective-permute-start | bytes 884744 | tf_op jit(solution)/shard_map/ppermute | solution.py:828
  115.0 63.6 %collective-permute-start.12 = (bf16[2,96,768]{2,1,0:T(8,128)(2,1)S(1)}, bf16[2,96,768]{2,1,0:T(8,128)(2,1)S(1)}, u32[]{:S(2)}, u32[]{:S(2)}) collective-permute-start(bf16[2,96,768]{2,1,0:T(8,128)(2,1)S(1)} %pad_maximum_fusion.refs_0_), channel_id=1, source_target_pairs={{0,8},{4,12},{8,0},{12,4},{16,24},{20,28},{24,16},{28,20},{1,9},{5... | collective-permute-start | bytes 884744 | tf_op jit(solution)/shard_map/ppermute | solution.py:828
  175.5 29.7 %all-to-all-start.2 = ((bf16[32,24,576]{2,1,0:T(8,128)(2,1)}), bf16[32,24,576]{2,1,0:T(8,128)(2,1)S(1)}, u32[]{:S(2)}, u32[]{:S(2)}) async-start(bf16[32,24,576]{2,1,0:T(8,128)(2,1)} %get-tuple-element.88), calls=%async_computation.2 | async-start | bytes 1966080 | tf_op jit(solution)/shard_map/all_to_all | solution.py:926
  215.4 30.1 %collective-permute-start.15 = (bf16[2,1,2,256,768]{4,3,2,1,0:T(8,128)(2,1)}, bf16[2,1,2,256,768]{4,3,2,1,0:T(8,128)(2,1)}, u32[]{:S(2)}, u32[]{:S(2)}) collective-permute-start(bf16[2,1,2,256,768]{4,3,2,1,0:T(8,128)(2,1)} %get-tuple-element.103), channel_id=1, source_target_pairs={{0,1},{1,0},{2,3},{3,2},{4,5},{5,4},{6,7},{7,6},{8,9},{9,8},{10,11... | collective-permute-start | bytes 4718600 | tf_op jit(solution)/shard_map/ppermute | solution.py:828
  215.6 28.6 %collective-permute-start.16 = (bf16[4,120,768]{2,1,0:T(8,128)(2,1)}, bf16[4,120,768]{2,1,0:T(8,128)(2,1)}, u32[]{:S(2)}, u32[]{:S(2)}) collective-permute-start(bf16[4,120,768]{2,1,0:T(8,128)(2,1)} %get-tuple-element.106), channel_id=1, source_target_pairs={{0,4},{4,0},{8,12},{12,8},{16,20},{20,16},{24,28},{28,24},{1,5},{5... | collective-permute-start | bytes 2211848 | tf_op jit(solution)/shard_map/ppermute | solution.py:828
  215.9 118.8 %all-to-all-start.4 = ((bf16[32,28,768]{2,1,0:T(8,128)(2,1)}), bf16[32,28,768]{2,1,0:T(8,128)(2,1)S(1)}, u32[]{:S(2)}, u32[]{:S(2)}) async-start(bf16[32,28,768]{2,1,0:T(8,128)(2,1)} %get-tuple-element.119), calls=%async_computation.4 | async-start | bytes 3145728 | tf_op jit(solution)/shard_map/all_to_all | solution.py:926
  232.2 28.0 %collective-permute-start.19 = (bf16[2,1,2,256,768]{4,3,2,1,0:T(8,128)(2,1)S(1)}, bf16[2,1,2,256,768]{4,3,2,1,0:T(8,128)(2,1)S(1)}, u32[]{:S(2)}, u32[]{:S(2)}) collective-permute-start(bf16[2,1,2,256,768]{4,3,2,1,0:T(8,128)(2,1)S(1)} %get-tuple-element.111), channel_id=1, source_target_pairs={{0,1},{1,0},{2,3},{3,2},{4,5},{5,4},{6,7},{7,6},{8,9},{9,8},{10,11... | collective-permute-start | bytes 4718600 | tf_op jit(solution)/shard_map/ppermute | solution.py:828
  258.0 38.2 %collective-permute-start.21 = (bf16[1,2,256,768]{3,2,1,0:T(8,128)(2,1)}, bf16[1,2,256,768]{3,2,1,0:T(8,128)(2,1)}, u32[]{:S(2)}, u32[]{:S(2)}) collective-permute-start(bf16[1,2,256,768]{3,2,1,0:T(8,128)(2,1)} %fusion), channel_id=1, source_target_pairs={{0,2},{1,3},{2,0},{3,1},{4,6},{5,7},{6,4},{7,5},{8,10},{9,11},{10,... | collective-permute-start | bytes 2359304 | tf_op jit(solution)/shard_map/ppermute | solution.py:828
  261.5 62.0 %collective-permute-start.20 = (bf16[1,2,256,768]{3,2,1,0:T(8,128)(2,1)}, bf16[1,2,256,768]{3,2,1,0:T(8,128)(2,1)}, u32[]{:S(2)}, u32[]{:S(2)}) collective-permute-start(bf16[1,2,256,768]{3,2,1,0:T(8,128)(2,1)} %fusion.2), channel_id=1, source_target_pairs={{0,2},{1,3},{2,0},{3,1},{4,6},{5,7},{6,4},{7,5},{8,10},{9,11},{10,... | collective-permute-start | bytes 2359304 | tf_op jit(solution)/shard_map/ppermute | solution.py:828
  262.9 74.3 %collective-permute-start.18 = (bf16[1,2,256,768]{3,2,1,0:T(8,128)(2,1)}, bf16[1,2,256,768]{3,2,1,0:T(8,128)(2,1)S(1)}, u32[]{:S(2)}, u32[]{:S(2)}) collective-permute-start(bf16[1,2,256,768]{3,2,1,0:T(8,128)(2,1)} %fusion.1), channel_id=1, source_target_pairs={{0,2},{1,3},{2,0},{3,1},{4,6},{5,7},{6,4},{7,5},{8,10},{9,11},{10,... | collective-permute-start | bytes 2359304 | tf_op jit(solution)/shard_map/ppermute | solution.py:828
  287.2 47.5 %collective-permute-start.26 = (f32[24,768]{1,0:T(8,128)}, f32[24,768]{1,0:T(8,128)S(1)}, u32[]{:S(2)}, u32[]{:S(2)}) collective-permute-start(f32[24,768]{1,0:T(8,128)} %get-tuple-element.124), channel_id=1, source_target_pairs={{0,0},{1,13},{2,19},{3,26},{4,7},{5,14},{6,20},{7,5},{8,8},{9,2},{... | collective-permute-start | bytes 221192 | tf_op jit(solution)/shard_map/ppermute | solution.py:980
  294.2 40.6 %collective-permute-start.27 = (f32[24,768]{1,0:T(8,128)}, f32[24,768]{1,0:T(8,128)S(1)}, u32[]{:S(2)}, u32[]{:S(2)}) collective-permute-start(f32[24,768]{1,0:T(8,128)} %get-tuple-element.125), channel_id=1, source_target_pairs={{0,6},{1,13},{2,19},{3,4},{4,7},{5,1},{6,20},{7,26},{8,8},{9,14},{... | collective-permute-start | bytes 221192 | tf_op jit(solution)/shard_map/ppermute | solution.py:980
  296.2 38.5 %collective-permute-start.28 = (f32[24,768]{1,0:T(8,128)}, f32[24,768]{1,0:T(8,128)S(1)}, u32[]{:S(2)}, u32[]{:S(2)}) collective-permute-start(f32[24,768]{1,0:T(8,128)} %get-tuple-element.126), channel_id=1, source_target_pairs={{0,6},{1,1},{2,19},{3,25},{4,7},{5,13},{6,20},{7,26},{8,8},{9,14},... | collective-permute-start | bytes 221192 | tf_op jit(solution)/shard_map/ppermute | solution.py:980
  (44 other events, 745.4 us)

commit v4 on v3

--- a/solution.py
+++ b/solution.py
@@ -110,73 +110,83 @@
     )(*hbm(ids, w_in))
 
 
-def before_kernel(at_ref, table_hbm, ids_hbm, gain_hbm, x_hbm, cot_hbm, wout_hbm, *refs):
-    outs, (table_ref, ids_ref, gain_ref, x_ref, cot_ref, wout_ref, pay_ref, in_sem, out_sem) = refs[:-9], refs[-9:]
-    seqs = x_ref.shape[0]
-    pays, unit_refs = outs[:2], outs[2:]
-    ins = [
-        pltpu.make_async_copy(a, b, in_sem.at[i])
-        for i, (a, b) in enumerate(
-            ((x_hbm, x_ref), (cot_hbm, cot_ref), (ids_hbm, ids_ref), (gain_hbm, gain_ref), (table_hbm, table_ref), (wout_hbm, wout_ref))
-        )
-    ]
-    for copy in ins:
-        copy.start()
-    for copy in ins:
-        copy.wait()
-    for k, ref in enumerate(unit_refs):
-        ref[...] = wout_ref[table_ref[at_ref[0], k]]
-    copies = []
-    for s in range(seqs):
-        unit, _ = normalize(x_ref[s].astype(F32))
-        live = column(jnp.where(ids_ref[s : s + 1, :] >= 0, 1.0, 0.0))
-        pay_ref[s, 0] = (unit * gain_ref[...]).astype(BF)
-        pay_ref[s, 1] = (live * cot_ref[s].astype(F32)).astype(BF)
-        copies.append(pltpu.make_async_copy(pay_ref.at[s], pays[0].at[s] if s < seqs - 1 else pays[1].at[0], out_sem.at[s]))
-        copies[-1].start()
-    for copy in copies:
-        copy.wait()
-
-
-def before(at, table, ids, gain, x, cot, w_out):
+def before(at, table, w_out, ids, gain, x, cot, first):
     seqs, part, dim = x.shape
+
     per, unit, _ = w_out.shape
-    outs = [jax.ShapeDtypeStruct((seqs - 1, 2, part, dim), BF), jax.ShapeDtypeStruct((1, 2, part, dim), BF)]
-    outs += [jax.ShapeDtypeStruct((unit, dim), BF)] * per
+
+    def kernel(at_ref, table_hbm, wout_hbm, ids_hbm, gain_hbm, x_hbm, cot_hbm, out0_hbm, out1_hbm, *refs):
+        unit_refs, (table_ref, wout_ref, ids_ref, gain_ref, x_ref, cot_ref, pay_ref, in_sem, x_sem, out_sem) = refs[:per], refs[per:]
+        ins = [
+            pltpu.make_async_copy(a, b, in_sem.at[i])
+            for i, (a, b) in enumerate(((table_hbm, table_ref), (wout_hbm, wout_ref), (ids_hbm, ids_ref), (gain_hbm, gain_ref)))
+        ]
+        loads = [
+            [pltpu.make_async_copy(a.at[s], b.at[s], x_sem.at[s, k]) for k, (a, b) in enumerate(((x_hbm, x_ref), (cot_hbm, cot_ref)))]
+            for s in range(seqs)
+        ]
+        for copy in ins + sum(loads, []):
+            copy.start()
+        for copy in ins:
+            copy.wait()
+        for k, ref in enumerate(unit_refs):
+            ref[...] = wout_ref[table_ref[at_ref[0], k]]
+        copies = []
+        for s in range(seqs):
+            for copy in loads[s]:
+                copy.wait()
+            unit, _ = normalize(x_ref[s].astype(F32))
+            live = column(jnp.where(ids_ref[s : s + 1, :] >= 0, 1.0, 0.0))
+            pay_ref[s, 0] = (unit * gain_ref[...]).astype(BF)
+            pay_ref[s, 1] = (live * cot_ref[s].astype(F32)).astype(BF)
+            to = out0_hbm.at[s] if s < first else out1_hbm.at[s - first]
+            copies.append(pltpu.make_async_copy(pay_ref.at[s], to, out_sem.at[s]))
+            copies[-1].start()
+        for copy in copies:
+            copy.wait()
+
     return pl.pallas_call(
-        before_kernel,
-        out_shape=outs,
+        kernel,
+        out_shape=[jax.ShapeDtypeStruct((n, 2, part, dim), BF) for n in (first, seqs - first)]
+        + [jax.ShapeDtypeStruct((unit, dim), BF)] * per,
         in_specs=[SMEM] + [HBM] * 6,
         out_specs=[HBM] * 2 + [VMEM] * per,
         scratch_shapes=[
             pltpu.SMEM(table.shape, jnp.int32),
+            pltpu.VMEM(w_out.shape, BF),
             pltpu.VMEM(ids.shape, jnp.int32),
             pltpu.VMEM(gain.shape, F32),
             pltpu.VMEM(x.shape, BF),
             pltpu.VMEM(x.shape, BF),
-            pltpu.VMEM(w_out.shape, BF),
             pltpu.VMEM((seqs, 2, part, dim), BF),
-            pltpu.SemaphoreType.DMA((6,)),
+            pltpu.SemaphoreType.DMA((4,)),
+            pltpu.SemaphoreType.DMA((seqs, 2)),
             pltpu.SemaphoreType.DMA((seqs,)),
         ],
         cost_estimate=SMALL,
         compiler_params=pltpu.CompilerParams(vmem_limit_bytes=32 * MIB),
         name="before",
-    )(at, *hbm(table, ids, gain, x, cot, w_out))
-
-
-def join(at, got, seqs, part):
+    )(at, *hbm(table, w_out, ids, gain, x, cot))
+
+
+def join(at, got, wo_parts, seqs, part):
     count, high, wide = got.shape
     unit = high - 2
     dim = count * unit
-
-    def kernel(at_ref, got_ref, w_ref, ids_ref, all_ref):
+    nb = count // SLOTS
+
+    def kernel(at_ref, got_ref, *refs):
+        ins, (w_ref, wo_ref, ids_ref, all_ref) = refs[:-4], refs[-4:]
+
         def move(i, carry):
             all_ref[i] = got_ref[i, :unit]
             return carry
 
         lax.fori_loop(0, count, move, 0)
         w_ref[...] = all_ref[...].reshape(dim, wide).T
+        for ref, (_, masks) in zip(ins, wo_parts):
+            for i, mask in enumerate(masks):
+                wo_ref[at_ref[2] ^ mask] = ref[i]
         for slot in range(SLOTS):
             i = at_ref[2] * SLOTS + (at_ref[1] ^ slot)
             row = jnp.concatenate([got_ref[i, unit : unit + 1], got_ref[i, unit + 1 :]], axis=1)
@@ -186,41 +196,38 @@
 
     return pl.pallas_call(
         kernel,
-        out_shape=[jax.ShapeDtypeStruct((wide, dim), BF), jax.ShapeDtypeStruct((seqs, 1, SLOTS * part), jnp.int32)],
-        in_specs=[SMEM, VMEM],
-        out_specs=[VMEM] * 2,
+        out_shape=[
+            jax.ShapeDtypeStruct((wide, dim), BF),
+            jax.ShapeDtypeStruct((nb,) + wo_parts[0][0].shape[1:], BF),
+            jax.ShapeDtypeStruct((seqs, 1, SLOTS * part), jnp.int32),
+        ],
+        in_specs=[SMEM] + [VMEM] * (1 + len(wo_parts)),
+        out_specs=[VMEM] * 3,
         scratch_shapes=[pltpu.VMEM((count, unit, wide), BF)],
         cost_estimate=SMALL,
         compiler_params=pltpu.CompilerParams(vmem_limit_bytes=32 * MIB),
         name="join",
-    )(at, got)
-
-
-def pack_out(at, table, got, nb):
+    )(at, got, *[a for a, _ in wo_parts])
+
+
+def pack_out(at, table, got):
     unit, dim = got[0].shape
     per = len(got)
 
     def kernel(at_ref, table_ref, *refs):
-        got_refs, (wo_hbm, ff_hbm, all_ref, wo_sem, ff_sem) = refs[:per], refs[per:]
+        got_refs, (wo_ref, ff_ref, all_ref) = refs[:per], refs[per:]
         for k, ref in enumerate(got_refs):
             all_ref[table_ref[at_ref[0], per + k]] = ref[...]
-        copies = [pltpu.make_async_copy(all_ref.at[0], wo_hbm.at[b], wo_sem.at[b]) for b in range(nb)]
-        copies.append(pltpu.make_async_copy(all_ref.at[pl.ds(1, per - 1)], ff_hbm, ff_sem))
-        for copy in copies:
-            copy.start()
-        for copy in copies:
-            copy.wait()
+        wo_ref[...] = all_ref[0]
+        for k in range(per - 1):
+            ff_ref[k] = all_ref[k + 1]
 
     return pl.pallas_call(
         kernel,
-        out_shape=[jax.ShapeDtypeStruct((nb, unit, dim), BF), jax.ShapeDtypeStruct((per - 1, unit, dim), BF)],
+        out_shape=[jax.ShapeDtypeStruct((unit, dim), BF), jax.ShapeDtypeStruct((per - 1, unit, dim), BF)],
         in_specs=[SMEM] * 2 + [VMEM] * per,
-        out_specs=[HBM] * 2,
-        scratch_shapes=[
-            pltpu.VMEM((per, unit, dim), BF),
-            pltpu.SemaphoreType.DMA((nb,)),
-            pltpu.SemaphoreType.DMA,
-        ],
+        out_specs=[VMEM] * 2,
+        scratch_shapes=[pltpu.VMEM((per, unit, dim), BF)],
         cost_estimate=SMALL,
         name="pack_out",
     )(at, table, *got)
@@ -233,7 +240,7 @@
     return total
 
 
-def sum_qkv(up, nt):
+def sum_up(up, nt):
     count, unit, dim = up.shape
 
     def kernel(up_ref, out_ref):
@@ -247,7 +254,7 @@
         out_specs=VMEM,
         cost_estimate=SMALL,
         compiler_params=pltpu.CompilerParams(vmem_limit_bytes=32 * MIB),
-        name="sum_qkv",
+        name="sum_up",
     )(up)
 
 
@@ -276,43 +283,50 @@
     )(at, keep, *got)
 
 
-def split_rows(odd, grad, send_ref, keep_ref, start, rows):
-    for z in range(send_ref.shape[0]):
+def split_rows(odd, grad, send_ref, keep_ref):
+    parts, rows, _ = send_ref.shape
+    for z in range(parts):
         low = grad[2 * z * rows : (2 * z + 1) * rows]
         high = grad[(2 * z + 1) * rows : (2 * z + 2) * rows]
-        send_ref[z, start : start + rows] = jnp.where(odd, low, high).astype(BF)
-        keep_ref[z, start : start + rows] = jnp.where(odd, high, low)
-
-
-def leave(at, table, terms):
-    per = table.shape[1] // 2
-    _, high, dim = terms[0].shape
-    unit = high // per
+        send_ref[z] = jnp.where(odd, low, high).astype(BF)
+        keep_ref[z] = jnp.where(odd, high, low)
+
+
+def leave(at, table, heads, ff):
+    _, unit, dim = heads[0].shape
+    per = 1 + ff[0].shape[1] // unit
 
     def kernel(at_ref, table_ref, *refs):
-        term_refs, out_refs, all_ref = refs[: len(terms)], refs[len(terms) : -1], refs[-1]
-        total = term_refs[0][0]
-        for ref in term_refs[1:]:
-            total = total + ref[0].astype(F32)
-        for k in range(per):
-            all_ref[k] = total[k * unit : (k + 1) * unit]
+        terms, refs = refs[: 2 * len(heads)], refs[2 * len(heads) :]
+        out_refs, (all_ref,) = refs[:-1], refs[-1:]
+        for j, group in enumerate((terms[: len(heads)], terms[len(heads) :])):
+            total = group[0][0]
+            for ref in group[1:]:
+                total = total + ref[0].astype(F32)
+            if j == 0:
+                all_ref[0] = total
+            else:
+                for k in range(per - 1):
+                    all_ref[k + 1] = total[k * unit : (k + 1) * unit]
         for k, ref in enumerate(out_refs):
             ref[...] = all_ref[table_ref[at_ref[0], per + k]]
 
     return pl.pallas_call(
         kernel,
         out_shape=[jax.ShapeDtypeStruct((unit, dim), F32)] * per,
-        in_specs=[SMEM] * 2 + [VMEM] * len(terms),
+        in_specs=[SMEM] * 2 + [VMEM] * (2 * len(heads)),
         out_specs=[VMEM] * per,
         scratch_shapes=[pltpu.VMEM((per, unit, dim), F32)],
         cost_estimate=SMALL,
         name="leave",
-    )(at, table, *terms)
+    )(at, table, *heads, *ff)
 
 
 def place(at, table, qkv, up, got):
-    nt, unit, width = qkv.shape
-    count, high, dim = up.shape
+    count, high, width = qkv.shape
+    unit, dim = got[0].shape
+    nt = up.shape[0]
+    nb = count // nt
     per = len(got)
     local = width // 3
     wide = nt * (width + dim)
@@ -320,18 +334,18 @@
     def kernel(at_ref, table_ref, qkv_ref, up_ref, *refs):
         got_refs, (in_ref, out_ref, norm_ref, q_ref, k_ref) = refs[:per], refs[per:]
         for t in range(nt):
+            total = add_blocks(qkv_ref, nb, nt, t, slice(0, unit))
             for k in range(3):
-                to = k * nt * local + t * local
-                in_ref[:, to : to + local] = qkv_ref[t, :, k * local : (k + 1) * local]
-            to = nt * width + t * dim
-            in_ref[:, to : to + dim] = add_blocks(up_ref, count // nt, nt, t, slice(0, unit))
+                in_ref[:, k * nt * local + t * local : k * nt * local + (t + 1) * local] = total[:, k * local : (k + 1) * local]
+            in_ref[:, nt * width + t * dim : nt * width + (t + 1) * dim] = up_ref[t]
         for k, ref in enumerate(got_refs):
             out_ref[table_ref[at_ref[0], k]] = ref[...]
-        small = add_blocks(up_ref, count, 1, 0, slice(unit, high))
+        small = add_blocks(qkv_ref, count, 1, 0, slice(unit, high))
         small = small[0:2] + small[2:4]
-        norm_ref[...] = small[0:1]
-        q_ref[...] = small[1:2, :HD]
-        k_ref[...] = small[1:2, HD : 2 * HD]
+        norm_ref[:, :width] = small[0:1]
+        norm_ref[:, width:] = small[1:2, : dim - width]
+        q_ref[...] = small[1:2, dim - width : dim - width + HD]
+        k_ref[...] = small[1:2, dim - width + HD : dim - width + 2 * HD]
 
     return pl.pallas_call(
         kernel,
@@ -382,13 +396,18 @@
 
 
 def attention_kernel(
-    heads, block, groups,
-    ids_ref, qg_ref, kg_ref, wqkv_hbm, wo_hbm, *refs,
+    heads, block, last,
+    at_ref, ids_ref, qg_ref, kg_ref, wqkv_hbm, wo_hbm, *refs,
 ):
-    pays, refs = refs[: SLOTS * len(groups)], refs[SLOTS * len(groups) :]
-    (o_hbm, grad_hbm, sendq_ref, go_ref, np_ref, sums_ref), refs = refs[:6], refs[6:]
+    pays, refs = refs[:SLOTS], refs[SLOTS:]
+    if last:
+        (acc_sums_ref, fnp_ref, gain_ref, accq_hbm, acco_hbm, hid_hbm, gup_hbm, wff_hbm, wup_hbm), refs = refs[:9], refs[9:]
+        (keep_hbm, leave_hbm, sendq_ref, sendo_ref, keepo_ref, sums_ref), refs = refs[:6], refs[6:]
+        (hid_ref, gup_ref, wff_ref, wup_ref, res_ref, res_sem, act_sem), refs = refs[:7], refs[7:]
+    else:
+        (o_hbm, grad_hbm, sums_ref, newq_hbm, newo_hbm), refs = refs[:5], refs[5:]
     (
-        wqkv_ref, wo_ref, norm_ref, gb_ref, o_ref, grad_ref, gq_ref, acc_ref, raw_ref,
+        wqkv_ref, wo_ref, norm_ref, gb_ref, o_ref, grad_ref, gq_ref, go_ref, raw_ref,
         qt_ref, qn_ref, kt_ref, ka_ref, vt_ref, va_ref, do_ref, dq_ref, dk_ref, dv_ref, pad_ref, vm_ref,
         w_sem, sem, out_sem,
     ) = refs
@@ -399,22 +418,41 @@
     loads = [pltpu.make_async_copy(wqkv_hbm, wqkv_ref, w_sem.at[0]), pltpu.make_async_copy(wo_hbm, wo_ref, w_sem.at[1])]
     loads[0].start()
 
-    def pay_copy(s, j, t, source):
+    def pay_copy(s, j, t):
         to = (norm_ref, gb_ref)[j].at[s, pl.ds(t * part, part), :]
-        return pltpu.make_async_copy(source, to, sem.at[s, j * SLOTS + t])
-
-    s = 0
-    for g, size in enumerate(groups):
-        for i in range(size):
-            for j in range(2):
-                for t in range(SLOTS):
-                    pay_copy(s, j, t, pays[g * SLOTS + t].at[i, j]).start()
-                if s + j == 0:
-                    loads[1].start()
-            s += 1
-    gq_ref[...] = jnp.zeros_like(gq_ref)
-    go_ref[...] = jnp.zeros_like(go_ref)
-    acc_ref[...] = jnp.zeros_like(acc_ref)
+        return pltpu.make_async_copy(pays[t].at[s, j], to, sem.at[s, j * SLOTS + t])
+
+    for s in range(seqs):
+        for j in range(2):
+            for t in range(SLOTS):
+                pay_copy(s, j, t).start()
+            if s + j == 0:
+                loads[1].start()
+    if last:
+        loads.append(pltpu.make_async_copy(accq_hbm, gq_ref, w_sem.at[2]))
+        loads.append(pltpu.make_async_copy(acco_hbm, go_ref, w_sem.at[3]))
+        loads.append(pltpu.make_async_copy(wff_hbm, wff_ref, act_sem.at[2 * seqs]))
+        loads.append(pltpu.make_async_copy(wup_hbm, wup_ref, act_sem.at[2 * seqs + 1]))
+        for copy in loads[2:]:
+            copy.start()
+        skip = hid_hbm.shape[0] // length - seqs
+
+        def act_copies(s):
+            rows = pl.ds(pl.multiple_of((skip + s) * length, length), length)
+            return [
+                pltpu.make_async_copy(hid_hbm.at[rows, :], hid_ref.at[s], act_sem.at[2 * s]),
+                pltpu.make_async_copy(gup_hbm.at[rows, :], gup_ref.at[s], act_sem.at[2 * s + 1]),
+            ]
+
+        for s in range(seqs):
+            for copy in act_copies(s):
+                copy.start()
+        outs = Outputs(keep_hbm, leave_hbm, res_ref, res_sem, wo_ref, wff_ref, wqkv_ref, wup_ref)
+        sums_ref[...] = acc_sums_ref[...]
+    else:
+        gq_ref[...] = jnp.zeros_like(gq_ref)
+        go_ref[...] = jnp.zeros_like(go_ref)
+        sums_ref[...] = jnp.zeros_like(sums_ref)
     gain_q = qg_ref[...]
     gain_k = kg_ref[...]
     marks = lax.broadcasted_iota(jnp.int32, (HD, length), 0)
@@ -454,10 +492,10 @@
         for i in range(blocks):
             pad_ref[i] = cut(pad, i)
         for t in range(SLOTS):
-            pay_copy(s, 0, t, pays[0].at[0, 0]).wait()
+            pay_copy(s, 0, t).wait()
         raw_ref[...] = mm(wqkv_ref[...], norm_ref[s], NT)
         for t in range(SLOTS):
-            pay_copy(s, 1, t, pays[0].at[0, 0]).wait()
+            pay_copy(s, 1, t).wait()
         do_all = mm(wo_ref[...], gb_ref[s], NT).astype(BF)
         for h in range(heads):
             for i in range(blocks):
@@ -518,7 +556,7 @@
             for k, (g, gain_col) in enumerate(((gq, gain_q), (gk, gain_k))):
                 unit, inverse = unit_of(k * width + h * HD)
                 g = (g * scale).astype(BF).astype(F32)
-                acc_ref[k] += lanes(g * unit)
+                sums_ref[k] += lanes(g * unit)
                 g = g * gain_col
                 back = inverse * (
                     g - jnp.mean(g, axis=0, keepdims=True) - unit * jnp.mean(g * unit, axis=0, keepdims=True)
@@ -530,50 +568,86 @@
             return carry
 
         lax.fori_loop(0, heads, finish, 0)
-        for copy in stores(s):
-            copy.start()
+        if last:
+
+            @pl.when(s == 0)
+            def _():
+                for copy in loads[2:]:
+                    copy.wait()
+
+            for copy in act_copies(s):
+                copy.wait()
+            outs.compute(s, o_ref.at[s], hid_ref.at[s], grad_ref.at[s], gup_ref.at[s])
+        else:
+            for copy in stores(s):
+                copy.start()
         gq_ref[...] += mm(grad_ref[s], norm_ref[s])
         go_ref[...] += mm(o_ref[s], gb_ref[s])
         return carry
 
     lax.fori_loop(0, seqs, sequence, 0)
+    if not last:
+        ends = [pltpu.make_async_copy(gq_ref, newq_hbm, w_sem.at[2]), pltpu.make_async_copy(go_ref, newo_hbm, w_sem.at[3])]
+        for copy in ends:
+            copy.start()
+        for copy in ends:
+            copy.wait()
+        for s in range(seqs):
+            for copy in stores(s):
+                copy.wait()
+        return
+    outs.wait()
     g_q = gq_ref[...]
-    np_ref[...] = jnp.sum(wqkv_ref[...].astype(F32) * g_q, axis=0, keepdims=True)
-    sums_ref[...] = jnp.concatenate([jnp.sum(acc_ref[k].T, axis=0, keepdims=True) for k in range(2)], axis=1)
+    first_row = (jnp.sum(wqkv_ref[...].astype(F32) * g_q, axis=0, keepdims=True) + fnp_ref[...]) / gain_ref[...]
+    second_row = jnp.concatenate([jnp.sum(sums_ref[k].T, axis=0, keepdims=True) for k in range(2)], axis=1)
+    wide = 3 * width
+    line = jnp.concatenate([first_row[:, wide:], second_row, jnp.zeros((1, 2 * wide - dim - 2 * HD), F32)], axis=1)
+    small = jnp.concatenate([first_row[:, :wide], line], axis=0)
+    high = small.astype(BF)
+    small = jnp.concatenate([high.astype(F32), small - high.astype(F32)], axis=0).astype(BF)
     g_q = g_q.T.astype(BF)
     count, rows, _ = sendq_ref.shape
+    rows = rows - 4
     for i in range(count):
-        sendq_ref[i] = g_q[i * rows : (i + 1) * rows]
-    for s in range(seqs):
-        for copy in stores(s):
-            copy.wait()
-
-
-def attention(ids, wqkv, wo, qg, kg, groups, count):
+        sendq_ref[i, :rows] = g_q[i * rows : (i + 1) * rows]
+        sendq_ref[i, rows:] = small
+    split_rows((at_ref[2] & 1) > 0, go_ref[...], sendo_ref, keepo_ref)
+
+
+def attention(at, ids, wqkv, wo, qg, kg, pays, count, more=()):
     wide, dim = wqkv.shape
     width = wo.shape[0]
     heads = width // HD
-    sizes = [g[0].shape[0] for g in groups]
-    seqs, part = sum(sizes), groups[0][0].shape[2]
+    seqs, _, part, _ = pays[0].shape
     length = part * SLOTS
     block = 512
     blocks = length // block
-    ins = [ids, qg, kg, *hbm(wqkv, wo, *[p for g in groups for p in g])]
-    outs = [
-        jax.ShapeDtypeStruct((seqs, width, length), BF),
-        jax.ShapeDtypeStruct((seqs, wide, length), BF),
-        jax.ShapeDtypeStruct((count, dim // count, wide), BF),
-        jax.ShapeDtypeStruct((width, dim), F32),
-        jax.ShapeDtypeStruct((1, dim), F32),
-        jax.ShapeDtypeStruct((1, 2 * HD), F32),
-    ]
+    last = bool(more)
+    ins = [at, ids, qg, kg, *hbm(wqkv, wo, *pays), *more[:3], *hbm(*more[3:])]
+    specs = [SMEM] + [VMEM] * 3 + [HBM] * (2 + SLOTS) + ([VMEM] * 3 + [HBM] * 6 if last else [])
+    scratch = []
+    if last:
+        outs = [jax.ShapeDtypeStruct((SLOTS // 2, seqs, 2, part, dim), BF)] * 2
+        outs += [jax.ShapeDtypeStruct((count, dim // count + 4, wide), BF)]
+        outs += [jax.ShapeDtypeStruct((count // (2 * SLOTS), SLOTS * width // count, dim), t) for t in (BF, F32)]
+        scratch = [pltpu.VMEM((2, HD, 128), F32)]
+        scratch += [pltpu.VMEM((seqs, length, dim), BF)] * 2 + [pltpu.VMEM((dim, dim), BF)] * 2
+        scratch += Outputs.scratch(seqs, length, dim) + [pltpu.SemaphoreType.DMA((2 * seqs + 2,))]
+    else:
+        outs = [jax.ShapeDtypeStruct((seqs, width, length), BF), jax.ShapeDtypeStruct((seqs, wide, length), BF)]
+        outs += [
+            jax.ShapeDtypeStruct((2, HD, 128), F32),
+            jax.ShapeDtypeStruct((wide, dim), F32),
+            jax.ShapeDtypeStruct((width, dim), F32),
+        ]
     flops = seqs * (2 * length * dim * width * 8 + heads * 6 * 2 * length * length * HD)
     return pl.pallas_call(
-        functools.partial(attention_kernel, heads, block, sizes),
+        functools.partial(attention_kernel, heads, block, last),
         out_shape=outs,
-        in_specs=[VMEM] * 3 + [HBM] * (2 + SLOTS * len(groups)),
-        out_specs=[HBM] * 2 + [VMEM] * 4,
-        scratch_shapes=[
+        in_specs=specs,
+        out_specs=[HBM] * 2 + ([VMEM] * 3 if last else [VMEM, HBM, HBM]),
+        scratch_shapes=scratch
+        + [
             pltpu.VMEM((wide, dim), BF),
             pltpu.VMEM((width, dim), BF),
             pltpu.VMEM((seqs, length, dim), BF),
@@ -581,7 +655,7 @@
             pltpu.VMEM((seqs, width, length), BF),
             pltpu.VMEM((seqs, wide, length), BF),
             pltpu.VMEM((wide, dim), F32),
-            pltpu.VMEM((2, HD, 128), F32),
+            pltpu.VMEM((width, dim), F32),
             pltpu.VMEM((wide, length), F32),
             pltpu.VMEM((heads * blocks, 2 * HD, block), BF),
             pltpu.VMEM((heads * blocks, block, HD), BF),
@@ -605,17 +679,17 @@
     )(*ins)
 
 
-def ffn_kernel(block, groups, plan, at_ref, go_ref, anp_ref, sums_ref, gain_ref, wup_hbm, *refs):
+def ffn_kernel(block, groups, plan, at_ref, wup_hbm, wqkv_hbm, wo_hbm, o_hbm, gq_hbm, *refs):
     pieces, refs = refs[: len(plan)], refs[len(plan) :]
     pays, refs = refs[: len(groups) * SLOTS], refs[len(groups) * SLOTS :]
-    (hid_hbm, gup_hbm, wff_hbm, sendu_ref, sendf_ref, keepf_ref), refs = refs[:6], refs[6:]
-    norm_ref, gb_ref, hid_ref, gup_ref, wup_ref, wff_ref, gin_ref, gff_ref, sem, out_sem, w_sem = refs
+    (hid_hbm, gup_hbm, wff_hbm, keep_hbm, leave_hbm, sendu_ref, sendf_ref, keepf_ref, np_ref), refs = refs[:9], refs[9:]
+    norm_ref, gb_ref, hid_ref, gup_ref, wup_ref, wff_ref, gin_ref, gff_ref, sem, out_sem, w_sem, *refs = refs
+    wqkv_ref, wo_ref, o_ref, gq_ref, res_ref, res_sem, late_sem = refs
     dim = wup_ref.shape[0]
     part = pays[0].shape[2]
     total = norm_ref.shape[0]
     weights = [pltpu.make_async_copy(wup_hbm, wup_ref, w_sem.at[0])]
-    head_rows = go_ref.shape[0] // (2 * sendf_ref.shape[0])
-    rows = sendf_ref.shape[1] - head_rows
+    rows = sendf_ref.shape[1]
     for ref, masks in zip(pieces, plan):
         for i, mask in enumerate(masks):
             to = wff_ref.at[pl.ds(pl.multiple_of((at_ref[2] ^ mask) * rows, rows), rows), :]
@@ -630,6 +704,12 @@
                     source = pays[g * SLOTS + t].at[s, k]
                     pltpu.make_async_copy(source, to.at[pl.ds(n * part, part), :], sem.at[k, n]).start()
                 n += 1
+    late = [
+        pltpu.make_async_copy(a, b, late_sem.at[i])
+        for i, (a, b) in enumerate(((wqkv_hbm, wqkv_ref), (wo_hbm, wo_ref), (o_hbm, o_ref), (gq_hbm, gq_ref)))
+    ]
+    for copy in late:
+        copy.start()
     gin_ref[...] = jnp.zeros_like(gin_ref)
     gff_ref[...] = jnp.zeros_like(gff_ref)
     for copy in weights:
@@ -665,21 +745,19 @@
         return carry
 
     lax.fori_loop(0, total // block, step, 0)
+    for copy in late:
+        copy.wait()
+    results = Outputs(keep_hbm, leave_hbm, res_ref, res_sem, wo_ref, wff_ref, wqkv_ref, wup_ref)
+    length = SLOTS * part
+    for s in range(results.seqs):
+        rows_s = pl.ds(s * length, length)
+        results.compute(s, o_ref.at[s], hid_ref.at[rows_s, :], gq_ref.at[s], gup_ref.at[rows_s, :])
     line = jnp.sum(wup_ref[...].astype(F32) * gin_ref[...], axis=1, keepdims=True)
-    first = (jnp.broadcast_to(line, (dim, 128)).T[0:1] + anp_ref[...]) / gain_ref[...]
-    second = jnp.concatenate([sums_ref[...], jnp.zeros((1, dim - 2 * HD), F32)], axis=1)
-    small = jnp.concatenate([first, second], axis=0)
-    high = small.astype(BF).astype(F32)
-    small = jnp.concatenate([high, small - high], axis=0).astype(BF)
-    count, unit, _ = sendu_ref.shape
-    unit = unit - 4
-    for i in range(count):
-        sendu_ref[i, :unit] = gin_ref[i * unit : (i + 1) * unit, :].astype(BF)
-        sendu_ref[i, unit:] = small
-    odd = (at_ref[2] & 1) > 0
-    split_rows(odd, go_ref[...], sendf_ref, keepf_ref, 0, head_rows)
-    split_rows(odd, gff_ref[...], sendf_ref, keepf_ref, head_rows, rows)
+    np_ref[...] = jnp.broadcast_to(line, (dim, 128)).T[0:1]
+    sendu_ref[...] = gin_ref[...].astype(BF)
+    split_rows((at_ref[2] & 1) > 0, gff_ref[...], sendf_ref, keepf_ref)
     joined.wait()
+    results.wait()
 
     def drain(i, carry):
         for copy in outs(i):
@@ -689,7 +767,7 @@
     lax.fori_loop(0, total // block, drain, 0)
 
 
-def ffn(at, go, anp, sums, gain, wup, ff_parts, groups, count, block=512):
+def ffn(at, wup, ff_parts, groups, count, wqkv, wo, o, gq, block=512):
     dim, units = wup.shape
     sizes = [g[0].shape[0] for g in groups]
     part = groups[0][0].shape[2]
@@ -702,12 +780,14 @@
             act,
             act,
             jax.ShapeDtypeStruct((units, dim), BF),
-            jax.ShapeDtypeStruct((count * SLOTS, dim // (count * SLOTS) + 4, units), BF),
-            jax.ShapeDtypeStruct((count // 2, (units + go.shape[0]) // count, dim), BF),
-            jax.ShapeDtypeStruct((count // 2, (units + go.shape[0]) // count, dim), F32),
+            *[jax.ShapeDtypeStruct((SLOTS // 2, o.shape[0], 2, part, dim), BF)] * 2,
+            jax.ShapeDtypeStruct((dim, units), BF),
+            jax.ShapeDtypeStruct((count // 2, units // count, dim), BF),
+            jax.ShapeDtypeStruct((count // 2, units // count, dim), F32),
+            jax.ShapeDtypeStruct((1, dim), F32),
         ],
-        in_specs=[SMEM] + [VMEM] * 4 + [HBM] * (1 + len(ff_parts) + len(pieces)),
-        out_specs=[HBM] * 3 + [VMEM] * 3,
+        in_specs=[SMEM] + [HBM] * (5 + len(ff_parts) + len(pieces)),
+        out_specs=[HBM] * 5 + [VMEM] * 4,
         scratch_shapes=[
             pltpu.VMEM((total, dim), BF),
             pltpu.VMEM((total, dim), BF),
@@ -720,108 +800,56 @@
             pltpu.SemaphoreType.DMA((2, total // part)),
             pltpu.SemaphoreType.DMA((2, total // block)),
             pltpu.SemaphoreType.DMA((1 + count,)),
+            *[pltpu.VMEM(a.shape, BF) for a in (wqkv, wo, o, gq)],
+            *Outputs.scratch(o.shape[0], SLOTS * part, dim),
+            pltpu.SemaphoreType.DMA((4,)),
         ],
         cost_estimate=LARGE,
         compiler_params=pltpu.CompilerParams(vmem_limit_bytes=58 * MIB),
         name="ffn",
-    )(at, go, anp, sums, gain, *hbm(wup, *[a for a, _ in ff_parts], *pieces))
-
-
-def outputs(start, first, seqs, o, hid, gq, gu, wo, wff, wqkv, wup):
-    length = o.shape[2]
-    dim = wo.shape[1]
-    part = length // SLOTS
-
-    def kernel(o_hbm, hid_hbm, gq_hbm, gu_hbm, wo_hbm, wff_hbm, wqkv_hbm, wup_hbm, keep_hbm, send_hbm, *scratch):
-        o_ref, hid_ref, gq_ref, gu_ref, wo_ref, wff_ref, wqkv_ref, wup_ref, res_ref, w_sem, sem, out_sem = scratch
-
-        def load(k, s):
-            rows = pl.ds((start + s) * length, length)
-            source, to = (
-                (hid_hbm.at[rows, :], hid_ref), (o_hbm.at[first + s], o_ref), (gu_hbm.at[rows, :], gu_ref), (gq_hbm.at[first + s], gq_ref)
-            )[k]
-            return pltpu.make_async_copy(source, to.at[s], sem.at[s, k])
-
-        weights = [
-            pltpu.make_async_copy(a, b, w_sem.at[k])
-            for k, (a, b) in enumerate(((wff_hbm, wff_ref), (wo_hbm, wo_ref), (wup_hbm, wup_ref), (wqkv_hbm, wqkv_ref)))
-        ]
-        for k in range(4):
-            weights[k].start()
-            load(k, 0).start()
-        for s in range(1, seqs):
-            for k in range(4):
-                load(k, s).start()
-
-        weights[0].wait()
-        weights[1].wait()
-        half = length // 2
-
-        def step(n, carry):
-            s, i = n // 2, n % 2
-            lanes = pl.ds(pl.multiple_of(i * half, half), half)
-
-            @pl.when(i == 0)
-            def _():
-                load(0, s).wait()
-                load(1, s).wait()
-
-            res_ref[s, 0, lanes, :] = (mm(o_ref[s, :, lanes], wo_ref[...], TN) + mm(hid_ref[s, lanes, :], wff_ref[...])).astype(BF)
-
-            @pl.when(n == 0)
-            def _():
-                weights[2].wait()
-                weights[3].wait()
-
-            @pl.when(i == 0)
-            def _():
-                load(2, s).wait()
-                load(3, s).wait()
-
-            res_ref[s, 1, lanes, :] = (
-                mm(gq_ref[s, :, lanes], wqkv_ref[...], TN) + mm(gu_ref[s, lanes, :], wup_ref[...], NT)
-            ).astype(BF)
-            for copy in moves(s, i):
+    )(at, *hbm(wup, wqkv, wo, o, gq, *[a for a, _ in ff_parts], *pieces))
+
+
+class Outputs:
+    def __init__(self, keep, send, res, sem, wo, wff, wqkv, wup):
+        self.keep, self.send, self.res, self.sem = keep, send, res, sem
+        self.wo, self.wff, self.wqkv, self.wup = wo, wff, wqkv, wup
+        self.seqs, _, self.length, _ = res.shape
+
+    @staticmethod
+    def scratch(seqs, length, dim):
+        return [pltpu.VMEM((seqs, 2, length, dim), BF), pltpu.SemaphoreType.DMA((seqs, 2, SLOTS))]
+
+    def moves(self, s, i):
+        half = self.length // 2
+        part = half // 2
+        out = []
+        for j in range(2):
+            for k, to in enumerate((self.keep, self.send)):
+                rows = pl.ds(pl.multiple_of(i * half + k * part, part), part)
+                out.append(pltpu.make_async_copy(self.res.at[s, j, rows, :], to.at[i, s, j], self.sem.at[s, j, 2 * i + k]))
+        return out
+
+    def compute(self, s, o, hid, gq, gu):
+        half = self.length // 2
+
+        def step(i, carry):
+            rows = pl.ds(pl.multiple_of(i * half, half), half)
+            branch = mm(o[:, rows], self.wo[...], TN) + mm(hid[rows, :], self.wff[...])
+            self.res[s, 0, rows, :] = branch.astype(BF)
+            gn = mm(gq[:, rows], self.wqkv[...], TN) + mm(gu[rows, :], self.wup[...], NT)
+            self.res[s, 1, rows, :] = gn.astype(BF)
+            for copy in self.moves(s, i):
                 copy.start()
             return carry
 
-        def moves(s, i):
-            out = []
-            for j in range(2):
-                for k, to in enumerate((keep_hbm, send_hbm)):
-                    rows = pl.ds(pl.multiple_of(i * half + k * part, part), part)
-                    out.append(pltpu.make_async_copy(res_ref.at[s, j, rows, :], to.at[i, s, j], out_sem.at[s, j, 2 * i + k]))
-            return out
-
-        lax.fori_loop(0, 2 * seqs, step, 0)
-        for s in range(seqs):
+        lax.fori_loop(0, 2, step, 0)
+
+    def wait(self):
+        for s in range(self.seqs):
             for i in range(2):
-                for copy in moves(s, i):
+                for copy in self.moves(s, i):
                     copy.wait()
-
-    return pl.pallas_call(
-        kernel,
-        out_shape=[jax.ShapeDtypeStruct((SLOTS // 2, seqs, 2, part, dim), BF)] * 2,
-        in_specs=[HBM] * 8,
-        out_specs=[HBM] * 2,
-        scratch_shapes=[
-            pltpu.VMEM((seqs,) + o.shape[1:], BF),
-            pltpu.VMEM((seqs, length, hid.shape[1]), BF),
-            pltpu.VMEM((seqs,) + gq.shape[1:], BF),
-            pltpu.VMEM((seqs, length, gu.shape[1]), BF),
-            pltpu.VMEM(wo.shape, BF),
-            pltpu.VMEM(wff.shape, BF),
-            pltpu.VMEM(wqkv.shape, BF),
-            pltpu.VMEM(wup.shape, BF),
-            pltpu.VMEM((seqs, 2, length, dim), BF),
-            pltpu.SemaphoreType.DMA((4,)),
-            pltpu.SemaphoreType.DMA((seqs, 4)),
-            pltpu.SemaphoreType.DMA((seqs, 2, SLOTS)),
-        ],
-        cost_estimate=SMALL,
-        compiler_params=pltpu.CompilerParams(vmem_limit_bytes=48 * MIB),
-        name="outputs",
-    )(*hbm(o, hid, gq, gu, wo, wff, wqkv, wup))
 
 
 def swap(value, axis, count, mask):
@@ -927,62 +955,69 @@
 
     groups = bit_groups(nb)
 
+    lead = 1
     a_src, u_src = prepare(image_ids, in_weight, nb, nt)
     a_got = exchange(a_src.reshape(nb * nt, rows_in + 2, 3 * local), both)
     own0, own1, *unit_sends = before(
-        at, table, image_ids, gain, tie(patches, a_src), cotangent, out_weight.reshape(per, unit, dim)
+        at, table, out_weight.reshape(per, unit, dim), image_ids, gain, tie(patches, a_src), cotangent, lead
     )
-    far0 = swap(own0, "tok", nt, 2)
     got = [lax.ppermute(v, both, perm) for v, perm in zip(unit_sends, perms)]
-    wo_src, ff_src = pack_out(at, table, got, nb)
+    wo_src, ff_src = pack_out(at, table, got)
+    far0 = swap(tie(own0, *got), "tok", nt, 2)
+    wo_parts = gather_batch(wo_src, nb, groups)
     ff_parts = gather_batch(ff_src.reshape((per - 1) * unit, dim), nb, groups[::-1])
-    wo = exchange(tie(wo_src, a_got), "batch").reshape(local, dim)
-    wqkv, ids = join(at, a_got, seqs, part)
-    far1 = swap(tie(own1, far0, wo_src), "tok", nt, 2)
-    slots0 = [own0, swap(own0, "tok", nt, 1), far0, swap(tie(far0, wo_src), "tok", nt, 1)]
+    wqkv, wo, ids = join(at, a_got, wo_parts, seqs, part)
+    wo = wo.reshape(local, dim)
+    far1 = swap(tie(own1, far0), "tok", nt, 2)
+    slots0 = [own0, swap(own0, "tok", nt, 1), far0, swap(far0, "tok", nt, 1)]
     slots1 = [own1, swap(own1, "tok", nt, 1), far1, swap(far1, "tok", nt, 1)]
-    wup = exchange(tie(u_src, wo).reshape(nb * nt, unit, dim), both).reshape(dim, units)
+    wup = exchange(tie(u_src, a_got).reshape(nb * nt, unit, dim), both).reshape(dim, units)
 
     qg = query_gain.reshape(HD, 1)
     kg = key_gain.reshape(HD, 1)
 
-    def leave_core(s, i, o, gq):
-        keep, send = outputs(s, i, 1, o, hid, gq, gup, wo, wff, wqkv, wup)
-        return keep, swap(send, "tok", nt, 1)
-
-    def leave_chip(keep, near):
+    def leave_chip(keep, near, *hold):
         value = (keep[1].astype(F32) + near[1].astype(F32)).astype(BF)
-        return value, swap(value, "tok", nt, 2)
-
-    o, gq, a_q, go, a_np, sums = attention(ids, wqkv, tie(wo, ff_parts[0][0]), qg, kg, [slots0, slots1], nb * nt)
-    a_q = sum_qkv(exchange(a_q, both), nt)
-    hid, gup, wff, f_up, f_send, f_keep = ffn(at, go, a_np, sums, gain, wup, ff_parts, [slots0, slots1], nb)
-    f_up = exchange(tie(f_up, a_q), both)
-    terms = [f_keep, swap(f_send, "batch", nb, 1)]
-    group = []
-    o = tie(o, a_q)
-    for s in range(seqs):
-        if s == seqs - 1:
-            value, away = leave_chip(*group[0])
-            group[0].append(away)
-            o = tie(o, value)
-            for bits in groups[:-1][::-1]:
-                own, *sends = fold(at, bits[-1], terms[0], terms[1:])
-                terms = [own] + [swap(v, "batch", nb, (k + 1) << bits[-1]) for k, v in enumerate(sends)]
-                o = tie(o, own)
-        keep, near = leave_core(s, s, o, gq)
-        group.append([keep, near])
-        o = tie(o, keep)
-    for s in range(1, seqs):
-        group[s].append(leave_chip(*group[s])[1])
-
-    sends = leave(at, table, terms)
+        return value, swap(tie(value, *hold) if hold else value, "tok", nt, 2)
+
+    def reduce_batch(keep, came):
+        terms = [keep, came]
+        for bits in groups[:-1][::-1]:
+            own, *sends = fold(at, bits[-1], terms[0], terms[1:])
+            terms = [own] + [swap(value, "batch", nb, (s + 1) << bits[-1]) for s, value in enumerate(sends)]
+        return terms
+
+    o0, gq0, sums, acc_q, acc_o = attention(at, ids[:lead], wqkv, tie(wo, ff_parts[0][0]), qg, kg, slots0, nb * nt)
+    hid, gup, wff, keep0, send0, f_up, f_send, f_keep, f_np = ffn(
+        at, wup, ff_parts, [slots0, slots1], nb, wqkv, wo, o0, gq0
+    )
+    f_up = exchange(f_up.reshape(nb * nt, unit, dim), both)
+    f_came = swap(f_send, "batch", nb, 1)
+    near0 = swap(send0, "tok", nt, 1)
+    value0, away0 = leave_chip(keep0, near0)
+    keep1, send1, a_q, a_send, a_keep = attention(
+        at, ids[lead:], wqkv, tie(wo, value0), qg, kg, slots1, nb * nt,
+        (sums, f_np, gain, acc_q, acc_o, hid, gup, wff, wup),
+    )
+    send1, a_q, a_send = (tie(value, f_up, f_came, away0) for value in (send1, a_q, a_send))
+    a_q = exchange(a_q, both)
+    a_came = swap(a_send, "batch", nb, 1)
+    near1 = swap(send1, "tok", nt, 1)
+    ff_terms = reduce_batch(f_keep, f_came)
+    o_terms = reduce_batch(a_keep, a_came)
+    value1, away1 = leave_chip(keep1, tie(near1, a_came))
+    up = sum_up(f_up, nt)
+    group = [(0, s, keep0, near0, away0) for s in range(lead)]
+    group += [(lead, s, keep1, near1, away1) for s in range(lead, seqs)]
+
+    sends = leave(at, table, o_terms, ff_terms)
     got = [lax.ppermute(v, both, [(b, a) for a, b in perm]) for v, perm in zip(sends, perms)]
-    in_grad, out_grad, norm_grad, query_grad, key_grad = place(at, table, a_q, f_up, got)
+    in_grad, out_grad, norm_grad, query_grad, key_grad = place(at, table, a_q, up, got)
 
     earlier = []
     for s in range(seqs):
-        earlier = after(s, 0, image_ids, patches, cotangent, gain, *group[s], earlier)
+        start, _, *arrays = group[s]
+        earlier = after(s, s - start, image_ids, patches, cotangent, gain, *arrays, earlier)
     block_out, patch_grad = earlier
     return (
         block_out,

time: 343 us -> 324 us (0.945)
  starting transfers between devices: 121 us -> 92 us
  waiting for transfers between devices: 64.6 us -> 82.7 us
  Pallas kernels: 140 us -> 128 us
    ppermute x20 -> x26, waiting for transfers between devices: 49.8 us -> 79 us  [swap(): return lax.ppermute(value, axis, [(i, i ^ mask) for i in range(count)])]
    ppermute x5, starting transfers between devices: 37.4 us -> 15.2 us  [per_device(): lax.ppermute(v, both, [(b, a) for a, b in perm])]
    ppermute x5, starting transfers between devices: 42.1 us -> 20.1 us  [per_device(): got = [lax.ppermute(v, both, perm) for v, perm in zip(unit_sends, perms)]]
    pallas_call x7 -> x5, Pallas kernels: 94.9 us -> 78.1 us  [the longest x2 72.8 us: attention(): pl.pallas_call(functools.partial(attention_kernel, heads, block, last), o...]
    ppermute x20 -> x26, starting transfers between devices: 19.4 us -> 30.6 us  [swap(): return lax.ppermute(value, axis, [(i, i ^ mask) for i in range(count)])]
    ppermute x5, waiting for transfers between devices: 9.69 us -> 1.54 us  [per_device(): got = [lax.ppermute(v, both, perm) for v, perm in zip(unit_sends, perms)]]
    all_to_all x5 -> x4, starting transfers between devices: 21.7 us -> 26.3 us  [exchange(): return lax.all_to_all(value, axis, split_axis=0, concat_axis=0, tiled=True)]
    pallas_call x1, Pallas kernels: 25.8 us -> 30.4 us  [ffn(): pl.pallas_call(functools.partial(ffn_kernel, block, sizes, [masks for _,...]
  transfers between devices with their start and end apart: 35 -> 40, of which waited for: 9 -> 12; matrix products, arithmetic and copies ran while one was open for 2% -> 3% of each run, Pallas kernels for 35% -> 26%
where the time goes in v4:
time: 324 us; the launch traced here: 322 us
  Pallas kernels  128 us (40%)
  starting transfers between devices  92 us (28%)
  waiting for transfers between devices  82.7 us (26%)
  local copies, waits for them, and re-layouts  10.5 us (3%)
  other arithmetic  7.57 us (2%)
    ppermute x26, waiting for transfers between devices, swap(): return lax.ppermute(value, axis, [(i, i ^ mask) for i in range(count)])  79 us
    pallas_call x2, Pallas kernels, attention(): pl.pallas_call(functools.partial(attention_kernel, heads, block, last), o...  72.8 us
    ppermute x26, starting transfers between devices, swap(): return lax.ppermute(value, axis, [(i, i ^ mask) for i in range(count)])  30.6 us
    pallas_call x1, Pallas kernels, ffn(): pl.pallas_call(functools.partial(ffn_kernel, block, sizes, [masks for _,...  30.4 us
    all_to_all x4, starting transfers between devices, exchange(): return lax.all_to_all(value, axis, split_axis=0, concat_axis=0, tiled=True)  26.3 us
    ppermute x5, starting transfers between devices, per_device(): got = [lax.ppermute(v, both, perm) for v, perm in zip(unit_sends, perms)]  20.1 us
    ppermute x5, starting transfers between devices, per_device(): lax.ppermute(v, both, [(b, a) for a, b in perm])  15.2 us
    pallas_call x3, Pallas kernels, after(): pl.pallas_call(functools.partial(after_kernel, s), grid=(1,), out_shape=[...  10.4 us
  transfers between devices with their start and end apart: 40, of which 12 were waited for; matrix products, arithmetic and copies ran while one was open for 3% of the time, Pallas kernels for 26%

profile of v4, /device:TPU:2, one launch (start us, length us, event | category | flops | bytes accessed | tf_op | source)
XLA Modules:
  0.0 321.7 jit_solution(5020035815461463851)
XLA Ops:
  4.5 3.4 %before.1 = (bf16[1,2,256,768]{3,2,1,0:T(8,128)(2,1)}, bf16[2,2,256,768]{3,2,1,0:T(8,128)(2,1)S(1)}, bf16[24,768]{1,0:T(8,128)(2,1)S(1)}, bf16[24,768]{1,0:T(8,1...) custom-call(s32[3]{0:T(128)S(1)} %pad_add_fusion.at_ref, ...), custom_call_target="tpu_custom_call" | custom-call | flops 1 | bytes 1 | tf_op jit(solution)/shard_map/before/pallas_call | solution.py:148
  7.9 5.6 %collective-permute-start = (bf16[24,768]{1,0:T(8,128)(2,1)S(1)}, bf16[24,768]{1,0:T(8,128)(2,1)S(1)}, u32[]{:S(2)}, u32[]{:S(2)}) collective-permute-start(bf16[24,768]{1,0:T(8,128)(2,1)S(1)} %get-tuple-element.76), channel_id=1, source_target_pairs={{7,0},{13,1},{3,2},{26,3},{0,4},{14,5},{20,6},{27,7},{8,8},{15,9},... | collective-permute-start | bytes 110600 | tf_op jit(solution)/shard_map/ppermute | solution.py:964
  16.4 3.7 %collective-permute-start.2 = (bf16[24,768]{1,0:T(8,128)(2,1)S(1)}, bf16[24,768]{1,0:T(8,128)(2,1)S(1)}, u32[]{:S(2)}, u32[]{:S(2)}) collective-permute-start(bf16[24,768]{1,0:T(8,128)(2,1)S(1)} %get-tuple-element.78), channel_id=1, source_target_pairs={{6,0},{13,1},{19,2},{4,3},{7,4},{1,5},{20,6},{26,7},{8,8},{14,9},{... | collective-permute-start | bytes 110600 | tf_op jit(solution)/shard_map/ppermute | solution.py:964
  23.0 5.0 %collective-permute-start.4 = (bf16[24,768]{1,0:T(8,128)(2,1)S(1)}, bf16[24,768]{1,0:T(8,128)(2,1)S(1)}, u32[]{:S(2)}, u32[]{:S(2)}) collective-permute-start(bf16[24,768]{1,0:T(8,128)(2,1)S(1)} %get-tuple-element.80), channel_id=1, source_target_pairs={{6,0},{12,1},{19,2},{25,3},{7,4},{13,5},{3,6},{26,7},{0,8},{14,9},... | collective-permute-start | bytes 110600 | tf_op jit(solution)/shard_map/ppermute | solution.py:964
  29.6 7.3 %all-to-all-start = ((bf16[32,26,576]{2,1,0:T(8,128)(2,1)}), bf16[32,26,576]{2,1,0:T(8,128)(2,1)S(1)}, u32[]{:S(2)}, u32[]{:S(2)}) async-start(bf16[32,26,576]{2,1,0:T(8,128)(2,1)} %bitcast.3), calls=%async_computation | async-start | bytes 2621440 | tf_op jit(solution)/shard_map/all_to_all | solution.py:954
  36.9 24.0 %collective-permute-done.11.refs_2_.refs_6_ = bf16[1,2,256,768]{3,2,1,0:T(8,128)(2,1)} collective-permute-done((bf16[1,2,256,768]{3,2,1,0:T(8,128)(2,1)}, bf16[1,2,256,768]{3,2,1,0:T(8,128)(2,1)}, u32[]{:S(2)}, u32[]{:S(2)}) %collective-permute-start.11) | collective-permute-done | bytes 786464 | tf_op jit(solution)/shard_map/ppermute | solution.py:856
  85.5 5.2 %all-to-all-start.1 = ((bf16[32,24,768]{2,1,0:T(8,128)(2,1)}), bf16[32,24,768]{2,1,0:T(8,128)(2,1)S(1)}, u32[]{:S(2)}, u32[]{:S(2)}) async-start(bf16[32,24,768]{2,1,0:T(8,128)(2,1)} %bitcast.9), calls=%async_computation.1 | async-start | bytes 2359296 | tf_op jit(solution)/shard_map/all_to_all | solution.py:954
  94.6 13.3 %collective-permute-done.17.refs_10_.refs_2_ = bf16[2,2,256,768]{3,2,1,0:T(8,128)(2,1)} collective-permute-done((bf16[2,2,256,768]{3,2,1,0:T(8,128)(2,1)S(1)}, bf16[2,2,256,768]{3,2,1,0:T(8,128)(2,1)}, u32[]{:S(2)}, u32[]{:S(2)}) %collective-permute-start.17) | collective-permute-done | bytes 1572896 | tf_op jit(solution)/shard_map/ppermute | solution.py:856
  107.9 22.2 %attention.2 = (bf16[1,192,1024]{2,1,0:T(8,128)(2,1)}, bf16[1,576,1024]{2,1,0:T(8,128)(2,1)}, f32[2,64,128]{2,1,0:T(8,128)}, f32[576,768]{1,0:T(8,128)}, f32[192,768]{1,0:T(8,128)}) custom-call(s32[3]{0:T(128)} %copy-done.7, s32[1,1,1024]{2,1,0:T(1,128)} %slice.19.ids_ref, f32[64,1]{1,0:T(8,128)} %copy.22.qg_ref, f32[64,1]{1,0:T(8,128)} %copy.23.kg_ref, ...), custom_call_target="tpu_custom_call" | custom-call | flops 60000002048 | bytes 1 | tf_op jit(solution)/shard_map/attention/pallas_call | solution.py:644
  130.1 8.7 %collective-permute-done.14.refs_2_ = bf16[2,96,768]{2,1,0:T(8,128)(2,1)S(1)} collective-permute-done((bf16[2,96,768]{2,1,0:T(8,128)(2,1)S(1)}, bf16[2,96,768]{2,1,0:T(8,128)(2,1)S(1)}, u32[]{:S(2)}, u32[]{:S(2)}) %collective-permute-start.14) | collective-permute-done | bytes 294944 | tf_op jit(solution)/shard_map/ppermute | solution.py:856
  140.6 30.4 %ffn.1 = (bf16[3072,768]{1,0:T(8,128)(2,1)}, bf16[3072,768]{1,0:T(8,128)(2,1)}, bf16[768,768]{1,0:T(8,128)(2,1)}, bf16[2,1,2,256,768]{4,3,2,1,0:T(8,128)(2,1)}, ...) custom-call(s32[3]{0:T(128)} %copy-done.7, ...), custom_call_target="tpu_custom_call" | custom-call | flops 60000002048 | bytes 1 | tf_op jit(solution)/shard_map/ffn/pallas_call | solution.py:777
  172.3 8.9 %all-to-all-start.2 = ((bf16[32,24,768]{2,1,0:T(8,128)(2,1)}), bf16[32,24,768]{2,1,0:T(8,128)(2,1)S(1)}, u32[]{:S(2)}, u32[]{:S(2)}) async-start(bf16[32,24,768]{2,1,0:T(8,128)(2,1)} %bitcast.25), calls=%async_computation.2 | async-start | bytes 2359296 | tf_op jit(solution)/shard_map/all_to_all | solution.py:954
  184.3 50.5 %attention.3 = (bf16[2,2,2,256,768]{4,3,2,1,0:T(8,128)(2,1)}, bf16[2,2,2,256,768]{4,3,2,1,0:T(8,128)(2,1)}, bf16[32,28,576]{2,1,0:T(8,128)(2,1)}, bf16[4,24,768]{2,1,0:T(8,128)(2,1)}, f32[4,24,768]{2,1,0:T(8,128)}) custom-call(s32[3]{0:T(128)} %copy-done.7, s32[2,1,1024]{2,1,0:T(1,128)} %slice.18.ids_ref, f32[64,1]{1,0:T(8,128)} %copy.22.qg_ref, ...), custom_call_target="tpu_custom_call" | custom-call | flops 60000002048 | bytes 1 | tf_op jit(solution)/shard_map/attention/pallas_call | solution.py:644
  235.5 4.9 %all-to-all-start.3 = ((bf16[32,28,576]{2,1,0:T(8,128)(2,1)}), bf16[32,28,576]{2,1,0:T(8,128)(2,1)S(1)}, u32[]{:S(2)}, u32[]{:S(2)}) async-start(bf16[32,28,576]{2,1,0:T(8,128)(2,1)} %get-tuple-element.120), calls=%async_computation.3 | async-start | bytes 2621440 | tf_op jit(solution)/shard_map/all_to_all | solution.py:954
  241.4 3.5 %fusion = bf16[2,2,256,768]{3,2,1,0:T(8,128)(2,1)} fusion(bf16[2,2,2,256,768]{4,3,2,1,0:T(8,128)(2,1)} %collective-permute-done.22.near_ref, bf16[2,2,2,256,768]{4,3,2,1,0:T(8,128)(2,1)} %get-tuple-element.105.keep_ref), kind=kLoop, calls=%fused_computation.1 | loop fusion | flops 3145728 | bytes 4718592 | tf_op jit(solution)/shard_map/convert_element_type | solution.py:980
  253.1 12.7 %collective-permute-done.28.refs_5_ = bf16[1,96,768]{2,1,0:T(8,128)(2,1)S(1)} collective-permute-done((bf16[1,96,768]{2,1,0:T(8,128)(2,1)S(1)}, bf16[1,96,768]{2,1,0:T(8,128)(2,1)S(1)}, u32[]{:S(2)}, u32[]{:S(2)}) %collective-permute-start.28) | collective-permute-done | bytes 147488 | tf_op jit(solution)/shard_map/ppermute | solution.py:856
  265.8 4.4 %collective-permute-start.26 = (bf16[1,24,768]{2,1,0:T(8,128)(2,1)S(1)}, bf16[1,24,768]{2,1,0:T(8,128)(2,1)S(1)}, u32[]{:S(2)}, u32[]{:S(2)}) collective-permute-start(bf16[1,24,768]{2,1,0:T(8,128)(2,1)S(1)} %get-tuple-element.124), channel_id=1, source_target_pairs={{0,16},{4,20},{8,24},{12,28},{16,0},{20,4},{24,8},{28,12},{1,17},{... | collective-permute-start | bytes 110600 | tf_op jit(solution)/shard_map/ppermute | solution.py:856
  270.2 12.6 %collective-permute-done.29.refs_6_ = bf16[1,96,768]{2,1,0:T(8,128)(2,1)S(1)} collective-permute-done((bf16[1,96,768]{2,1,0:T(8,128)(2,1)S(1)}, bf16[1,96,768]{2,1,0:T(8,128)(2,1)S(1)}, u32[]{:S(2)}, u32[]{:S(2)}) %collective-permute-start.29) | collective-permute-done | bytes 147488 | tf_op jit(solution)/shard_map/ppermute | solution.py:856
  295.7 3.2 collective-permute-start.33
  298.9 3.3 %collective-permute-start.34 = (f32[24,768]{1,0:T(8,128)}, f32[24,768]{1,0:T(8,128)S(1)}, u32[]{:S(2)}, u32[]{:S(2)}) collective-permute-start(f32[24,768]{1,0:T(8,128)} %get-tuple-element.134), channel_id=1, source_target_pairs={{0,6},{1,1},{2,19},{3,25},{4,7},{5,13},{6,20},{7,26},{8,8},{9,14},... | collective-permute-start | bytes 221192 | tf_op jit(solution)/shard_map/ppermute | solution.py:1014
  302.2 4.2 %collective-permute-start.35 = (f32[24,768]{1,0:T(8,128)}, f32[24,768]{1,0:T(8,128)S(1)}, u32[]{:S(2)}, u32[]{:S(2)}) collective-permute-start(f32[24,768]{1,0:T(8,128)} %get-tuple-element.135), channel_id=1, source_target_pairs={{0,6},{1,12},{2,19},{3,25},{4,7},{5,13},{6,3},{7,26},{8,0},{9,14},... | collective-permute-start | bytes 221192 | tf_op jit(solution)/shard_map/ppermute | solution.py:1014
  306.7 3.5 %after.3 = (bf16[3,256,768]{2,1,0:T(8,128)(2,1)}, bf16[3,256,768]{2,1,0:T(8,128)(2,1)}) custom-call(s32[3,256]{1,0:T(4,128)S(1)} %copy-done.4, bf16[3,256,768]{2,1,0:T(8,128)(2,1)} %x_ref.5, bf16[3,256,768]{2,1,0:T(8,128)(2,1)} %cot_ref.5, f32[1,768]{1,0:T(1,128)S(1)} %copy-done.5, bf16[2,1,2,256,768]{4,3,2,1,0:T(8,128)(2,1)} %get-tuple-element.95.keep_ref, ...), custom_call_target="tpu_custom_call" | custom-call | flops 1 | bytes 1 | tf_op jit(solution)/shard_map/after/pallas_call | solution.py:385
  314.8 3.5 %after.4 = (bf16[3,256,768]{2,1,0:T(8,128)(2,1)}, bf16[3,256,768]{2,1,0:T(8,128)(2,1)}) custom-call(s32[3,256]{1,0:T(4,128)S(1)} %copy-done.4, bf16[3,256,768]{2,1,0:T(8,128)(2,1)} %x_ref.5, bf16[3,256,768]{2,1,0:T(8,128)(2,1)} %cot_ref.5, f32[1,768]{1,0:T(1,128)S(1)} %copy-done.5, ...), custom_call_target="tpu_custom_call", output_to_operand_aliasing={{0}: (7, {}), {1}: (8, {})} | custom-call | flops 1 | bytes 1 | tf_op jit(solution)/shard_map/after/pallas_call | solution.py:385
  318.3 3.5 %after.5 = (bf16[3,256,768]{2,1,0:T(8,128)(2,1)}, bf16[3,256,768]{2,1,0:T(8,128)(2,1)}) custom-call(s32[3,256]{1,0:T(4,128)S(1)} %copy-done.4, bf16[3,256,768]{2,1,0:T(8,128)(2,1)} %x_ref.5, bf16[3,256,768]{2,1,0:T(8,128)(2,1)} %cot_ref.5, f32[1,768]{1,0:T(1,128)S(1)} %copy-done.5, ...), custom_call_target="tpu_custom_call", output_to_operand_aliasing={{0}: (7, {}), {1}: (8, {})} | custom-call | flops 1 | bytes 1 | tf_op jit(solution)/shard_map/after/pallas_call | solution.py:385
  (146 shorter events, 73.3 us)
Async XLA Ops:
  7.9 20.1 %collective-permute-start = (bf16[24,768]{1,0:T(8,128)(2,1)S(1)}, bf16[24,768]{1,0:T(8,128)(2,1)S(1)}, u32[]{:S(2)}, u32[]{:S(2)}) collective-permute-start(bf16[24,768]{1,0:T(8,128)(2,1)S(1)} %get-tuple-element.76), channel_id=1, source_target_pairs={{7,0},{13,1},{3,2},{26,3},{0,4},{14,5},{20,6},{27,7},{8,8},{15,9},... | collective-permute-start | bytes 110600 | tf_op jit(solution)/shard_map/ppermute | solution.py:964
  13.5 14.5 %collective-permute-start.1 = (bf16[24,768]{1,0:T(8,128)(2,1)S(1)}, bf16[24,768]{1,0:T(8,128)(2,1)S(1)}, u32[]{:S(2)}, u32[]{:S(2)}) collective-permute-start(bf16[24,768]{1,0:T(8,128)(2,1)S(1)} %get-tuple-element.77), channel_id=1, source_target_pairs={{0,0},{13,1},{19,2},{26,3},{7,4},{14,5},{20,6},{5,7},{8,8},{2,9},{... | collective-permute-start | bytes 110600 | tf_op jit(solution)/shard_map/ppermute | solution.py:964
  29.6 31.3 %collective-permute-start.11 = (bf16[1,2,256,768]{3,2,1,0:T(8,128)(2,1)}, bf16[1,2,256,768]{3,2,1,0:T(8,128)(2,1)}, u32[]{:S(2)}, u32[]{:S(2)}) collective-permute-start(bf16[1,2,256,768]{3,2,1,0:T(8,128)(2,1)} %get-tuple-element.90.refs_0_.refs_4_), channel_id=1, source_target_pairs={{0,2},{1,3},{2,0},{3,1},{4,6},{5,7},{6,4},{7,5},{8,10},{9,11},{10,... | collective-permute-start | bytes 2359304 | tf_op jit(solution)/shard_map/ppermute | solution.py:856
  29.6 51.8 %all-to-all-start = ((bf16[32,26,576]{2,1,0:T(8,128)(2,1)}), bf16[32,26,576]{2,1,0:T(8,128)(2,1)S(1)}, u32[]{:S(2)}, u32[]{:S(2)}) async-start(bf16[32,26,576]{2,1,0:T(8,128)(2,1)} %bitcast.3), calls=%async_computation | async-start | bytes 2621440 | tf_op jit(solution)/shard_map/all_to_all | solution.py:954
  60.9 47.0 %collective-permute-start.17 = (bf16[2,2,256,768]{3,2,1,0:T(8,128)(2,1)S(1)}, bf16[2,2,256,768]{3,2,1,0:T(8,128)(2,1)}, u32[]{:S(2)}, u32[]{:S(2)}) collective-permute-start(bf16[2,2,256,768]{3,2,1,0:T(8,128)(2,1)S(1)} %get-tuple-element.94.refs_8_.refs_0_), channel_id=1, source_target_pairs={{0,2},{1,3},{2,0},{3,1},{4,6},{5,7},{6,4},{7,5},{8,10},{9,11},{10,... | collective-permute-start | bytes 4718600 | tf_op jit(solution)/shard_map/ppermute | solution.py:856
  60.9 29.8 %collective-permute-start.10 = (bf16[1,2,256,768]{3,2,1,0:T(8,128)(2,1)}, bf16[1,2,256,768]{3,2,1,0:T(8,128)(2,1)}, u32[]{:S(2)}, u32[]{:S(2)}) collective-permute-start(bf16[1,2,256,768]{3,2,1,0:T(8,128)(2,1)} %get-tuple-element.90.refs_0_.refs_4_), channel_id=1, source_target_pairs={{0,1},{1,0},{2,3},{3,2},{4,5},{5,4},{6,7},{7,6},{8,9},{9,8},{10,11... | collective-permute-start | bytes 2359304 | tf_op jit(solution)/shard_map/ppermute | solution.py:856
  61.5 31.6 %collective-permute-start.12 = (bf16[1,2,256,768]{3,2,1,0:T(8,128)(2,1)}, bf16[1,2,256,768]{3,2,1,0:T(8,128)(2,1)}, u32[]{:S(2)}, u32[]{:S(2)}) collective-permute-start(bf16[1,2,256,768]{3,2,1,0:T(8,128)(2,1)} %collective-permute-done.11.refs_2_.refs_6_), channel_id=1, source_target_pairs={{0,1},{1,0},{2,3},{3,2},{4,5},{5,4},{6,7},{7,6},{8,9},{9,8},{10,11... | collective-permute-start | bytes 2359304 | tf_op jit(solution)/shard_map/ppermute | solution.py:856
  79.5 59.3 %collective-permute-start.16 = (bf16[2,2,256,768]{3,2,1,0:T(8,128)(2,1)S(1)}, bf16[2,2,256,768]{3,2,1,0:T(8,128)(2,1)}, u32[]{:S(2)}, u32[]{:S(2)}) collective-permute-start(bf16[2,2,256,768]{3,2,1,0:T(8,128)(2,1)S(1)} %get-tuple-element.94.refs_8_.refs_0_), channel_id=1, source_target_pairs={{0,1},{1,0},{2,3},{3,2},{4,5},{5,4},{6,7},{7,6},{8,9},{9,8},{10,11... | collective-permute-start | bytes 4718600 | tf_op jit(solution)/shard_map/ppermute | solution.py:856
  80.6 49.5 %collective-permute-start.13 = (bf16[2,96,768]{2,1,0:T(8,128)(2,1)S(1)}, bf16[2,96,768]{2,1,0:T(8,128)(2,1)}, u32[]{:S(2)}, u32[]{:S(2)}) collective-permute-start(bf16[2,96,768]{2,1,0:T(8,128)(2,1)S(1)} %pad_maximum_fusion.refs_0_), channel_id=1, source_target_pairs={{0,8},{4,12},{8,0},{12,4},{16,24},{20,28},{24,16},{28,20},{1,9},{5... | collective-permute-start | bytes 884744 | tf_op jit(solution)/shard_map/ppermute | solution.py:856
  85.5 54.1 %all-to-all-start.1 = ((bf16[32,24,768]{2,1,0:T(8,128)(2,1)}), bf16[32,24,768]{2,1,0:T(8,128)(2,1)S(1)}, u32[]{:S(2)}, u32[]{:S(2)}) async-start(bf16[32,24,768]{2,1,0:T(8,128)(2,1)} %bitcast.9), calls=%async_computation.1 | async-start | bytes 2359296 | tf_op jit(solution)/shard_map/all_to_all | solution.py:954
  90.7 48.2 %collective-permute-start.14 = (bf16[2,96,768]{2,1,0:T(8,128)(2,1)S(1)}, bf16[2,96,768]{2,1,0:T(8,128)(2,1)S(1)}, u32[]{:S(2)}, u32[]{:S(2)}) collective-permute-start(bf16[2,96,768]{2,1,0:T(8,128)(2,1)S(1)} %pad_maximum_fusion.refs_0_), channel_id=1, source_target_pairs={{0,16},{4,20},{8,24},{12,28},{16,0},{20,4},{24,8},{28,12},{1,17},{... | collective-permute-start | bytes 884744 | tf_op jit(solution)/shard_map/ppermute | solution.py:856
  93.1 45.7 %collective-permute-start.15 = (bf16[2,96,768]{2,1,0:T(8,128)(2,1)S(1)}, bf16[2,96,768]{2,1,0:T(8,128)(2,1)S(1)}, u32[]{:S(2)}, u32[]{:S(2)}) collective-permute-start(bf16[2,96,768]{2,1,0:T(8,128)(2,1)S(1)} %pad_maximum_fusion.refs_0_), channel_id=1, source_target_pairs={{0,24},{4,28},{8,16},{12,20},{16,8},{20,12},{24,0},{28,4},{1,25},{... | collective-permute-start | bytes 884744 | tf_op jit(solution)/shard_map/ppermute | solution.py:856
  107.9 31.7 %collective-permute-start.18 = (bf16[2,2,256,768]{3,2,1,0:T(8,128)(2,1)}, bf16[2,2,256,768]{3,2,1,0:T(8,128)(2,1)}, u32[]{:S(2)}, u32[]{:S(2)}) collective-permute-start(bf16[2,2,256,768]{3,2,1,0:T(8,128)(2,1)} %collective-permute-done.17.refs_10_.refs_2_), channel_id=1, source_target_pairs={{0,1},{1,0},{2,3},{3,2},{4,5},{5,4},{6,7},{7,6},{8,9},{9,8},{10,11... | collective-permute-start | bytes 4718600 | tf_op jit(solution)/shard_map/ppermute | solution.py:856
  171.7 63.1 %collective-permute-start.20 = (bf16[4,96,768]{2,1,0:T(8,128)(2,1)}, bf16[4,96,768]{2,1,0:T(8,128)(2,1)S(1)}, u32[]{:S(2)}, u32[]{:S(2)}) collective-permute-start(bf16[4,96,768]{2,1,0:T(8,128)(2,1)} %get-tuple-element.108), channel_id=1, source_target_pairs={{0,4},{4,0},{8,12},{12,8},{16,20},{20,16},{24,28},{28,24},{1,5},{5... | collective-permute-start | bytes 1769480 | tf_op jit(solution)/shard_map/ppermute | solution.py:856
  172.3 62.5 %all-to-all-start.2 = ((bf16[32,24,768]{2,1,0:T(8,128)(2,1)}), bf16[32,24,768]{2,1,0:T(8,128)(2,1)S(1)}, u32[]{:S(2)}, u32[]{:S(2)}) async-start(bf16[32,24,768]{2,1,0:T(8,128)(2,1)} %bitcast.25), calls=%async_computation.2 | async-start | bytes 2359296 | tf_op jit(solution)/shard_map/all_to_all | solution.py:954
  182.7 52.1 %collective-permute-start.21 = (bf16[1,2,256,768]{3,2,1,0:T(8,128)(2,1)S(1)}, bf16[1,2,256,768]{3,2,1,0:T(8,128)(2,1)}, u32[]{:S(2)}, u32[]{:S(2)}) collective-permute-start(bf16[1,2,256,768]{3,2,1,0:T(8,128)(2,1)S(1)} %fusion.1), channel_id=1, source_target_pairs={{0,2},{1,3},{2,0},{3,1},{4,6},{5,7},{6,4},{7,5},{8,10},{9,11},{10,... | collective-permute-start | bytes 2359304 | tf_op jit(solution)/shard_map/ppermute | solution.py:856
  235.5 76.8 %all-to-all-start.3 = ((bf16[32,28,576]{2,1,0:T(8,128)(2,1)}), bf16[32,28,576]{2,1,0:T(8,128)(2,1)S(1)}, u32[]{:S(2)}, u32[]{:S(2)}) async-start(bf16[32,28,576]{2,1,0:T(8,128)(2,1)} %get-tuple-element.120), calls=%async_computation.3 | async-start | bytes 2621440 | tf_op jit(solution)/shard_map/all_to_all | solution.py:954
  244.9 69.9 %collective-permute-start.24 = (bf16[2,2,256,768]{3,2,1,0:T(8,128)(2,1)}, bf16[2,2,256,768]{3,2,1,0:T(8,128)(2,1)}, u32[]{:S(2)}, u32[]{:S(2)}) collective-permute-start(bf16[2,2,256,768]{3,2,1,0:T(8,128)(2,1)} %fusion), channel_id=1, source_target_pairs={{0,2},{1,3},{2,0},{3,1},{4,6},{5,7},{6,4},{7,5},{8,10},{9,11},{10,... | collective-permute-start | bytes 4718600 | tf_op jit(solution)/shard_map/ppermute | solution.py:856
  246.9 18.9 %collective-permute-start.28 = (bf16[1,96,768]{2,1,0:T(8,128)(2,1)S(1)}, bf16[1,96,768]{2,1,0:T(8,128)(2,1)S(1)}, u32[]{:S(2)}, u32[]{:S(2)}) collective-permute-start(bf16[1,96,768]{2,1,0:T(8,128)(2,1)S(1)} %get-tuple-element.128), channel_id=1, source_target_pairs={{0,8},{4,12},{8,0},{12,4},{16,24},{20,28},{24,16},{28,20},{1,9},{5... | collective-permute-start | bytes 442376 | tf_op jit(solution)/shard_map/ppermute | solution.py:856
  248.4 34.4 %collective-permute-start.29 = (bf16[1,96,768]{2,1,0:T(8,128)(2,1)S(1)}, bf16[1,96,768]{2,1,0:T(8,128)(2,1)S(1)}, u32[]{:S(2)}, u32[]{:S(2)}) collective-permute-start(bf16[1,96,768]{2,1,0:T(8,128)(2,1)S(1)} %get-tuple-element.129), channel_id=1, source_target_pairs={{0,16},{4,20},{8,24},{12,28},{16,0},{20,4},{24,8},{28,12},{1,17},{... | collective-permute-start | bytes 442376 | tf_op jit(solution)/shard_map/ppermute | solution.py:856
  250.9 33.0 %collective-permute-start.30 = (bf16[1,96,768]{2,1,0:T(8,128)(2,1)S(1)}, bf16[1,96,768]{2,1,0:T(8,128)(2,1)S(1)}, u32[]{:S(2)}, u32[]{:S(2)}) collective-permute-start(bf16[1,96,768]{2,1,0:T(8,128)(2,1)S(1)} %get-tuple-element.130), channel_id=1, source_target_pairs={{0,24},{4,28},{8,16},{12,20},{16,8},{20,12},{24,0},{28,4},{1,25},{... | collective-permute-start | bytes 442376 | tf_op jit(solution)/shard_map/ppermute | solution.py:856
  252.5 31.3 %collective-permute-start.25 = (bf16[1,24,768]{2,1,0:T(8,128)(2,1)S(1)}, bf16[1,24,768]{2,1,0:T(8,128)(2,1)S(1)}, u32[]{:S(2)}, u32[]{:S(2)}) collective-permute-start(bf16[1,24,768]{2,1,0:T(8,128)(2,1)S(1)} %get-tuple-element.123), channel_id=1, source_target_pairs={{0,8},{4,12},{8,0},{12,4},{16,24},{20,28},{24,16},{28,20},{1,9},{5... | collective-permute-start | bytes 110600 | tf_op jit(solution)/shard_map/ppermute | solution.py:856
  265.8 21.2 %collective-permute-start.26 = (bf16[1,24,768]{2,1,0:T(8,128)(2,1)S(1)}, bf16[1,24,768]{2,1,0:T(8,128)(2,1)S(1)}, u32[]{:S(2)}, u32[]{:S(2)}) collective-permute-start(bf16[1,24,768]{2,1,0:T(8,128)(2,1)S(1)} %get-tuple-element.124), channel_id=1, source_target_pairs={{0,16},{4,20},{8,24},{12,28},{16,0},{20,4},{24,8},{28,12},{1,17},{... | collective-permute-start | bytes 110600 | tf_op jit(solution)/shard_map/ppermute | solution.py:856
  293.8 16.4 %collective-permute-start.32 = (f32[24,768]{1,0:T(8,128)}, f32[24,768]{1,0:T(8,128)S(1)}, u32[]{:S(2)}, u32[]{:S(2)}) collective-permute-start(f32[24,768]{1,0:T(8,128)} %get-tuple-element.132), channel_id=1, source_target_pairs={{0,0},{1,13},{2,19},{3,26},{4,7},{5,14},{6,20},{7,5},{8,8},{9,2},{... | collective-permute-start | bytes 221192 | tf_op jit(solution)/shard_map/ppermute | solution.py:1014
  (48 other events, 718.2 us)

commit v5 on v4

--- a/solution.py
+++ b/solution.py
@@ -188,7 +188,7 @@
             for i, mask in enumerate(masks):
                 wo_ref[at_ref[2] ^ mask] = ref[i]
         for slot in range(SLOTS):
-            i = at_ref[2] * SLOTS + (at_ref[1] ^ slot)
+            i = at_ref[2] * SLOTS + slot
             row = jnp.concatenate([got_ref[i, unit : unit + 1], got_ref[i, unit + 1 :]], axis=1)
             row = row.astype(F32).astype(jnp.int32)
             for s in range(seqs):
@@ -240,47 +240,36 @@
     return total
 
 
-def sum_up(up, nt):
-    count, unit, dim = up.shape
-
-    def kernel(up_ref, out_ref):
-        for t in range(nt):
-            out_ref[t] = add_blocks(up_ref, count // nt, nt, t, slice(None))
-
-    return pl.pallas_call(
-        kernel,
-        out_shape=jax.ShapeDtypeStruct((nt, unit, dim), F32),
-        in_specs=[VMEM],
-        out_specs=VMEM,
-        cost_estimate=SMALL,
-        compiler_params=pltpu.CompilerParams(vmem_limit_bytes=32 * MIB),
-        name="sum_up",
-    )(up)
-
-
-def fold(at, low, keep, got):
-    n, high, dim = keep.shape
-
-    def kernel(at_ref, keep_ref, *refs):
-        got_refs, (own_ref, *send_refs) = refs[: len(got)], refs[len(got) :]
+def fold(at, low, terms):
+    n, _, dim = terms[0][0].shape
+    counts = [len(group) for group in terms]
+    rows = [group[0].shape[1] for group in terms]
+
+    def kernel(at_ref, *refs):
+        ins, (own_ref, *send_refs) = refs[: sum(counts)], refs[sum(counts) :]
         mine = (at_ref[2] >> low) & 3
-        for i in range(n // 4):
-            for s, to in enumerate([own_ref] + send_refs):
-                total = keep_ref[i * 4 + (mine ^ s)]
-                for ref in got_refs:
-                    total = total + ref[i * 4 + (mine ^ s)].astype(F32)
-                to[i] = total.astype(to.dtype)
-
-    out = lambda t: jax.ShapeDtypeStruct((n // 4, high, dim), t)
+        k, start = 0, 0
+        for count, high in zip(counts, rows):
+            for i in range(n // 4):
+                for s, to in enumerate([own_ref] + send_refs):
+                    block = i * 4 + (mine ^ s)
+                    total = ins[k][block].astype(F32)
+                    for ref in ins[k + 1 : k + count]:
+                        total = total + ref[block].astype(F32)
+                    to[i, start : start + high] = total.astype(to.dtype)
+            k += count
+            start += high
+
+    out = lambda t: jax.ShapeDtypeStruct((n // 4, sum(rows), dim), t)
     return pl.pallas_call(
         kernel,
         out_shape=[out(F32)] + [out(BF)] * 3,
-        in_specs=[SMEM] + [VMEM] * (1 + len(got)),
+        in_specs=[SMEM] + [VMEM] * sum(counts),
         out_specs=[VMEM] * 4,
         cost_estimate=SMALL,
         compiler_params=pltpu.CompilerParams(vmem_limit_bytes=32 * MIB),
         name="fold",
-    )(at, keep, *got)
+    )(at, *sum(terms, []))
 
 
 def split_rows(odd, grad, send_ref, keep_ref):
@@ -293,33 +282,29 @@
 
 
 def leave(at, table, heads, ff):
-    _, unit, dim = heads[0].shape
-    per = 1 + ff[0].shape[1] // unit
-
-    def kernel(at_ref, table_ref, *refs):
-        terms, refs = refs[: 2 * len(heads)], refs[2 * len(heads) :]
-        out_refs, (all_ref,) = refs[:-1], refs[-1:]
-        for j, group in enumerate((terms[: len(heads)], terms[len(heads) :])):
-            total = group[0][0]
-            for ref in group[1:]:
-                total = total + ref[0].astype(F32)
-            if j == 0:
-                all_ref[0] = total
-            else:
-                for k in range(per - 1):
-                    all_ref[k + 1] = total[k * unit : (k + 1) * unit]
+    per_ff, unit, dim = ff.shape
+    per = 1 + per_ff
+
+    def kernel(at_ref, table_ref, ff_ref, *refs):
+        terms, out_refs, all_ref = refs[: len(heads)], refs[len(heads) : -1], refs[-1]
+        total = terms[0][0]
+        for ref in terms[1:]:
+            total = total + ref[0].astype(F32)
+        all_ref[0] = total
+        for k in range(per_ff):
+            all_ref[k + 1] = ff_ref[k].astype(F32)
         for k, ref in enumerate(out_refs):
             ref[...] = all_ref[table_ref[at_ref[0], per + k]]
 
     return pl.pallas_call(
         kernel,
         out_shape=[jax.ShapeDtypeStruct((unit, dim), F32)] * per,
-        in_specs=[SMEM] * 2 + [VMEM] * (2 * len(heads)),
+        in_specs=[SMEM] * 2 + [VMEM] * (1 + len(heads)),
         out_specs=[VMEM] * per,
         scratch_shapes=[pltpu.VMEM((per, unit, dim), F32)],
         cost_estimate=SMALL,
         name="leave",
-    )(at, table, *heads, *ff)
+    )(at, table, ff, *heads)
 
 
 def place(at, table, qkv, up, got):
@@ -337,7 +322,7 @@
             total = add_blocks(qkv_ref, nb, nt, t, slice(0, unit))
             for k in range(3):
                 in_ref[:, k * nt * local + t * local : k * nt * local + (t + 1) * local] = total[:, k * local : (k + 1) * local]
-            in_ref[:, nt * width + t * dim : nt * width + (t + 1) * dim] = up_ref[t]
+            in_ref[:, nt * width + t * dim : nt * width + (t + 1) * dim] = up_ref[t].astype(F32)
         for k, ref in enumerate(got_refs):
             out_ref[table_ref[at_ref[0], k]] = ref[...]
         small = add_blocks(qkv_ref, count, 1, 0, slice(unit, high))
@@ -399,7 +384,7 @@
     heads, block, last,
     at_ref, ids_ref, qg_ref, kg_ref, wqkv_hbm, wo_hbm, *refs,
 ):
-    pays, refs = refs[:SLOTS], refs[SLOTS:]
+    pays, refs = refs[0], refs[1:]
     if last:
         (acc_sums_ref, fnp_ref, gain_ref, accq_hbm, acco_hbm, hid_hbm, gup_hbm, wff_hbm, wup_hbm), refs = refs[:9], refs[9:]
         (keep_hbm, leave_hbm, sendq_ref, sendo_ref, keepo_ref, sums_ref), refs = refs[:6], refs[6:]
@@ -420,7 +405,7 @@
 
     def pay_copy(s, j, t):
         to = (norm_ref, gb_ref)[j].at[s, pl.ds(t * part, part), :]
-        return pltpu.make_async_copy(pays[t].at[s, j], to, sem.at[s, j * SLOTS + t])
+        return pltpu.make_async_copy(pays.at[t, s, j], to, sem.at[s, j * SLOTS + t])
 
     for s in range(seqs):
         for j in range(2):
@@ -447,7 +432,7 @@
         for s in range(seqs):
             for copy in act_copies(s):
                 copy.start()
-        outs = Outputs(keep_hbm, leave_hbm, res_ref, res_sem, wo_ref, wff_ref, wqkv_ref, wup_ref)
+        outs = Outputs(at_ref[1], keep_hbm, leave_hbm, res_ref, res_sem, wo_ref, wff_ref, wqkv_ref, wup_ref)
         sums_ref[...] = acc_sums_ref[...]
     else:
         gq_ref[...] = jnp.zeros_like(gq_ref)
@@ -618,13 +603,13 @@
     wide, dim = wqkv.shape
     width = wo.shape[0]
     heads = width // HD
-    seqs, _, part, _ = pays[0].shape
+    _, seqs, _, part, _ = pays.shape
     length = part * SLOTS
     block = 512
     blocks = length // block
     last = bool(more)
-    ins = [at, ids, qg, kg, *hbm(wqkv, wo, *pays), *more[:3], *hbm(*more[3:])]
-    specs = [SMEM] + [VMEM] * 3 + [HBM] * (2 + SLOTS) + ([VMEM] * 3 + [HBM] * 6 if last else [])
+    ins = [at, ids, qg, kg, *hbm(wqkv, wo, pays), *more[:3], *hbm(*more[3:])]
+    specs = [SMEM] + [VMEM] * 3 + [HBM] * 3 + ([VMEM] * 3 + [HBM] * 6 if last else [])
     scratch = []
     if last:
         outs = [jax.ShapeDtypeStruct((SLOTS // 2, seqs, 2, part, dim), BF)] * 2
@@ -681,15 +666,15 @@
 
 def ffn_kernel(block, groups, plan, at_ref, wup_hbm, wqkv_hbm, wo_hbm, o_hbm, gq_hbm, *refs):
     pieces, refs = refs[: len(plan)], refs[len(plan) :]
-    pays, refs = refs[: len(groups) * SLOTS], refs[len(groups) * SLOTS :]
-    (hid_hbm, gup_hbm, wff_hbm, keep_hbm, leave_hbm, sendu_ref, sendf_ref, keepf_ref, np_ref), refs = refs[:9], refs[9:]
+    pays, refs = refs[: len(groups)], refs[len(groups) :]
+    (hid_hbm, gup_hbm, wff_hbm, keep_hbm, leave_hbm, send_ref, np_ref), refs = refs[:7], refs[7:]
     norm_ref, gb_ref, hid_ref, gup_ref, wup_ref, wff_ref, gin_ref, gff_ref, sem, out_sem, w_sem, *refs = refs
     wqkv_ref, wo_ref, o_ref, gq_ref, res_ref, res_sem, late_sem = refs
     dim = wup_ref.shape[0]
-    part = pays[0].shape[2]
+    part = pays[0].shape[3]
     total = norm_ref.shape[0]
     weights = [pltpu.make_async_copy(wup_hbm, wup_ref, w_sem.at[0])]
-    rows = sendf_ref.shape[1]
+    rows = send_ref.shape[2]
     for ref, masks in zip(pieces, plan):
         for i, mask in enumerate(masks):
             to = wff_ref.at[pl.ds(pl.multiple_of((at_ref[2] ^ mask) * rows, rows), rows), :]
@@ -701,7 +686,7 @@
         for s in range(seqs):
             for t in range(SLOTS):
                 for k, to in enumerate((norm_ref, gb_ref)):
-                    source = pays[g * SLOTS + t].at[s, k]
+                    source = pays[g].at[t, s, k]
                     pltpu.make_async_copy(source, to.at[pl.ds(n * part, part), :], sem.at[k, n]).start()
                 n += 1
     late = [
@@ -729,7 +714,7 @@
     def step(i, carry):
         for j in range(block // part):
             for k, to in enumerate((norm_ref, gb_ref)):
-                pltpu.make_async_copy(pays[0].at[0, 0], to.at[pl.ds(0, part), :], sem.at[k, i * (block // part) + j]).wait()
+                pltpu.make_async_copy(pays[0].at[0, 0, 0], to.at[pl.ds(0, part), :], sem.at[k, i * (block // part) + j]).wait()
         at_rows = pl.ds(pl.multiple_of(i * block, block), block)
         up = mm(norm_ref[at_rows, :], wup_ref[...])
         gh = mm(gb_ref[at_rows, :], wff_ref[...], NT)
@@ -747,15 +732,16 @@
     lax.fori_loop(0, total // block, step, 0)
     for copy in late:
         copy.wait()
-    results = Outputs(keep_hbm, leave_hbm, res_ref, res_sem, wo_ref, wff_ref, wqkv_ref, wup_ref)
+    results = Outputs(at_ref[1], keep_hbm, leave_hbm, res_ref, res_sem, wo_ref, wff_ref, wqkv_ref, wup_ref)
     length = SLOTS * part
     for s in range(results.seqs):
         rows_s = pl.ds(s * length, length)
         results.compute(s, o_ref.at[s], hid_ref.at[rows_s, :], gq_ref.at[s], gup_ref.at[rows_s, :])
     line = jnp.sum(wup_ref[...].astype(F32) * gin_ref[...], axis=1, keepdims=True)
     np_ref[...] = jnp.broadcast_to(line, (dim, 128)).T[0:1]
-    sendu_ref[...] = gin_ref[...].astype(BF)
-    split_rows((at_ref[2] & 1) > 0, gff_ref[...], sendf_ref, keepf_ref)
+    for b in range(dim // rows):
+        for k, g in enumerate((gin_ref, gff_ref)):
+            send_ref[b, k] = g[b * rows : (b + 1) * rows, :].astype(BF)
     joined.wait()
     results.wait()
 
@@ -769,10 +755,10 @@
 
 def ffn(at, wup, ff_parts, groups, count, wqkv, wo, o, gq, block=512):
     dim, units = wup.shape
-    sizes = [g[0].shape[0] for g in groups]
-    part = groups[0][0].shape[2]
+    sizes = [g.shape[1] for g in groups]
+    part = groups[0].shape[3]
     total = SLOTS * part * sum(sizes)
-    pieces = [p for g in groups for p in g]
+    pieces = groups
     act = jax.ShapeDtypeStruct((total, units), BF)
     return pl.pallas_call(
         functools.partial(ffn_kernel, block, sizes, [masks for _, masks in ff_parts]),
@@ -781,13 +767,11 @@
             act,
             jax.ShapeDtypeStruct((units, dim), BF),
             *[jax.ShapeDtypeStruct((SLOTS // 2, o.shape[0], 2, part, dim), BF)] * 2,
-            jax.ShapeDtypeStruct((dim, units), BF),
-            jax.ShapeDtypeStruct((count // 2, units // count, dim), BF),
-            jax.ShapeDtypeStruct((count // 2, units // count, dim), F32),
+            jax.ShapeDtypeStruct((count, 2, units // count, dim), BF),
             jax.ShapeDtypeStruct((1, dim), F32),
         ],
         in_specs=[SMEM] + [HBM] * (5 + len(ff_parts) + len(pieces)),
-        out_specs=[HBM] * 5 + [VMEM] * 4,
+        out_specs=[HBM] * 5 + [VMEM] * 2,
         scratch_shapes=[
             pltpu.VMEM((total, dim), BF),
             pltpu.VMEM((total, dim), BF),
@@ -811,7 +795,8 @@
 
 
 class Outputs:
-    def __init__(self, keep, send, res, sem, wo, wff, wqkv, wup):
+    def __init__(self, me, keep, send, res, sem, wo, wff, wqkv, wup):
+        self.me = me
         self.keep, self.send, self.res, self.sem = keep, send, res, sem
         self.wo, self.wff, self.wqkv, self.wup = wo, wff, wqkv, wup
         self.seqs, _, self.length, _ = res.shape
@@ -826,8 +811,9 @@
         out = []
         for j in range(2):
             for k, to in enumerate((self.keep, self.send)):
-                rows = pl.ds(pl.multiple_of(i * half + k * part, part), part)
-                out.append(pltpu.make_async_copy(self.res.at[s, j, rows, :], to.at[i, s, j], self.sem.at[s, j, 2 * i + k]))
+                rows = pl.ds(pl.multiple_of(i * half + (k ^ (self.me & 1)) * part, part), part)
+                source = self.res.at[s, j, rows, :]
+                out.append(pltpu.make_async_copy(source, to.at[i ^ (self.me >> 1), s, j], self.sem.at[s, j, 2 * i + k]))
         return out
 
     def compute(self, s, o, hid, gq, gu):
@@ -955,22 +941,20 @@
 
     groups = bit_groups(nb)
 
-    lead = 1
+    lead = 2
     a_src, u_src = prepare(image_ids, in_weight, nb, nt)
     a_got = exchange(a_src.reshape(nb * nt, rows_in + 2, 3 * local), both)
     own0, own1, *unit_sends = before(
         at, table, out_weight.reshape(per, unit, dim), image_ids, gain, tie(patches, a_src), cotangent, lead
     )
     got = [lax.ppermute(v, both, perm) for v, perm in zip(unit_sends, perms)]
-    wo_src, ff_src = pack_out(at, table, got)
-    far0 = swap(tie(own0, *got), "tok", nt, 2)
+    wo_src, ff_src = pack_out(at, table, tie(got, a_got))
+    slots0 = lax.all_gather(own0, "tok", axis=0)
+    slots1 = lax.all_gather(own1, "tok", axis=0)
     wo_parts = gather_batch(wo_src, nb, groups)
     ff_parts = gather_batch(ff_src.reshape((per - 1) * unit, dim), nb, groups[::-1])
     wqkv, wo, ids = join(at, a_got, wo_parts, seqs, part)
     wo = wo.reshape(local, dim)
-    far1 = swap(tie(own1, far0), "tok", nt, 2)
-    slots0 = [own0, swap(own0, "tok", nt, 1), far0, swap(far0, "tok", nt, 1)]
-    slots1 = [own1, swap(own1, "tok", nt, 1), far1, swap(far1, "tok", nt, 1)]
     wup = exchange(tie(u_src, a_got).reshape(nb * nt, unit, dim), both).reshape(dim, units)
 
     qg = query_gain.reshape(HD, 1)
@@ -980,37 +964,30 @@
         value = (keep[1].astype(F32) + near[1].astype(F32)).astype(BF)
         return value, swap(tie(value, *hold) if hold else value, "tok", nt, 2)
 
-    def reduce_batch(keep, came):
-        terms = [keep, came]
-        for bits in groups[:-1][::-1]:
-            own, *sends = fold(at, bits[-1], terms[0], terms[1:])
-            terms = [own] + [swap(value, "batch", nb, (s + 1) << bits[-1]) for s, value in enumerate(sends)]
-        return terms
-
     o0, gq0, sums, acc_q, acc_o = attention(at, ids[:lead], wqkv, tie(wo, ff_parts[0][0]), qg, kg, slots0, nb * nt)
-    hid, gup, wff, keep0, send0, f_up, f_send, f_keep, f_np = ffn(
-        at, wup, ff_parts, [slots0, slots1], nb, wqkv, wo, o0, gq0
+    hid, gup, wff, keep0, send0, f_grad, f_np = ffn(
+        at, tie(wup, o0), ff_parts, [slots0, slots1], nb, wqkv, wo, o0, gq0
     )
-    f_up = exchange(f_up.reshape(nb * nt, unit, dim), both)
-    f_came = swap(f_send, "batch", nb, 1)
+    f_mine = lax.psum_scatter(f_grad, "batch", scatter_dimension=0, tiled=True).reshape(2, nt, unit, dim)
     near0 = swap(send0, "tok", nt, 1)
     value0, away0 = leave_chip(keep0, near0)
     keep1, send1, a_q, a_send, a_keep = attention(
         at, ids[lead:], wqkv, tie(wo, value0), qg, kg, slots1, nb * nt,
         (sums, f_np, gain, acc_q, acc_o, hid, gup, wff, wup),
     )
-    send1, a_q, a_send = (tie(value, f_up, f_came, away0) for value in (send1, a_q, a_send))
-    a_q = exchange(a_q, both)
     a_came = swap(a_send, "batch", nb, 1)
-    near1 = swap(send1, "tok", nt, 1)
-    ff_terms = reduce_batch(f_keep, f_came)
-    o_terms = reduce_batch(a_keep, a_came)
-    value1, away1 = leave_chip(keep1, tie(near1, a_came))
-    up = sum_up(f_up, nt)
+    terms = [a_keep, a_came]
+    for bits in groups[:-1][::-1]:
+        own, *sends = fold(at, bits[-1], [terms])
+        terms = [own] + [swap(value, "batch", nb, (s + 1) << bits[-1]) for s, value in enumerate(sends)]
+    near1 = swap(tie(send1, away0, *terms[1:]), "tok", nt, 1)
+    a_q = exchange(tie(a_q, *terms[1:]), both)
+    value1, away1 = leave_chip(keep1, near1)
+    up = exchange(tie(f_mine[0], a_q), "tok")
     group = [(0, s, keep0, near0, away0) for s in range(lead)]
     group += [(lead, s, keep1, near1, away1) for s in range(lead, seqs)]
 
-    sends = leave(at, table, o_terms, ff_terms)
+    sends = leave(at, table, terms, f_mine[1])
     got = [lax.ppermute(v, both, [(b, a) for a, b in perm]) for v, perm in zip(sends, perms)]
     in_grad, out_grad, norm_grad, query_grad, key_grad = place(at, table, a_q, up, got)
 

time: 324 us -> 301 us (0.929)
  waiting for transfers between devices: 82.7 us -> 65 us
  starting transfers between devices: 92 us -> 75 us
  between operations: 1.17 us -> 14.2 us
    ppermute x26 -> x16, waiting for transfers between devices: 79 us -> 21.9 us  [swap(): return lax.ppermute(value, axis, [(i, i ^ mask) for i in range(count)])]
    all_to_all x4, waiting for transfers between devices: 0.01 us -> 22.4 us  [exchange(): return lax.all_to_all(value, axis, split_axis=0, concat_axis=0, tiled=True)]
    reduce_scatter x0 -> x1, waiting for transfers between devices: none -> 15.7 us  [per_device(): lax.psum_scatter(f_grad, 'batch', scatter_dimension=0, tiled=True)]
    ppermute x26 -> x16, starting transfers between devices: 30.6 us -> 21 us  [swap(): return lax.ppermute(value, axis, [(i, i ^ mask) for i in range(count)])]
    all_to_all x4, starting transfers between devices: 26.3 us -> 18.5 us  [exchange(): return lax.all_to_all(value, axis, split_axis=0, concat_axis=0, tiled=True)]
    pallas_call x1, Pallas kernels: 30.4 us -> 35.1 us  [ffn(): pl.pallas_call(functools.partial(ffn_kernel, block, sizes, [masks for _,...]
    pallas_call x2, Pallas kernels: 72.8 us -> 68.7 us  [attention(): pl.pallas_call(functools.partial(attention_kernel, heads, block, last), o...]
    unnamed x64 -> x50, local copies, waits for them, and re-layouts: 6.73 us -> 3.33 us
  transfers between devices with their start and end apart: 40 -> 33, of which waited for: 12 -> 14; matrix products, arithmetic and copies ran while one was open for 3% -> 4% of each run, Pallas kernels for 26% -> 28%
where the time goes in v5:
time: 301 us; the launch traced here: 298 us
  Pallas kernels  128 us (43%)
  starting transfers between devices  75 us (25%)
  waiting for transfers between devices  65 us (22%)
  between operations  14.2 us (5%)
  local copies, waits for them, and re-layouts  8.91 us (3%)
  other arithmetic  6.41 us (2%)
    pallas_call x2, Pallas kernels, attention(): pl.pallas_call(functools.partial(attention_kernel, heads, block, last), o...  68.7 us
    pallas_call x1, Pallas kernels, ffn(): pl.pallas_call(functools.partial(ffn_kernel, block, sizes, [masks for _,...  35.1 us
    all_to_all x4, waiting for transfers between devices, exchange(): return lax.all_to_all(value, axis, split_axis=0, concat_axis=0, tiled=True)  22.4 us
    ppermute x16, waiting for transfers between devices, swap(): return lax.ppermute(value, axis, [(i, i ^ mask) for i in range(count)])  21.9 us
    ppermute x16, starting transfers between devices, swap(): return lax.ppermute(value, axis, [(i, i ^ mask) for i in range(count)])  21 us
    ppermute x5, starting transfers between devices, per_device(): got = [lax.ppermute(v, both, perm) for v, perm in zip(unit_sends, perms)]  20 us
    all_to_all x4, starting transfers between devices, exchange(): return lax.all_to_all(value, axis, split_axis=0, concat_axis=0, tiled=True)  18.5 us
    reduce_scatter x1, waiting for transfers between devices, per_device(): lax.psum_scatter(f_grad, 'batch', scatter_dimension=0, tiled=True)  15.7 us
  transfers between devices with their start and end apart: 33, of which 14 were waited for; matrix products, arithmetic and copies ran while one was open for 4% of the time, Pallas kernels for 28%

profile of v5, /device:TPU:2, one launch (start us, length us, event | category | flops | bytes accessed | tf_op | source)
XLA Modules:
  0.0 297.6 jit_solution(13311473433740897430)
XLA Ops:
  11.2 4.2 %before.1 = (bf16[2,2,256,768]{3,2,1,0:T(8,128)(2,1)}, bf16[1,2,256,768]{3,2,1,0:T(8,128)(2,1)}, bf16[24,768]{1,0:T(8,128)(2,1)S(1)}, bf16[24,768]{1,0:T(8,128)(...) custom-call(s32[3]{0:T(128)S(1)} %pad_add_fusion.at_ref, ...), custom_call_target="tpu_custom_call" | custom-call | flops 1 | bytes 1 | tf_op jit(solution)/shard_map/before/pallas_call | solution.py:148
  15.4 6.1 %all-to-all-start = ((bf16[32,26,576]{2,1,0:T(8,128)(2,1)}), bf16[32,26,576]{2,1,0:T(8,128)(2,1)S(1)}, u32[]{:S(2)}, u32[]{:S(2)}) async-start(bf16[32,26,576]{2,1,0:T(8,128)(2,1)} %bitcast.3), calls=%async_computation | async-start | bytes 2621440 | tf_op jit(solution)/shard_map/all_to_all | solution.py:940
  21.6 5.2 %collective-permute-start = (bf16[24,768]{1,0:T(8,128)(2,1)S(1)}, bf16[24,768]{1,0:T(8,128)(2,1)S(1)}, u32[]{:S(2)}, u32[]{:S(2)}) collective-permute-start(bf16[24,768]{1,0:T(8,128)(2,1)S(1)} %get-tuple-element.73), channel_id=1, source_target_pairs={{7,0},{13,1},{3,2},{26,3},{0,4},{14,5},{20,6},{27,7},{8,8},{15,9},... | collective-permute-start | bytes 110600 | tf_op jit(solution)/shard_map/ppermute | solution.py:950
  29.9 3.7 %collective-permute-start.2 = (bf16[24,768]{1,0:T(8,128)(2,1)S(1)}, bf16[24,768]{1,0:T(8,128)(2,1)S(1)}, u32[]{:S(2)}, u32[]{:S(2)}) collective-permute-start(bf16[24,768]{1,0:T(8,128)(2,1)S(1)} %get-tuple-element.75), channel_id=1, source_target_pairs={{6,0},{13,1},{19,2},{4,3},{7,4},{1,5},{20,6},{26,7},{8,8},{14,9},{... | collective-permute-start | bytes 110600 | tf_op jit(solution)/shard_map/ppermute | solution.py:950
  36.3 5.2 %collective-permute-start.4 = (bf16[24,768]{1,0:T(8,128)(2,1)S(1)}, bf16[24,768]{1,0:T(8,128)(2,1)S(1)}, u32[]{:S(2)}, u32[]{:S(2)}) collective-permute-start(bf16[24,768]{1,0:T(8,128)(2,1)S(1)} %get-tuple-element.77), channel_id=1, source_target_pairs={{6,0},{12,1},{19,2},{25,3},{7,4},{13,5},{3,6},{26,7},{0,8},{14,9},... | collective-permute-start | bytes 110600 | tf_op jit(solution)/shard_map/ppermute | solution.py:950
  46.4 9.4 %all-to-all-done.got_ref = bf16[32,26,576]{2,1,0:T(8,128)(2,1)S(1)} async-done(((bf16[32,26,576]{2,1,0:T(8,128)(2,1)}), bf16[32,26,576]{2,1,0:T(8,128)(2,1)S(1)}, u32[]{:S(2)}, u32[]{:S(2)}) %all-to-all-start) | async-done | bytes 958496 | tf_op jit(solution)/shard_map/all_to_all | solution.py:940
  57.6 3.3 %collective-permute-start.7 = (bf16[1,24,768]{2,1,0:T(8,128)(2,1)}, bf16[1,24,768]{2,1,0:T(8,128)(2,1)S(1)}, u32[]{:S(2)}, u32[]{:S(2)}) collective-permute-start(bf16[1,24,768]{2,1,0:T(8,128)(2,1)} %bitcast.32), channel_id=1, source_target_pairs={{0,24},{4,28},{8,16},{12,20},{16,8},{20,12},{24,0},{28,4},{1,25},{... | collective-permute-start | bytes 110600 | tf_op jit(solution)/shard_map/ppermute | solution.py:842
  70.8 4.8 %all-to-all-start.1 = ((bf16[32,24,768]{2,1,0:T(8,128)(2,1)}), bf16[32,24,768]{2,1,0:T(8,128)(2,1)S(1)}, u32[]{:S(2)}, u32[]{:S(2)}) async-start(bf16[32,24,768]{2,1,0:T(8,128)(2,1)} %bitcast.9), calls=%async_computation.1 | async-start | bytes 2359296 | tf_op jit(solution)/shard_map/all_to_all | solution.py:940
  75.9 3.4 %collective-permute-start.12 = (bf16[2,96,768]{2,1,0:T(8,128)(2,1)S(1)}, bf16[2,96,768]{2,1,0:T(8,128)(2,1)}, u32[]{:S(2)}, u32[]{:S(2)}) collective-permute-start(bf16[2,96,768]{2,1,0:T(8,128)(2,1)S(1)} %pad_maximum_fusion.refs_0_), channel_id=1, source_target_pairs={{0,24},{4,28},{8,16},{12,20},{16,8},{20,12},{24,0},{28,4},{1,25},{... | collective-permute-start | bytes 884744 | tf_op jit(solution)/shard_map/ppermute | solution.py:842
  83.7 41.6 %attention.2 = (bf16[2,192,1024]{2,1,0:T(8,128)(2,1)}, bf16[2,576,1024]{2,1,0:T(8,128)(2,1)}, f32[2,64,128]{2,1,0:T(8,128)}, f32[576,768]{1,0:T(8,128)}, f32[192,768]{1,0:T(8,128)}) custom-call(s32[3]{0:T(128)} %copy-done.5, s32[2,1,1024]{2,1,0:T(1,128)} %slice.27.ids_ref, f32[64,1]{1,0:T(8,128)} %copy.26.qg_ref, f32[64,1]{1,0:T(8,128)} %copy.27.kg_ref, ...), custom_call_target="tpu_custom_call" | custom-call | flops 60000002048 | bytes 1 | tf_op jit(solution)/shard_map/attention/pallas_call | solution.py:629
  125.4 4.4 %collective-permute-done.11.refs_2_ = bf16[2,96,768]{2,1,0:T(8,128)(2,1)} collective-permute-done((bf16[2,96,768]{2,1,0:T(8,128)(2,1)S(1)}, bf16[2,96,768]{2,1,0:T(8,128)(2,1)}, u32[]{:S(2)}, u32[]{:S(2)}) %collective-permute-start.11) | collective-permute-done | bytes 294944 | tf_op jit(solution)/shard_map/ppermute | solution.py:842
  129.8 35.1 %ffn.1 = (bf16[3072,768]{1,0:T(8,128)(2,1)}, bf16[3072,768]{1,0:T(8,128)(2,1)}, bf16[768,768]{1,0:T(8,128)(2,1)}, bf16[2,2,2,256,768]{4,3,2,1,0:T(8,128)(2,1)}, ...) custom-call(s32[3]{0:T(128)} %copy-done.5, bf16[768,768]{1,0:T(8,128)(2,1)} %bitcast.26, ...), custom_call_target="tpu_custom_call" | custom-call | flops 60000002048 | bytes 1 | tf_op jit(solution)/shard_map/ffn/pallas_call | solution.py:763
  165.6 5.4 %collective-permute-done.13.near_ref = bf16[2,2,2,256,768]{4,3,2,1,0:T(8,128)(2,1)} collective-permute-done((bf16[2,2,2,256,768]{4,3,2,1,0:T(8,128)(2,1)}, bf16[2,2,2,256,768]{4,3,2,1,0:T(8,128)(2,1)}, u32[]{:S(2)}, u32[]{:S(2)}) %collective-permute-start.13) | collective-permute-done | bytes 3145760 | tf_op jit(solution)/shard_map/ppermute | solution.py:842
  174.9 27.1 %attention.3 = (bf16[2,1,2,256,768]{4,3,2,1,0:T(8,128)(2,1)}, bf16[2,1,2,256,768]{4,3,2,1,0:T(8,128)(2,1)}, bf16[32,28,576]{2,1,0:T(8,128)(2,1)}, bf16[4,24,768]{2,1,0:T(8,128)(2,1)}, f32[4,24,768]{2,1,0:T(8,128)}) custom-call(s32[3]{0:T(128)} %copy-done.5, s32[1,1,1024]{2,1,0:T(1,128)} %slice.26.ids_ref, f32[64,1]{1,0:T(8,128)} %copy.26.qg_ref, ...), custom_call_target="tpu_custom_call" | custom-call | flops 60000002048 | bytes 1 | tf_op jit(solution)/shard_map/attention/pallas_call | solution.py:629
  202.7 6.2 %collective-permute-done.15.refs_1_ = bf16[4,24,768]{2,1,0:T(8,128)(2,1)S(1)} collective-permute-done((bf16[4,24,768]{2,1,0:T(8,128)(2,1)}, bf16[4,24,768]{2,1,0:T(8,128)(2,1)S(1)}, u32[]{:S(2)}, u32[]{:S(2)}) %collective-permute-start.15) | collective-permute-done | bytes 147488 | tf_op jit(solution)/shard_map/ppermute | solution.py:842
  218.8 4.2 %all-to-all-start.2 = ((bf16[32,28,576]{2,1,0:T(8,128)(2,1)}), bf16[32,28,576]{2,1,0:T(8,128)(2,1)S(1)}, u32[]{:S(2)}, u32[]{:S(2)}) async-start(bf16[32,28,576]{2,1,0:T(8,128)(2,1)} %get-tuple-element.121), calls=%async_computation.2 | async-start | bytes 2621440 | tf_op jit(solution)/shard_map/all_to_all | solution.py:940
  227.0 15.7 %reduce-scatter.2.cloned.1.call-done = bf16[1,2,96,768]{3,2,1,0:T(8,128)(2,1)} async-done(((bf16[8,2,96,768]{3,2,1,0:T(8,128)(2,1)}), bf16[1,2,96,768]{3,2,1,0:T(8,128)(2,1)}) %reduce-scatter.2.cloned.1.call-update) | async-done | bytes 294928 | tf_op jit(solution)/shard_map/reduce_scatter | solution.py:971
  248.3 13.1 %all-to-all-done.2.qkv_ref = bf16[32,28,576]{2,1,0:T(8,128)(2,1)S(1)} async-done(((bf16[32,28,576]{2,1,0:T(8,128)(2,1)}), bf16[32,28,576]{2,1,0:T(8,128)(2,1)S(1)}, u32[]{:S(2)}, u32[]{:S(2)}) %all-to-all-start.2) | async-done | bytes 1032224 | tf_op jit(solution)/shard_map/all_to_all | solution.py:940
  261.3 3.3 %all-to-all-start.3 = ((bf16[4,24,768]{2,1,0:T(8,128)(2,1)}), bf16[4,24,768]{2,1,0:T(8,128)(2,1)S(1)}, u32[]{:S(2)}, u32[]{:S(2)}) async-start(bf16[4,24,768]{2,1,0:T(8,128)(2,1)} %bitcast.16), calls=%async_computation.4 | async-start | bytes 294912 | tf_op jit(solution)/shard_map/all_to_all | solution.py:940
  264.7 3.6 %collective-permute-start.22 = (f32[24,768]{1,0:T(8,128)}, f32[24,768]{1,0:T(8,128)S(1)}, u32[]{:S(2)}, u32[]{:S(2)}) collective-permute-start(f32[24,768]{1,0:T(8,128)} %get-tuple-element.126), channel_id=1, source_target_pairs={{0,0},{1,13},{2,19},{3,26},{4,7},{5,14},{6,20},{7,5},{8,8},{9,2},{... | collective-permute-start | bytes 221192 | tf_op jit(solution)/shard_map/ppermute | solution.py:991
  273.0 5.0 %collective-permute-start.25 = (f32[24,768]{1,0:T(8,128)}, f32[24,768]{1,0:T(8,128)S(1)}, u32[]{:S(2)}, u32[]{:S(2)}) collective-permute-start(f32[24,768]{1,0:T(8,128)} %get-tuple-element.129), channel_id=1, source_target_pairs={{0,6},{1,12},{2,19},{3,25},{4,7},{5,13},{6,3},{7,26},{8,0},{9,14},... | collective-permute-start | bytes 221192 | tf_op jit(solution)/shard_map/ppermute | solution.py:991
  278.1 3.5 %after.3 = (bf16[3,256,768]{2,1,0:T(8,128)(2,1)}, bf16[3,256,768]{2,1,0:T(8,128)(2,1)}) custom-call(s32[3,256]{1,0:T(4,128)S(1)} %copy-done.2, bf16[3,256,768]{2,1,0:T(8,128)(2,1)} %x_ref.5, bf16[3,256,768]{2,1,0:T(8,128)(2,1)} %cot_ref.5, f32[1,768]{1,0:T(1,128)S(1)} %copy-done.3, bf16[2,2,2,256,768]{4,3,2,1,0:T(8,128)(2,1)} %get-tuple-element.96.keep_ref, ...), custom_call_target="tpu_custom_call" | custom-call | flops 1 | bytes 1 | tf_op jit(solution)/shard_map/after/pallas_call | solution.py:370
  281.5 3.5 %after.4 = (bf16[3,256,768]{2,1,0:T(8,128)(2,1)}, bf16[3,256,768]{2,1,0:T(8,128)(2,1)}) custom-call(s32[3,256]{1,0:T(4,128)S(1)} %copy-done.2, bf16[3,256,768]{2,1,0:T(8,128)(2,1)} %x_ref.5, bf16[3,256,768]{2,1,0:T(8,128)(2,1)} %cot_ref.5, f32[1,768]{1,0:T(1,128)S(1)} %copy-done.3, ...), custom_call_target="tpu_custom_call", output_to_operand_aliasing={{0}: (7, {}), {1}: (8, {})} | custom-call | flops 1 | bytes 1 | tf_op jit(solution)/shard_map/after/pallas_call | solution.py:370
  287.6 3.5 %after.5 = (bf16[3,256,768]{2,1,0:T(8,128)(2,1)}, bf16[3,256,768]{2,1,0:T(8,128)(2,1)}) custom-call(s32[3,256]{1,0:T(4,128)S(1)} %copy-done.2, bf16[3,256,768]{2,1,0:T(8,128)(2,1)} %x_ref.5, bf16[3,256,768]{2,1,0:T(8,128)(2,1)} %cot_ref.5, f32[1,768]{1,0:T(1,128)S(1)} %copy-done.3, ...), custom_call_target="tpu_custom_call", output_to_operand_aliasing={{0}: (7, {}), {1}: (8, {})} | custom-call | flops 1 | bytes 1 | tf_op jit(solution)/shard_map/after/pallas_call | solution.py:370
  (120 shorter events, 62.9 us)
Async XLA Ops:
  7.2 76.6 %all-gather.5.cloned.1.call-start = ((), (), s32[]{:S(2)}) async-start(), calls=%async_computation.6 | async-start | bytes 7864320 | tf_op jit(solution)/shard_map/all_gather | solution.py:952
  15.4 40.4 %all-to-all-start = ((bf16[32,26,576]{2,1,0:T(8,128)(2,1)}), bf16[32,26,576]{2,1,0:T(8,128)(2,1)S(1)}, u32[]{:S(2)}, u32[]{:S(2)}) async-start(bf16[32,26,576]{2,1,0:T(8,128)(2,1)} %bitcast.3), calls=%async_computation | async-start | bytes 2621440 | tf_op jit(solution)/shard_map/all_to_all | solution.py:940
  21.5 108.3 %all-gather.7.cloned.1.call-start = ((), (), s32[]{:S(2)}) async-start(), calls=%async_computation.7 | async-start | bytes 3932160 | tf_op jit(solution)/shard_map/all_gather | solution.py:953
  21.6 22.9 %collective-permute-start = (bf16[24,768]{1,0:T(8,128)(2,1)S(1)}, bf16[24,768]{1,0:T(8,128)(2,1)S(1)}, u32[]{:S(2)}, u32[]{:S(2)}) collective-permute-start(bf16[24,768]{1,0:T(8,128)(2,1)S(1)} %get-tuple-element.73), channel_id=1, source_target_pairs={{7,0},{13,1},{3,2},{26,3},{0,4},{14,5},{20,6},{27,7},{8,8},{15,9},... | collective-permute-start | bytes 110600 | tf_op jit(solution)/shard_map/ppermute | solution.py:950
  26.8 18.5 %collective-permute-start.1 = (bf16[24,768]{1,0:T(8,128)(2,1)S(1)}, bf16[24,768]{1,0:T(8,128)(2,1)S(1)}, u32[]{:S(2)}, u32[]{:S(2)}) collective-permute-start(bf16[24,768]{1,0:T(8,128)(2,1)S(1)} %get-tuple-element.74), channel_id=1, source_target_pairs={{0,0},{13,1},{19,2},{26,3},{7,4},{14,5},{20,6},{5,7},{8,8},{2,9},{... | collective-permute-start | bytes 110600 | tf_op jit(solution)/shard_map/ppermute | solution.py:950
  29.9 15.3 %collective-permute-start.2 = (bf16[24,768]{1,0:T(8,128)(2,1)S(1)}, bf16[24,768]{1,0:T(8,128)(2,1)S(1)}, u32[]{:S(2)}, u32[]{:S(2)}) collective-permute-start(bf16[24,768]{1,0:T(8,128)(2,1)S(1)} %get-tuple-element.75), channel_id=1, source_target_pairs={{6,0},{13,1},{19,2},{4,3},{7,4},{1,5},{20,6},{26,7},{8,8},{14,9},{... | collective-permute-start | bytes 110600 | tf_op jit(solution)/shard_map/ppermute | solution.py:950
  33.6 12.4 %collective-permute-start.3 = (bf16[24,768]{1,0:T(8,128)(2,1)S(1)}, bf16[24,768]{1,0:T(8,128)(2,1)S(1)}, u32[]{:S(2)}, u32[]{:S(2)}) collective-permute-start(bf16[24,768]{1,0:T(8,128)(2,1)S(1)} %get-tuple-element.76), channel_id=1, source_target_pairs={{6,0},{1,1},{19,2},{25,3},{7,4},{13,5},{20,6},{26,7},{8,8},{14,9},... | collective-permute-start | bytes 110600 | tf_op jit(solution)/shard_map/ppermute | solution.py:950
  36.3 10.1 %collective-permute-start.4 = (bf16[24,768]{1,0:T(8,128)(2,1)S(1)}, bf16[24,768]{1,0:T(8,128)(2,1)S(1)}, u32[]{:S(2)}, u32[]{:S(2)}) collective-permute-start(bf16[24,768]{1,0:T(8,128)(2,1)S(1)} %get-tuple-element.77), channel_id=1, source_target_pairs={{6,0},{12,1},{19,2},{25,3},{7,4},{13,5},{3,6},{26,7},{0,8},{14,9},... | collective-permute-start | bytes 110600 | tf_op jit(solution)/shard_map/ppermute | solution.py:950
  63.1 12.8 %collective-permute-start.9 = (bf16[1,96,768]{2,1,0:T(8,128)(2,1)}, bf16[1,96,768]{2,1,0:T(8,128)(2,1)S(1)}, u32[]{:S(2)}, u32[]{:S(2)}) collective-permute-start(bf16[1,96,768]{2,1,0:T(8,128)(2,1)} %bitcast.30), channel_id=1, source_target_pairs={{0,4},{4,0},{8,12},{12,8},{16,20},{20,16},{24,28},{28,24},{1,5},{5... | collective-permute-start | bytes 442376 | tf_op jit(solution)/shard_map/ppermute | solution.py:842
  67.5 12.9 %collective-permute-start.8 = (bf16[4,24,768]{2,1,0:T(8,128)(2,1)S(1)}, bf16[4,24,768]{2,1,0:T(8,128)(2,1)S(1)}, u32[]{:S(2)}, u32[]{:S(2)}) collective-permute-start(bf16[4,24,768]{2,1,0:T(8,128)(2,1)S(1)} %pad_maximum_fusion.1.refs_0_), channel_id=1, source_target_pairs={{0,4},{4,0},{8,12},{12,8},{16,20},{20,16},{24,28},{28,24},{1,5},{5... | collective-permute-start | bytes 442376 | tf_op jit(solution)/shard_map/ppermute | solution.py:842
  70.8 54.5 %all-to-all-start.1 = ((bf16[32,24,768]{2,1,0:T(8,128)(2,1)}), bf16[32,24,768]{2,1,0:T(8,128)(2,1)S(1)}, u32[]{:S(2)}, u32[]{:S(2)}) async-start(bf16[32,24,768]{2,1,0:T(8,128)(2,1)} %bitcast.9), calls=%async_computation.1 | async-start | bytes 2359296 | tf_op jit(solution)/shard_map/all_to_all | solution.py:940
  75.6 167.1 %reduce-scatter.2.cloned.1.call-start = ((), (), s32[]{:S(2)}) async-start(), calls=%async_computation.5 | async-start | bytes 2654208 | tf_op jit(solution)/shard_map/reduce_scatter | solution.py:971
  75.9 49.4 %collective-permute-start.12 = (bf16[2,96,768]{2,1,0:T(8,128)(2,1)S(1)}, bf16[2,96,768]{2,1,0:T(8,128)(2,1)}, u32[]{:S(2)}, u32[]{:S(2)}) collective-permute-start(bf16[2,96,768]{2,1,0:T(8,128)(2,1)S(1)} %pad_maximum_fusion.refs_0_), channel_id=1, source_target_pairs={{0,24},{4,28},{8,16},{12,20},{16,8},{20,12},{24,0},{28,4},{1,25},{... | collective-permute-start | bytes 884744 | tf_op jit(solution)/shard_map/ppermute | solution.py:842
  79.3 50.4 %collective-permute-start.11 = (bf16[2,96,768]{2,1,0:T(8,128)(2,1)S(1)}, bf16[2,96,768]{2,1,0:T(8,128)(2,1)}, u32[]{:S(2)}, u32[]{:S(2)}) collective-permute-start(bf16[2,96,768]{2,1,0:T(8,128)(2,1)S(1)} %pad_maximum_fusion.refs_0_), channel_id=1, source_target_pairs={{0,16},{4,20},{8,24},{12,28},{16,0},{20,4},{24,8},{28,12},{1,17},{... | collective-permute-start | bytes 884744 | tf_op jit(solution)/shard_map/ppermute | solution.py:842
  79.3 50.4 %collective-permute-start.10 = (bf16[2,96,768]{2,1,0:T(8,128)(2,1)S(1)}, bf16[2,96,768]{2,1,0:T(8,128)(2,1)}, u32[]{:S(2)}, u32[]{:S(2)}) collective-permute-start(bf16[2,96,768]{2,1,0:T(8,128)(2,1)S(1)} %pad_maximum_fusion.refs_0_), channel_id=1, source_target_pairs={{0,8},{4,12},{8,0},{12,4},{16,24},{20,28},{24,16},{28,20},{1,9},{5... | collective-permute-start | bytes 884744 | tf_op jit(solution)/shard_map/ppermute | solution.py:842
  173.4 45.3 %collective-permute-start.14 = (bf16[2,2,256,768]{3,2,1,0:T(8,128)(2,1)S(1)}, bf16[2,2,256,768]{3,2,1,0:T(8,128)(2,1)S(1)}, u32[]{:S(2)}, u32[]{:S(2)}) collective-permute-start(bf16[2,2,256,768]{3,2,1,0:T(8,128)(2,1)S(1)} %fusion), channel_id=1, source_target_pairs={{0,2},{1,3},{2,0},{3,1},{4,6},{5,7},{6,4},{7,5},{8,10},{9,11},{10,... | collective-permute-start | bytes 4718600 | tf_op jit(solution)/shard_map/ppermute | solution.py:842
  218.8 42.5 %all-to-all-start.2 = ((bf16[32,28,576]{2,1,0:T(8,128)(2,1)}), bf16[32,28,576]{2,1,0:T(8,128)(2,1)S(1)}, u32[]{:S(2)}, u32[]{:S(2)}) async-start(bf16[32,28,576]{2,1,0:T(8,128)(2,1)} %get-tuple-element.121), calls=%async_computation.2 | async-start | bytes 2621440 | tf_op jit(solution)/shard_map/all_to_all | solution.py:940
  225.5 62.1 %collective-permute-start.20 = (bf16[1,2,256,768]{3,2,1,0:T(8,128)(2,1)}, bf16[1,2,256,768]{3,2,1,0:T(8,128)(2,1)}, u32[]{:S(2)}, u32[]{:S(2)}) collective-permute-start(bf16[1,2,256,768]{3,2,1,0:T(8,128)(2,1)} %fusion.1), channel_id=1, source_target_pairs={{0,2},{1,3},{2,0},{3,1},{4,6},{5,7},{6,4},{7,5},{8,10},{9,11},{10,... | collective-permute-start | bytes 2359304 | tf_op jit(solution)/shard_map/ppermute | solution.py:842
  246.3 26.6 %collective-permute-start.21 = (f32[24,768]{1,0:T(8,128)}, f32[24,768]{1,0:T(8,128)S(1)}, u32[]{:S(2)}, u32[]{:S(2)}) collective-permute-start(f32[24,768]{1,0:T(8,128)} %get-tuple-element.125), channel_id=1, source_target_pairs={{0,7},{1,13},{2,3},{3,26},{4,0},{5,14},{6,20},{7,27},{8,8},{9,15},... | collective-permute-start | bytes 221192 | tf_op jit(solution)/shard_map/ppermute | solution.py:991
  261.3 23.7 %all-to-all-start.3 = ((bf16[4,24,768]{2,1,0:T(8,128)(2,1)}), bf16[4,24,768]{2,1,0:T(8,128)(2,1)S(1)}, u32[]{:S(2)}, u32[]{:S(2)}) async-start(bf16[4,24,768]{2,1,0:T(8,128)(2,1)} %bitcast.16), calls=%async_computation.4 | async-start | bytes 294912 | tf_op jit(solution)/shard_map/all_to_all | solution.py:940
  264.7 20.3 %collective-permute-start.22 = (f32[24,768]{1,0:T(8,128)}, f32[24,768]{1,0:T(8,128)S(1)}, u32[]{:S(2)}, u32[]{:S(2)}) collective-permute-start(f32[24,768]{1,0:T(8,128)} %get-tuple-element.126), channel_id=1, source_target_pairs={{0,0},{1,13},{2,19},{3,26},{4,7},{5,14},{6,20},{7,5},{8,8},{9,2},{... | collective-permute-start | bytes 221192 | tf_op jit(solution)/shard_map/ppermute | solution.py:991
  268.3 16.7 %collective-permute-start.23 = (f32[24,768]{1,0:T(8,128)}, f32[24,768]{1,0:T(8,128)S(1)}, u32[]{:S(2)}, u32[]{:S(2)}) collective-permute-start(f32[24,768]{1,0:T(8,128)} %get-tuple-element.127), channel_id=1, source_target_pairs={{0,6},{1,13},{2,19},{3,4},{4,7},{5,1},{6,20},{7,26},{8,8},{9,14},{... | collective-permute-start | bytes 221192 | tf_op jit(solution)/shard_map/ppermute | solution.py:991
  270.3 14.7 %collective-permute-start.24 = (f32[24,768]{1,0:T(8,128)}, f32[24,768]{1,0:T(8,128)S(1)}, u32[]{:S(2)}, u32[]{:S(2)}) collective-permute-start(f32[24,768]{1,0:T(8,128)} %get-tuple-element.128), channel_id=1, source_target_pairs={{0,6},{1,1},{2,19},{3,25},{4,7},{5,13},{6,20},{7,26},{8,8},{9,14},... | collective-permute-start | bytes 221192 | tf_op jit(solution)/shard_map/ppermute | solution.py:991
  273.0 12.0 %collective-permute-start.25 = (f32[24,768]{1,0:T(8,128)}, f32[24,768]{1,0:T(8,128)S(1)}, u32[]{:S(2)}, u32[]{:S(2)}) collective-permute-start(f32[24,768]{1,0:T(8,128)} %get-tuple-element.129), channel_id=1, source_target_pairs={{0,6},{1,12},{2,19},{3,25},{4,7},{5,13},{6,3},{7,26},{8,0},{9,14},... | collective-permute-start | bytes 221192 | tf_op jit(solution)/shard_map/ppermute | solution.py:991
  (34 other events, 471.3 us)
Sparse Core Ops, SparseCore 0:
  15.5 60.9 all-gather.4
  78.6 30.8 all-gather.6
  165.7 77.0 reduce-scatter.1

commit v6 on v5

--- a/solution.py
+++ b/solution.py
@@ -50,6 +50,10 @@
         - jnp.mean(grad_unit, axis=-1, keepdims=True)
         - unit_rows * jnp.mean(grad_unit * unit_rows, axis=-1, keepdims=True)
     )
+
+
+def as_row(ref):
+    return ref[...].reshape(1, ref.shape[0])
 
 
 def column(row):
@@ -137,7 +141,7 @@
                 copy.wait()
             unit, _ = normalize(x_ref[s].astype(F32))
             live = column(jnp.where(ids_ref[s : s + 1, :] >= 0, 1.0, 0.0))
-            pay_ref[s, 0] = (unit * gain_ref[...]).astype(BF)
+            pay_ref[s, 0] = (unit * as_row(gain_ref)).astype(BF)
             pay_ref[s, 1] = (live * cot_ref[s].astype(F32)).astype(BF)
             to = out0_hbm.at[s] if s < first else out1_hbm.at[s - first]
             copies.append(pltpu.make_async_copy(pay_ref.at[s], to, out_sem.at[s]))
@@ -281,48 +285,52 @@
         keep_ref[z] = jnp.where(odd, high, low)
 
 
-def leave(at, table, heads, ff):
-    per_ff, unit, dim = ff.shape
+def leave(at, table, heads, ffn):
+    _, per_ff, unit, dim = ffn.shape
     per = 1 + per_ff
 
-    def kernel(at_ref, table_ref, ff_ref, *refs):
-        terms, out_refs, all_ref = refs[: len(heads)], refs[len(heads) : -1], refs[-1]
+    def kernel(at_ref, table_ref, ffn_ref, *refs):
+        terms, outs, all_ref = refs[: len(heads)], refs[len(heads) : -1], refs[-1]
         total = terms[0][0]
         for ref in terms[1:]:
             total = total + ref[0].astype(F32)
-        all_ref[0] = total
+        all_ref[0] = total.astype(all_ref.dtype)
         for k in range(per_ff):
-            all_ref[k + 1] = ff_ref[k].astype(F32)
-        for k, ref in enumerate(out_refs):
-            ref[...] = all_ref[table_ref[at_ref[0], per + k]]
+            all_ref[k + 1] = ffn_ref[1, k].astype(all_ref.dtype)
+        for k in range(per):
+            outs[k][...] = all_ref[table_ref[at_ref[0], per + k]]
+        for s in range(SLOTS):
+            outs[per + s][...] = ffn_ref[0, at_ref[1] ^ s]
 
     return pl.pallas_call(
         kernel,
-        out_shape=[jax.ShapeDtypeStruct((unit, dim), F32)] * per,
+        out_shape=[jax.ShapeDtypeStruct((unit, dim), F32)] * per + [jax.ShapeDtypeStruct((unit, dim), BF)] * SLOTS,
         in_specs=[SMEM] * 2 + [VMEM] * (1 + len(heads)),
-        out_specs=[VMEM] * per,
+        out_specs=[VMEM] * (per + SLOTS),
         scratch_shapes=[pltpu.VMEM((per, unit, dim), F32)],
         cost_estimate=SMALL,
         name="leave",
-    )(at, table, ff, *heads)
+    )(at, table, ffn, *heads)
 
 
 def place(at, table, qkv, up, got):
     count, high, width = qkv.shape
     unit, dim = got[0].shape
-    nt = up.shape[0]
+    nt = len(up)
     nb = count // nt
     per = len(got)
     local = width // 3
     wide = nt * (width + dim)
 
-    def kernel(at_ref, table_ref, qkv_ref, up_ref, *refs):
-        got_refs, (in_ref, out_ref, norm_ref, q_ref, k_ref) = refs[:per], refs[per:]
+    def kernel(at_ref, table_ref, qkv_ref, *refs):
+        up_refs, got_refs, (in_ref, out_ref, norm_ref, q_ref, k_ref) = refs[:nt], refs[nt : nt + per], refs[nt + per :]
+        for s, ref in enumerate(up_refs):
+            to = pl.multiple_of(nt * width + (at_ref[1] ^ s) * dim, 128)
+            in_ref[:, pl.ds(to, dim)] = ref[...].astype(F32)
         for t in range(nt):
             total = add_blocks(qkv_ref, nb, nt, t, slice(0, unit))
             for k in range(3):
                 in_ref[:, k * nt * local + t * local : k * nt * local + (t + 1) * local] = total[:, k * local : (k + 1) * local]
-            in_ref[:, nt * width + t * dim : nt * width + (t + 1) * dim] = up_ref[t].astype(F32)
         for k, ref in enumerate(got_refs):
             out_ref[table_ref[at_ref[0], k]] = ref[...]
         small = add_blocks(qkv_ref, count, 1, 0, slice(unit, high))
@@ -341,47 +349,48 @@
             jax.ShapeDtypeStruct((1, HD), F32),
             jax.ShapeDtypeStruct((1, HD), F32),
         ],
-        in_specs=[SMEM] * 2 + [VMEM] * (2 + per),
+        in_specs=[SMEM] * 2 + [VMEM] * (1 + nt + per),
         out_specs=[VMEM] * 5,
         cost_estimate=SMALL,
         compiler_params=pltpu.CompilerParams(vmem_limit_bytes=32 * MIB),
         name="place",
-    )(at, table, qkv, up, *got)
-
-
-def after_kernel(s, ids_ref, x_ref, cot_ref, gain_ref, keep_ref, near_ref, far_ref, *rest):
-    out_ref, grad_ref = rest[-2:]
-    unit, inverse = normalize(x_ref[0].astype(F32))
-    live = column(jnp.where(ids_ref[s : s + 1, :] >= 0, 1.0, 0.0))
-    both = keep_ref[0, 0].astype(F32) + near_ref[0, 0].astype(F32) + far_ref[0].astype(F32)
-    out_ref[0] = (live * (x_ref[0].astype(F32) + both[0])).astype(BF)
-    grad_ref[0] = (
-        live * cot_ref[0].astype(F32) + norm_back(both[1] * gain_ref[...], unit, inverse)
-    ).astype(BF)
-
-
-def after(s, i, ids, x, cot, gain, keep, near, far, earlier):
-    x, cot, keep, near, far = (pltpu.with_memory_space_constraint(a, pltpu.HBM) for a in (x, cot, keep, near, far))
+    )(at, table, qkv, *up, *got)
+
+
+def after(start, ids, x, cot, gain, keep, near, far, earlier):
     seqs, part, dim = x.shape
-    one = pl.BlockSpec((1, part, dim), lambda g: (s, 0, 0))
-    pair = pl.BlockSpec((1, 1, 2, part, dim), lambda g: (0, i, 0, 0, 0))
-    lone = pl.BlockSpec((1, 2, part, dim), lambda g: (i, 0, 0, 0))
-    fixed = lambda a: pl.BlockSpec(a.shape, lambda g: (0,) * a.ndim)
+    count = far.shape[0]
+
+    def kernel(ids_ref, x_ref, cot_ref, gain_ref, keep_ref, near_ref, far_ref, *rest):
+        out_ref, grad_ref = rest[-2:]
+        unit, inverse = normalize(x_ref[0].astype(F32))
+        live = column(jnp.where(ids_ref[0] >= 0, 1.0, 0.0))
+        branch, gn = (keep_ref[0, 0, j].astype(F32) + near_ref[0, 0, j].astype(F32) + far_ref[0, j].astype(F32) for j in range(2))
+        out_ref[0] = (live * (x_ref[0].astype(F32) + branch)).astype(BF)
+        grad_ref[0] = (live * cot_ref[0].astype(F32) + norm_back(gn * as_row(gain_ref), unit, inverse)).astype(BF)
+
+    one = pl.BlockSpec((1, part, dim), lambda g: (start + g, 0, 0))
+    pair = pl.BlockSpec((1, 1, 2, part, dim), lambda g: (0, g, 0, 0, 0))
+    lone = pl.BlockSpec((1, 2, part, dim), lambda g: (g, 0, 0, 0))
     return pl.pallas_call(
-        functools.partial(after_kernel, s),
-        grid=(1,),
+        kernel,
+        grid=(count,),
         out_shape=[jax.ShapeDtypeStruct(x.shape, BF)] * 2,
-        in_specs=[fixed(ids), one, one, fixed(gain), pair, pair, lone] + [ANY] * len(earlier),
+        in_specs=[
+            pl.BlockSpec((1, 1, part), lambda g: (start + g, 0, 0)), one, one,
+            pl.BlockSpec(gain.shape, lambda g: (0,)), pair, pair, lone,
+        ]
+        + [ANY] * len(earlier),
         out_specs=[one, one],
         input_output_aliases={7 + i: i for i in range(len(earlier))},
         cost_estimate=SMALL,
         compiler_params=pltpu.CompilerParams(vmem_limit_bytes=32 * MIB),
         name="after",
-    )(ids, x, cot, gain, keep, near, far, *earlier)
+    )(ids.reshape(seqs, 1, part), *hbm(x, cot), gain, *hbm(keep, near, far), *earlier)
 
 
 def attention_kernel(
-    heads, block, last,
+    heads, block, last, start,
     at_ref, ids_ref, qg_ref, kg_ref, wqkv_hbm, wo_hbm, *refs,
 ):
     pays, refs = refs[0], refs[1:]
@@ -438,8 +447,8 @@
         gq_ref[...] = jnp.zeros_like(gq_ref)
         go_ref[...] = jnp.zeros_like(go_ref)
         sums_ref[...] = jnp.zeros_like(sums_ref)
-    gain_q = qg_ref[...]
-    gain_k = kg_ref[...]
+    gain_q = column(as_row(qg_ref))
+    gain_k = column(as_row(kg_ref))
     marks = lax.broadcasted_iota(jnp.int32, (HD, length), 0)
     v_tail = jnp.where(lax.broadcasted_iota(jnp.int32, (length, HD), 1) < 2, 1.0, 0.0).astype(BF)
     ones = jnp.where(lax.broadcasted_iota(jnp.int32, (16, length), 0) == 0, 1.0, 0.0).astype(BF)
@@ -469,7 +478,7 @@
     loads[1].wait()
 
     def sequence(s, carry):
-        ids = ids_ref[s]
+        ids = ids_ref[start + s]
         same = marks == ids + 1
         k_tail = jnp.where(same, 1.0, 0.0).T.astype(BF)
         q_tail = jnp.where((same & (ids >= 0)) | (marks > 4), 0.0, -BIG).astype(BF)
@@ -583,7 +592,7 @@
         return
     outs.wait()
     g_q = gq_ref[...]
-    first_row = (jnp.sum(wqkv_ref[...].astype(F32) * g_q, axis=0, keepdims=True) + fnp_ref[...]) / gain_ref[...]
+    first_row = (jnp.sum(wqkv_ref[...].astype(F32) * g_q, axis=0, keepdims=True) + fnp_ref[...]) / as_row(gain_ref)
     second_row = jnp.concatenate([jnp.sum(sums_ref[k].T, axis=0, keepdims=True) for k in range(2)], axis=1)
     wide = 3 * width
     line = jnp.concatenate([first_row[:, wide:], second_row, jnp.zeros((1, 2 * wide - dim - 2 * HD), F32)], axis=1)
@@ -599,7 +608,7 @@
     split_rows((at_ref[2] & 1) > 0, go_ref[...], sendo_ref, keepo_ref)
 
 
-def attention(at, ids, wqkv, wo, qg, kg, pays, count, more=()):
+def attention(at, start, ids, wqkv, wo, qg, kg, pays, count, more=()):
     wide, dim = wqkv.shape
     width = wo.shape[0]
     heads = width // HD
@@ -627,7 +636,7 @@
         ]
     flops = seqs * (2 * length * dim * width * 8 + heads * 6 * 2 * length * length * HD)
     return pl.pallas_call(
-        functools.partial(attention_kernel, heads, block, last),
+        functools.partial(attention_kernel, heads, block, last, start),
         out_shape=outs,
         in_specs=specs,
         out_specs=[HBM] * 2 + ([VMEM] * 3 if last else [VMEM, HBM, HBM]),
@@ -857,10 +866,12 @@
     return groups
 
 
-def gather_batch(block, count, groups):
+def gather_batch(block, count, groups, hold=None):
     held, masks = block[None], [0]
     for bits in groups:
         low = bits[-1]
+        if hold is not None and bits is groups[-1]:
+            held = tie(held, hold)
         parts = [(held, masks)]
         for s in range(1, 1 << len(bits)):
             parts.append((swap(held, "batch", count, s << low), [m ^ (s << low) for m in masks]))
@@ -934,7 +945,7 @@
     me_t = lax.axis_index("tok")
     at = jnp.stack([me_b * nt + me_t, me_t, me_b])
     table = jnp.asarray(table)
-    gain = norm_gain.reshape(1, dim)
+    gain = norm_gain
 
     def exchange(value, axis):
         return lax.all_to_all(value, axis, split_axis=0, concat_axis=0, tiled=True)
@@ -948,23 +959,22 @@
         at, table, out_weight.reshape(per, unit, dim), image_ids, gain, tie(patches, a_src), cotangent, lead
     )
     got = [lax.ppermute(v, both, perm) for v, perm in zip(unit_sends, perms)]
-    wo_src, ff_src = pack_out(at, table, tie(got, a_got))
+    wo_src, ff_src = pack_out(at, table, got)
     slots0 = lax.all_gather(own0, "tok", axis=0)
     slots1 = lax.all_gather(own1, "tok", axis=0)
-    wo_parts = gather_batch(wo_src, nb, groups)
+    wo_parts = gather_batch(wo_src, nb, groups, a_got)
     ff_parts = gather_batch(ff_src.reshape((per - 1) * unit, dim), nb, groups[::-1])
     wqkv, wo, ids = join(at, a_got, wo_parts, seqs, part)
     wo = wo.reshape(local, dim)
     wup = exchange(tie(u_src, a_got).reshape(nb * nt, unit, dim), both).reshape(dim, units)
 
-    qg = query_gain.reshape(HD, 1)
-    kg = key_gain.reshape(HD, 1)
+    qg, kg = query_gain, key_gain
 
     def leave_chip(keep, near, *hold):
         value = (keep[1].astype(F32) + near[1].astype(F32)).astype(BF)
         return value, swap(tie(value, *hold) if hold else value, "tok", nt, 2)
 
-    o0, gq0, sums, acc_q, acc_o = attention(at, ids[:lead], wqkv, tie(wo, ff_parts[0][0]), qg, kg, slots0, nb * nt)
+    o0, gq0, sums, acc_q, acc_o = attention(at, 0, ids, wqkv, tie(wo, ff_parts[0][0]), qg, kg, slots0, nb * nt)
     hid, gup, wff, keep0, send0, f_grad, f_np = ffn(
         at, tie(wup, o0), ff_parts, [slots0, slots1], nb, wqkv, wo, o0, gq0
     )
@@ -972,7 +982,7 @@
     near0 = swap(send0, "tok", nt, 1)
     value0, away0 = leave_chip(keep0, near0)
     keep1, send1, a_q, a_send, a_keep = attention(
-        at, ids[lead:], wqkv, tie(wo, value0), qg, kg, slots1, nb * nt,
+        at, lead, ids, wqkv, tie(wo, value0), qg, kg, slots1, nb * nt,
         (sums, f_np, gain, acc_q, acc_o, hid, gup, wff, wup),
     )
     a_came = swap(a_send, "batch", nb, 1)
@@ -981,20 +991,16 @@
         own, *sends = fold(at, bits[-1], [terms])
         terms = [own] + [swap(value, "batch", nb, (s + 1) << bits[-1]) for s, value in enumerate(sends)]
     near1 = swap(tie(send1, away0, *terms[1:]), "tok", nt, 1)
-    a_q = exchange(tie(a_q, *terms[1:]), both)
+    a_q = exchange(a_q, both)
     value1, away1 = leave_chip(keep1, near1)
-    up = exchange(tie(f_mine[0], a_q), "tok")
-    group = [(0, s, keep0, near0, away0) for s in range(lead)]
-    group += [(lead, s, keep1, near1, away1) for s in range(lead, seqs)]
-
-    sends = leave(at, table, terms, f_mine[1])
+    earlier = after(0, image_ids, patches, cotangent, gain, keep0, near0, away0, [])
+    outs = leave(at, table, terms, tie(f_mine, *earlier))
+    sends, up = outs[:per], outs[per:]
+    up = [up[0]] + [swap(up[s], "tok", nt, s) for s in range(1, nt)]
     got = [lax.ppermute(v, both, [(b, a) for a, b in perm]) for v, perm in zip(sends, perms)]
     in_grad, out_grad, norm_grad, query_grad, key_grad = place(at, table, a_q, up, got)
 
-    earlier = []
-    for s in range(seqs):
-        start, _, *arrays = group[s]
-        earlier = after(s, s - start, image_ids, patches, cotangent, gain, *arrays, earlier)
+    earlier = after(lead, image_ids, patches, cotangent, gain, keep1, near1, away1, earlier)
     block_out, patch_grad = earlier
     return (
         block_out,

time: 301 us -> 291 us (0.967)
  waiting for transfers between devices: 65 us -> 51.6 us
  starting transfers between devices: 75 us -> 82.3 us
    all_to_all x4 -> x3, waiting for transfers between devices: 22.4 us -> 0.01 us  [exchange(): return lax.all_to_all(value, axis, split_axis=0, concat_axis=0, tiled=True)]
    ppermute x16 -> x19, waiting for transfers between devices: 21.9 us -> 32.6 us  [swap(): return lax.ppermute(value, axis, [(i, i ^ mask) for i in range(count)])]
    ppermute x16 -> x19, starting transfers between devices: 21 us -> 30.7 us  [swap(): return lax.ppermute(value, axis, [(i, i ^ mask) for i in range(count)])]
    reduce_scatter x1, waiting for transfers between devices: 15.7 us -> 8.41 us  [per_device(): lax.psum_scatter(f_grad, 'batch', scatter_dimension=0, tiled=True)]
    ppermute x5, waiting for transfers between devices: 0.01 us -> 5.74 us  [per_device(): lax.ppermute(v, both, [(b, a) for a, b in perm])]
    unnamed x50 -> x56, local copies, waits for them, and re-layouts: 3.33 us -> 8.63 us
    all_to_all x4 -> x3, starting transfers between devices: 18.5 us -> 13.6 us  [exchange(): return lax.all_to_all(value, axis, split_axis=0, concat_axis=0, tiled=True)]
    pallas_call x5 -> x4, Pallas kernels: 79.1 us -> 76.4 us  [the longest x2 68.5 us: attention(): pl.pallas_call(functools.partial(attention_kernel, heads, block, last, st...]
  transfers between devices with their start and end apart: 33 -> 35, of which waited for: 14 -> 14; matrix products, arithmetic and copies ran while one was open for 4% -> 3% of each run, Pallas kernels for 28% -> 28%
where the time goes in v6:
time: 291 us; the launch traced here: 290 us
  Pallas kernels  125 us (43%)
  starting transfers between devices  82.3 us (28%)
  waiting for transfers between devices  51.6 us (18%)
  between operations  14.2 us (5%)
  local copies, waits for them, and re-layouts  8.63 us (3%)
  other arithmetic  7.58 us (3%)
    pallas_call x2, Pallas kernels, attention(): pl.pallas_call(functools.partial(attention_kernel, heads, block, last, st...  68.5 us
    pallas_call x1, Pallas kernels, ffn(): pl.pallas_call(functools.partial(ffn_kernel, block, sizes, [masks for _,...  35.1 us
    ppermute x19, waiting for transfers between devices, swap(): return lax.ppermute(value, axis, [(i, i ^ mask) for i in range(count)])  32.6 us
    ppermute x19, starting transfers between devices, swap(): return lax.ppermute(value, axis, [(i, i ^ mask) for i in range(count)])  30.7 us
    ppermute x5, starting transfers between devices, per_device(): got = [lax.ppermute(v, both, perm) for v, perm in zip(unit_sends, perms)]  20 us
    ppermute x5, starting transfers between devices, per_device(): lax.ppermute(v, both, [(b, a) for a, b in perm])  17.7 us
    all_to_all x3, starting transfers between devices, exchange(): return lax.all_to_all(value, axis, split_axis=0, concat_axis=0, tiled=True)  13.6 us
    unnamed x56, local copies, waits for them, and re-layouts  8.63 us
  transfers between devices with their start and end apart: 35, of which 14 were waited for; matrix products, arithmetic and copies ran while one was open for 3% of the time, Pallas kernels for 28%

profile of v6, /device:TPU:2, one launch (start us, length us, event | category | flops | bytes accessed | tf_op | source)
XLA Modules:
  0.0 289.7 jit_solution(17256959737064096365)
XLA Ops:
  9.9 4.2 %before.1 = (bf16[2,2,256,768]{3,2,1,0:T(8,128)(2,1)}, bf16[1,2,256,768]{3,2,1,0:T(8,128)(2,1)}, bf16[24,768]{1,0:T(8,128)(2,1)S(1)}, bf16[24,768]{1,0:T(8,128)(...) custom-call(s32[3]{0:T(128)S(1)} %pad_add_fusion.at_ref, ...), custom_call_target="tpu_custom_call" | custom-call | flops 1 | bytes 1 | tf_op jit(solution)/shard_map/before/pallas_call | solution.py:152
  14.1 6.1 %all-to-all-start = ((bf16[32,26,576]{2,1,0:T(8,128)(2,1)}), bf16[32,26,576]{2,1,0:T(8,128)(2,1)S(1)}, u32[]{:S(2)}, u32[]{:S(2)}) async-start(bf16[32,26,576]{2,1,0:T(8,128)(2,1)} %bitcast.3), calls=%async_computation | async-start | bytes 2621440 | tf_op jit(solution)/shard_map/all_to_all | solution.py:951
  20.3 5.2 %collective-permute-start = (bf16[24,768]{1,0:T(8,128)(2,1)S(1)}, bf16[24,768]{1,0:T(8,128)(2,1)S(1)}, u32[]{:S(2)}, u32[]{:S(2)}) collective-permute-start(bf16[24,768]{1,0:T(8,128)(2,1)S(1)} %get-tuple-element.70), channel_id=1, source_target_pairs={{7,0},{13,1},{3,2},{26,3},{0,4},{14,5},{20,6},{27,7},{8,8},{15,9},... | collective-permute-start | bytes 110600 | tf_op jit(solution)/shard_map/ppermute | solution.py:961
  25.5 3.1 %collective-permute-start.1 = (bf16[24,768]{1,0:T(8,128)(2,1)S(1)}, bf16[24,768]{1,0:T(8,128)(2,1)S(1)}, u32[]{:S(2)}, u32[]{:S(2)}) collective-permute-start(bf16[24,768]{1,0:T(8,128)(2,1)S(1)} %get-tuple-element.71), channel_id=1, source_target_pairs={{0,0},{13,1},{19,2},{26,3},{7,4},{14,5},{20,6},{5,7},{8,8},{2,9},{... | collective-permute-start | bytes 110600 | tf_op jit(solution)/shard_map/ppermute | solution.py:961
  28.6 3.7 %collective-permute-start.2 = (bf16[24,768]{1,0:T(8,128)(2,1)S(1)}, bf16[24,768]{1,0:T(8,128)(2,1)S(1)}, u32[]{:S(2)}, u32[]{:S(2)}) collective-permute-start(bf16[24,768]{1,0:T(8,128)(2,1)S(1)} %get-tuple-element.72), channel_id=1, source_target_pairs={{6,0},{13,1},{19,2},{4,3},{7,4},{1,5},{20,6},{26,7},{8,8},{14,9},{... | collective-permute-start | bytes 110600 | tf_op jit(solution)/shard_map/ppermute | solution.py:961
  35.0 5.2 %collective-permute-start.4 = (bf16[24,768]{1,0:T(8,128)(2,1)S(1)}, bf16[24,768]{1,0:T(8,128)(2,1)S(1)}, u32[]{:S(2)}, u32[]{:S(2)}) collective-permute-start(bf16[24,768]{1,0:T(8,128)(2,1)S(1)} %get-tuple-element.74), channel_id=1, source_target_pairs={{6,0},{12,1},{19,2},{25,3},{7,4},{13,5},{3,6},{26,7},{0,8},{14,9},... | collective-permute-start | bytes 110600 | tf_op jit(solution)/shard_map/ppermute | solution.py:961
  40.3 2.9 %collective-permute-done.refs_0_ = bf16[24,768]{1,0:T(8,128)(2,1)S(1)} collective-permute-done((bf16[24,768]{1,0:T(8,128)(2,1)S(1)}, bf16[24,768]{1,0:T(8,128)(2,1)S(1)}, u32[]{:S(2)}, u32[]{:S(2)}) %collective-permute-start) | collective-permute-done | bytes 36896 | tf_op jit(solution)/shard_map/ppermute | solution.py:961
  47.7 9.7 %collective-permute-start.5 = (bf16[1,24,768]{2,1,0:T(8,128)(2,1)}, bf16[1,24,768]{2,1,0:T(8,128)(2,1)S(1)}, u32[]{:S(2)}, u32[]{:S(2)}) collective-permute-start(bf16[1,24,768]{2,1,0:T(8,128)(2,1)} %bitcast.29), channel_id=1, source_target_pairs={{0,8},{4,12},{8,0},{12,4},{16,24},{20,28},{24,16},{28,20},{1,9},{5... | collective-permute-start | bytes 110600 | tf_op jit(solution)/shard_map/ppermute | solution.py:851
  57.4 4.1 %collective-permute-start.6 = (bf16[1,24,768]{2,1,0:T(8,128)(2,1)}, bf16[1,24,768]{2,1,0:T(8,128)(2,1)S(1)}, u32[]{:S(2)}, u32[]{:S(2)}) collective-permute-start(bf16[1,24,768]{2,1,0:T(8,128)(2,1)} %bitcast.30), channel_id=1, source_target_pairs={{0,16},{4,20},{8,24},{12,28},{16,0},{20,4},{24,8},{28,12},{1,17},{... | collective-permute-start | bytes 110600 | tf_op jit(solution)/shard_map/ppermute | solution.py:851
  64.0 3.5 %collective-permute-done.7 = bf16[1,24,768]{2,1,0:T(8,128)(2,1)S(1)} collective-permute-done((bf16[1,24,768]{2,1,0:T(8,128)(2,1)}, bf16[1,24,768]{2,1,0:T(8,128)(2,1)S(1)}, u32[]{:S(2)}, u32[]{:S(2)}) %collective-permute-start.7) | collective-permute-done | bytes 36896 | tf_op jit(solution)/shard_map/ppermute | solution.py:851
  75.1 4.7 %all-to-all-start.1 = ((bf16[32,24,768]{2,1,0:T(8,128)(2,1)}), bf16[32,24,768]{2,1,0:T(8,128)(2,1)S(1)}, u32[]{:S(2)}, u32[]{:S(2)}) async-start(bf16[32,24,768]{2,1,0:T(8,128)(2,1)} %bitcast.7), calls=%async_computation.1 | async-start | bytes 2359296 | tf_op jit(solution)/shard_map/all_to_all | solution.py:951
  83.3 41.4 %attention.2 = (bf16[2,192,1024]{2,1,0:T(8,128)(2,1)}, bf16[2,576,1024]{2,1,0:T(8,128)(2,1)}, f32[2,64,128]{2,1,0:T(8,128)}, f32[576,768]{1,0:T(8,128)}, f32[192,768]{1,0:T(8,128)}) custom-call(s32[3]{0:T(128)} %copy-done.5, s32[3,1,1024]{2,1,0:T(1,128)} %copy-done.11, f32[64]{0:T(128)} %qg_ref.3, f32[64]{0:T(128)} %kg_ref.3, bf16[576,768]{1,0:T(8,128)(2,1)} %copy-done.9, ...), custom_call_target="tpu_custom_call" | custom-call | flops 60000002048 | bytes 1 | tf_op jit(solution)/shard_map/attention/pallas_call | solution.py:638
  125.8 35.1 %ffn.1 = (bf16[3072,768]{1,0:T(8,128)(2,1)}, bf16[3072,768]{1,0:T(8,128)(2,1)}, bf16[768,768]{1,0:T(8,128)(2,1)}, bf16[2,2,2,256,768]{4,3,2,1,0:T(8,128)(2,1)}, ...) custom-call(s32[3]{0:T(128)} %copy-done.5, bf16[768,768]{1,0:T(8,128)(2,1)} %bitcast.23, ...), custom_call_target="tpu_custom_call" | custom-call | flops 60000002048 | bytes 1 | tf_op jit(solution)/shard_map/ffn/pallas_call | solution.py:772
  161.2 5.7 %collective-permute-done.13.near_ref = bf16[2,2,2,256,768]{4,3,2,1,0:T(8,128)(2,1)S(1)} collective-permute-done((bf16[2,2,2,256,768]{4,3,2,1,0:T(8,128)(2,1)}, bf16[2,2,2,256,768]{4,3,2,1,0:T(8,128)(2,1)S(1)}, u32[]{:S(2)}, u32[]{:S(2)}) %collective-permute-start.13) | collective-permute-done | bytes 3145760 | tf_op jit(solution)/shard_map/ppermute | solution.py:851
  166.9 2.9 %fusion = bf16[2,2,256,768]{3,2,1,0:T(8,128)(2,1)S(1)} fusion(bf16[2,2,2,256,768]{4,3,2,1,0:T(8,128)(2,1)S(1)} %collective-permute-done.13.near_ref, bf16[2,2,2,256,768]{4,3,2,1,0:T(8,128)(2,1)} %get-tuple-element.89.keep_ref), kind=kLoop, calls=%fused_computation.1 | loop fusion | flops 3145728 | bytes 4718592 | tf_op jit(solution)/shard_map/convert_element_type | solution.py:974
  171.4 27.1 %attention.3 = (bf16[2,1,2,256,768]{4,3,2,1,0:T(8,128)(2,1)}, bf16[2,1,2,256,768]{4,3,2,1,0:T(8,128)(2,1)}, bf16[32,28,576]{2,1,0:T(8,128)(2,1)}, bf16[4,24,768]{2,1,0:T(8,128)(2,1)}, f32[4,24,768]{2,1,0:T(8,128)}) custom-call(s32[3]{0:T(128)} %copy-done.5, s32[3,1,1024]{2,1,0:T(1,128)} %copy-done.11, f32[64]{0:T(128)} %qg_ref.3, f32[64]{0:T(128)} %kg_ref.3, ...), custom_call_target="tpu_custom_call" | custom-call | flops 60000002048 | bytes 1 | tf_op jit(solution)/shard_map/attention/pallas_call | solution.py:638
  199.0 6.4 %collective-permute-done.15.refs_1_ = bf16[4,24,768]{2,1,0:T(8,128)(2,1)S(1)} collective-permute-done((bf16[4,24,768]{2,1,0:T(8,128)(2,1)}, bf16[4,24,768]{2,1,0:T(8,128)(2,1)S(1)}, u32[]{:S(2)}, u32[]{:S(2)}) %collective-permute-start.15) | collective-permute-done | bytes 147488 | tf_op jit(solution)/shard_map/ppermute | solution.py:851
  225.4 4.5 %after.2 = (bf16[3,256,768]{2,1,0:T(8,128)(2,1)}, bf16[3,256,768]{2,1,0:T(8,128)(2,1)}) custom-call(s32[3,1,256]{2,1,0:T(1,128)S(1)} %reshape.88.ids_ref, bf16[3,256,768]{2,1,0:T(8,128)(2,1)} %x_ref.3, bf16[3,256,768]{2,1,0:T(8,128)(2,1)} %cot_ref.3, f32[768]{0:T(1024)S(1)} %copy-done.3, bf16[2,2,2,256,768]{4,3,2,1,0:T(8,128)(2,1)} %get-tuple-element.89.keep_ref, ...), custom_call_target="tpu_custom_call" | custom-call | flops 1 | bytes 1 | tf_op jit(solution)/shard_map/after/pallas_call | solution.py:375
  229.8 8.4 %reduce-scatter.2.cloned.1.call-done = bf16[1,2,96,768]{3,2,1,0:T(8,128)(2,1)} async-done(((bf16[8,2,96,768]{3,2,1,0:T(8,128)(2,1)}), bf16[1,2,96,768]{3,2,1,0:T(8,128)(2,1)}) %reduce-scatter.2.cloned.1.call-update) | async-done | bytes 294928 | tf_op jit(solution)/shard_map/reduce_scatter | solution.py:981
  247.1 9.5 %collective-permute-done.22.refs_2_ = bf16[24,768]{1,0:T(8,128)(2,1)S(1)} collective-permute-done((bf16[24,768]{1,0:T(8,128)(2,1)}, bf16[24,768]{1,0:T(8,128)(2,1)S(1)}, u32[]{:S(2)}, u32[]{:S(2)}) %collective-permute-start.22) | collective-permute-done | bytes 36896 | tf_op jit(solution)/shard_map/ppermute | solution.py:851
  258.5 6.9 %collective-permute-start.27 = (f32[24,768]{1,0:T(8,128)}, f32[24,768]{1,0:T(8,128)S(1)}, u32[]{:S(2)}, u32[]{:S(2)}) collective-permute-start(f32[24,768]{1,0:T(8,128)} %get-tuple-element.122), channel_id=1, source_target_pairs={{0,6},{1,1},{2,19},{3,25},{4,7},{5,13},{6,20},{7,26},{8,8},{9,14},... | collective-permute-start | bytes 221192 | tf_op jit(solution)/shard_map/ppermute | solution.py:1000
  265.4 4.3 %collective-permute-start.28 = (f32[24,768]{1,0:T(8,128)}, f32[24,768]{1,0:T(8,128)S(1)}, u32[]{:S(2)}, u32[]{:S(2)}) collective-permute-start(f32[24,768]{1,0:T(8,128)} %get-tuple-element.123), channel_id=1, source_target_pairs={{0,6},{1,12},{2,19},{3,25},{4,7},{5,13},{6,3},{7,26},{8,0},{9,14},... | collective-permute-start | bytes 221192 | tf_op jit(solution)/shard_map/ppermute | solution.py:1000
  269.8 5.7 %collective-permute-done.28.refs_8_ = f32[24,768]{1,0:T(8,128)S(1)} collective-permute-done((f32[24,768]{1,0:T(8,128)}, f32[24,768]{1,0:T(8,128)S(1)}, u32[]{:S(2)}, u32[]{:S(2)}) %collective-permute-start.28) | collective-permute-done | bytes 73760 | tf_op jit(solution)/shard_map/ppermute | solution.py:1000
  279.7 3.4 %after.3 = (bf16[3,256,768]{2,1,0:T(8,128)(2,1)}, bf16[3,256,768]{2,1,0:T(8,128)(2,1)}) custom-call(s32[3,1,256]{2,1,0:T(1,128)S(1)} %reshape.88.ids_ref, bf16[3,256,768]{2,1,0:T(8,128)(2,1)} %x_ref.3, bf16[3,256,768]{2,1,0:T(8,128)(2,1)} %cot_ref.3, f32[768]{0:T(1024)S(1)} %copy-done.3, ...), custom_call_target="tpu_custom_call", output_to_operand_aliasing={{0}: (7, {}), {1}: (8, {})} | custom-call | flops 1 | bytes 1 | tf_op jit(solution)/shard_map/after/pallas_call | solution.py:375
  (124 shorter events, 61.7 us)
Async XLA Ops:
  7.2 76.1 %all-gather.5.cloned.1.call-start = ((), (), s32[]{:S(2)}) async-start(), calls=%async_computation.5 | async-start | bytes 7864320 | tf_op jit(solution)/shard_map/all_gather | solution.py:963
  14.1 54.2 %all-to-all-start = ((bf16[32,26,576]{2,1,0:T(8,128)(2,1)}), bf16[32,26,576]{2,1,0:T(8,128)(2,1)S(1)}, u32[]{:S(2)}, u32[]{:S(2)}) async-start(bf16[32,26,576]{2,1,0:T(8,128)(2,1)} %bitcast.3), calls=%async_computation | async-start | bytes 2621440 | tf_op jit(solution)/shard_map/all_to_all | solution.py:951
  20.2 104.6 %all-gather.7.cloned.1.call-start = ((), (), s32[]{:S(2)}) async-start(), calls=%async_computation.6 | async-start | bytes 3932160 | tf_op jit(solution)/shard_map/all_gather | solution.py:964
  20.3 22.9 %collective-permute-start = (bf16[24,768]{1,0:T(8,128)(2,1)S(1)}, bf16[24,768]{1,0:T(8,128)(2,1)S(1)}, u32[]{:S(2)}, u32[]{:S(2)}) collective-permute-start(bf16[24,768]{1,0:T(8,128)(2,1)S(1)} %get-tuple-element.70), channel_id=1, source_target_pairs={{7,0},{13,1},{3,2},{26,3},{0,4},{14,5},{20,6},{27,7},{8,8},{15,9},... | collective-permute-start | bytes 110600 | tf_op jit(solution)/shard_map/ppermute | solution.py:961
  25.5 18.5 %collective-permute-start.1 = (bf16[24,768]{1,0:T(8,128)(2,1)S(1)}, bf16[24,768]{1,0:T(8,128)(2,1)S(1)}, u32[]{:S(2)}, u32[]{:S(2)}) collective-permute-start(bf16[24,768]{1,0:T(8,128)(2,1)S(1)} %get-tuple-element.71), channel_id=1, source_target_pairs={{0,0},{13,1},{19,2},{26,3},{7,4},{14,5},{20,6},{5,7},{8,8},{2,9},{... | collective-permute-start | bytes 110600 | tf_op jit(solution)/shard_map/ppermute | solution.py:961
  28.6 15.3 %collective-permute-start.2 = (bf16[24,768]{1,0:T(8,128)(2,1)S(1)}, bf16[24,768]{1,0:T(8,128)(2,1)S(1)}, u32[]{:S(2)}, u32[]{:S(2)}) collective-permute-start(bf16[24,768]{1,0:T(8,128)(2,1)S(1)} %get-tuple-element.72), channel_id=1, source_target_pairs={{6,0},{13,1},{19,2},{4,3},{7,4},{1,5},{20,6},{26,7},{8,8},{14,9},{... | collective-permute-start | bytes 110600 | tf_op jit(solution)/shard_map/ppermute | solution.py:961
  32.3 12.4 %collective-permute-start.3 = (bf16[24,768]{1,0:T(8,128)(2,1)S(1)}, bf16[24,768]{1,0:T(8,128)(2,1)S(1)}, u32[]{:S(2)}, u32[]{:S(2)}) collective-permute-start(bf16[24,768]{1,0:T(8,128)(2,1)S(1)} %get-tuple-element.73), channel_id=1, source_target_pairs={{6,0},{1,1},{19,2},{25,3},{7,4},{13,5},{20,6},{26,7},{8,8},{14,9},... | collective-permute-start | bytes 110600 | tf_op jit(solution)/shard_map/ppermute | solution.py:961
  35.0 10.1 %collective-permute-start.4 = (bf16[24,768]{1,0:T(8,128)(2,1)S(1)}, bf16[24,768]{1,0:T(8,128)(2,1)S(1)}, u32[]{:S(2)}, u32[]{:S(2)}) collective-permute-start(bf16[24,768]{1,0:T(8,128)(2,1)S(1)} %get-tuple-element.74), channel_id=1, source_target_pairs={{6,0},{12,1},{19,2},{25,3},{7,4},{13,5},{3,6},{26,7},{0,8},{14,9},... | collective-permute-start | bytes 110600 | tf_op jit(solution)/shard_map/ppermute | solution.py:961
  47.7 15.2 %collective-permute-start.5 = (bf16[1,24,768]{2,1,0:T(8,128)(2,1)}, bf16[1,24,768]{2,1,0:T(8,128)(2,1)S(1)}, u32[]{:S(2)}, u32[]{:S(2)}) collective-permute-start(bf16[1,24,768]{2,1,0:T(8,128)(2,1)} %bitcast.29), channel_id=1, source_target_pairs={{0,8},{4,12},{8,0},{12,4},{16,24},{20,28},{24,16},{28,20},{1,9},{5... | collective-permute-start | bytes 110600 | tf_op jit(solution)/shard_map/ppermute | solution.py:851
  68.3 11.7 %collective-permute-start.8 = (bf16[4,24,768]{2,1,0:T(8,128)(2,1)S(1)}, bf16[4,24,768]{2,1,0:T(8,128)(2,1)S(1)}, u32[]{:S(2)}, u32[]{:S(2)}) collective-permute-start(bf16[4,24,768]{2,1,0:T(8,128)(2,1)S(1)} %pad_maximum_fusion.1.refs_0_), channel_id=1, source_target_pairs={{0,4},{4,0},{8,12},{12,8},{16,20},{20,16},{24,28},{28,24},{1,5},{5... | collective-permute-start | bytes 442376 | tf_op jit(solution)/shard_map/ppermute | solution.py:851
  70.6 54.2 %collective-permute-start.10 = (bf16[2,96,768]{2,1,0:T(8,128)(2,1)S(1)}, bf16[2,96,768]{2,1,0:T(8,128)(2,1)S(1)}, u32[]{:S(2)}, u32[]{:S(2)}) collective-permute-start(bf16[2,96,768]{2,1,0:T(8,128)(2,1)S(1)} %pad_maximum_fusion.refs_0_), channel_id=1, source_target_pairs={{0,8},{4,12},{8,0},{12,4},{16,24},{20,28},{24,16},{28,20},{1,9},{5... | collective-permute-start | bytes 884744 | tf_op jit(solution)/shard_map/ppermute | solution.py:851
  71.4 53.4 %collective-permute-start.11 = (bf16[2,96,768]{2,1,0:T(8,128)(2,1)S(1)}, bf16[2,96,768]{2,1,0:T(8,128)(2,1)}, u32[]{:S(2)}, u32[]{:S(2)}) collective-permute-start(bf16[2,96,768]{2,1,0:T(8,128)(2,1)S(1)} %pad_maximum_fusion.refs_0_), channel_id=1, source_target_pairs={{0,16},{4,20},{8,24},{12,28},{16,0},{20,4},{24,8},{28,12},{1,17},{... | collective-permute-start | bytes 884744 | tf_op jit(solution)/shard_map/ppermute | solution.py:851
  73.2 51.6 %collective-permute-start.12 = (bf16[2,96,768]{2,1,0:T(8,128)(2,1)S(1)}, bf16[2,96,768]{2,1,0:T(8,128)(2,1)}, u32[]{:S(2)}, u32[]{:S(2)}) collective-permute-start(bf16[2,96,768]{2,1,0:T(8,128)(2,1)S(1)} %pad_maximum_fusion.refs_0_), channel_id=1, source_target_pairs={{0,24},{4,28},{8,16},{12,20},{16,8},{20,12},{24,0},{28,4},{1,25},{... | collective-permute-start | bytes 884744 | tf_op jit(solution)/shard_map/ppermute | solution.py:851
  75.1 49.7 %all-to-all-start.1 = ((bf16[32,24,768]{2,1,0:T(8,128)(2,1)}), bf16[32,24,768]{2,1,0:T(8,128)(2,1)S(1)}, u32[]{:S(2)}, u32[]{:S(2)}) async-start(bf16[32,24,768]{2,1,0:T(8,128)(2,1)} %bitcast.7), calls=%async_computation.1 | async-start | bytes 2359296 | tf_op jit(solution)/shard_map/all_to_all | solution.py:951
  79.7 158.5 %reduce-scatter.2.cloned.1.call-start = ((), (), s32[]{:S(2)}) async-start(), calls=%async_computation.4 | async-start | bytes 2654208 | tf_op jit(solution)/shard_map/reduce_scatter | solution.py:981
  169.8 47.7 %collective-permute-start.14 = (bf16[2,2,256,768]{3,2,1,0:T(8,128)(2,1)S(1)}, bf16[2,2,256,768]{3,2,1,0:T(8,128)(2,1)S(1)}, u32[]{:S(2)}, u32[]{:S(2)}) collective-permute-start(bf16[2,2,256,768]{3,2,1,0:T(8,128)(2,1)S(1)} %fusion), channel_id=1, source_target_pairs={{0,2},{1,3},{2,0},{3,1},{4,6},{5,7},{6,4},{7,5},{8,10},{9,11},{10,... | collective-permute-start | bytes 4718600 | tf_op jit(solution)/shard_map/ppermute | solution.py:851
  218.7 56.8 %all-to-all-start.2 = ((bf16[32,28,576]{2,1,0:T(8,128)(2,1)}), bf16[32,28,576]{2,1,0:T(8,128)(2,1)S(1)}, u32[]{:S(2)}, u32[]{:S(2)}) async-start(bf16[32,28,576]{2,1,0:T(8,128)(2,1)} %get-tuple-element.111), calls=%async_computation.2 | async-start | bytes 2621440 | tf_op jit(solution)/shard_map/all_to_all | solution.py:951
  224.7 54.1 %collective-permute-start.20 = (bf16[1,2,256,768]{3,2,1,0:T(8,128)(2,1)}, bf16[1,2,256,768]{3,2,1,0:T(8,128)(2,1)S(1)}, u32[]{:S(2)}, u32[]{:S(2)}) collective-permute-start(bf16[1,2,256,768]{3,2,1,0:T(8,128)(2,1)} %fusion.1), channel_id=1, source_target_pairs={{0,2},{1,3},{2,0},{3,1},{4,6},{5,7},{6,4},{7,5},{8,10},{9,11},{10,... | collective-permute-start | bytes 2359304 | tf_op jit(solution)/shard_map/ppermute | solution.py:851
  240.1 25.3 %collective-permute-start.24 = (f32[24,768]{1,0:T(8,128)}, f32[24,768]{1,0:T(8,128)S(1)}, u32[]{:S(2)}, u32[]{:S(2)}) collective-permute-start(f32[24,768]{1,0:T(8,128)} %get-tuple-element.119), channel_id=1, source_target_pairs={{0,7},{1,13},{2,3},{3,26},{4,0},{5,14},{6,20},{7,27},{8,8},{9,15},... | collective-permute-start | bytes 221192 | tf_op jit(solution)/shard_map/ppermute | solution.py:1000
  242.9 13.6 %collective-permute-start.22 = (bf16[24,768]{1,0:T(8,128)(2,1)}, bf16[24,768]{1,0:T(8,128)(2,1)S(1)}, u32[]{:S(2)}, u32[]{:S(2)}) collective-permute-start(bf16[24,768]{1,0:T(8,128)(2,1)} %get-tuple-element.117), channel_id=1, source_target_pairs={{0,2},{1,3},{2,0},{3,1},{4,6},{5,7},{6,4},{7,5},{8,10},{9,11},{10,... | collective-permute-start | bytes 110600 | tf_op jit(solution)/shard_map/ppermute | solution.py:851
  243.4 15.1 %collective-permute-start.23 = (bf16[24,768]{1,0:T(8,128)(2,1)}, bf16[24,768]{1,0:T(8,128)(2,1)S(1)}, u32[]{:S(2)}, u32[]{:S(2)}) collective-permute-start(bf16[24,768]{1,0:T(8,128)(2,1)} %get-tuple-element.118), channel_id=1, source_target_pairs={{0,3},{1,2},{2,1},{3,0},{4,7},{5,6},{6,5},{7,4},{8,11},{9,10},{10,... | collective-permute-start | bytes 110600 | tf_op jit(solution)/shard_map/ppermute | solution.py:851
  244.4 25.4 %collective-permute-start.25 = (f32[24,768]{1,0:T(8,128)}, f32[24,768]{1,0:T(8,128)S(1)}, u32[]{:S(2)}, u32[]{:S(2)}) collective-permute-start(f32[24,768]{1,0:T(8,128)} %get-tuple-element.120), channel_id=1, source_target_pairs={{0,0},{1,13},{2,19},{3,26},{4,7},{5,14},{6,20},{7,5},{8,8},{9,2},{... | collective-permute-start | bytes 221192 | tf_op jit(solution)/shard_map/ppermute | solution.py:1000
  256.6 13.2 %collective-permute-start.26 = (f32[24,768]{1,0:T(8,128)}, f32[24,768]{1,0:T(8,128)S(1)}, u32[]{:S(2)}, u32[]{:S(2)}) collective-permute-start(f32[24,768]{1,0:T(8,128)} %get-tuple-element.121), channel_id=1, source_target_pairs={{0,6},{1,13},{2,19},{3,4},{4,7},{5,1},{6,20},{7,26},{8,8},{9,14},{... | collective-permute-start | bytes 221192 | tf_op jit(solution)/shard_map/ppermute | solution.py:1000
  258.5 11.3 %collective-permute-start.27 = (f32[24,768]{1,0:T(8,128)}, f32[24,768]{1,0:T(8,128)S(1)}, u32[]{:S(2)}, u32[]{:S(2)}) collective-permute-start(f32[24,768]{1,0:T(8,128)} %get-tuple-element.122), channel_id=1, source_target_pairs={{0,6},{1,1},{2,19},{3,25},{4,7},{5,13},{6,20},{7,26},{8,8},{9,14},... | collective-permute-start | bytes 221192 | tf_op jit(solution)/shard_map/ppermute | solution.py:1000
  (39 other events, 309.2 us)
Sparse Core Ops, SparseCore 0:
  14.2 60.9 all-gather.4
  77.3 34.2 all-gather.6
  161.3 76.8 reduce-scatter.1

commit v7 on v6

--- a/solution.py
+++ b/solution.py
@@ -298,13 +298,13 @@
         for k in range(per_ff):
             all_ref[k + 1] = ffn_ref[1, k].astype(all_ref.dtype)
         for k in range(per):
-            outs[k][...] = all_ref[table_ref[at_ref[0], per + k]]
+            outs[k][...] = all_ref[table_ref[at_ref[0], per + k]].astype(BF)
         for s in range(SLOTS):
             outs[per + s][...] = ffn_ref[0, at_ref[1] ^ s]
 
     return pl.pallas_call(
         kernel,
-        out_shape=[jax.ShapeDtypeStruct((unit, dim), F32)] * per + [jax.ShapeDtypeStruct((unit, dim), BF)] * SLOTS,
+        out_shape=[jax.ShapeDtypeStruct((unit, dim), BF)] * (per + SLOTS),
         in_specs=[SMEM] * 2 + [VMEM] * (1 + len(heads)),
         out_specs=[VMEM] * (per + SLOTS),
         scratch_shapes=[pltpu.VMEM((per, unit, dim), F32)],
@@ -332,7 +332,7 @@
             for k in range(3):
                 in_ref[:, k * nt * local + t * local : k * nt * local + (t + 1) * local] = total[:, k * local : (k + 1) * local]
         for k, ref in enumerate(got_refs):
-            out_ref[table_ref[at_ref[0], k]] = ref[...]
+            out_ref[table_ref[at_ref[0], k]] = ref[...].astype(F32)
         small = add_blocks(qkv_ref, count, 1, 0, slice(unit, high))
         small = small[0:2] + small[2:4]
         norm_ref[:, :width] = small[0:1]
@@ -519,7 +519,7 @@
             dv_ref[h] = jnp.zeros(dv_ref.shape[1:], F32)
             return carry
 
-        lax.fori_loop(0, heads, prepare, 0)
+        lax.fori_loop(0, heads, prepare, 0, unroll=True)
 
         def step(n, carry):
             h = n // blocks
@@ -537,7 +537,7 @@
             ds = (e * mm(va_ref[h], doa.astype(BF))).astype(BF)
             dq_ref[n] = mm(kt_ref[h], ds)
             dk_ref[h] += mm(ds, qn_ref[n])
-            dv_ref[h] += mm(eb, doa.T.astype(BF))
+            dv_ref[h] += mm(dos, eb, NT)
             do_ref[n] = jnp.where(padb > 0, vm_ref[h], o).astype(BF)
             return carry
 
@@ -556,12 +556,12 @@
                     g - jnp.mean(g, axis=0, keepdims=True) - unit * jnp.mean(g * unit, axis=0, keepdims=True)
                 )
                 grad_ref[s, rows(k * width), :] = back.astype(BF)
-            grad_ref[s, rows(2 * width), :] = dv_ref[h].T[:HD].astype(BF)
+            grad_ref[s, rows(2 * width), :] = dv_ref[h].astype(BF)
             for i in range(blocks):
                 o_ref[s, rows(0), pl.ds(i * block, block)] = do_ref[h * blocks + i]
             return carry
 
-        lax.fori_loop(0, heads, finish, 0)
+        lax.fori_loop(0, heads, finish, 0, unroll=True)
         if last:
 
             @pl.when(s == 0)
@@ -614,7 +614,7 @@
     heads = width // HD
     _, seqs, _, part, _ = pays.shape
     length = part * SLOTS
-    block = 512
+    block = 1024
     blocks = length // block
     last = bool(more)
     ins = [at, ids, qg, kg, *hbm(wqkv, wo, pays), *more[:3], *hbm(*more[3:])]
@@ -660,7 +660,7 @@
             pltpu.VMEM((heads * blocks, HD, block), BF),
             pltpu.VMEM((heads * blocks, HD, block), F32),
             pltpu.VMEM((heads, length, HD), F32),
-            pltpu.VMEM((heads, length, 2 * HD), F32),
+            pltpu.VMEM((heads, HD, length), F32),
             pltpu.VMEM((blocks, 1, block), F32),
             pltpu.VMEM((heads, HD, 1), F32),
             pltpu.SemaphoreType.DMA((4,)),
@@ -720,32 +720,54 @@
             pltpu.make_async_copy(gup_ref.at[at_rows, :], gup_hbm.at[at_rows, :], out_sem.at[1, i]),
         )
 
-    def step(i, carry):
+    def arrive(i):
         for j in range(block // part):
             for k, to in enumerate((norm_ref, gb_ref)):
                 pltpu.make_async_copy(pays[0].at[0, 0, 0], to.at[pl.ds(0, part), :], sem.at[k, i * (block // part) + j]).wait()
-        at_rows = pl.ds(pl.multiple_of(i * block, block), block)
-        up = mm(norm_ref[at_rows, :], wup_ref[...])
-        gh = mm(gb_ref[at_rows, :], wff_ref[...], NT)
+
+    def rows_of(i):
+        return pl.ds(pl.multiple_of(i * block, block), block)
+
+    def units(i):
+        up = mm(norm_ref[rows_of(i), :], wup_ref[...])
+        gh = mm(gb_ref[rows_of(i), :], wff_ref[...], NT)
         sq = up * up
         t = jnp.tanh(up * (c0 + (c0 * c1) * sq))
         half = 0.5 + 0.5 * t
-        hid_ref[at_rows, :] = (up * half).astype(BF)
-        gup_ref[at_rows, :] = (gh * (half + (0.5 * up) * (1.0 - t * t) * (c0 + (3.0 * c0 * c1) * sq))).astype(BF)
-        for copy in outs(i):
+        hid_ref[rows_of(i), :] = (up * half).astype(BF)
+        gup_ref[rows_of(i), :] = (gh * (half + (0.5 * up) * (1.0 - t * t) * (c0 + (3.0 * c0 * c1) * sq))).astype(BF)
+
+    def grads(i):
+        gin_ref[...] += mm(norm_ref[rows_of(i), :], gup_ref[rows_of(i), :], TN)
+        gff_ref[...] += mm(hid_ref[rows_of(i), :], gb_ref[rows_of(i), :], TN)
+
+    count = total // block
+    arrive(0)
+    units(0)
+
+    def step(i, carry):
+        for copy in outs(i - 1):
             copy.start()
-        gin_ref[...] += mm(norm_ref[at_rows, :], gup_ref[at_rows, :], TN)
-        gff_ref[...] += mm(hid_ref[at_rows, :], gb_ref[at_rows, :], TN)
+        arrive(i)
+        grads(i - 1)
+        units(i)
         return carry
 
-    lax.fori_loop(0, total // block, step, 0)
+    lax.fori_loop(1, count, step, 0)
+    for copy in outs(count - 1):
+        copy.start()
+    grads(count - 1)
     for copy in late:
         copy.wait()
     results = Outputs(at_ref[1], keep_hbm, leave_hbm, res_ref, res_sem, wo_ref, wff_ref, wqkv_ref, wup_ref)
     length = SLOTS * part
-    for s in range(results.seqs):
-        rows_s = pl.ds(s * length, length)
+
+    def result(s, carry):
+        rows_s = pl.ds(pl.multiple_of(s * length, length), length)
         results.compute(s, o_ref.at[s], hid_ref.at[rows_s, :], gq_ref.at[s], gup_ref.at[rows_s, :])
+        return carry
+
+    lax.fori_loop(0, results.seqs, result, 0)
     line = jnp.sum(wup_ref[...].astype(F32) * gin_ref[...], axis=1, keepdims=True)
     np_ref[...] = jnp.broadcast_to(line, (dim, 128)).T[0:1]
     for b in range(dim // rows):
@@ -998,9 +1020,9 @@
     sends, up = outs[:per], outs[per:]
     up = [up[0]] + [swap(up[s], "tok", nt, s) for s in range(1, nt)]
     got = [lax.ppermute(v, both, [(b, a) for a, b in perm]) for v, perm in zip(sends, perms)]
-    in_grad, out_grad, norm_grad, query_grad, key_grad = place(at, table, a_q, up, got)
-
     earlier = after(lead, image_ids, patches, cotangent, gain, keep1, near1, away1, earlier)
+    in_grad, out_grad, norm_grad, query_grad, key_grad = place(at, table, tie(a_q, *earlier), up, got)
+
     block_out, patch_grad = earlier
     return (
         block_out,

time: 291 us -> 276 us (0.948)
  waiting for transfers between devices: 51.6 us -> 44.4 us
  Pallas kernels: 125 us -> 118 us
    ppermute x19, waiting for transfers between devices: 32.6 us -> 25.7 us  [swap(): return lax.ppermute(value, axis, [(i, i ^ mask) for i in range(count)])]
    pallas_call x2, Pallas kernels: 68.5 us -> 61.8 us  [attention(): pl.pallas_call(functools.partial(attention_kernel, heads, block, last, st...]
    ppermute x5, waiting for transfers between devices: 5.74 us -> 1.9 us  [per_device(): lax.ppermute(v, both, [(b, a) for a, b in perm])]
    reduce_scatter x1, waiting for transfers between devices: 8.41 us -> 11.5 us  [per_device(): lax.psum_scatter(f_grad, 'batch', scatter_dimension=0, tiled=True)]
  transfers between devices with their start and end apart: 35 -> 35, of which waited for: 14 -> 15; matrix products, arithmetic and copies ran while one was open for 3% -> 3% of each run, Pallas kernels for 28% -> 27%
where the time goes in v7:
time: 276 us; the launch traced here: 275 us
  Pallas kernels  118 us (43%)
  starting transfers between devices  84.3 us (31%)
  waiting for transfers between devices  44.4 us (16%)
  between operations  14.2 us (5%)
  other arithmetic  7.64 us (3%)
  local copies, waits for them, and re-layouts  6.99 us (3%)
    pallas_call x2, Pallas kernels, attention(): pl.pallas_call(functools.partial(attention_kernel, heads, block, last, st...  61.8 us
    pallas_call x1, Pallas kernels, ffn(): pl.pallas_call(functools.partial(ffn_kernel, block, sizes, [masks for _,...  34 us
    ppermute x19, starting transfers between devices, swap(): return lax.ppermute(value, axis, [(i, i ^ mask) for i in range(count)])  31 us
    ppermute x19, waiting for transfers between devices, swap(): return lax.ppermute(value, axis, [(i, i ^ mask) for i in range(count)])  25.7 us
    ppermute x5, starting transfers between devices, per_device(): got = [lax.ppermute(v, both, perm) for v, perm in zip(unit_sends, perms)]  20 us
    ppermute x5, starting transfers between devices, per_device(): lax.ppermute(v, both, [(b, a) for a, b in perm])  18.9 us
    all_to_all x3, starting transfers between devices, exchange(): return lax.all_to_all(value, axis, split_axis=0, concat_axis=0, tiled=True)  14.1 us
    reduce_scatter x1, waiting for transfers between devices, per_device(): lax.psum_scatter(f_grad, 'batch', scatter_dimension=0, tiled=True)  11.5 us
  transfers between devices with their start and end apart: 35, of which 15 were waited for; matrix products, arithmetic and copies ran while one was open for 3% of the time, Pallas kernels for 27%

profile of v7, /device:TPU:2, one launch (start us, length us, event | category | flops | bytes accessed | tf_op | source)
XLA Modules:
  0.0 275.2 jit_solution(3598570205081991829)
XLA Ops:
  9.9 4.2 %before.1 = (bf16[2,2,256,768]{3,2,1,0:T(8,128)(2,1)}, bf16[1,2,256,768]{3,2,1,0:T(8,128)(2,1)}, bf16[24,768]{1,0:T(8,128)(2,1)S(1)}, bf16[24,768]{1,0:T(8,128)(...) custom-call(s32[3]{0:T(128)S(1)} %pad_add_fusion.at_ref, ...), custom_call_target="tpu_custom_call" | custom-call | flops 1 | bytes 1 | tf_op jit(solution)/shard_map/before/pallas_call | solution.py:152
  14.1 6.1 %all-to-all-start = ((bf16[32,26,576]{2,1,0:T(8,128)(2,1)}), bf16[32,26,576]{2,1,0:T(8,128)(2,1)S(1)}, u32[]{:S(2)}, u32[]{:S(2)}) async-start(bf16[32,26,576]{2,1,0:T(8,128)(2,1)} %bitcast.3), calls=%async_computation | async-start | bytes 2621440 | tf_op jit(solution)/shard_map/all_to_all | solution.py:973
  20.3 5.2 %collective-permute-start = (bf16[24,768]{1,0:T(8,128)(2,1)S(1)}, bf16[24,768]{1,0:T(8,128)(2,1)S(1)}, u32[]{:S(2)}, u32[]{:S(2)}) collective-permute-start(bf16[24,768]{1,0:T(8,128)(2,1)S(1)} %get-tuple-element.71), channel_id=1, source_target_pairs={{7,0},{13,1},{3,2},{26,3},{0,4},{14,5},{20,6},{27,7},{8,8},{15,9},... | collective-permute-start | bytes 110600 | tf_op jit(solution)/shard_map/ppermute | solution.py:983
  25.5 3.1 %collective-permute-start.1 = (bf16[24,768]{1,0:T(8,128)(2,1)S(1)}, bf16[24,768]{1,0:T(8,128)(2,1)S(1)}, u32[]{:S(2)}, u32[]{:S(2)}) collective-permute-start(bf16[24,768]{1,0:T(8,128)(2,1)S(1)} %get-tuple-element.72), channel_id=1, source_target_pairs={{0,0},{13,1},{19,2},{26,3},{7,4},{14,5},{20,6},{5,7},{8,8},{2,9},{... | collective-permute-start | bytes 110600 | tf_op jit(solution)/shard_map/ppermute | solution.py:983
  28.6 3.7 %collective-permute-start.2 = (bf16[24,768]{1,0:T(8,128)(2,1)S(1)}, bf16[24,768]{1,0:T(8,128)(2,1)S(1)}, u32[]{:S(2)}, u32[]{:S(2)}) collective-permute-start(bf16[24,768]{1,0:T(8,128)(2,1)S(1)} %get-tuple-element.73), channel_id=1, source_target_pairs={{6,0},{13,1},{19,2},{4,3},{7,4},{1,5},{20,6},{26,7},{8,8},{14,9},{... | collective-permute-start | bytes 110600 | tf_op jit(solution)/shard_map/ppermute | solution.py:983
  35.0 5.2 %collective-permute-start.4 = (bf16[24,768]{1,0:T(8,128)(2,1)S(1)}, bf16[24,768]{1,0:T(8,128)(2,1)S(1)}, u32[]{:S(2)}, u32[]{:S(2)}) collective-permute-start(bf16[24,768]{1,0:T(8,128)(2,1)S(1)} %get-tuple-element.75), channel_id=1, source_target_pairs={{6,0},{12,1},{19,2},{25,3},{7,4},{13,5},{3,6},{26,7},{0,8},{14,9},... | collective-permute-start | bytes 110600 | tf_op jit(solution)/shard_map/ppermute | solution.py:983
  47.7 9.7 %collective-permute-start.5 = (bf16[1,24,768]{2,1,0:T(8,128)(2,1)}, bf16[1,24,768]{2,1,0:T(8,128)(2,1)S(1)}, u32[]{:S(2)}, u32[]{:S(2)}) collective-permute-start(bf16[1,24,768]{2,1,0:T(8,128)(2,1)} %bitcast.29), channel_id=1, source_target_pairs={{0,8},{4,12},{8,0},{12,4},{16,24},{20,28},{24,16},{28,20},{1,9},{5... | collective-permute-start | bytes 110600 | tf_op jit(solution)/shard_map/ppermute | solution.py:873
  57.4 4.1 %collective-permute-start.6 = (bf16[1,24,768]{2,1,0:T(8,128)(2,1)}, bf16[1,24,768]{2,1,0:T(8,128)(2,1)S(1)}, u32[]{:S(2)}, u32[]{:S(2)}) collective-permute-start(bf16[1,24,768]{2,1,0:T(8,128)(2,1)} %bitcast.30), channel_id=1, source_target_pairs={{0,16},{4,20},{8,24},{12,28},{16,0},{20,4},{24,8},{28,12},{1,17},{... | collective-permute-start | bytes 110600 | tf_op jit(solution)/shard_map/ppermute | solution.py:873
  64.0 3.5 %collective-permute-done.7 = bf16[1,24,768]{2,1,0:T(8,128)(2,1)S(1)} collective-permute-done((bf16[1,24,768]{2,1,0:T(8,128)(2,1)}, bf16[1,24,768]{2,1,0:T(8,128)(2,1)S(1)}, u32[]{:S(2)}, u32[]{:S(2)}) %collective-permute-start.7) | collective-permute-done | bytes 36896 | tf_op jit(solution)/shard_map/ppermute | solution.py:873
  75.1 4.7 %all-to-all-start.1 = ((bf16[32,24,768]{2,1,0:T(8,128)(2,1)}), bf16[32,24,768]{2,1,0:T(8,128)(2,1)S(1)}, u32[]{:S(2)}, u32[]{:S(2)}) async-start(bf16[32,24,768]{2,1,0:T(8,128)(2,1)} %bitcast.7), calls=%async_computation.1 | async-start | bytes 2359296 | tf_op jit(solution)/shard_map/all_to_all | solution.py:973
  83.3 36.4 %attention.2 = (bf16[2,192,1024]{2,1,0:T(8,128)(2,1)}, bf16[2,576,1024]{2,1,0:T(8,128)(2,1)}, f32[2,64,128]{2,1,0:T(8,128)}, f32[576,768]{1,0:T(8,128)}, f32[192,768]{1,0:T(8,128)}) custom-call(s32[3]{0:T(128)} %copy-done.5, s32[3,1,1024]{2,1,0:T(1,128)} %copy-done.11, f32[64]{0:T(128)} %qg_ref.3, f32[64]{0:T(128)} %kg_ref.3, bf16[576,768]{1,0:T(8,128)(2,1)} %copy-done.9, ...), custom_call_target="tpu_custom_call" | custom-call | flops 60000002048 | bytes 1 | tf_op jit(solution)/shard_map/attention/pallas_call | solution.py:638
  121.3 34.0 %ffn.1 = (bf16[3072,768]{1,0:T(8,128)(2,1)}, bf16[3072,768]{1,0:T(8,128)(2,1)}, bf16[768,768]{1,0:T(8,128)(2,1)}, bf16[2,2,2,256,768]{4,3,2,1,0:T(8,128)(2,1)}, ...) custom-call(s32[3]{0:T(128)} %copy-done.5, bf16[768,768]{1,0:T(8,128)(2,1)} %bitcast.23, ...), custom_call_target="tpu_custom_call" | custom-call | flops 60000002048 | bytes 1 | tf_op jit(solution)/shard_map/ffn/pallas_call | solution.py:794
  155.6 5.7 %collective-permute-done.13.near_ref = bf16[2,2,2,256,768]{4,3,2,1,0:T(8,128)(2,1)S(1)} collective-permute-done((bf16[2,2,2,256,768]{4,3,2,1,0:T(8,128)(2,1)}, bf16[2,2,2,256,768]{4,3,2,1,0:T(8,128)(2,1)S(1)}, u32[]{:S(2)}, u32[]{:S(2)}) %collective-permute-start.13) | collective-permute-done | bytes 3145760 | tf_op jit(solution)/shard_map/ppermute | solution.py:873
  161.3 2.9 %fusion = bf16[2,2,256,768]{3,2,1,0:T(8,128)(2,1)S(1)} fusion(bf16[2,2,2,256,768]{4,3,2,1,0:T(8,128)(2,1)S(1)} %collective-permute-done.13.near_ref, bf16[2,2,2,256,768]{4,3,2,1,0:T(8,128)(2,1)} %get-tuple-element.90.keep_ref), kind=kLoop, calls=%fused_computation.1 | loop fusion | flops 3145728 | bytes 4718592 | tf_op jit(solution)/shard_map/convert_element_type | solution.py:996
  166.2 25.4 %attention.3 = (bf16[2,1,2,256,768]{4,3,2,1,0:T(8,128)(2,1)}, bf16[2,1,2,256,768]{4,3,2,1,0:T(8,128)(2,1)}, bf16[32,28,576]{2,1,0:T(8,128)(2,1)}, bf16[4,24,768]{2,1,0:T(8,128)(2,1)}, f32[4,24,768]{2,1,0:T(8,128)}) custom-call(s32[3]{0:T(128)} %copy-done.5, s32[3,1,1024]{2,1,0:T(1,128)} %copy-done.11, f32[64]{0:T(128)} %qg_ref.3, f32[64]{0:T(128)} %kg_ref.3, ...), custom_call_target="tpu_custom_call" | custom-call | flops 60000002048 | bytes 1 | tf_op jit(solution)/shard_map/attention/pallas_call | solution.py:638
  192.0 6.7 %collective-permute-done.15.refs_1_ = bf16[4,24,768]{2,1,0:T(8,128)(2,1)S(1)} collective-permute-done((bf16[4,24,768]{2,1,0:T(8,128)(2,1)}, bf16[4,24,768]{2,1,0:T(8,128)(2,1)S(1)}, u32[]{:S(2)}, u32[]{:S(2)}) %collective-permute-start.15) | collective-permute-done | bytes 147488 | tf_op jit(solution)/shard_map/ppermute | solution.py:873
  210.7 3.3 %all-to-all-start.2 = ((bf16[32,28,576]{2,1,0:T(8,128)(2,1)}), bf16[32,28,576]{2,1,0:T(8,128)(2,1)S(1)}, u32[]{:S(2)}, u32[]{:S(2)}) async-start(bf16[32,28,576]{2,1,0:T(8,128)(2,1)} %get-tuple-element.112), calls=%async_computation.2 | async-start | bytes 2621440 | tf_op jit(solution)/shard_map/all_to_all | solution.py:973
  217.9 4.4 %after.2 = (bf16[3,256,768]{2,1,0:T(8,128)(2,1)}, bf16[3,256,768]{2,1,0:T(8,128)(2,1)}) custom-call(s32[3,1,256]{2,1,0:T(1,128)S(1)} %reshape.88.ids_ref, bf16[3,256,768]{2,1,0:T(8,128)(2,1)} %x_ref.3, bf16[3,256,768]{2,1,0:T(8,128)(2,1)} %cot_ref.3, f32[768]{0:T(1024)S(1)} %copy-done.3, bf16[2,2,2,256,768]{4,3,2,1,0:T(8,128)(2,1)} %get-tuple-element.90.keep_ref, ...), custom_call_target="tpu_custom_call" | custom-call | flops 1 | bytes 1 | tf_op jit(solution)/shard_map/after/pallas_call | solution.py:375
  222.4 11.5 %reduce-scatter.2.cloned.1.call-done = bf16[1,2,96,768]{3,2,1,0:T(8,128)(2,1)} async-done(((bf16[8,2,96,768]{3,2,1,0:T(8,128)(2,1)}), bf16[1,2,96,768]{3,2,1,0:T(8,128)(2,1)}) %reduce-scatter.2.cloned.1.call-update) | async-done | bytes 294928 | tf_op jit(solution)/shard_map/reduce_scatter | solution.py:1003
  239.6 4.6 %collective-permute-start.25 = (bf16[24,768]{1,0:T(8,128)(2,1)}, bf16[24,768]{1,0:T(8,128)(2,1)S(1)}, u32[]{:S(2)}, u32[]{:S(2)}) collective-permute-start(bf16[24,768]{1,0:T(8,128)(2,1)} %get-tuple-element.122), channel_id=1, source_target_pairs={{0,0},{1,13},{2,19},{3,26},{4,7},{5,14},{6,20},{7,5},{8,8},{9,2},{... | collective-permute-start | bytes 110600 | tf_op jit(solution)/shard_map/ppermute | solution.py:1022
  244.2 4.0 %collective-permute-done.22.refs_2_ = bf16[24,768]{1,0:T(8,128)(2,1)S(1)} collective-permute-done((bf16[24,768]{1,0:T(8,128)(2,1)}, bf16[24,768]{1,0:T(8,128)(2,1)S(1)}, u32[]{:S(2)}, u32[]{:S(2)}) %collective-permute-start.22) | collective-permute-done | bytes 36896 | tf_op jit(solution)/shard_map/ppermute | solution.py:873
  250.1 6.1 %collective-permute-start.27 = (bf16[24,768]{1,0:T(8,128)(2,1)}, bf16[24,768]{1,0:T(8,128)(2,1)S(1)}, u32[]{:S(2)}, u32[]{:S(2)}) collective-permute-start(bf16[24,768]{1,0:T(8,128)(2,1)} %get-tuple-element.124), channel_id=1, source_target_pairs={{0,6},{1,1},{2,19},{3,25},{4,7},{5,13},{6,20},{7,26},{8,8},{9,14},... | collective-permute-start | bytes 110600 | tf_op jit(solution)/shard_map/ppermute | solution.py:1022
  256.3 4.4 %collective-permute-start.28 = (bf16[24,768]{1,0:T(8,128)(2,1)}, bf16[24,768]{1,0:T(8,128)(2,1)S(1)}, u32[]{:S(2)}, u32[]{:S(2)}) collective-permute-start(bf16[24,768]{1,0:T(8,128)(2,1)} %get-tuple-element.125), channel_id=1, source_target_pairs={{0,6},{1,12},{2,19},{3,25},{4,7},{5,13},{6,3},{7,26},{8,0},{9,14},... | collective-permute-start | bytes 110600 | tf_op jit(solution)/shard_map/ppermute | solution.py:1022
  260.7 3.5 %after.3 = (bf16[3,256,768]{2,1,0:T(8,128)(2,1)}, bf16[3,256,768]{2,1,0:T(8,128)(2,1)}) custom-call(s32[3,1,256]{2,1,0:T(1,128)S(1)} %reshape.88.ids_ref, bf16[3,256,768]{2,1,0:T(8,128)(2,1)} %x_ref.3, bf16[3,256,768]{2,1,0:T(8,128)(2,1)} %cot_ref.3, f32[768]{0:T(1024)S(1)} %copy-done.3, ...), custom_call_target="tpu_custom_call", output_to_operand_aliasing={{0}: (7, {}), {1}: (8, {})} | custom-call | flops 1 | bytes 1 | tf_op jit(solution)/shard_map/after/pallas_call | solution.py:375
  (124 shorter events, 58.5 us)
Async XLA Ops:
  7.2 76.1 %all-gather.5.cloned.1.call-start = ((), (), s32[]{:S(2)}) async-start(), calls=%async_computation.5 | async-start | bytes 7864320 | tf_op jit(solution)/shard_map/all_gather | solution.py:985
  14.1 54.2 %all-to-all-start = ((bf16[32,26,576]{2,1,0:T(8,128)(2,1)}), bf16[32,26,576]{2,1,0:T(8,128)(2,1)S(1)}, u32[]{:S(2)}, u32[]{:S(2)}) async-start(bf16[32,26,576]{2,1,0:T(8,128)(2,1)} %bitcast.3), calls=%async_computation | async-start | bytes 2621440 | tf_op jit(solution)/shard_map/all_to_all | solution.py:973
  20.2 100.0 %all-gather.7.cloned.1.call-start = ((), (), s32[]{:S(2)}) async-start(), calls=%async_computation.6 | async-start | bytes 3932160 | tf_op jit(solution)/shard_map/all_gather | solution.py:986
  20.3 22.9 %collective-permute-start = (bf16[24,768]{1,0:T(8,128)(2,1)S(1)}, bf16[24,768]{1,0:T(8,128)(2,1)S(1)}, u32[]{:S(2)}, u32[]{:S(2)}) collective-permute-start(bf16[24,768]{1,0:T(8,128)(2,1)S(1)} %get-tuple-element.71), channel_id=1, source_target_pairs={{7,0},{13,1},{3,2},{26,3},{0,4},{14,5},{20,6},{27,7},{8,8},{15,9},... | collective-permute-start | bytes 110600 | tf_op jit(solution)/shard_map/ppermute | solution.py:983
  25.5 18.5 %collective-permute-start.1 = (bf16[24,768]{1,0:T(8,128)(2,1)S(1)}, bf16[24,768]{1,0:T(8,128)(2,1)S(1)}, u32[]{:S(2)}, u32[]{:S(2)}) collective-permute-start(bf16[24,768]{1,0:T(8,128)(2,1)S(1)} %get-tuple-element.72), channel_id=1, source_target_pairs={{0,0},{13,1},{19,2},{26,3},{7,4},{14,5},{20,6},{5,7},{8,8},{2,9},{... | collective-permute-start | bytes 110600 | tf_op jit(solution)/shard_map/ppermute | solution.py:983
  28.6 15.3 %collective-permute-start.2 = (bf16[24,768]{1,0:T(8,128)(2,1)S(1)}, bf16[24,768]{1,0:T(8,128)(2,1)S(1)}, u32[]{:S(2)}, u32[]{:S(2)}) collective-permute-start(bf16[24,768]{1,0:T(8,128)(2,1)S(1)} %get-tuple-element.73), channel_id=1, source_target_pairs={{6,0},{13,1},{19,2},{4,3},{7,4},{1,5},{20,6},{26,7},{8,8},{14,9},{... | collective-permute-start | bytes 110600 | tf_op jit(solution)/shard_map/ppermute | solution.py:983
  32.3 12.4 %collective-permute-start.3 = (bf16[24,768]{1,0:T(8,128)(2,1)S(1)}, bf16[24,768]{1,0:T(8,128)(2,1)S(1)}, u32[]{:S(2)}, u32[]{:S(2)}) collective-permute-start(bf16[24,768]{1,0:T(8,128)(2,1)S(1)} %get-tuple-element.74), channel_id=1, source_target_pairs={{6,0},{1,1},{19,2},{25,3},{7,4},{13,5},{20,6},{26,7},{8,8},{14,9},... | collective-permute-start | bytes 110600 | tf_op jit(solution)/shard_map/ppermute | solution.py:983
  35.0 10.1 %collective-permute-start.4 = (bf16[24,768]{1,0:T(8,128)(2,1)S(1)}, bf16[24,768]{1,0:T(8,128)(2,1)S(1)}, u32[]{:S(2)}, u32[]{:S(2)}) collective-permute-start(bf16[24,768]{1,0:T(8,128)(2,1)S(1)} %get-tuple-element.75), channel_id=1, source_target_pairs={{6,0},{12,1},{19,2},{25,3},{7,4},{13,5},{3,6},{26,7},{0,8},{14,9},... | collective-permute-start | bytes 110600 | tf_op jit(solution)/shard_map/ppermute | solution.py:983
  47.7 15.2 %collective-permute-start.5 = (bf16[1,24,768]{2,1,0:T(8,128)(2,1)}, bf16[1,24,768]{2,1,0:T(8,128)(2,1)S(1)}, u32[]{:S(2)}, u32[]{:S(2)}) collective-permute-start(bf16[1,24,768]{2,1,0:T(8,128)(2,1)} %bitcast.29), channel_id=1, source_target_pairs={{0,8},{4,12},{8,0},{12,4},{16,24},{20,28},{24,16},{28,20},{1,9},{5... | collective-permute-start | bytes 110600 | tf_op jit(solution)/shard_map/ppermute | solution.py:873
  68.3 11.7 %collective-permute-start.8 = (bf16[4,24,768]{2,1,0:T(8,128)(2,1)S(1)}, bf16[4,24,768]{2,1,0:T(8,128)(2,1)S(1)}, u32[]{:S(2)}, u32[]{:S(2)}) collective-permute-start(bf16[4,24,768]{2,1,0:T(8,128)(2,1)S(1)} %pad_maximum_fusion.1.refs_0_), channel_id=1, source_target_pairs={{0,4},{4,0},{8,12},{12,8},{16,20},{20,16},{24,28},{28,24},{1,5},{5... | collective-permute-start | bytes 442376 | tf_op jit(solution)/shard_map/ppermute | solution.py:873
  70.6 49.6 %collective-permute-start.10 = (bf16[2,96,768]{2,1,0:T(8,128)(2,1)S(1)}, bf16[2,96,768]{2,1,0:T(8,128)(2,1)S(1)}, u32[]{:S(2)}, u32[]{:S(2)}) collective-permute-start(bf16[2,96,768]{2,1,0:T(8,128)(2,1)S(1)} %pad_maximum_fusion.refs_0_), channel_id=1, source_target_pairs={{0,8},{4,12},{8,0},{12,4},{16,24},{20,28},{24,16},{28,20},{1,9},{5... | collective-permute-start | bytes 884744 | tf_op jit(solution)/shard_map/ppermute | solution.py:873
  71.4 48.8 %collective-permute-start.11 = (bf16[2,96,768]{2,1,0:T(8,128)(2,1)S(1)}, bf16[2,96,768]{2,1,0:T(8,128)(2,1)}, u32[]{:S(2)}, u32[]{:S(2)}) collective-permute-start(bf16[2,96,768]{2,1,0:T(8,128)(2,1)S(1)} %pad_maximum_fusion.refs_0_), channel_id=1, source_target_pairs={{0,16},{4,20},{8,24},{12,28},{16,0},{20,4},{24,8},{28,12},{1,17},{... | collective-permute-start | bytes 884744 | tf_op jit(solution)/shard_map/ppermute | solution.py:873
  73.2 47.0 %collective-permute-start.12 = (bf16[2,96,768]{2,1,0:T(8,128)(2,1)S(1)}, bf16[2,96,768]{2,1,0:T(8,128)(2,1)}, u32[]{:S(2)}, u32[]{:S(2)}) collective-permute-start(bf16[2,96,768]{2,1,0:T(8,128)(2,1)S(1)} %pad_maximum_fusion.refs_0_), channel_id=1, source_target_pairs={{0,24},{4,28},{8,16},{12,20},{16,8},{20,12},{24,0},{28,4},{1,25},{... | collective-permute-start | bytes 884744 | tf_op jit(solution)/shard_map/ppermute | solution.py:873
  75.1 45.1 %all-to-all-start.1 = ((bf16[32,24,768]{2,1,0:T(8,128)(2,1)}), bf16[32,24,768]{2,1,0:T(8,128)(2,1)S(1)}, u32[]{:S(2)}, u32[]{:S(2)}) async-start(bf16[32,24,768]{2,1,0:T(8,128)(2,1)} %bitcast.7), calls=%async_computation.1 | async-start | bytes 2359296 | tf_op jit(solution)/shard_map/all_to_all | solution.py:973
  79.7 154.2 %reduce-scatter.2.cloned.1.call-start = ((), (), s32[]{:S(2)}) async-start(), calls=%async_computation.4 | async-start | bytes 2654208 | tf_op jit(solution)/shard_map/reduce_scatter | solution.py:1003
  164.2 45.3 %collective-permute-start.14 = (bf16[2,2,256,768]{3,2,1,0:T(8,128)(2,1)S(1)}, bf16[2,2,256,768]{3,2,1,0:T(8,128)(2,1)S(1)}, u32[]{:S(2)}, u32[]{:S(2)}) collective-permute-start(bf16[2,2,256,768]{3,2,1,0:T(8,128)(2,1)S(1)} %fusion), channel_id=1, source_target_pairs={{0,2},{1,3},{2,0},{3,1},{4,6},{5,7},{6,4},{7,5},{8,10},{9,11},{10,... | collective-permute-start | bytes 4718600 | tf_op jit(solution)/shard_map/ppermute | solution.py:873
  210.7 53.5 %all-to-all-start.2 = ((bf16[32,28,576]{2,1,0:T(8,128)(2,1)}), bf16[32,28,576]{2,1,0:T(8,128)(2,1)S(1)}, u32[]{:S(2)}, u32[]{:S(2)}) async-start(bf16[32,28,576]{2,1,0:T(8,128)(2,1)} %get-tuple-element.112), calls=%async_computation.2 | async-start | bytes 2621440 | tf_op jit(solution)/shard_map/all_to_all | solution.py:973
  216.8 39.5 %collective-permute-start.20 = (bf16[1,2,256,768]{3,2,1,0:T(8,128)(2,1)}, bf16[1,2,256,768]{3,2,1,0:T(8,128)(2,1)S(1)}, u32[]{:S(2)}, u32[]{:S(2)}) collective-permute-start(bf16[1,2,256,768]{3,2,1,0:T(8,128)(2,1)} %fusion.1), channel_id=1, source_target_pairs={{0,2},{1,3},{2,0},{3,1},{4,6},{5,7},{6,4},{7,5},{8,10},{9,11},{10,... | collective-permute-start | bytes 2359304 | tf_op jit(solution)/shard_map/ppermute | solution.py:873
  235.8 12.4 %collective-permute-start.22 = (bf16[24,768]{1,0:T(8,128)(2,1)}, bf16[24,768]{1,0:T(8,128)(2,1)S(1)}, u32[]{:S(2)}, u32[]{:S(2)}) collective-permute-start(bf16[24,768]{1,0:T(8,128)(2,1)} %get-tuple-element.119), channel_id=1, source_target_pairs={{0,2},{1,3},{2,0},{3,1},{4,6},{5,7},{6,4},{7,5},{8,10},{9,11},{10,... | collective-permute-start | bytes 110600 | tf_op jit(solution)/shard_map/ppermute | solution.py:873
  236.5 13.6 %collective-permute-start.23 = (bf16[24,768]{1,0:T(8,128)(2,1)}, bf16[24,768]{1,0:T(8,128)(2,1)S(1)}, u32[]{:S(2)}, u32[]{:S(2)}) collective-permute-start(bf16[24,768]{1,0:T(8,128)(2,1)} %get-tuple-element.120), channel_id=1, source_target_pairs={{0,3},{1,2},{2,1},{3,0},{4,7},{5,6},{6,5},{7,4},{8,11},{9,10},{10,... | collective-permute-start | bytes 110600 | tf_op jit(solution)/shard_map/ppermute | solution.py:873
  237.7 26.5 %collective-permute-start.24 = (bf16[24,768]{1,0:T(8,128)(2,1)}, bf16[24,768]{1,0:T(8,128)(2,1)S(1)}, u32[]{:S(2)}, u32[]{:S(2)}) collective-permute-start(bf16[24,768]{1,0:T(8,128)(2,1)} %get-tuple-element.121), channel_id=1, source_target_pairs={{0,7},{1,13},{2,3},{3,26},{4,0},{5,14},{6,20},{7,27},{8,8},{9,15},... | collective-permute-start | bytes 110600 | tf_op jit(solution)/shard_map/ppermute | solution.py:1022
  239.6 24.6 %collective-permute-start.25 = (bf16[24,768]{1,0:T(8,128)(2,1)}, bf16[24,768]{1,0:T(8,128)(2,1)S(1)}, u32[]{:S(2)}, u32[]{:S(2)}) collective-permute-start(bf16[24,768]{1,0:T(8,128)(2,1)} %get-tuple-element.122), channel_id=1, source_target_pairs={{0,0},{1,13},{2,19},{3,26},{4,7},{5,14},{6,20},{7,5},{8,8},{9,2},{... | collective-permute-start | bytes 110600 | tf_op jit(solution)/shard_map/ppermute | solution.py:1022
  248.2 16.0 %collective-permute-start.26 = (bf16[24,768]{1,0:T(8,128)(2,1)}, bf16[24,768]{1,0:T(8,128)(2,1)S(1)}, u32[]{:S(2)}, u32[]{:S(2)}) collective-permute-start(bf16[24,768]{1,0:T(8,128)(2,1)} %get-tuple-element.123), channel_id=1, source_target_pairs={{0,6},{1,13},{2,19},{3,4},{4,7},{5,1},{6,20},{7,26},{8,8},{9,14},{... | collective-permute-start | bytes 110600 | tf_op jit(solution)/shard_map/ppermute | solution.py:1022
  250.1 14.1 %collective-permute-start.27 = (bf16[24,768]{1,0:T(8,128)(2,1)}, bf16[24,768]{1,0:T(8,128)(2,1)S(1)}, u32[]{:S(2)}, u32[]{:S(2)}) collective-permute-start(bf16[24,768]{1,0:T(8,128)(2,1)} %get-tuple-element.124), channel_id=1, source_target_pairs={{0,6},{1,1},{2,19},{3,25},{4,7},{5,13},{6,20},{7,26},{8,8},{9,14},... | collective-permute-start | bytes 110600 | tf_op jit(solution)/shard_map/ppermute | solution.py:1022
  (39 other events, 239.3 us)
Sparse Core Ops, SparseCore 0:
  14.2 60.9 all-gather.4
  77.3 34.3 all-gather.6
  155.7 78.1 reduce-scatter.1

commit v8 on v7

--- a/solution.py
+++ b/solution.py
@@ -335,19 +335,19 @@
             out_ref[table_ref[at_ref[0], k]] = ref[...].astype(F32)
         small = add_blocks(qkv_ref, count, 1, 0, slice(unit, high))
         small = small[0:2] + small[2:4]
-        norm_ref[:, :width] = small[0:1]
-        norm_ref[:, width:] = small[1:2, : dim - width]
-        q_ref[...] = small[1:2, dim - width : dim - width + HD]
-        k_ref[...] = small[1:2, dim - width + HD : dim - width + 2 * HD]
+        tail = dim - width
+        norm_ref[...] = jnp.concatenate([small[0:1], small[1:2, :tail]], axis=1).reshape(dim)
+        q_ref[...] = small[1:2, tail : tail + HD].reshape(HD)
+        k_ref[...] = small[1:2, tail + HD : tail + 2 * HD].reshape(HD)
 
     return pl.pallas_call(
         kernel,
         out_shape=[
             jax.ShapeDtypeStruct((unit, wide), F32),
             jax.ShapeDtypeStruct((per, unit, dim), F32),
-            jax.ShapeDtypeStruct((1, dim), F32),
-            jax.ShapeDtypeStruct((1, HD), F32),
-            jax.ShapeDtypeStruct((1, HD), F32),
+            jax.ShapeDtypeStruct((dim,), F32),
+            jax.ShapeDtypeStruct((HD,), F32),
+            jax.ShapeDtypeStruct((HD,), F32),
         ],
         in_specs=[SMEM] * 2 + [VMEM] * (1 + nt + per),
         out_specs=[VMEM] * 5,
@@ -617,8 +617,8 @@
     block = 1024
     blocks = length // block
     last = bool(more)
-    ins = [at, ids, qg, kg, *hbm(wqkv, wo, pays), *more[:3], *hbm(*more[3:])]
-    specs = [SMEM] + [VMEM] * 3 + [HBM] * 3 + ([VMEM] * 3 + [HBM] * 6 if last else [])
+    ins = [at, ids, qg, kg, wqkv, wo, *hbm(pays), *more[:3], *hbm(*more[3:])]
+    specs = [SMEM] + [VMEM] * 3 + [ANY] * 2 + [HBM] + ([VMEM] * 3 + [HBM] * 6 if last else [])
     scratch = []
     if last:
         outs = [jax.ShapeDtypeStruct((SLOTS // 2, seqs, 2, part, dim), BF)] * 2
@@ -668,7 +668,7 @@
             pltpu.SemaphoreType.DMA((seqs, 2)),
         ],
         cost_estimate=LARGE,
-        compiler_params=pltpu.CompilerParams(vmem_limit_bytes=56 * MIB),
+        compiler_params=pltpu.CompilerParams(vmem_limit_bytes=40 * MIB),
         name="attention",
     )(*ins)
 
@@ -801,7 +801,7 @@
             jax.ShapeDtypeStruct((count, 2, units // count, dim), BF),
             jax.ShapeDtypeStruct((1, dim), F32),
         ],
-        in_specs=[SMEM] + [HBM] * (5 + len(ff_parts) + len(pieces)),
+        in_specs=[SMEM] + [ANY] * 3 + [HBM] * (2 + len(ff_parts) + len(pieces)),
         out_specs=[HBM] * 5 + [VMEM] * 2,
         scratch_shapes=[
             pltpu.VMEM((total, dim), BF),
@@ -822,7 +822,7 @@
         cost_estimate=LARGE,
         compiler_params=pltpu.CompilerParams(vmem_limit_bytes=58 * MIB),
         name="ffn",
-    )(at, *hbm(wup, wqkv, wo, o, gq, *[a for a, _ in ff_parts], *pieces))
+    )(at, wup, wqkv, wo, *hbm(o, gq, *[a for a, _ in ff_parts], *pieces))
 
 
 class Outputs:
@@ -1027,9 +1027,9 @@
     return (
         block_out,
         patch_grad,
-        norm_grad.reshape(dim),
-        query_grad.reshape(HD),
-        key_grad.reshape(HD),
+        norm_grad,
+        query_grad,
+        key_grad,
         in_grad,
         out_grad.reshape(per * unit, dim),
     )

time: 276 us -> 274 us (level)
  Pallas kernels: 118 us -> 115 us
    pallas_call x2, Pallas kernels: 61.8 us -> 58.7 us  [attention(): pl.pallas_call(functools.partial(attention_kernel, heads, block, last, st...]
    unnamed x56 -> x66, local copies, waits for them, and re-layouts: 6.98 us -> 8.94 us
  transfers between devices with their start and end apart: 35 -> 35, of which waited for: 15 -> 15; matrix products, arithmetic and copies ran while one was open for 3% -> 2% of each run, Pallas kernels for 27% -> 26%
where the time goes in v8:
time: 274 us; the launch traced here: 273 us
  Pallas kernels  115 us (42%)
  starting transfers between devices  85.1 us (31%)
  waiting for transfers between devices  43.4 us (16%)
  between operations  14.2 us (5%)
  local copies, waits for them, and re-layouts  8.95 us (3%)
  other arithmetic  6.41 us (2%)
    pallas_call x2, Pallas kernels, attention(): pl.pallas_call(functools.partial(attention_kernel, heads, block, last, st...  58.7 us
    pallas_call x1, Pallas kernels, ffn(): pl.pallas_call(functools.partial(ffn_kernel, block, sizes, [masks for _,...  34.2 us
    ppermute x19, starting transfers between devices, swap(): return lax.ppermute(value, axis, [(i, i ^ mask) for i in range(count)])  31.2 us
    ppermute x19, waiting for transfers between devices, swap(): return lax.ppermute(value, axis, [(i, i ^ mask) for i in range(count)])  23.5 us
    ppermute x5, starting transfers between devices, per_device(): got = [lax.ppermute(v, both, perm) for v, perm in zip(unit_sends, perms)]  20 us
    ppermute x5, starting transfers between devices, per_device(): lax.ppermute(v, both, [(b, a) for a, b in perm])  19.1 us
    all_to_all x3, starting transfers between devices, exchange(): return lax.all_to_all(value, axis, split_axis=0, concat_axis=0, tiled=True)  14.4 us
    reduce_scatter x1, waiting for transfers between devices, per_device(): lax.psum_scatter(f_grad, 'batch', scatter_dimension=0, tiled=True)  12.9 us
  transfers between devices with their start and end apart: 35, of which 15 were waited for; matrix products, arithmetic and copies ran while one was open for 2% of the time, Pallas kernels for 26%

profile of v8, /device:TPU:2, one launch (start us, length us, event | category | flops | bytes accessed | tf_op | source)
XLA Modules:
  0.0 272.8 jit_solution(11203245999722181151)
XLA Ops:
  9.9 4.2 %before.1 = (bf16[2,2,256,768]{3,2,1,0:T(8,128)(2,1)}, bf16[1,2,256,768]{3,2,1,0:T(8,128)(2,1)}, bf16[24,768]{1,0:T(8,128)(2,1)S(1)}, bf16[24,768]{1,0:T(8,128)(...) custom-call(s32[3]{0:T(128)S(1)} %pad_add_fusion.at_ref, ...), custom_call_target="tpu_custom_call" | custom-call | flops 1 | bytes 1 | tf_op jit(solution)/shard_map/before/pallas_call | solution.py:152
  14.1 6.1 %all-to-all-start = ((bf16[32,26,576]{2,1,0:T(8,128)(2,1)}), bf16[32,26,576]{2,1,0:T(8,128)(2,1)S(1)}, u32[]{:S(2)}, u32[]{:S(2)}) async-start(bf16[32,26,576]{2,1,0:T(8,128)(2,1)} %bitcast.3), calls=%async_computation | async-start | bytes 2621440 | tf_op jit(solution)/shard_map/all_to_all | solution.py:973
  20.3 5.2 %collective-permute-start = (bf16[24,768]{1,0:T(8,128)(2,1)S(1)}, bf16[24,768]{1,0:T(8,128)(2,1)S(1)}, u32[]{:S(2)}, u32[]{:S(2)}) collective-permute-start(bf16[24,768]{1,0:T(8,128)(2,1)S(1)} %get-tuple-element.71), channel_id=1, source_target_pairs={{7,0},{13,1},{3,2},{26,3},{0,4},{14,5},{20,6},{27,7},{8,8},{15,9},... | collective-permute-start | bytes 110600 | tf_op jit(solution)/shard_map/ppermute | solution.py:983
  25.5 3.1 %collective-permute-start.1 = (bf16[24,768]{1,0:T(8,128)(2,1)S(1)}, bf16[24,768]{1,0:T(8,128)(2,1)S(1)}, u32[]{:S(2)}, u32[]{:S(2)}) collective-permute-start(bf16[24,768]{1,0:T(8,128)(2,1)S(1)} %get-tuple-element.72), channel_id=1, source_target_pairs={{0,0},{13,1},{19,2},{26,3},{7,4},{14,5},{20,6},{5,7},{8,8},{2,9},{... | collective-permute-start | bytes 110600 | tf_op jit(solution)/shard_map/ppermute | solution.py:983
  28.7 3.7 %collective-permute-start.2 = (bf16[24,768]{1,0:T(8,128)(2,1)S(1)}, bf16[24,768]{1,0:T(8,128)(2,1)S(1)}, u32[]{:S(2)}, u32[]{:S(2)}) collective-permute-start(bf16[24,768]{1,0:T(8,128)(2,1)S(1)} %get-tuple-element.73), channel_id=1, source_target_pairs={{6,0},{13,1},{19,2},{4,3},{7,4},{1,5},{20,6},{26,7},{8,8},{14,9},{... | collective-permute-start | bytes 110600 | tf_op jit(solution)/shard_map/ppermute | solution.py:983
  32.3 2.7 collective-permute-start.3
  35.1 5.2 %collective-permute-start.4 = (bf16[24,768]{1,0:T(8,128)(2,1)S(1)}, bf16[24,768]{1,0:T(8,128)(2,1)S(1)}, u32[]{:S(2)}, u32[]{:S(2)}) collective-permute-start(bf16[24,768]{1,0:T(8,128)(2,1)S(1)} %get-tuple-element.75), channel_id=1, source_target_pairs={{6,0},{12,1},{19,2},{25,3},{7,4},{13,5},{3,6},{26,7},{0,8},{14,9},... | collective-permute-start | bytes 110600 | tf_op jit(solution)/shard_map/ppermute | solution.py:983
  40.3 2.9 %collective-permute-done.refs_0_ = bf16[24,768]{1,0:T(8,128)(2,1)S(1)} collective-permute-done((bf16[24,768]{1,0:T(8,128)(2,1)S(1)}, bf16[24,768]{1,0:T(8,128)(2,1)S(1)}, u32[]{:S(2)}, u32[]{:S(2)}) %collective-permute-start) | collective-permute-done | bytes 36896 | tf_op jit(solution)/shard_map/ppermute | solution.py:983
  47.7 9.7 %collective-permute-start.5 = (bf16[1,24,768]{2,1,0:T(8,128)(2,1)}, bf16[1,24,768]{2,1,0:T(8,128)(2,1)S(1)}, u32[]{:S(2)}, u32[]{:S(2)}) collective-permute-start(bf16[1,24,768]{2,1,0:T(8,128)(2,1)} %bitcast.25), channel_id=1, source_target_pairs={{0,8},{4,12},{8,0},{12,4},{16,24},{20,28},{24,16},{28,20},{1,9},{5... | collective-permute-start | bytes 110600 | tf_op jit(solution)/shard_map/ppermute | solution.py:873
  57.4 4.1 %collective-permute-start.6 = (bf16[1,24,768]{2,1,0:T(8,128)(2,1)}, bf16[1,24,768]{2,1,0:T(8,128)(2,1)S(1)}, u32[]{:S(2)}, u32[]{:S(2)}) collective-permute-start(bf16[1,24,768]{2,1,0:T(8,128)(2,1)} %bitcast.26), channel_id=1, source_target_pairs={{0,16},{4,20},{8,24},{12,28},{16,0},{20,4},{24,8},{28,12},{1,17},{... | collective-permute-start | bytes 110600 | tf_op jit(solution)/shard_map/ppermute | solution.py:873
  64.0 3.5 %collective-permute-done.7 = bf16[1,24,768]{2,1,0:T(8,128)(2,1)S(1)} collective-permute-done((bf16[1,24,768]{2,1,0:T(8,128)(2,1)}, bf16[1,24,768]{2,1,0:T(8,128)(2,1)S(1)}, u32[]{:S(2)}, u32[]{:S(2)}) %collective-permute-start.7) | collective-permute-done | bytes 36896 | tf_op jit(solution)/shard_map/ppermute | solution.py:873
  75.1 4.7 %all-to-all-start.1 = ((bf16[32,24,768]{2,1,0:T(8,128)(2,1)}), bf16[32,24,768]{2,1,0:T(8,128)(2,1)}, u32[]{:S(2)}, u32[]{:S(2)}) async-start(bf16[32,24,768]{2,1,0:T(8,128)(2,1)} %bitcast.7), calls=%async_computation.1 | async-start | bytes 2359296 | tf_op jit(solution)/shard_map/all_to_all | solution.py:973
  81.2 34.2 %attention.2 = (bf16[2,192,1024]{2,1,0:T(8,128)(2,1)S(1)}, bf16[2,576,1024]{2,1,0:T(8,128)(2,1)S(1)}, f32[2,64,128]{2,1,0:T(8,128)S(1)}, f32[576,768]{1,0:T(8,128)S(1)}, f32[192,768]{1,0:T(8,128)S(1)}) custom-call(s32[3]{0:T(128)S(1)} %copy-done.7, s32[3,1,1024]{2,1,0:T(1,128)S(1)} %get-tuple-element.78.ids_ref, f32[64]{0:T(128)S(1)} %copy-done.14, ...), custom_call_target="tpu_custom_call" | custom-call | flops 60000002048 | bytes 1 | tf_op jit(solution)/shard_map/attention/pallas_call | solution.py:638
  121.0 34.2 %ffn.1 = (bf16[3072,768]{1,0:T(8,128)(2,1)}, bf16[3072,768]{1,0:T(8,128)(2,1)}, bf16[768,768]{1,0:T(8,128)(2,1)}, bf16[2,2,2,256,768]{4,3,2,1,0:T(8,128)(2,1)}, ...) custom-call(s32[3]{0:T(128)} %copy-done.6, ...), custom_call_target="tpu_custom_call" | custom-call | flops 60000002048 | bytes 1 | tf_op jit(solution)/shard_map/ffn/pallas_call | solution.py:794
  155.5 5.9 %collective-permute-done.13.near_ref = bf16[2,2,2,256,768]{4,3,2,1,0:T(8,128)(2,1)} collective-permute-done((bf16[2,2,2,256,768]{4,3,2,1,0:T(8,128)(2,1)}, bf16[2,2,2,256,768]{4,3,2,1,0:T(8,128)(2,1)}, u32[]{:S(2)}, u32[]{:S(2)}) %collective-permute-start.13) | collective-permute-done | bytes 3145760 | tf_op jit(solution)/shard_map/ppermute | solution.py:873
  165.8 24.5 %attention.3 = (bf16[2,1,2,256,768]{4,3,2,1,0:T(8,128)(2,1)S(1)}, bf16[2,1,2,256,768]{4,3,2,1,0:T(8,128)(2,1)}, bf16[32,28,576]{2,1,0:T(8,128)(2,1)S(1)}, bf16[4...) custom-call(s32[3]{0:T(128)S(1)} %copy-done.8, s32[3,1,1024]{2,1,0:T(1,128)S(1)} %get-tuple-element.78.ids_ref, ...), custom_call_target="tpu_custom_call" | custom-call | flops 60000002048 | bytes 1 | tf_op jit(solution)/shard_map/attention/pallas_call | solution.py:638
  191.8 6.5 %collective-permute-done.15.refs_1_ = bf16[4,24,768]{2,1,0:T(8,128)(2,1)S(1)} collective-permute-done((bf16[4,24,768]{2,1,0:T(8,128)(2,1)S(1)}, bf16[4,24,768]{2,1,0:T(8,128)(2,1)S(1)}, u32[]{:S(2)}, u32[]{:S(2)}) %collective-permute-start.15) | collective-permute-done | bytes 147488 | tf_op jit(solution)/shard_map/ppermute | solution.py:873
  209.1 3.6 %all-to-all-start.2 = ((bf16[32,28,576]{2,1,0:T(8,128)(2,1)}), bf16[32,28,576]{2,1,0:T(8,128)(2,1)S(1)}, u32[]{:S(2)}, u32[]{:S(2)}) async-start(bf16[32,28,576]{2,1,0:T(8,128)(2,1)} %copy-done.1), calls=%async_computation.2 | async-start | bytes 2621440 | tf_op jit(solution)/shard_map/all_to_all | solution.py:973
  216.5 4.4 %after.2 = (bf16[3,256,768]{2,1,0:T(8,128)(2,1)}, bf16[3,256,768]{2,1,0:T(8,128)(2,1)}) custom-call(s32[3,1,256]{2,1,0:T(1,128)S(1)} %reshape.79.ids_ref, bf16[3,256,768]{2,1,0:T(8,128)(2,1)} %x_ref.3, bf16[3,256,768]{2,1,0:T(8,128)(2,1)} %cot_ref.3, f32[768]{0:T(1024)S(1)} %copy-done.4, bf16[2,2,2,256,768]{4,3,2,1,0:T(8,128)(2,1)} %get-tuple-element.90.keep_ref, ...), custom_call_target="tpu_custom_call" | custom-call | flops 1 | bytes 1 | tf_op jit(solution)/shard_map/after/pallas_call | solution.py:375
  221.0 12.9 %reduce-scatter.2.cloned.1.call-done = bf16[1,2,96,768]{3,2,1,0:T(8,128)(2,1)} async-done(((bf16[8,2,96,768]{3,2,1,0:T(8,128)(2,1)}), bf16[1,2,96,768]{3,2,1,0:T(8,128)(2,1)}) %reduce-scatter.2.cloned.1.call-update) | async-done | bytes 294928 | tf_op jit(solution)/shard_map/reduce_scatter | solution.py:1003
  239.6 4.2 %collective-permute-start.25 = (bf16[24,768]{1,0:T(8,128)(2,1)}, bf16[24,768]{1,0:T(8,128)(2,1)S(1)}, u32[]{:S(2)}, u32[]{:S(2)}) collective-permute-start(bf16[24,768]{1,0:T(8,128)(2,1)} %get-tuple-element.122), channel_id=1, source_target_pairs={{0,0},{1,13},{2,19},{3,26},{4,7},{5,14},{6,20},{7,5},{8,8},{9,2},{... | collective-permute-start | bytes 110600 | tf_op jit(solution)/shard_map/ppermute | solution.py:1022
  248.1 6.4 %collective-permute-start.27 = (bf16[24,768]{1,0:T(8,128)(2,1)}, bf16[24,768]{1,0:T(8,128)(2,1)S(1)}, u32[]{:S(2)}, u32[]{:S(2)}) collective-permute-start(bf16[24,768]{1,0:T(8,128)(2,1)} %get-tuple-element.124), channel_id=1, source_target_pairs={{0,6},{1,1},{2,19},{3,25},{4,7},{5,13},{6,20},{7,26},{8,8},{9,14},... | collective-permute-start | bytes 110600 | tf_op jit(solution)/shard_map/ppermute | solution.py:1022
  254.6 4.7 %collective-permute-start.28 = (bf16[24,768]{1,0:T(8,128)(2,1)}, bf16[24,768]{1,0:T(8,128)(2,1)S(1)}, u32[]{:S(2)}, u32[]{:S(2)}) collective-permute-start(bf16[24,768]{1,0:T(8,128)(2,1)} %get-tuple-element.125), channel_id=1, source_target_pairs={{0,6},{1,12},{2,19},{3,25},{4,7},{5,13},{6,3},{7,26},{8,0},{9,14},... | collective-permute-start | bytes 110600 | tf_op jit(solution)/shard_map/ppermute | solution.py:1022
  259.3 3.5 %after.3 = (bf16[3,256,768]{2,1,0:T(8,128)(2,1)}, bf16[3,256,768]{2,1,0:T(8,128)(2,1)}) custom-call(s32[3,1,256]{2,1,0:T(1,128)S(1)} %reshape.79.ids_ref, bf16[3,256,768]{2,1,0:T(8,128)(2,1)} %x_ref.3, bf16[3,256,768]{2,1,0:T(8,128)(2,1)} %cot_ref.3, f32[768]{0:T(1024)S(1)} %copy-done.4, ...), custom_call_target="tpu_custom_call", output_to_operand_aliasing={{0}: (7, {}), {1}: (8, {})} | custom-call | flops 1 | bytes 1 | tf_op jit(solution)/shard_map/after/pallas_call | solution.py:375
  (133 shorter events, 58.4 us)
Async XLA Ops:
  7.2 74.0 %all-gather.5.cloned.1.call-start = ((), (), s32[]{:S(2)}) async-start(), calls=%async_computation.5 | async-start | bytes 7864320 | tf_op jit(solution)/shard_map/all_gather | solution.py:985
  14.1 54.2 %all-to-all-start = ((bf16[32,26,576]{2,1,0:T(8,128)(2,1)}), bf16[32,26,576]{2,1,0:T(8,128)(2,1)S(1)}, u32[]{:S(2)}, u32[]{:S(2)}) async-start(bf16[32,26,576]{2,1,0:T(8,128)(2,1)} %bitcast.3), calls=%async_computation | async-start | bytes 2621440 | tf_op jit(solution)/shard_map/all_to_all | solution.py:973
  20.2 100.1 %all-gather.7.cloned.1.call-start = ((), (), s32[]{:S(2)}) async-start(), calls=%async_computation.6 | async-start | bytes 3932160 | tf_op jit(solution)/shard_map/all_gather | solution.py:986
  20.3 22.9 %collective-permute-start = (bf16[24,768]{1,0:T(8,128)(2,1)S(1)}, bf16[24,768]{1,0:T(8,128)(2,1)S(1)}, u32[]{:S(2)}, u32[]{:S(2)}) collective-permute-start(bf16[24,768]{1,0:T(8,128)(2,1)S(1)} %get-tuple-element.71), channel_id=1, source_target_pairs={{7,0},{13,1},{3,2},{26,3},{0,4},{14,5},{20,6},{27,7},{8,8},{15,9},... | collective-permute-start | bytes 110600 | tf_op jit(solution)/shard_map/ppermute | solution.py:983
  25.5 18.5 %collective-permute-start.1 = (bf16[24,768]{1,0:T(8,128)(2,1)S(1)}, bf16[24,768]{1,0:T(8,128)(2,1)S(1)}, u32[]{:S(2)}, u32[]{:S(2)}) collective-permute-start(bf16[24,768]{1,0:T(8,128)(2,1)S(1)} %get-tuple-element.72), channel_id=1, source_target_pairs={{0,0},{13,1},{19,2},{26,3},{7,4},{14,5},{20,6},{5,7},{8,8},{2,9},{... | collective-permute-start | bytes 110600 | tf_op jit(solution)/shard_map/ppermute | solution.py:983
  28.7 15.3 %collective-permute-start.2 = (bf16[24,768]{1,0:T(8,128)(2,1)S(1)}, bf16[24,768]{1,0:T(8,128)(2,1)S(1)}, u32[]{:S(2)}, u32[]{:S(2)}) collective-permute-start(bf16[24,768]{1,0:T(8,128)(2,1)S(1)} %get-tuple-element.73), channel_id=1, source_target_pairs={{6,0},{13,1},{19,2},{4,3},{7,4},{1,5},{20,6},{26,7},{8,8},{14,9},{... | collective-permute-start | bytes 110600 | tf_op jit(solution)/shard_map/ppermute | solution.py:983
  32.3 12.4 %collective-permute-start.3 = (bf16[24,768]{1,0:T(8,128)(2,1)S(1)}, bf16[24,768]{1,0:T(8,128)(2,1)S(1)}, u32[]{:S(2)}, u32[]{:S(2)}) collective-permute-start(bf16[24,768]{1,0:T(8,128)(2,1)S(1)} %get-tuple-element.74), channel_id=1, source_target_pairs={{6,0},{1,1},{19,2},{25,3},{7,4},{13,5},{20,6},{26,7},{8,8},{14,9},... | collective-permute-start | bytes 110600 | tf_op jit(solution)/shard_map/ppermute | solution.py:983
  35.1 10.1 %collective-permute-start.4 = (bf16[24,768]{1,0:T(8,128)(2,1)S(1)}, bf16[24,768]{1,0:T(8,128)(2,1)S(1)}, u32[]{:S(2)}, u32[]{:S(2)}) collective-permute-start(bf16[24,768]{1,0:T(8,128)(2,1)S(1)} %get-tuple-element.75), channel_id=1, source_target_pairs={{6,0},{12,1},{19,2},{25,3},{7,4},{13,5},{3,6},{26,7},{0,8},{14,9},... | collective-permute-start | bytes 110600 | tf_op jit(solution)/shard_map/ppermute | solution.py:983
  47.7 15.2 %collective-permute-start.5 = (bf16[1,24,768]{2,1,0:T(8,128)(2,1)}, bf16[1,24,768]{2,1,0:T(8,128)(2,1)S(1)}, u32[]{:S(2)}, u32[]{:S(2)}) collective-permute-start(bf16[1,24,768]{2,1,0:T(8,128)(2,1)} %bitcast.25), channel_id=1, source_target_pairs={{0,8},{4,12},{8,0},{12,4},{16,24},{20,28},{24,16},{28,20},{1,9},{5... | collective-permute-start | bytes 110600 | tf_op jit(solution)/shard_map/ppermute | solution.py:873
  68.3 11.7 %collective-permute-start.8 = (bf16[4,24,768]{2,1,0:T(8,128)(2,1)S(1)}, bf16[4,24,768]{2,1,0:T(8,128)(2,1)S(1)}, u32[]{:S(2)}, u32[]{:S(2)}) collective-permute-start(bf16[4,24,768]{2,1,0:T(8,128)(2,1)S(1)} %pad_maximum_fusion.1.refs_0_), channel_id=1, source_target_pairs={{0,4},{4,0},{8,12},{12,8},{16,20},{20,16},{24,28},{28,24},{1,5},{5... | collective-permute-start | bytes 442376 | tf_op jit(solution)/shard_map/ppermute | solution.py:873
  70.6 49.7 %collective-permute-start.10 = (bf16[2,96,768]{2,1,0:T(8,128)(2,1)S(1)}, bf16[2,96,768]{2,1,0:T(8,128)(2,1)S(1)}, u32[]{:S(2)}, u32[]{:S(2)}) collective-permute-start(bf16[2,96,768]{2,1,0:T(8,128)(2,1)S(1)} %pad_maximum_fusion.refs_0_), channel_id=1, source_target_pairs={{0,8},{4,12},{8,0},{12,4},{16,24},{20,28},{24,16},{28,20},{1,9},{5... | collective-permute-start | bytes 884744 | tf_op jit(solution)/shard_map/ppermute | solution.py:873
  71.4 48.9 %collective-permute-start.11 = (bf16[2,96,768]{2,1,0:T(8,128)(2,1)S(1)}, bf16[2,96,768]{2,1,0:T(8,128)(2,1)}, u32[]{:S(2)}, u32[]{:S(2)}) collective-permute-start(bf16[2,96,768]{2,1,0:T(8,128)(2,1)S(1)} %pad_maximum_fusion.refs_0_), channel_id=1, source_target_pairs={{0,16},{4,20},{8,24},{12,28},{16,0},{20,4},{24,8},{28,12},{1,17},{... | collective-permute-start | bytes 884744 | tf_op jit(solution)/shard_map/ppermute | solution.py:873
  73.2 47.1 %collective-permute-start.12 = (bf16[2,96,768]{2,1,0:T(8,128)(2,1)S(1)}, bf16[2,96,768]{2,1,0:T(8,128)(2,1)}, u32[]{:S(2)}, u32[]{:S(2)}) collective-permute-start(bf16[2,96,768]{2,1,0:T(8,128)(2,1)S(1)} %pad_maximum_fusion.refs_0_), channel_id=1, source_target_pairs={{0,24},{4,28},{8,16},{12,20},{16,8},{20,12},{24,0},{28,4},{1,25},{... | collective-permute-start | bytes 884744 | tf_op jit(solution)/shard_map/ppermute | solution.py:873
  75.1 45.3 %all-to-all-start.1 = ((bf16[32,24,768]{2,1,0:T(8,128)(2,1)}), bf16[32,24,768]{2,1,0:T(8,128)(2,1)}, u32[]{:S(2)}, u32[]{:S(2)}) async-start(bf16[32,24,768]{2,1,0:T(8,128)(2,1)} %bitcast.7), calls=%async_computation.1 | async-start | bytes 2359296 | tf_op jit(solution)/shard_map/all_to_all | solution.py:973
  79.8 154.1 %reduce-scatter.2.cloned.1.call-start = ((), (), s32[]{:S(2)}) async-start(), calls=%async_computation.4 | async-start | bytes 2654208 | tf_op jit(solution)/shard_map/reduce_scatter | solution.py:1003
  163.7 44.3 %collective-permute-start.14 = (bf16[2,2,256,768]{3,2,1,0:T(8,128)(2,1)S(1)}, bf16[2,2,256,768]{3,2,1,0:T(8,128)(2,1)S(1)}, u32[]{:S(2)}, u32[]{:S(2)}) collective-permute-start(bf16[2,2,256,768]{3,2,1,0:T(8,128)(2,1)S(1)} %fusion), channel_id=1, source_target_pairs={{0,2},{1,3},{2,0},{3,1},{4,6},{5,7},{6,4},{7,5},{8,10},{9,11},{10,... | collective-permute-start | bytes 4718600 | tf_op jit(solution)/shard_map/ppermute | solution.py:873
  209.1 53.6 %all-to-all-start.2 = ((bf16[32,28,576]{2,1,0:T(8,128)(2,1)}), bf16[32,28,576]{2,1,0:T(8,128)(2,1)S(1)}, u32[]{:S(2)}, u32[]{:S(2)}) async-start(bf16[32,28,576]{2,1,0:T(8,128)(2,1)} %copy-done.1), calls=%async_computation.2 | async-start | bytes 2621440 | tf_op jit(solution)/shard_map/all_to_all | solution.py:973
  215.1 39.4 %collective-permute-start.20 = (bf16[1,2,256,768]{3,2,1,0:T(8,128)(2,1)}, bf16[1,2,256,768]{3,2,1,0:T(8,128)(2,1)}, u32[]{:S(2)}, u32[]{:S(2)}) collective-permute-start(bf16[1,2,256,768]{3,2,1,0:T(8,128)(2,1)} %fusion.1), channel_id=1, source_target_pairs={{0,2},{1,3},{2,0},{3,1},{4,6},{5,7},{6,4},{7,5},{8,10},{9,11},{10,... | collective-permute-start | bytes 2359304 | tf_op jit(solution)/shard_map/ppermute | solution.py:873
  235.8 10.4 %collective-permute-start.22 = (bf16[24,768]{1,0:T(8,128)(2,1)}, bf16[24,768]{1,0:T(8,128)(2,1)S(1)}, u32[]{:S(2)}, u32[]{:S(2)}) collective-permute-start(bf16[24,768]{1,0:T(8,128)(2,1)} %get-tuple-element.119), channel_id=1, source_target_pairs={{0,2},{1,3},{2,0},{3,1},{4,6},{5,7},{6,4},{7,5},{8,10},{9,11},{10,... | collective-permute-start | bytes 110600 | tf_op jit(solution)/shard_map/ppermute | solution.py:873
  236.5 11.6 %collective-permute-start.23 = (bf16[24,768]{1,0:T(8,128)(2,1)}, bf16[24,768]{1,0:T(8,128)(2,1)S(1)}, u32[]{:S(2)}, u32[]{:S(2)}) collective-permute-start(bf16[24,768]{1,0:T(8,128)(2,1)} %get-tuple-element.120), channel_id=1, source_target_pairs={{0,3},{1,2},{2,1},{3,0},{4,7},{5,6},{6,5},{7,4},{8,11},{9,10},{10,... | collective-permute-start | bytes 110600 | tf_op jit(solution)/shard_map/ppermute | solution.py:873
  237.7 25.1 %collective-permute-start.24 = (bf16[24,768]{1,0:T(8,128)(2,1)}, bf16[24,768]{1,0:T(8,128)(2,1)S(1)}, u32[]{:S(2)}, u32[]{:S(2)}) collective-permute-start(bf16[24,768]{1,0:T(8,128)(2,1)} %get-tuple-element.121), channel_id=1, source_target_pairs={{0,7},{1,13},{2,3},{3,26},{4,0},{5,14},{6,20},{7,27},{8,8},{9,15},... | collective-permute-start | bytes 110600 | tf_op jit(solution)/shard_map/ppermute | solution.py:1022
  239.6 23.1 %collective-permute-start.25 = (bf16[24,768]{1,0:T(8,128)(2,1)}, bf16[24,768]{1,0:T(8,128)(2,1)S(1)}, u32[]{:S(2)}, u32[]{:S(2)}) collective-permute-start(bf16[24,768]{1,0:T(8,128)(2,1)} %get-tuple-element.122), channel_id=1, source_target_pairs={{0,0},{1,13},{2,19},{3,26},{4,7},{5,14},{6,20},{7,5},{8,8},{9,2},{... | collective-permute-start | bytes 110600 | tf_op jit(solution)/shard_map/ppermute | solution.py:1022
  246.2 16.6 %collective-permute-start.26 = (bf16[24,768]{1,0:T(8,128)(2,1)}, bf16[24,768]{1,0:T(8,128)(2,1)S(1)}, u32[]{:S(2)}, u32[]{:S(2)}) collective-permute-start(bf16[24,768]{1,0:T(8,128)(2,1)} %get-tuple-element.123), channel_id=1, source_target_pairs={{0,6},{1,13},{2,19},{3,4},{4,7},{5,1},{6,20},{7,26},{8,8},{9,14},{... | collective-permute-start | bytes 110600 | tf_op jit(solution)/shard_map/ppermute | solution.py:1022
  248.1 14.7 %collective-permute-start.27 = (bf16[24,768]{1,0:T(8,128)(2,1)}, bf16[24,768]{1,0:T(8,128)(2,1)S(1)}, u32[]{:S(2)}, u32[]{:S(2)}) collective-permute-start(bf16[24,768]{1,0:T(8,128)(2,1)} %get-tuple-element.124), channel_id=1, source_target_pairs={{0,6},{1,1},{2,19},{3,25},{4,7},{5,13},{6,20},{7,26},{8,8},{9,14},... | collective-permute-start | bytes 110600 | tf_op jit(solution)/shard_map/ppermute | solution.py:1022
  (44 other events, 308.3 us)
Sparse Core Ops, SparseCore 0:
  14.2 60.9 all-gather.4
  76.8 34.6 all-gather.6
  155.6 78.2 reduce-scatter.1

commit v9 on v8

--- a/solution.py
+++ b/solution.py
@@ -541,7 +541,7 @@
             do_ref[n] = jnp.where(padb > 0, vm_ref[h], o).astype(BF)
             return carry
 
-        lax.fori_loop(0, heads * blocks, step, 0)
+        lax.fori_loop(0, heads * blocks, step, 0, unroll=True)
 
         def finish(h, carry):
             rows = lambda at: pl.ds(pl.multiple_of(at + h * HD, HD), HD)

time: 274 us -> 275 us (level); the launches traced: 273 us -> 271 us
  Pallas kernels: 115 us -> 109 us
    pallas_call x2, Pallas kernels: 58.7 us -> 53.4 us  [attention(): pl.pallas_call(functools.partial(attention_kernel, heads, block, last, st...]
    all_to_all x3, waiting for transfers between devices: 0.48 us -> 3.62 us  [exchange(): return lax.all_to_all(value, axis, split_axis=0, concat_axis=0, tiled=True)]
  transfers between devices with their start and end apart: 35 -> 35, of which waited for: 15 -> 14; matrix products, arithmetic and copies ran while one was open for 2% -> 2% of each run, Pallas kernels for 26% -> 25%
where the time goes in v9:
time: 275 us; the launch traced here: 271 us
  Pallas kernels  109 us (40%)
  starting transfers between devices  85.7 us (31%)
  waiting for transfers between devices  45.8 us (17%)
  between operations  14.5 us (5%)
  local copies, waits for them, and re-layouts  8.95 us (3%)
  other arithmetic  6.58 us (2%)
    pallas_call x2, Pallas kernels, attention(): pl.pallas_call(functools.partial(attention_kernel, heads, block, last, st...  53.4 us
    pallas_call x1, Pallas kernels, ffn(): pl.pallas_call(functools.partial(ffn_kernel, block, sizes, [masks for _,...  34 us
    ppermute x19, starting transfers between devices, swap(): return lax.ppermute(value, axis, [(i, i ^ mask) for i in range(count)])  31.4 us
    ppermute x19, waiting for transfers between devices, swap(): return lax.ppermute(value, axis, [(i, i ^ mask) for i in range(count)])  21.1 us
    ppermute x5, starting transfers between devices, per_device(): got = [lax.ppermute(v, both, perm) for v, perm in zip(unit_sends, perms)]  20 us
    ppermute x5, starting transfers between devices, per_device(): lax.ppermute(v, both, [(b, a) for a, b in perm])  18.9 us
    all_to_all x3, starting transfers between devices, exchange(): return lax.all_to_all(value, axis, split_axis=0, concat_axis=0, tiled=True)  14.8 us
    reduce_scatter x1, waiting for transfers between devices, per_device(): lax.psum_scatter(f_grad, 'batch', scatter_dimension=0, tiled=True)  14.2 us
  transfers between devices with their start and end apart: 35, of which 14 were waited for; matrix products, arithmetic and copies ran while one was open for 2% of the time, Pallas kernels for 25%

profile of v9, /device:TPU:2, one launch (start us, length us, event | category | flops | bytes accessed | tf_op | source)
XLA Modules:
  0.0 270.8 jit_solution(3214764667966595779)
XLA Ops:
  9.9 4.2 %before.1 = (bf16[2,2,256,768]{3,2,1,0:T(8,128)(2,1)}, bf16[1,2,256,768]{3,2,1,0:T(8,128)(2,1)}, bf16[24,768]{1,0:T(8,128)(2,1)S(1)}, bf16[24,768]{1,0:T(8,128)(...) custom-call(s32[3]{0:T(128)S(1)} %pad_add_fusion.at_ref, ...), custom_call_target="tpu_custom_call" | custom-call | flops 1 | bytes 1 | tf_op jit(solution)/shard_map/before/pallas_call | solution.py:152
  14.1 6.1 %all-to-all-start = ((bf16[32,26,576]{2,1,0:T(8,128)(2,1)}), bf16[32,26,576]{2,1,0:T(8,128)(2,1)S(1)}, u32[]{:S(2)}, u32[]{:S(2)}) async-start(bf16[32,26,576]{2,1,0:T(8,128)(2,1)} %bitcast.3), calls=%async_computation | async-start | bytes 2621440 | tf_op jit(solution)/shard_map/all_to_all | solution.py:973
  20.3 5.2 %collective-permute-start = (bf16[24,768]{1,0:T(8,128)(2,1)S(1)}, bf16[24,768]{1,0:T(8,128)(2,1)S(1)}, u32[]{:S(2)}, u32[]{:S(2)}) collective-permute-start(bf16[24,768]{1,0:T(8,128)(2,1)S(1)} %get-tuple-element.71), channel_id=1, source_target_pairs={{7,0},{13,1},{3,2},{26,3},{0,4},{14,5},{20,6},{27,7},{8,8},{15,9},... | collective-permute-start | bytes 110600 | tf_op jit(solution)/shard_map/ppermute | solution.py:983
  25.5 3.1 %collective-permute-start.1 = (bf16[24,768]{1,0:T(8,128)(2,1)S(1)}, bf16[24,768]{1,0:T(8,128)(2,1)S(1)}, u32[]{:S(2)}, u32[]{:S(2)}) collective-permute-start(bf16[24,768]{1,0:T(8,128)(2,1)S(1)} %get-tuple-element.72), channel_id=1, source_target_pairs={{0,0},{13,1},{19,2},{26,3},{7,4},{14,5},{20,6},{5,7},{8,8},{2,9},{... | collective-permute-start | bytes 110600 | tf_op jit(solution)/shard_map/ppermute | solution.py:983
  28.7 3.7 %collective-permute-start.2 = (bf16[24,768]{1,0:T(8,128)(2,1)S(1)}, bf16[24,768]{1,0:T(8,128)(2,1)S(1)}, u32[]{:S(2)}, u32[]{:S(2)}) collective-permute-start(bf16[24,768]{1,0:T(8,128)(2,1)S(1)} %get-tuple-element.73), channel_id=1, source_target_pairs={{6,0},{13,1},{19,2},{4,3},{7,4},{1,5},{20,6},{26,7},{8,8},{14,9},{... | collective-permute-start | bytes 110600 | tf_op jit(solution)/shard_map/ppermute | solution.py:983
  35.1 5.2 %collective-permute-start.4 = (bf16[24,768]{1,0:T(8,128)(2,1)S(1)}, bf16[24,768]{1,0:T(8,128)(2,1)S(1)}, u32[]{:S(2)}, u32[]{:S(2)}) collective-permute-start(bf16[24,768]{1,0:T(8,128)(2,1)S(1)} %get-tuple-element.75), channel_id=1, source_target_pairs={{6,0},{12,1},{19,2},{25,3},{7,4},{13,5},{3,6},{26,7},{0,8},{14,9},... | collective-permute-start | bytes 110600 | tf_op jit(solution)/shard_map/ppermute | solution.py:983
  40.3 2.9 %collective-permute-done.refs_0_ = bf16[24,768]{1,0:T(8,128)(2,1)S(1)} collective-permute-done((bf16[24,768]{1,0:T(8,128)(2,1)S(1)}, bf16[24,768]{1,0:T(8,128)(2,1)S(1)}, u32[]{:S(2)}, u32[]{:S(2)}) %collective-permute-start) | collective-permute-done | bytes 36896 | tf_op jit(solution)/shard_map/ppermute | solution.py:983
  47.7 9.7 %collective-permute-start.5 = (bf16[1,24,768]{2,1,0:T(8,128)(2,1)}, bf16[1,24,768]{2,1,0:T(8,128)(2,1)S(1)}, u32[]{:S(2)}, u32[]{:S(2)}) collective-permute-start(bf16[1,24,768]{2,1,0:T(8,128)(2,1)} %bitcast.25), channel_id=1, source_target_pairs={{0,8},{4,12},{8,0},{12,4},{16,24},{20,28},{24,16},{28,20},{1,9},{5... | collective-permute-start | bytes 110600 | tf_op jit(solution)/shard_map/ppermute | solution.py:873
  57.4 4.1 %collective-permute-start.6 = (bf16[1,24,768]{2,1,0:T(8,128)(2,1)}, bf16[1,24,768]{2,1,0:T(8,128)(2,1)S(1)}, u32[]{:S(2)}, u32[]{:S(2)}) collective-permute-start(bf16[1,24,768]{2,1,0:T(8,128)(2,1)} %bitcast.26), channel_id=1, source_target_pairs={{0,16},{4,20},{8,24},{12,28},{16,0},{20,4},{24,8},{28,12},{1,17},{... | collective-permute-start | bytes 110600 | tf_op jit(solution)/shard_map/ppermute | solution.py:873
  64.0 3.5 %collective-permute-done.7 = bf16[1,24,768]{2,1,0:T(8,128)(2,1)S(1)} collective-permute-done((bf16[1,24,768]{2,1,0:T(8,128)(2,1)}, bf16[1,24,768]{2,1,0:T(8,128)(2,1)S(1)}, u32[]{:S(2)}, u32[]{:S(2)}) %collective-permute-start.7) | collective-permute-done | bytes 36896 | tf_op jit(solution)/shard_map/ppermute | solution.py:873
  75.1 4.7 %all-to-all-start.1 = ((bf16[32,24,768]{2,1,0:T(8,128)(2,1)}), bf16[32,24,768]{2,1,0:T(8,128)(2,1)}, u32[]{:S(2)}, u32[]{:S(2)}) async-start(bf16[32,24,768]{2,1,0:T(8,128)(2,1)} %bitcast.7), calls=%async_computation.1 | async-start | bytes 2359296 | tf_op jit(solution)/shard_map/all_to_all | solution.py:973
  81.5 30.7 %attention.2 = (bf16[2,192,1024]{2,1,0:T(8,128)(2,1)S(1)}, bf16[2,576,1024]{2,1,0:T(8,128)(2,1)S(1)}, f32[2,64,128]{2,1,0:T(8,128)S(1)}, f32[576,768]{1,0:T(8,128)S(1)}, f32[192,768]{1,0:T(8,128)S(1)}) custom-call(s32[3]{0:T(128)S(1)} %copy-done.7, s32[3,1,1024]{2,1,0:T(1,128)S(1)} %get-tuple-element.78.ids_ref, f32[64]{0:T(128)S(1)} %copy-done.14, ...), custom_call_target="tpu_custom_call" | custom-call | flops 60000002048 | bytes 1 | tf_op jit(solution)/shard_map/attention/pallas_call | solution.py:638
  116.7 3.6 %all-to-all-done.1 = bf16[32,24,768]{2,1,0:T(8,128)(2,1)} async-done(((bf16[32,24,768]{2,1,0:T(8,128)(2,1)}), bf16[32,24,768]{2,1,0:T(8,128)(2,1)}, u32[]{:S(2)}, u32[]{:S(2)}) %all-to-all-start.1) | async-done | bytes 1179680 | tf_op jit(solution)/shard_map/all_to_all | solution.py:973
  121.0 34.0 %ffn.1 = (bf16[3072,768]{1,0:T(8,128)(2,1)}, bf16[3072,768]{1,0:T(8,128)(2,1)}, bf16[768,768]{1,0:T(8,128)(2,1)}, bf16[2,2,2,256,768]{4,3,2,1,0:T(8,128)(2,1)}, ...) custom-call(s32[3]{0:T(128)} %copy-done.6, ...), custom_call_target="tpu_custom_call" | custom-call | flops 60000002048 | bytes 1 | tf_op jit(solution)/shard_map/ffn/pallas_call | solution.py:794
  155.2 5.9 %collective-permute-done.13.near_ref = bf16[2,2,2,256,768]{4,3,2,1,0:T(8,128)(2,1)} collective-permute-done((bf16[2,2,2,256,768]{4,3,2,1,0:T(8,128)(2,1)}, bf16[2,2,2,256,768]{4,3,2,1,0:T(8,128)(2,1)}, u32[]{:S(2)}, u32[]{:S(2)}) %collective-permute-start.13) | collective-permute-done | bytes 3145760 | tf_op jit(solution)/shard_map/ppermute | solution.py:873
  165.7 22.7 %attention.3 = (bf16[2,1,2,256,768]{4,3,2,1,0:T(8,128)(2,1)S(1)}, bf16[2,1,2,256,768]{4,3,2,1,0:T(8,128)(2,1)}, bf16[32,28,576]{2,1,0:T(8,128)(2,1)S(1)}, bf16[4...) custom-call(s32[3]{0:T(128)S(1)} %copy-done.8, s32[3,1,1024]{2,1,0:T(1,128)S(1)} %get-tuple-element.78.ids_ref, ...), custom_call_target="tpu_custom_call" | custom-call | flops 60000002048 | bytes 1 | tf_op jit(solution)/shard_map/attention/pallas_call | solution.py:638
  190.0 6.8 %collective-permute-done.15.refs_1_ = bf16[4,24,768]{2,1,0:T(8,128)(2,1)S(1)} collective-permute-done((bf16[4,24,768]{2,1,0:T(8,128)(2,1)S(1)}, bf16[4,24,768]{2,1,0:T(8,128)(2,1)S(1)}, u32[]{:S(2)}, u32[]{:S(2)}) %collective-permute-start.15) | collective-permute-done | bytes 147488 | tf_op jit(solution)/shard_map/ppermute | solution.py:873
  207.1 4.0 %all-to-all-start.2 = ((bf16[32,28,576]{2,1,0:T(8,128)(2,1)}), bf16[32,28,576]{2,1,0:T(8,128)(2,1)S(1)}, u32[]{:S(2)}, u32[]{:S(2)}) async-start(bf16[32,28,576]{2,1,0:T(8,128)(2,1)} %copy-done.1), calls=%async_computation.2 | async-start | bytes 2621440 | tf_op jit(solution)/shard_map/all_to_all | solution.py:973
  214.8 4.4 %after.2 = (bf16[3,256,768]{2,1,0:T(8,128)(2,1)}, bf16[3,256,768]{2,1,0:T(8,128)(2,1)}) custom-call(s32[3,1,256]{2,1,0:T(1,128)S(1)} %reshape.79.ids_ref, bf16[3,256,768]{2,1,0:T(8,128)(2,1)} %x_ref.3, bf16[3,256,768]{2,1,0:T(8,128)(2,1)} %cot_ref.3, f32[768]{0:T(1024)S(1)} %copy-done.4, bf16[2,2,2,256,768]{4,3,2,1,0:T(8,128)(2,1)} %get-tuple-element.90.keep_ref, ...), custom_call_target="tpu_custom_call" | custom-call | flops 1 | bytes 1 | tf_op jit(solution)/shard_map/after/pallas_call | solution.py:375
  219.2 14.2 %reduce-scatter.2.cloned.1.call-done = bf16[1,2,96,768]{3,2,1,0:T(8,128)(2,1)} async-done(((bf16[8,2,96,768]{3,2,1,0:T(8,128)(2,1)}), bf16[1,2,96,768]{3,2,1,0:T(8,128)(2,1)}) %reduce-scatter.2.cloned.1.call-update) | async-done | bytes 294928 | tf_op jit(solution)/shard_map/reduce_scatter | solution.py:1003
  239.2 5.2 %collective-permute-start.25 = (bf16[24,768]{1,0:T(8,128)(2,1)}, bf16[24,768]{1,0:T(8,128)(2,1)S(1)}, u32[]{:S(2)}, u32[]{:S(2)}) collective-permute-start(bf16[24,768]{1,0:T(8,128)(2,1)} %get-tuple-element.122), channel_id=1, source_target_pairs={{0,0},{1,13},{2,19},{3,26},{4,7},{5,14},{6,20},{7,5},{8,8},{9,2},{... | collective-permute-start | bytes 110600 | tf_op jit(solution)/shard_map/ppermute | solution.py:1022
  246.7 5.5 %collective-permute-start.27 = (bf16[24,768]{1,0:T(8,128)(2,1)}, bf16[24,768]{1,0:T(8,128)(2,1)S(1)}, u32[]{:S(2)}, u32[]{:S(2)}) collective-permute-start(bf16[24,768]{1,0:T(8,128)(2,1)} %get-tuple-element.124), channel_id=1, source_target_pairs={{0,6},{1,1},{2,19},{3,25},{4,7},{5,13},{6,20},{7,26},{8,8},{9,14},... | collective-permute-start | bytes 110600 | tf_op jit(solution)/shard_map/ppermute | solution.py:1022
  252.3 4.3 %collective-permute-start.28 = (bf16[24,768]{1,0:T(8,128)(2,1)}, bf16[24,768]{1,0:T(8,128)(2,1)S(1)}, u32[]{:S(2)}, u32[]{:S(2)}) collective-permute-start(bf16[24,768]{1,0:T(8,128)(2,1)} %get-tuple-element.125), channel_id=1, source_target_pairs={{0,6},{1,12},{2,19},{3,25},{4,7},{5,13},{6,3},{7,26},{8,0},{9,14},... | collective-permute-start | bytes 110600 | tf_op jit(solution)/shard_map/ppermute | solution.py:1022
  256.6 3.5 %after.3 = (bf16[3,256,768]{2,1,0:T(8,128)(2,1)}, bf16[3,256,768]{2,1,0:T(8,128)(2,1)}) custom-call(s32[3,1,256]{2,1,0:T(1,128)S(1)} %reshape.79.ids_ref, bf16[3,256,768]{2,1,0:T(8,128)(2,1)} %x_ref.3, bf16[3,256,768]{2,1,0:T(8,128)(2,1)} %cot_ref.3, f32[768]{0:T(1024)S(1)} %copy-done.4, ...), custom_call_target="tpu_custom_call", output_to_operand_aliasing={{0}: (7, {}), {1}: (8, {})} | custom-call | flops 1 | bytes 1 | tf_op jit(solution)/shard_map/after/pallas_call | solution.py:375
  (133 shorter events, 59.0 us)
Async XLA Ops:
  7.2 74.4 %all-gather.5.cloned.1.call-start = ((), (), s32[]{:S(2)}) async-start(), calls=%async_computation.5 | async-start | bytes 7864320 | tf_op jit(solution)/shard_map/all_gather | solution.py:985
  14.1 54.2 %all-to-all-start = ((bf16[32,26,576]{2,1,0:T(8,128)(2,1)}), bf16[32,26,576]{2,1,0:T(8,128)(2,1)S(1)}, u32[]{:S(2)}, u32[]{:S(2)}) async-start(bf16[32,26,576]{2,1,0:T(8,128)(2,1)} %bitcast.3), calls=%async_computation | async-start | bytes 2621440 | tf_op jit(solution)/shard_map/all_to_all | solution.py:973
  20.2 100.1 %all-gather.7.cloned.1.call-start = ((), (), s32[]{:S(2)}) async-start(), calls=%async_computation.6 | async-start | bytes 3932160 | tf_op jit(solution)/shard_map/all_gather | solution.py:986
  20.3 22.9 %collective-permute-start = (bf16[24,768]{1,0:T(8,128)(2,1)S(1)}, bf16[24,768]{1,0:T(8,128)(2,1)S(1)}, u32[]{:S(2)}, u32[]{:S(2)}) collective-permute-start(bf16[24,768]{1,0:T(8,128)(2,1)S(1)} %get-tuple-element.71), channel_id=1, source_target_pairs={{7,0},{13,1},{3,2},{26,3},{0,4},{14,5},{20,6},{27,7},{8,8},{15,9},... | collective-permute-start | bytes 110600 | tf_op jit(solution)/shard_map/ppermute | solution.py:983
  25.5 18.5 %collective-permute-start.1 = (bf16[24,768]{1,0:T(8,128)(2,1)S(1)}, bf16[24,768]{1,0:T(8,128)(2,1)S(1)}, u32[]{:S(2)}, u32[]{:S(2)}) collective-permute-start(bf16[24,768]{1,0:T(8,128)(2,1)S(1)} %get-tuple-element.72), channel_id=1, source_target_pairs={{0,0},{13,1},{19,2},{26,3},{7,4},{14,5},{20,6},{5,7},{8,8},{2,9},{... | collective-permute-start | bytes 110600 | tf_op jit(solution)/shard_map/ppermute | solution.py:983
  28.7 15.3 %collective-permute-start.2 = (bf16[24,768]{1,0:T(8,128)(2,1)S(1)}, bf16[24,768]{1,0:T(8,128)(2,1)S(1)}, u32[]{:S(2)}, u32[]{:S(2)}) collective-permute-start(bf16[24,768]{1,0:T(8,128)(2,1)S(1)} %get-tuple-element.73), channel_id=1, source_target_pairs={{6,0},{13,1},{19,2},{4,3},{7,4},{1,5},{20,6},{26,7},{8,8},{14,9},{... | collective-permute-start | bytes 110600 | tf_op jit(solution)/shard_map/ppermute | solution.py:983
  32.3 12.4 %collective-permute-start.3 = (bf16[24,768]{1,0:T(8,128)(2,1)S(1)}, bf16[24,768]{1,0:T(8,128)(2,1)S(1)}, u32[]{:S(2)}, u32[]{:S(2)}) collective-permute-start(bf16[24,768]{1,0:T(8,128)(2,1)S(1)} %get-tuple-element.74), channel_id=1, source_target_pairs={{6,0},{1,1},{19,2},{25,3},{7,4},{13,5},{20,6},{26,7},{8,8},{14,9},... | collective-permute-start | bytes 110600 | tf_op jit(solution)/shard_map/ppermute | solution.py:983
  35.1 10.1 %collective-permute-start.4 = (bf16[24,768]{1,0:T(8,128)(2,1)S(1)}, bf16[24,768]{1,0:T(8,128)(2,1)S(1)}, u32[]{:S(2)}, u32[]{:S(2)}) collective-permute-start(bf16[24,768]{1,0:T(8,128)(2,1)S(1)} %get-tuple-element.75), channel_id=1, source_target_pairs={{6,0},{12,1},{19,2},{25,3},{7,4},{13,5},{3,6},{26,7},{0,8},{14,9},... | collective-permute-start | bytes 110600 | tf_op jit(solution)/shard_map/ppermute | solution.py:983
  47.7 15.2 %collective-permute-start.5 = (bf16[1,24,768]{2,1,0:T(8,128)(2,1)}, bf16[1,24,768]{2,1,0:T(8,128)(2,1)S(1)}, u32[]{:S(2)}, u32[]{:S(2)}) collective-permute-start(bf16[1,24,768]{2,1,0:T(8,128)(2,1)} %bitcast.25), channel_id=1, source_target_pairs={{0,8},{4,12},{8,0},{12,4},{16,24},{20,28},{24,16},{28,20},{1,9},{5... | collective-permute-start | bytes 110600 | tf_op jit(solution)/shard_map/ppermute | solution.py:873
  68.3 12.1 %collective-permute-start.8 = (bf16[4,24,768]{2,1,0:T(8,128)(2,1)S(1)}, bf16[4,24,768]{2,1,0:T(8,128)(2,1)S(1)}, u32[]{:S(2)}, u32[]{:S(2)}) collective-permute-start(bf16[4,24,768]{2,1,0:T(8,128)(2,1)S(1)} %pad_maximum_fusion.1.refs_0_), channel_id=1, source_target_pairs={{0,4},{4,0},{8,12},{12,8},{16,20},{20,16},{24,28},{28,24},{1,5},{5... | collective-permute-start | bytes 442376 | tf_op jit(solution)/shard_map/ppermute | solution.py:873
  70.6 49.7 %collective-permute-start.10 = (bf16[2,96,768]{2,1,0:T(8,128)(2,1)S(1)}, bf16[2,96,768]{2,1,0:T(8,128)(2,1)S(1)}, u32[]{:S(2)}, u32[]{:S(2)}) collective-permute-start(bf16[2,96,768]{2,1,0:T(8,128)(2,1)S(1)} %pad_maximum_fusion.refs_0_), channel_id=1, source_target_pairs={{0,8},{4,12},{8,0},{12,4},{16,24},{20,28},{24,16},{28,20},{1,9},{5... | collective-permute-start | bytes 884744 | tf_op jit(solution)/shard_map/ppermute | solution.py:873
  71.4 48.9 %collective-permute-start.11 = (bf16[2,96,768]{2,1,0:T(8,128)(2,1)S(1)}, bf16[2,96,768]{2,1,0:T(8,128)(2,1)}, u32[]{:S(2)}, u32[]{:S(2)}) collective-permute-start(bf16[2,96,768]{2,1,0:T(8,128)(2,1)S(1)} %pad_maximum_fusion.refs_0_), channel_id=1, source_target_pairs={{0,16},{4,20},{8,24},{12,28},{16,0},{20,4},{24,8},{28,12},{1,17},{... | collective-permute-start | bytes 884744 | tf_op jit(solution)/shard_map/ppermute | solution.py:873
  73.2 47.1 %collective-permute-start.12 = (bf16[2,96,768]{2,1,0:T(8,128)(2,1)S(1)}, bf16[2,96,768]{2,1,0:T(8,128)(2,1)}, u32[]{:S(2)}, u32[]{:S(2)}) collective-permute-start(bf16[2,96,768]{2,1,0:T(8,128)(2,1)S(1)} %pad_maximum_fusion.refs_0_), channel_id=1, source_target_pairs={{0,24},{4,28},{8,16},{12,20},{16,8},{20,12},{24,0},{28,4},{1,25},{... | collective-permute-start | bytes 884744 | tf_op jit(solution)/shard_map/ppermute | solution.py:873
  75.1 45.3 %all-to-all-start.1 = ((bf16[32,24,768]{2,1,0:T(8,128)(2,1)}), bf16[32,24,768]{2,1,0:T(8,128)(2,1)}, u32[]{:S(2)}, u32[]{:S(2)}) async-start(bf16[32,24,768]{2,1,0:T(8,128)(2,1)} %bitcast.7), calls=%async_computation.1 | async-start | bytes 2359296 | tf_op jit(solution)/shard_map/all_to_all | solution.py:973
  79.8 153.7 %reduce-scatter.2.cloned.1.call-start = ((), (), s32[]{:S(2)}) async-start(), calls=%async_computation.4 | async-start | bytes 2654208 | tf_op jit(solution)/shard_map/reduce_scatter | solution.py:1003
  163.6 42.3 %collective-permute-start.14 = (bf16[2,2,256,768]{3,2,1,0:T(8,128)(2,1)S(1)}, bf16[2,2,256,768]{3,2,1,0:T(8,128)(2,1)S(1)}, u32[]{:S(2)}, u32[]{:S(2)}) collective-permute-start(bf16[2,2,256,768]{3,2,1,0:T(8,128)(2,1)S(1)} %fusion), channel_id=1, source_target_pairs={{0,2},{1,3},{2,0},{3,1},{4,6},{5,7},{6,4},{7,5},{8,10},{9,11},{10,... | collective-permute-start | bytes 4718600 | tf_op jit(solution)/shard_map/ppermute | solution.py:873
  207.1 53.0 %all-to-all-start.2 = ((bf16[32,28,576]{2,1,0:T(8,128)(2,1)}), bf16[32,28,576]{2,1,0:T(8,128)(2,1)S(1)}, u32[]{:S(2)}, u32[]{:S(2)}) async-start(bf16[32,28,576]{2,1,0:T(8,128)(2,1)} %copy-done.1), calls=%async_computation.2 | async-start | bytes 2621440 | tf_op jit(solution)/shard_map/all_to_all | solution.py:973
  213.3 38.9 %collective-permute-start.20 = (bf16[1,2,256,768]{3,2,1,0:T(8,128)(2,1)}, bf16[1,2,256,768]{3,2,1,0:T(8,128)(2,1)}, u32[]{:S(2)}, u32[]{:S(2)}) collective-permute-start(bf16[1,2,256,768]{3,2,1,0:T(8,128)(2,1)} %fusion.1), channel_id=1, source_target_pairs={{0,2},{1,3},{2,0},{3,1},{4,6},{5,7},{6,4},{7,5},{8,10},{9,11},{10,... | collective-permute-start | bytes 2359304 | tf_op jit(solution)/shard_map/ppermute | solution.py:873
  236.1 10.7 %collective-permute-start.23 = (bf16[24,768]{1,0:T(8,128)(2,1)}, bf16[24,768]{1,0:T(8,128)(2,1)S(1)}, u32[]{:S(2)}, u32[]{:S(2)}) collective-permute-start(bf16[24,768]{1,0:T(8,128)(2,1)} %get-tuple-element.120), channel_id=1, source_target_pairs={{0,3},{1,2},{2,1},{3,0},{4,7},{5,6},{6,5},{7,4},{8,11},{9,10},{10,... | collective-permute-start | bytes 110600 | tf_op jit(solution)/shard_map/ppermute | solution.py:873
  237.2 22.8 %collective-permute-start.24 = (bf16[24,768]{1,0:T(8,128)(2,1)}, bf16[24,768]{1,0:T(8,128)(2,1)S(1)}, u32[]{:S(2)}, u32[]{:S(2)}) collective-permute-start(bf16[24,768]{1,0:T(8,128)(2,1)} %get-tuple-element.121), channel_id=1, source_target_pairs={{0,7},{1,13},{2,3},{3,26},{4,0},{5,14},{6,20},{7,27},{8,8},{9,15},... | collective-permute-start | bytes 110600 | tf_op jit(solution)/shard_map/ppermute | solution.py:1022
  239.2 20.8 %collective-permute-start.25 = (bf16[24,768]{1,0:T(8,128)(2,1)}, bf16[24,768]{1,0:T(8,128)(2,1)S(1)}, u32[]{:S(2)}, u32[]{:S(2)}) collective-permute-start(bf16[24,768]{1,0:T(8,128)(2,1)} %get-tuple-element.122), channel_id=1, source_target_pairs={{0,0},{1,13},{2,19},{3,26},{4,7},{5,14},{6,20},{7,5},{8,8},{9,2},{... | collective-permute-start | bytes 110600 | tf_op jit(solution)/shard_map/ppermute | solution.py:1022
  244.8 15.3 %collective-permute-start.26 = (bf16[24,768]{1,0:T(8,128)(2,1)}, bf16[24,768]{1,0:T(8,128)(2,1)S(1)}, u32[]{:S(2)}, u32[]{:S(2)}) collective-permute-start(bf16[24,768]{1,0:T(8,128)(2,1)} %get-tuple-element.123), channel_id=1, source_target_pairs={{0,6},{1,13},{2,19},{3,4},{4,7},{5,1},{6,20},{7,26},{8,8},{9,14},{... | collective-permute-start | bytes 110600 | tf_op jit(solution)/shard_map/ppermute | solution.py:1022
  246.7 13.3 %collective-permute-start.27 = (bf16[24,768]{1,0:T(8,128)(2,1)}, bf16[24,768]{1,0:T(8,128)(2,1)S(1)}, u32[]{:S(2)}, u32[]{:S(2)}) collective-permute-start(bf16[24,768]{1,0:T(8,128)(2,1)} %get-tuple-element.124), channel_id=1, source_target_pairs={{0,6},{1,1},{2,19},{3,25},{4,7},{5,13},{6,20},{7,26},{8,8},{9,14},... | collective-permute-start | bytes 110600 | tf_op jit(solution)/shard_map/ppermute | solution.py:1022
  252.3 9.8 %collective-permute-start.28 = (bf16[24,768]{1,0:T(8,128)(2,1)}, bf16[24,768]{1,0:T(8,128)(2,1)S(1)}, u32[]{:S(2)}, u32[]{:S(2)}) collective-permute-start(bf16[24,768]{1,0:T(8,128)(2,1)} %get-tuple-element.125), channel_id=1, source_target_pairs={{0,6},{1,12},{2,19},{3,25},{4,7},{5,13},{6,3},{7,26},{8,0},{9,14},... | collective-permute-start | bytes 110600 | tf_op jit(solution)/shard_map/ppermute | solution.py:1022
  (44 other events, 305.1 us)
Sparse Core Ops, SparseCore 0:
  14.2 60.9 all-gather.4
  76.8 34.6 all-gather.6
  155.3 78.0 reduce-scatter.1
